TPU v7x, 32 devices: a whole 2x2x4 slice. The times are simulated.
32 devices in a mesh: dp: 16 (over z, x, core), tensor: 2 (over y).
Axes of the slice: x: 2, y: 2, z: 4, core: 2. Of those that a mesh axis runs over, the one named last changes fastest.
Arguments:
- tokens: bfloat16 [16384, 1024], P('dp'), may hold values from -6 to 6
- lengths: int32 [16, 8], replicated, may hold values from 1 to 384, 768 in all within a row
- pairing: int32 [16, 8], P('dp', 'tensor'), may hold values from 0 to 127
- w_qkv: bfloat16 [3, 1024, 1024], P(None, 'dp', 'tensor'), may hold values from -0.1875 to 0.1875
- b_qv: bfloat16 [2, 1024], P(None, 'tensor'), may hold values from -3 to 3
- w_out: bfloat16 [1024, 1024], P('tensor', 'dp'), may hold values from -0.5 to 0.5
- b_out: bfloat16 [1024], replicated, may hold values from -3 to 3
- ln_gain: bfloat16 [2, 1024], replicated, may hold values from 0.5 to 1.5
- ln_bias: bfloat16 [2, 1024], replicated, may hold values from -3 to 3
- w_up: bfloat16 [1024, 4096], P('dp', 'tensor'), may hold values from -0.1875 to 0.1875
- b_up: bfloat16 [4096], P('tensor'), may hold values from -3 to 3
- w_down: bfloat16 [4096, 1024], P('tensor', 'dp'), may hold values from -0.09375 to 0.09375
- b_down: bfloat16 [1024], replicated, may hold values from -3 to 3
- w_proj: bfloat16 [1024, 128], replicated, may hold values from -0.1875 to 0.1875
- cot: bfloat16 [16384, 1024], P(('dp', 'tensor')), may hold values from -6 to 6
Outputs:
- y_out: bfloat16 [16384, 1024], P(('dp', 'tensor'))
- loss: float32 [16, 8], P('dp', 'tensor')
- x_grad: bfloat16 [16384, 1024], P(('dp', 'tensor'))
- w_qkv_grad: float32 [3, 1024, 1024], P(None, 'dp', 'tensor')
- b_qv_grad: float32 [2, 1024], P(None, 'tensor')
- w_out_grad: float32 [1024, 1024], P('tensor', 'dp')
- b_out_grad: float32 [1024], replicated
- ln_gain_grad: float32 [2, 1024], replicated
- ln_bias_grad: float32 [2, 1024], replicated
- w_up_grad: float32 [1024, 4096], P('dp', 'tensor')
- b_up_grad: float32 [4096], P('tensor')
- w_down_grad: float32 [4096, 1024], P('tensor', 'dp')
- b_down_grad: float32 [1024], replicated
- w_proj_grad: float32 [1024, 128], replicated
Inputs may be any that keep to these rules, and one draw needn't show every extreme that they name: lengths[r] are the token counts of row r's 8 documents, which follow its 8 queries of 32 tokens; each row sums to 768 and its largest is 384. pairing[r, q] numbers a document over all rows: its row times 8 plus its place in that row.
All inputs are finite; a program needn't handle non-finite values.
Results may differ from a plain program's by a relative error of at most 0.02.
Values may be sent and summed in bfloat16 or wider, within the bound.
No kernel may reach another device: no remote copies, remote signals or barrier semaphores. Data moves between devices by JAX's collectives and lax.ppermute only.
A program may use at most 192 MiB of HBM per device.

v0:
```python
from functools import partial

import jax
import jax.numpy as jnp
from jax import lax
from jax.experimental import pallas as pl
from jax.experimental.pallas import tpu as pltpu
from jax.sharding import Mesh, PartitionSpec as P

HEAD_DIM = 64
QLEN = 32
NQ_ROW = 8
NDOC = 8


EPS_NORM = 1e-05
EPS_EMBED = 1e-06
POOL_TEMP = 0.1
LOSS_TEMP = 0.1
FULL_PRECISION = lax.Precision.HIGHEST
MASKED_SCORE = -1e30


def shortened(shard):

    def short(part):
        return part.astype(jnp.bfloat16) if part.dtype == jnp.float32 else part

    return jax.tree.map(short, shard)


def contract_rows(left, right, precision=None):
    return lax.dot_general(
        left,
        right,
        (((0,), (0,)), ((), ())),
        precision=precision,
        preferred_element_type=jnp.float32,
    )


def contract_cols(left, right, precision=None):
    return lax.dot_general(
        left,
        right,
        (((1,), (1,)), ((), ())),
        precision=precision,
        preferred_element_type=jnp.float32,
    )


def norm_forward(value, gain, shift):
    centred = value - jnp.mean(value, axis=1, keepdims=True)
    rstd = lax.rsqrt(jnp.mean(centred * centred, axis=1, keepdims=True) + EPS_NORM)
    unit = centred * rstd
    return (unit * gain + shift, unit, rstd)


def norm_backward(grad, unit, rstd, gain):
    scaled = grad * gain
    return rstd * (
        scaled
        - jnp.mean(scaled, axis=1, keepdims=True)
        - unit * jnp.mean(scaled * unit, axis=1, keepdims=True)
    )


def segments_of(row_lengths, token_count):
    position = jnp.arange(token_count, dtype=jnp.int32)
    query_span = NQ_ROW * QLEN
    ends = jnp.cumsum(row_lengths)
    passed = jnp.sum((position[:, None] - query_span >= ends[None, :]).astype(jnp.int32), axis=1)
    return jnp.where(position < query_span, position // QLEN, NQ_ROW + passed)


def normalize_cut(raw, width):
    part = raw[:, :width]
    scale = lax.rsqrt(jnp.sum(part * part, axis=1, keepdims=True) + EPS_EMBED)
    return (part * scale, part, scale)


def normalize_back(grad, part, scale, full_width):
    result = scale * grad - part * (scale * scale * scale) * jnp.sum(
        part * grad, axis=1, keepdims=True
    )
    return jnp.pad(result, ((0, 0), (0, full_width - grad.shape[1])))


def masked_scores(query_block, key_rows, block_segments, segments):
    scores = jnp.einsum(
        "qhd,khd->hqk", query_block, key_rows, preferred_element_type=jnp.float32
    ) * HEAD_DIM ** (-0.5)
    return jnp.where((block_segments[:, None] == segments[None, :])[None], scores, MASKED_SCORE)


def attend_forward(query_rows, key_rows, value_rows, segments, block_rows):
    token_count = query_rows.shape[0]

    def one_block(block_start):
        query_block = lax.dynamic_slice_in_dim(query_rows, block_start, block_rows, 0)
        block_segments = lax.dynamic_slice_in_dim(segments, block_start, block_rows, 0)
        scores = masked_scores(query_block, key_rows, block_segments, segments)
        highest = jnp.max(scores, axis=2, keepdims=True)
        expo = jnp.exp(scores - highest)
        totals = jnp.sum(expo, axis=2, keepdims=True)
        weights = (expo / totals).astype(jnp.bfloat16)
        mixed = jnp.einsum("hqk,khd->qhd", weights, value_rows, preferred_element_type=jnp.float32)
        return (mixed.astype(jnp.bfloat16), (highest + jnp.log(totals))[:, :, 0])

    starts = jnp.arange(token_count // block_rows, dtype=jnp.int32) * block_rows
    mixed, log_totals = lax.map(one_block, starts)
    return (mixed.reshape(token_count, -1), log_totals)


def attend_backward(query_rows, key_rows, value_rows, segments, log_totals, grad_mixed, block_rows):
    token_count, local_heads, head_size = query_rows.shape
    scale = HEAD_DIM ** (-0.5)
    grad_heads = grad_mixed.reshape(token_count, local_heads, head_size)

    def one_block(carried, inputs):
        grad_keys, grad_values = carried
        block_start, block_lse = inputs
        query_block = lax.dynamic_slice_in_dim(query_rows, block_start, block_rows, 0)
        grad_block = lax.dynamic_slice_in_dim(grad_heads, block_start, block_rows, 0)
        block_segments = lax.dynamic_slice_in_dim(segments, block_start, block_rows, 0)
        scores = masked_scores(query_block, key_rows, block_segments, segments)
        probs = jnp.exp(scores - block_lse[:, :, None])
        grad_probs = jnp.einsum(
            "qhd,khd->hqk", grad_block, value_rows, preferred_element_type=jnp.float32
        )
        inner = jnp.sum(probs * grad_probs, axis=2, keepdims=True)
        grad_scores = (probs * (grad_probs - inner)).astype(jnp.bfloat16)
        grad_query = (
            jnp.einsum("hqk,khd->qhd", grad_scores, key_rows, preferred_element_type=jnp.float32)
            * scale
        )
        grad_keys = (
            grad_keys
            + jnp.einsum(
                "hqk,qhd->khd", grad_scores, query_block, preferred_element_type=jnp.float32
            )
            * scale
        )
        grad_values = grad_values + jnp.einsum(
            "hqk,qhd->khd",
            probs.astype(jnp.bfloat16),
            grad_block,
            preferred_element_type=jnp.float32,
        )
        return ((grad_keys, grad_values), grad_query)

    starts = jnp.arange(token_count // block_rows, dtype=jnp.int32) * block_rows
    zero_rows = jnp.zeros(key_rows.shape, jnp.float32)
    (grad_keys, grad_values), grad_queries = lax.scan(
        one_block, (zero_rows, zero_rows), (starts, log_totals)
    )
    flat_width = local_heads * head_size
    return (
        grad_queries.reshape(token_count, flat_width),
        grad_keys.reshape(token_count, flat_width),
        grad_values.reshape(token_count, flat_width),
    )


def local(
    tokens,
    lengths,
    pairing,
    w_qkv,
    b_qv,
    w_out,
    b_out,
    ln_gain,
    ln_bias,
    w_up,
    b_up,
    w_down,
    b_down,
    w_proj,
    cot,
):
    tensor_count = lax.axis_size("tensor")
    tensor_index = lax.axis_index("tensor")
    data_index = lax.axis_index("dp")
    token_count = tokens.shape[0]
    share_rows = token_count // tensor_count
    block_rows = min(512, token_count)
    own_start = tensor_index * share_rows
    full_qkv, full_out, full_up, full_down = (
        lax.all_gather(w_qkv, "dp", axis=1, tiled=True),
        lax.all_gather(w_out, "dp", axis=1, tiled=True),
        lax.all_gather(w_up, "dp", axis=0, tiled=True),
        lax.all_gather(w_down, "dp", axis=1, tiled=True),
    )
    head_width = full_qkv.shape[2]
    local_heads = head_width // HEAD_DIM
    row_lengths = lax.dynamic_index_in_dim(lengths, data_index, 0, keepdims=False)
    segments = segments_of(row_lengths, token_count)
    projected = jnp.einsum("td,kdw->ktw", tokens, full_qkv, preferred_element_type=jnp.float32)
    qv_bias = b_qv.astype(jnp.float32)
    query_rows = (
        (projected[0] + qv_bias[0]).astype(jnp.bfloat16).reshape(token_count, local_heads, HEAD_DIM)
    )
    key_rows = projected[1].astype(jnp.bfloat16).reshape(token_count, local_heads, HEAD_DIM)
    value_rows = (
        (projected[2] + qv_bias[1]).astype(jnp.bfloat16).reshape(token_count, local_heads, HEAD_DIM)
    )
    mixed, log_totals = attend_forward(query_rows, key_rows, value_rows, segments, block_rows)
    attn_terms = jnp.dot(mixed, full_out, preferred_element_type=jnp.float32)
    attn_sum = lax.psum_scatter(
        attn_terms.astype(jnp.bfloat16), "tensor", scatter_dimension=0, tiled=True
    ).astype(jnp.float32)
    own_tokens = lax.dynamic_slice_in_dim(tokens, own_start, share_rows, 0).astype(jnp.float32)
    gains = ln_gain.astype(jnp.float32)
    shifts = ln_bias.astype(jnp.float32)
    normed, unit_one, rstd_one = norm_forward(
        own_tokens + attn_sum + b_out.astype(jnp.float32), gains[0], shifts[0]
    )
    normed_all = lax.all_gather(normed.astype(jnp.bfloat16), "tensor", axis=0, tiled=True)
    up_value = jnp.dot(normed_all, full_up, preferred_element_type=jnp.float32) + b_up.astype(
        jnp.float32
    )
    activation = jax.nn.gelu(up_value, approximate=False).astype(jnp.bfloat16)
    ffn_terms = jnp.dot(activation, full_down, preferred_element_type=jnp.float32)
    ffn_sum = lax.psum_scatter(
        ffn_terms.astype(jnp.bfloat16), "tensor", scatter_dimension=0, tiled=True
    ).astype(jnp.float32)
    result, unit_two, rstd_two = norm_forward(
        normed + ffn_sum + b_down.astype(jnp.float32), gains[1], shifts[1]
    )
    result_low = result.astype(jnp.bfloat16)
    embed = jnp.dot(result_low, w_proj, preferred_element_type=jnp.float32).astype(jnp.bfloat16)
    embed_all = lax.all_gather(embed, ("dp", "tensor"), axis=0, tiled=True)
    row_count = lengths.shape[0]
    proj_width = w_proj.shape[1]
    widths = (proj_width, 3 * proj_width // 4, proj_width // 2)
    per_device = pairing.shape[1]
    query_count = per_device * QLEN
    query_span = NQ_ROW * QLEN
    emb_rows = embed_all.reshape(row_count, token_count, proj_width)
    my_row = lax.dynamic_index_in_dim(emb_rows, data_index, 0, keepdims=False)
    query_raw = lax.dynamic_slice_in_dim(my_row, tensor_index * query_count, query_count, 0).astype(
        jnp.float32
    )
    query_levels = [normalize_cut(query_raw, width) for width in widths]
    query_units = [level_parts[0].astype(jnp.bfloat16) for level_parts in query_levels]
    doc_numbers = jnp.arange(NDOC, dtype=jnp.int32)

    def row_pool(carried, inputs):
        row_emb, lengths_row = inputs
        row_hot = (
            segments_of(lengths_row, token_count)[:, None] == NQ_ROW + doc_numbers[None, :]
        ).astype(jnp.float32)
        row_raw = row_emb.astype(jnp.float32)
        pooled_list = []
        sums_list = []
        for width, query_unit in zip(widths, query_units):
            doc_unit = normalize_cut(row_raw, width)[0].astype(jnp.bfloat16)
            expo = jnp.exp(contract_cols(query_unit, doc_unit) / POOL_TEMP)
            sums = jnp.dot(expo, row_hot, precision=FULL_PRECISION)
            pooled = POOL_TEMP * jnp.log(sums / lengths_row.astype(jnp.float32))
            pooled_list.append(jnp.sum(pooled.reshape(per_device, QLEN, NDOC), axis=1))
            sums_list.append(sums)
        return (carried, (jnp.stack(pooled_list), jnp.stack(sums_list)))

    _, (row_scores, row_sums) = lax.scan(row_pool, 0, (emb_rows, lengths))
    logits = (
        jnp.transpose(row_scores, (2, 1, 0, 3)).reshape(per_device, 3, row_count * NDOC) / LOSS_TEMP
    )
    own_pairs = pairing[0]
    target = jnp.take_along_axis(
        logits, jnp.broadcast_to(own_pairs[:, None, None], (per_device, 3, 1)), axis=2
    )[:, :, 0]
    loss_out = jnp.sum(jax.nn.logsumexp(logits, axis=2) - target, axis=1).reshape(1, per_device)
    picked = (
        jnp.arange(row_count * NDOC, dtype=jnp.int32)[None, None, :] == own_pairs[:, None, None]
    ).astype(jnp.float32)
    grad_logits = (jax.nn.softmax(logits, axis=2) - picked) / LOSS_TEMP
    grad_rows = jnp.transpose(grad_logits.reshape(per_device, 3, row_count, NDOC), (2, 1, 0, 3))
    coefficient = jnp.repeat(grad_rows, QLEN, axis=2) / row_sums

    def row_back(carried, inputs):
        row_emb, lengths_row, row_coef = inputs
        row_hot = (
            segments_of(lengths_row, token_count)[:, None] == NQ_ROW + doc_numbers[None, :]
        ).astype(jnp.float32)
        row_raw = row_emb.astype(jnp.float32)
        new_carried = []
        row_grad = jnp.zeros((token_count, proj_width), jnp.float32)
        for level_index in range(3):
            width = widths[level_index]
            doc_unit_f, doc_part, doc_scale = normalize_cut(row_raw, width)
            doc_unit = doc_unit_f.astype(jnp.bfloat16)
            expo = jnp.exp(contract_cols(query_units[level_index], doc_unit) / POOL_TEMP)
            spread = contract_cols(row_coef[level_index], row_hot, FULL_PRECISION)
            grad_sim = (expo * spread).astype(jnp.bfloat16)
            new_carried.append(
                carried[level_index]
                + jnp.dot(grad_sim, doc_unit, preferred_element_type=jnp.float32)
            )
        return (tuple(new_carried), row_grad)

    zero_query = tuple((jnp.zeros((query_count, width), jnp.float32) for width in widths))
    query_grads, doc_grads = lax.scan(row_back, zero_query, (emb_rows, lengths, coefficient))
    grad_query = jnp.zeros((query_count, proj_width), jnp.float32)
    for level_index in range(3):
        level_parts = query_levels[level_index]
        grad_query = grad_query + normalize_back(
            query_grads[level_index], level_parts[1], level_parts[2], proj_width
        )
    coef_mine = jnp.transpose(coefficient, (2, 1, 0, 3)).reshape(query_count, 3, row_count * NDOC)
    coef_all, grad_query_all = (
        lax.all_gather(shortened(coef_mine), ("dp", "tensor"), axis=0, tiled=True).astype(
            coef_mine.dtype
        ),
        lax.all_gather(
            grad_query.astype(jnp.bfloat16), ("dp", "tensor"), axis=0, tiled=True
        ).astype(grad_query.dtype),
    )
    own_raw = embed.astype(jnp.float32)
    own_segments = lax.dynamic_slice_in_dim(segments, own_start, share_rows, 0)
    own_docs = jnp.where(own_segments >= NQ_ROW, data_index * NDOC + own_segments - NQ_ROW, -1)
    own_hot = (own_docs[:, None] == jnp.arange(row_count * NDOC, dtype=jnp.int32)[None, :]).astype(
        jnp.float32
    )
    queries_all = (
        emb_rows[:, :query_span].reshape(row_count * query_span, proj_width).astype(jnp.float32)
    )
    grad_embed = jnp.zeros((share_rows, proj_width), jnp.float32)
    for level_index in range(3):
        width = widths[level_index]
        query_unit_all = normalize_cut(queries_all, width)[0].astype(jnp.bfloat16)
        doc_unit_f, doc_part, doc_scale = normalize_cut(own_raw, width)
        expo = jnp.exp(contract_cols(query_unit_all, doc_unit_f.astype(jnp.bfloat16)) / POOL_TEMP)
        spread = contract_cols(coef_all[:, level_index], own_hot, FULL_PRECISION)
        grad_sim = (expo * spread).astype(jnp.bfloat16)
        grad_doc = contract_rows(grad_sim, query_unit_all)
        grad_embed = grad_embed + normalize_back(grad_doc, doc_part, doc_scale, proj_width)
    row_query_grads = lax.dynamic_slice_in_dim(
        grad_query_all, data_index * query_span, query_span, 0
    )
    padded = jnp.pad(row_query_grads, ((0, token_count - query_span), (0, 0)))
    grad_embed = grad_embed + lax.dynamic_slice_in_dim(padded, own_start, share_rows, 0)
    proj_float = w_proj.astype(jnp.float32)
    grad_result = cot.astype(jnp.float32) + contract_cols(grad_embed, proj_float, FULL_PRECISION)
    proj_grad = contract_rows(result_low.astype(jnp.float32), grad_embed, FULL_PRECISION)
    gain_two = jnp.sum(grad_result * unit_two, axis=0)
    shift_two = jnp.sum(grad_result, axis=0)
    grad_second = norm_backward(grad_result, unit_two, rstd_two, gains[1])
    grad_ffn = grad_second.astype(jnp.bfloat16)
    down_bias = jnp.sum(grad_ffn.astype(jnp.float32), axis=0)
    grad_ffn_all = lax.all_gather(grad_ffn, "tensor", axis=0, tiled=True)
    grad_act = contract_cols(grad_ffn_all, full_down)
    down_grad = contract_rows(activation, grad_ffn_all)
    _, gelu_pull = jax.vjp(partial(jax.nn.gelu, approximate=False), up_value)
    grad_up = gelu_pull(grad_act)[0].astype(jnp.bfloat16)
    up_bias = jnp.sum(grad_up.astype(jnp.float32), axis=0)
    up_grad = contract_rows(normed_all, grad_up)
    normed_terms = contract_cols(grad_up, full_up)
    grad_normed = (
        lax.psum_scatter(
            normed_terms.astype(jnp.bfloat16), "tensor", scatter_dimension=0, tiled=True
        ).astype(jnp.float32)
        + grad_second
    )
    gain_one = jnp.sum(grad_normed * unit_one, axis=0)
    shift_one = jnp.sum(grad_normed, axis=0)
    grad_first = norm_backward(grad_normed, unit_one, rstd_one, gains[0])
    grad_attn = grad_first.astype(jnp.bfloat16)
    out_bias = jnp.sum(grad_attn.astype(jnp.float32), axis=0)
    grad_attn_all = lax.all_gather(grad_attn, "tensor", axis=0, tiled=True)
    out_grad = contract_rows(mixed, grad_attn_all)
    grad_mixed = contract_cols(grad_attn_all, full_out).astype(jnp.bfloat16)
    grad_q, grad_k, grad_v = attend_backward(
        query_rows, key_rows, value_rows, segments, log_totals, grad_mixed, block_rows
    )
    stacked_grads = jnp.stack(
        [grad_q.astype(jnp.bfloat16), grad_k.astype(jnp.bfloat16), grad_v.astype(jnp.bfloat16)]
    )
    qkv_grad = jnp.einsum("td,ktw->kdw", tokens, stacked_grads, preferred_element_type=jnp.float32)
    input_terms = jnp.einsum(
        "ktw,kdw->td", stacked_grads, full_qkv, preferred_element_type=jnp.float32
    )
    grad_input = (
        lax.psum_scatter(
            input_terms.astype(jnp.bfloat16), "tensor", scatter_dimension=0, tiled=True
        ).astype(jnp.float32)
        + grad_first
    )
    qv_grad = jnp.stack(
        [
            jnp.sum(stacked_grads[0].astype(jnp.float32), axis=0),
            jnp.sum(stacked_grads[2].astype(jnp.float32), axis=0),
        ]
    )
    qkv_part, out_part, up_part, down_part = (
        lax.psum_scatter(
            qkv_grad.astype(jnp.bfloat16), "dp", scatter_dimension=1, tiled=True
        ).astype(jnp.float32),
        lax.psum_scatter(
            out_grad.astype(jnp.bfloat16), "dp", scatter_dimension=1, tiled=True
        ).astype(jnp.float32),
        lax.psum_scatter(
            up_grad.astype(jnp.bfloat16), "dp", scatter_dimension=0, tiled=True
        ).astype(jnp.float32),
        lax.psum_scatter(
            down_grad.astype(jnp.bfloat16), "dp", scatter_dimension=1, tiled=True
        ).astype(jnp.float32),
    )
    gain_sum, shift_sum, out_bias_sum, down_bias_sum, proj_sum = lax.psum(
        (
            jnp.stack([gain_one, gain_two]),
            jnp.stack([shift_one, shift_two]),
            out_bias,
            down_bias,
            proj_grad,
        ),
        ("dp", "tensor"),
    )
    qv_sum, up_bias_sum = lax.psum((qv_grad, up_bias), "dp")
    return (
        result_low,
        loss_out,
        grad_input.astype(jnp.bfloat16),
        qkv_part,
        qv_sum,
        out_part,
        out_bias_sum,
        gain_sum,
        shift_sum,
        up_part,
        up_bias_sum,
        down_part,
        down_bias_sum,
        proj_sum,
    )


SWAP = [(0, 1), (1, 0)]
TURN = [(0, 0), (1, 2), (2, 1), (3, 3)]
FAR = [(0, 3), (3, 0), (1, 2), (2, 1)]
NEAR = [(0, 1), (1, 0), (2, 3), (3, 2)]
BF = jnp.bfloat16
F32 = jnp.float32


def dot(left, right):
    return jnp.dot(left, right, preferred_element_type=F32)


CORES = ("c", "y")


def tie(value, *others):
    return lax.optimization_barrier((value,) + others)[0]


def tie_all(values, *others):
    return lax.optimization_barrier(tuple(values) + others)[: len(values)]


def exchange(*moves):
    return lax.optimization_barrier(
        tuple(lax.ppermute(value, axis, steps) for value, axis, steps in moves)
    )


def swap(value, axis):
    return lax.ppermute(value, axis, SWAP)


def pair_up(first, second, own_index, axis):
    return jnp.where(
        own_index == 0, jnp.stack([first, second], axis), jnp.stack([second, first], axis)
    )


def far_pair(value, far, z):
    return jnp.where(z < 2, jnp.stack([value, far]), jnp.stack([far, value]))


def whole_line(pair, other, z):
    return jnp.where(
        (z == 0) | (z == 3),
        jnp.stack([pair[0], other[0], other[1], pair[1]]),
        jnp.stack([other[0], pair[0], pair[1], other[1]]),
    )


def first_moves(line):
    half = line.shape[1] // 2
    return ((line[:, :half], "x", SWAP), (line[:, half:], "y", SWAP))


def first_parts(line, moved, x, y):
    half = line.shape[1] // 2
    return (pair_up(line[:, :half], moved[0], x, 1), pair_up(line[:, half:], moved[1], y, 1))


def last_moves(parts):
    return ((parts[0], "y", SWAP), (parts[1], "x", SWAP))


def full_rows(parts, moved, x, y):
    low = pair_up(parts[0], moved[0], y, 2)
    high = pair_up(parts[1], moved[1], x, 1)
    return jnp.concatenate([low, high], axis=3).reshape(-1, low.shape[-1])


def at(blocks, index, axis):
    return lax.dynamic_index_in_dim(blocks, index, axis, keepdims=False)


def side_move(blocks, axis_name, own_index, axis):
    return (at(blocks, 1 - own_index, axis).astype(BF), axis_name, SWAP)


def side_sum(blocks, got, own_index, axis):
    return at(blocks, own_index, axis).astype(F32) + got.astype(F32)


def near_move(line, z):
    ends = (z == 0) | (z == 3)
    outer, inner = jnp.stack([line[0], line[3]]), line[1:3]
    return (jnp.where(ends, inner, outer).astype(BF), "z", NEAR)


def near_sum(line, got, z):
    ends = (z == 0) | (z == 3)
    return jnp.where(ends, jnp.stack([line[0], line[3]]), line[1:3]) + got.astype(F32)


def far_move(pair, z):
    return (jnp.where(z < 2, pair[1], pair[0]).astype(BF), "z", FAR)


def far_sum(pair, got, z):
    return jnp.where(z < 2, pair[0], pair[1]) + got.astype(F32)


def blocks_of(left, right):
    return contract_rows(left, right).astype(BF).reshape(4, 2, 2, 64, right.shape[1])


def sum_moves(blocks, x, y):
    half = blocks.shape[3] // 2
    return (
        side_move(blocks[..., :half, :], "x", x, 1),
        side_move(blocks[..., half:, :], "y", y, 2),
    )


def sum_parts(blocks, moved, x, y):
    half = blocks.shape[3] // 2
    return (
        side_sum(blocks[..., :half, :], moved[0], x, 1),
        side_sum(blocks[..., half:, :], moved[1], y, 2),
    )


def line_moves(parts, x, y):
    return (side_move(parts[0], "y", y, 1), side_move(parts[1], "x", x, 1))


def line_of(parts, moved, x, y):
    return jnp.concatenate(
        [side_sum(parts[0], moved[0], y, 1), side_sum(parts[1], moved[1], x, 1)], axis=1
    )


def tile_bounds(row_lengths, token_count):
    ends = jnp.cumsum(row_lengths)
    span = NQ_ROW * QLEN
    first = jnp.arange(token_count // TILE, dtype=jnp.int32) * TILE - span
    last = first + TILE - 1
    begin = jnp.max(jnp.where(ends[None, :] <= first[:, None], ends[None, :], 0), axis=1)
    end = jnp.min(jnp.where(ends[None, :] > last[:, None], ends[None, :], token_count), axis=1)
    low = jnp.where(first < 0, 0, (begin + span) // TILE)
    high = jnp.where(first < 0, 1, (end + span + TILE - 1) // TILE)
    return jnp.stack([low, high]).astype(jnp.int32)


def token_spans(row_lengths, token_count):
    ends = jnp.cumsum(row_lengths)[:, None]
    span = NQ_ROW * QLEN
    place = jnp.arange(token_count, dtype=jnp.int32)[None, :]
    doc = place - span
    begin = jnp.max(jnp.where(ends <= doc, ends, 0), axis=0) + span
    end = jnp.min(jnp.where(ends > doc, ends, token_count), axis=0) + span
    query = place[0] // QLEN * QLEN
    return jnp.stack(
        [jnp.where(doc[0] < 0, query, begin), jnp.where(doc[0] < 0, query + QLEN, end)]
    ).astype(jnp.int32)


def rows_of(value, start, count):
    return lax.dynamic_slice_in_dim(value, start, count, 0)


TILE = 256
KEYS = 256
NEG = -1e30


def exact(left, right, dims):
    return lax.dot_general(left, right, (dims, ((), ())), preferred_element_type=F32)


def head_masks(value):
    lane = lax.broadcasted_iota(jnp.int32, value.shape, 1)
    zero = jnp.zeros_like(value)
    return (jnp.where(lane < HEAD_DIM, value, zero), jnp.where(lane < HEAD_DIM, zero, value))


def key_shift(step, spans):
    place = step * KEYS + lax.broadcasted_iota(jnp.int32, (KEYS, TILE), 0)
    inside = (place >= spans[0:1, :]) & (place < spans[1:2, :])
    return jnp.where(inside, 0.0, NEG)


def attend_kernel(bounds, own_ref, qkv_ref, spans, out_ref, lse_ref, held):
    block = pl.program_id(0)
    groups = 2
    pairs = out_ref.shape[1] // 128
    per_group = pairs // groups

    def column(pair, part):
        start = ((pair // per_group) * 3 + part) * per_group + pair % per_group
        return slice(start * 128, (start + 1) * 128)

    queries = [head_masks(own_ref[:, column(pair, 0)] * HEAD_DIM**-0.5) for pair in range(pairs)]
    heads = [(pair, head) for pair in range(pairs) for head in range(2)]

    def score(step, highest):
        rows = pl.ds(pl.multiple_of(step * KEYS, KEYS), KEYS)
        shift = key_shift(step, spans)
        fresh = []
        for index, (pair, head) in enumerate(heads):
            keys = qkv_ref[rows, column(pair, 1)]
            scores = exact(keys, queries[pair][head], ((1,), (1,))) + shift
            held[index, rows, :] = scores
            fresh.append(jnp.maximum(highest[index], jnp.max(scores, axis=0, keepdims=True)))
        return tuple(fresh)

    low = jnp.full((1, TILE), NEG, F32)
    highest = lax.fori_loop(bounds[0, block], bounds[1, block], score, (low,) * len(heads))

    def mix(step, carried):
        rows = pl.ds(pl.multiple_of(step * KEYS, KEYS), KEYS)
        fresh = []
        for index, (pair, head) in enumerate(heads):
            values = qkv_ref[rows, column(pair, 2)]
            total, mixed = carried[index]
            expo = jnp.exp(held[index, rows, :] - highest[index])
            product = exact(values, expo.astype(BF), ((0,), (0,)))
            fresh.append(
                (
                    total + jnp.sum(expo, axis=0, keepdims=True),
                    mixed + product[head * HEAD_DIM : (head + 1) * HEAD_DIM],
                )
            )
        return tuple(fresh)

    start = (jnp.zeros((1, TILE), F32), jnp.zeros((HEAD_DIM, TILE), F32))
    parts = lax.fori_loop(bounds[0, block], bounds[1, block], mix, (start,) * len(heads))
    for pair in range(pairs):
        both = [parts[2 * pair + head][1] / parts[2 * pair + head][0] for head in range(2)]
        mixed = jnp.transpose(jnp.concatenate(both, axis=0))
        out_ref[:, pair * 128 : (pair + 1) * 128] = mixed.astype(BF)
    for index in range(len(heads)):
        lse_ref[index : index + 1, :] = highest[index] + jnp.log(parts[index][0])


def attend(bounds, qkv, spans):
    count, wide = qkv.shape
    heads = wide // 3 // HEAD_DIM
    whole = lambda shape: pl.BlockSpec(shape, lambda i: (0, 0))
    return pl.pallas_call(
        attend_kernel,
        grid=(count // TILE,),
        in_specs=[
            pl.BlockSpec(memory_space=pltpu.SMEM),
            pl.BlockSpec((TILE, wide), lambda i: (i, 0)),
            whole((count, wide)),
            pl.BlockSpec((2, TILE), lambda i: (0, i)),
        ],
        out_specs=[
            pl.BlockSpec((TILE, wide // 3), lambda i: (i, 0)),
            pl.BlockSpec((heads, TILE), lambda i: (0, i)),
        ],
        out_shape=[
            jax.ShapeDtypeStruct((count, wide // 3), BF),
            jax.ShapeDtypeStruct((heads, count), F32),
        ],
        scratch_shapes=[pltpu.VMEM((heads, count, TILE), F32)],
        compiler_params=pltpu.CompilerParams(vmem_limit_bytes=40 << 20),
        cost_estimate=pl.CostEstimate(
            flops=4 * heads * count * count * 64,
            transcendentals=heads * count * count // 2,
            bytes_accessed=4 * count * wide * 2,
        ),
    )(bounds, qkv, qkv, spans)


def attend_back_kernel(
    first, bounds, own_ref, qkv_ref, out_ref, grad_ref, lse_ref, spans,
    grads_ref, sums_ref, key_sum, value_sum,
):
    block = pl.program_id(0)
    pairs = out_ref.shape[1] // 128
    heads = [(pair, head) for pair in range(pairs) for head in range(2)]
    cut = lambda index: slice(index * 128, (index + 1) * 128)

    @pl.when(block == 0)
    def _():
        key_sum[...] = jnp.zeros_like(key_sum)
        value_sum[...] = jnp.zeros_like(value_sum)
        sums_ref[...] = jnp.zeros_like(sums_ref)

    queries = [head_masks(own_ref[:, cut(pair)] * HEAD_DIM**-0.5) for pair in range(pairs)]
    grads = [head_masks(grad_ref[:, cut(pair)]) for pair in range(pairs)]
    picks = head_masks(jnp.ones((8, 128), BF))
    inner = []
    for pair, head in heads:
        product = grad_ref[:, cut(pair)].astype(F32) * out_ref[:, cut(pair)].astype(F32)
        high = product.astype(BF)
        rest = (product - high.astype(F32)).astype(BF)
        inner.append(
            (
                exact(picks[head], high, ((1,), (1,))) + exact(picks[head], rest, ((1,), (1,)))
            )[0:1]
        )
    lse = [lse_ref[first + index : first + index + 1, :] for index in range(len(heads))]

    def step_of(step, carried):
        rows = pl.ds(pl.multiple_of(step * KEYS, KEYS), KEYS)
        shift = key_shift(step, spans)
        fresh = []
        for pair in range(pairs):
            keys = qkv_ref[rows, cut(pairs + pair)]
            values = qkv_ref[rows, cut(2 * pairs + pair)]
            key_add = jnp.zeros((KEYS, 128), F32)
            value_add = jnp.zeros((KEYS, 128), F32)
            for head in range(2):
                index = 2 * pair + head
                scores = exact(keys, queries[pair][head], ((1,), (1,))) + shift
                probs = jnp.exp(scores - lse[index])
                grad_probs = exact(values, grads[pair][head], ((1,), (1,)))
                grad_scores = (probs * (grad_probs - inner[index])).astype(BF)
                value_add = value_add + exact(probs.astype(BF), grads[pair][head], ((1,), (0,)))
                key_add = key_add + exact(grad_scores, queries[pair][head], ((1,), (0,)))
                product = exact(keys, grad_scores, ((0,), (0,)))
                fresh.append(carried[index] + product[head * HEAD_DIM : (head + 1) * HEAD_DIM])
            key_sum[rows, cut(pair)] += key_add
            value_sum[rows, cut(pair)] += value_add
        return tuple(fresh)

    start = jnp.zeros((HEAD_DIM, TILE), F32)
    parts = lax.fori_loop(bounds[0, block], bounds[1, block], step_of, (start,) * len(heads))
    own = pl.ds(pl.multiple_of(block * TILE, TILE), TILE)
    for pair in range(pairs):
        grad_query = jnp.concatenate([parts[2 * pair], parts[2 * pair + 1]], axis=0)
        grad_query = jnp.transpose(grad_query * HEAD_DIM**-0.5).astype(BF)
        grads_ref[own, cut(pair)] = grad_query
        sums_ref[0:1, cut(pair)] += jnp.sum(grad_query.astype(F32), axis=0, keepdims=True)

    @pl.when(block == pl.num_programs(0) - 1)
    def _():
        wide = pairs * 128
        grad_value = value_sum[...].astype(BF)
        grads_ref[:, wide : 2 * wide] = key_sum[...].astype(BF)
        grads_ref[:, 2 * wide :] = grad_value
        sums_ref[1:2, :] = jnp.sum(grad_value.astype(F32), axis=0, keepdims=True)


def attend_back(bounds, group, qkv, mixed, grad_mixed, lse, spans):
    count = qkv.shape[0]
    wide = qkv.shape[1] // 2
    heads = wide // 3 // HEAD_DIM
    whole = lambda shape: pl.BlockSpec(shape, lambda i: (0, 0))
    return pl.pallas_call(
        partial(attend_back_kernel, group * heads),
        grid=(count // TILE,),
        in_specs=[
            pl.BlockSpec(memory_space=pltpu.SMEM),
            pl.BlockSpec((TILE, wide), lambda i: (i, group)),
            pl.BlockSpec((count, wide), lambda i: (0, group)),
            pl.BlockSpec((TILE, wide // 3), lambda i: (i, group)),
            pl.BlockSpec((TILE, wide // 3), lambda i: (i, group)),
            pl.BlockSpec((2 * heads, TILE), lambda i: (0, i)),
            pl.BlockSpec((2, TILE), lambda i: (0, i)),
        ],
        out_specs=[whole((count, wide)), whole((8, wide // 3))],
        out_shape=[
            jax.ShapeDtypeStruct((count, wide), BF),
            jax.ShapeDtypeStruct((8, wide // 3), F32),
        ],
        scratch_shapes=[
            pltpu.VMEM((count, wide // 3), F32),
            pltpu.VMEM((count, wide // 3), F32),
        ],
        compiler_params=pltpu.CompilerParams(vmem_limit_bytes=40 << 20),
        cost_estimate=pl.CostEstimate(
            flops=10 * heads * count * count * 64,
            transcendentals=heads * count * count // 2,
            bytes_accessed=8 * count * wide * 2,
        ),
    )(
        bounds, qkv, qkv, mixed, grad_mixed,
        lse, spans,
    )


ERFC = (
    -1.26551223, 1.00002368, 0.37409196, 0.09678418, -0.18628806,
    0.27886807, -1.13520398, 1.48851587, -0.82215223, 0.17087277,
)


def gelu_pair(value):
    size = jnp.abs(value) * 0.5**0.5
    ratio = 1.0 / (1.0 + 0.5 * size)
    series = jnp.full_like(value, ERFC[-1])
    for factor in ERFC[-2::-1]:
        series = series * ratio + factor
    bell = jnp.exp(-size * size)
    tail = 0.5 * ratio * bell * jnp.exp(series)
    phi = jnp.where(value < 0.0, tail, 1.0 - tail)
    return (value * phi, phi + value * bell * 0.3989422804014327)


def expand_kernel(x_ref, w_ref, b_ref, *refs):
    act_ref, slope_ref = refs[-2:]
    rows = 256
    for start in range(0, x_ref.shape[0], rows):
        part = slice(start, start + rows)
        value = exact(x_ref[part, :], w_ref[...], ((1,), (0,))) + b_ref[...]
        active, slope = gelu_pair(value)
        act_ref[part, :] = active.astype(BF)
        slope_ref[part, :] = slope.astype(BF)


def expand(value, weight, shift, first, tiles, filled=()):
    count, depth = value.shape
    width = shift.shape[1]
    tile = 256
    column = lambda rows: pl.BlockSpec((rows, tile), lambda i: (0, first + i))
    return pl.pallas_call(
        expand_kernel,
        grid=(tiles,),
        in_specs=[
            pl.BlockSpec((count, depth), lambda i: (0, 0)),
            column(depth),
            column(1),
        ]
        + [pl.BlockSpec(memory_space=pl.ANY)] * len(filled),
        out_specs=[column(count)] * 2,
        out_shape=[jax.ShapeDtypeStruct((count, width), BF)] * 2,
        input_output_aliases={3: 0, 4: 1} if filled else {},
        compiler_params=pltpu.CompilerParams(vmem_limit_bytes=32 << 20),
        cost_estimate=pl.CostEstimate(
            flops=2 * count * depth * tile * tiles,
            transcendentals=3 * count * tile * tiles,
            bytes_accessed=2 * (count * depth + depth * tile * tiles + 2 * count * tile * tiles),
        ),
    )(value, weight, shift, *filled)


def cut_levels(raw, cuts):
    lane = lax.broadcasted_iota(jnp.int32, raw.shape, 1)
    levels = []
    for cut in cuts:
        part = jnp.where(lane < cut, raw, 0.0)
        scale = lax.rsqrt(jnp.sum(part * part, axis=1, keepdims=True) + EPS_EMBED)
        levels.append(((part * scale).astype(BF), part, scale))
    return levels


def pool_kernel(cuts, span, q_ref, d_ref, seg_ref, out_ref, units, hot):
    @pl.when(pl.program_id(0) == 0)
    def _():
        raw = d_ref[span:, :].astype(F32)
        for level, parts in enumerate(cut_levels(raw, cuts)):
            units[level] = parts[0]
        doc = lax.broadcasted_iota(jnp.int32, hot.shape, 0)
        hot[...] = (seg_ref[:, span:] == NQ_ROW + doc).astype(F32).astype(BF)

    levels = cut_levels(q_ref[...].astype(F32), cuts)
    for level in range(len(cuts)):
        similar = exact(units[level], levels[level][0], ((1,), (1,)))
        expo = jnp.exp(similar * (1.0 / POOL_TEMP))
        high = expo.astype(BF)
        rest = (expo - high.astype(F32)).astype(BF)
        out_ref[level * NDOC : (level + 1) * NDOC, :] = exact(
            hot[...], high, ((1,), (0,))
        ) + exact(hot[...], rest, ((1,), (0,)))


def pool(cuts, span, queries, row_embed, seg_row):
    count, width = queries.shape
    tokens = row_embed.shape[0]
    whole = lambda shape: pl.BlockSpec(shape, lambda i: (0, 0))
    return pl.pallas_call(
        partial(pool_kernel, cuts, span),
        grid=(count // TILE,),
        in_specs=[
            pl.BlockSpec((TILE, width), lambda i: (i, 0)),
            whole((tokens, width)),
            whole((1, tokens)),
        ],
        out_specs=pl.BlockSpec((len(cuts) * NDOC, TILE), lambda i: (0, i)),
        out_shape=jax.ShapeDtypeStruct((len(cuts) * NDOC, count), F32),
        scratch_shapes=[
            pltpu.VMEM((len(cuts), tokens - span, width), BF),
            pltpu.VMEM((NDOC, tokens - span), BF),
        ],
        compiler_params=pltpu.CompilerParams(vmem_limit_bytes=32 << 20),
        cost_estimate=pl.CostEstimate(
            flops=2 * len(cuts) * count * tokens * 256,
            transcendentals=len(cuts) * count * tokens,
            bytes_accessed=2 * (count + tokens) * width,
        ),
    )(queries, row_embed, seg_row)


def level_back(grad, part, scale):
    return scale * grad - part * (scale * scale * scale) * jnp.sum(
        part * grad, axis=1, keepdims=True
    )


def pool_back_kernel(
    cuts, span, q_ref, d_ref, seg_ref, coef_ref, q_out, d_out, units, units_t, hot, sums
):
    step = pl.program_id(0)

    @pl.when(step == 0)
    def _():
        raw = d_ref[span:, :].astype(F32)
        for level, parts in enumerate(cut_levels(raw, cuts)):
            units[level] = parts[0]
            units_t[level] = jnp.transpose(parts[0])
        doc = lax.broadcasted_iota(jnp.int32, hot.shape, 0)
        wanted = NQ_ROW + jnp.where(doc < NDOC, doc, doc - NDOC)
        hot[...] = (seg_ref[:, span:] == wanted).astype(F32).astype(BF)
        sums[...] = jnp.zeros_like(sums)

    levels = cut_levels(q_ref[...].astype(F32), cuts)
    total = jnp.zeros(q_ref.shape, F32)
    for level in range(len(cuts)):
        unit, part, scale = levels[level]
        similar = exact(units[level], unit, ((1,), (1,)))
        coef = coef_ref[level * NDOC : (level + 1) * NDOC, :]
        high = coef.astype(BF).astype(F32)
        both = jnp.concatenate([high, coef - high], axis=0).astype(BF)
        spread = exact(hot[...], both, ((0,), (0,)))
        grad = (jnp.exp(similar * (1.0 / POOL_TEMP)) * spread).astype(BF)
        sums[level] += exact(grad, unit, ((1,), (0,)))
        grad_unit = jnp.transpose(exact(units_t[level], grad, ((1,), (0,))))
        total = total + level_back(grad_unit, part, scale)
    q_out[...] = total.astype(BF)

    @pl.when(step == pl.num_programs(0) - 1)
    def _():
        raw = d_ref[span:, :].astype(F32)
        result = jnp.zeros(raw.shape, F32)
        for level, parts in enumerate(cut_levels(raw, cuts)):
            lane = lax.broadcasted_iota(jnp.int32, raw.shape, 1)
            grad = jnp.where(lane < cuts[level], sums[level], 0.0)
            result = result + level_back(grad, parts[1], parts[2])
        d_out[...] = result


def pool_back(cuts, span, queries, row_embed, seg_row, coef):
    count, width = queries.shape
    tokens = row_embed.shape[0]
    docs = tokens - span
    whole = lambda shape: pl.BlockSpec(shape, lambda i: (0, 0))
    return pl.pallas_call(
        partial(pool_back_kernel, cuts, span),
        grid=(count // TILE,),
        in_specs=[
            pl.BlockSpec((TILE, width), lambda i: (i, 0)),
            whole((tokens, width)),
            whole((1, tokens)),
            pl.BlockSpec((len(cuts) * NDOC, TILE), lambda i: (0, i)),
        ],
        out_specs=[pl.BlockSpec((TILE, width), lambda i: (i, 0)), whole((docs, width))],
        out_shape=[
            jax.ShapeDtypeStruct((count, width), BF),
            jax.ShapeDtypeStruct((docs, width), F32),
        ],
        scratch_shapes=[
            pltpu.VMEM((len(cuts), docs, width), BF),
            pltpu.VMEM((len(cuts), width, docs), BF),
            pltpu.VMEM((2 * NDOC, docs), BF),
            pltpu.VMEM((len(cuts), docs, width), F32),
        ],
        compiler_params=pltpu.CompilerParams(vmem_limit_bytes=32 << 20),
        cost_estimate=pl.CostEstimate(
            flops=2 * len(cuts) * count * docs * 512,
            transcendentals=len(cuts) * count * docs,
            bytes_accessed=4 * (count + tokens) * width,
        ),
    )(queries, row_embed, seg_row, coef)


def local_chip(
    tokens,
    lengths,
    pairing,
    w_qkv,
    b_qv,
    w_out,
    b_out,
    ln_gain,
    ln_bias,
    w_up,
    b_up,
    w_down,
    b_down,
    w_proj,
    cot,
):
    z, x, c, y = (lax.axis_index(name) for name in ("z", "x", "c", "y"))
    chip = 4 * z + 2 * x + y
    token_count, width = tokens.shape
    share = token_count // 2
    own_start, other_start = c * share, (1 - c) * share
    gains, shifts = ln_gain.astype(F32), ln_bias.astype(F32)

    half_width = w_qkv.shape[2]
    up_wide = w_up.shape[1]
    chip_count = lengths.shape[0]
    half_queries = NQ_ROW // 2
    query_total = chip_count * half_queries
    quarter = half_width // 2
    qkv_rows = jnp.concatenate(
        [w_qkv[k][:, g * quarter : (g + 1) * quarter] for g in range(2) for k in range(3)], axis=1
    )
    pair_rows = jnp.pad(pairing.astype(BF), ((0, 63), (0, 128 - half_queries)))
    mid_rows = jnp.concatenate([w_up, w_out.T, pair_rows], axis=1)
    bias = jnp.concatenate([b_qv.reshape(-1), b_up])[None].astype(F32)
    got = exchange(
        (qkv_rows, CORES, TURN), (tokens, "c", SWAP), (bias, "y", SWAP)
    )
    qkv_rows = got[0]
    row = jnp.where(c == y, tokens, got[1])
    bias = jnp.where(c == y, bias, got[2])
    (rest_rows,) = exchange(
        (tie(jnp.concatenate([mid_rows, w_down.T], axis=1), row), CORES, TURN)
    )
    (far,) = exchange((qkv_rows, "z", FAR))
    qkv_pair = far_pair(qkv_rows, far, z)
    mid_wide = mid_rows.shape[1]
    rest_rows = tie(rest_rows, qkv_pair)
    mid_rows, down_rows = rest_rows[:, :mid_wide], rest_rows[:, mid_wide:]
    got = exchange((qkv_pair, "z", NEAR), (mid_rows, "z", FAR))
    qkv_line = whole_line(qkv_pair, got[0], z)
    mid_pair = far_pair(mid_rows, got[1], z)
    got = exchange(*first_moves(qkv_line), (mid_pair, "z", NEAR))
    qkv_parts = first_parts(qkv_line, got, x, y)
    mid_line = whole_line(mid_pair, got[2], z)
    last = last_moves(qkv_parts)
    got = exchange(*last, (tie(down_rows, mid_line), "z", FAR), *first_moves(mid_line))
    full_qkv = full_rows(qkv_parts, got, x, y)
    down_pair = far_pair(down_rows, got[2], z)
    mid_parts = first_parts(mid_line, got[3:], x, y)
    (near,) = exchange((down_pair, "z", NEAR))
    down_line = whole_line(down_pair, near, z)
    got = exchange(*last_moves(mid_parts), *first_moves(down_line))
    full_mid = full_rows(mid_parts, got, x, y)
    down_parts = first_parts(down_line, got[2:], x, y)
    full_out = full_mid[:, up_wide : up_wide + half_width]
    pairs = full_mid[:, up_wide + half_width :].reshape(chip_count, 64, 128)
    pairs = pairs[:, 0, :half_queries].astype(jnp.int32).reshape(1, query_total)
    row_lengths = lax.dynamic_index_in_dim(lengths, chip, 0, keepdims=False)
    segments = segments_of(row_lengths, token_count)
    seg_row, spans = segments[None, :], token_spans(row_lengths, token_count)
    query_span = NQ_ROW * QLEN
    bounds = tile_bounds(row_lengths, token_count)
    no_bias = jnp.zeros((1, quarter), F32)
    qkv_bias = jnp.concatenate(
        [
            part
            for g in range(2)
            for part in (
                bias[:, g * quarter : (g + 1) * quarter],
                no_bias,
                bias[:, half_width + g * quarter : half_width + (g + 1) * quarter],
            )
        ],
        axis=1,
    )
    qkv = (dot(row, full_qkv) + qkv_bias).astype(BF)
    mixed, lse = attend(bounds, tie(qkv, down_line), spans)

    def row_sum(left, weight_t, transposed):
        times = contract_cols if transposed else dot
        theirs = swap(times(left(1), weight_t).astype(BF), "c")
        return times(left(0), weight_t) + theirs.astype(F32)

    def mixed_half(which):
        return rows_of(mixed, other_start if which else own_start, share)

    other_attn = swap(contract_cols(mixed_half(1), full_out).astype(BF), "c")
    other_attn, second_norm = lax.optimization_barrier(
        (other_attn, jnp.stack([gains[1], shifts[1]]))
    )
    second_norm = swap(second_norm, "c")
    second_norm, cot_given, *down_parts = lax.optimization_barrier(
        (second_norm, cot) + tuple(down_parts)
    )
    down_got = exchange(*last_moves(down_parts), (cot_given, CORES, TURN))
    own_cot = down_got[2]
    attn_sum = contract_cols(mixed_half(0), full_out) + other_attn.astype(F32)
    own_tokens = rows_of(row, own_start, share).astype(F32)
    normed, unit_one, rstd_one = norm_forward(
        own_tokens + attn_sum + b_out.astype(F32), gains[0], shifts[0]
    )
    normed_low = normed.astype(BF)
    normed_all = jnp.concatenate([normed_low, swap(normed_low, "c")], axis=0)
    activation, slope = expand(
        normed_all, full_mid, bias[:, 2 * half_width :], 0, up_wide // 256
    )
    full_down = full_rows(down_parts, down_got, x, y)
    ffn_sum = row_sum(
        lambda which: activation[which * share : (which + 1) * share], full_down, True
    )
    result, unit_two, rstd_two = norm_forward(
        normed + ffn_sum + b_down.astype(F32), second_norm[0], second_norm[1]
    )
    result_low = result.astype(BF)
    embed = dot(result_low, w_proj).astype(BF)

    other_embed = swap(embed, "c")
    row_embed = jnp.where(
        c == 0,
        jnp.concatenate([embed, other_embed], axis=0),
        jnp.concatenate([other_embed, embed], axis=0),
    )
    half_span = query_span // 2
    own_queries = rows_of(row_embed, c * half_span, half_span)
    chips = ("z", "x", "y")
    queries = lax.all_to_all(
        jnp.broadcast_to(own_queries[None], (chip_count,) + own_queries.shape), chips, 0, 0
    ).reshape(chip_count * half_span, -1)
    proj_width = w_proj.shape[1]
    cuts = (proj_width, 3 * proj_width // 4, proj_width // 2)
    sums = pool(cuts, query_span, queries, row_embed, seg_row)
    doc_sizes = jnp.tile(row_lengths.astype(F32), 3)[:, None]
    group = (
        jnp.arange(query_total * QLEN, dtype=jnp.int32)[:, None] // QLEN
        == jnp.arange(query_total, dtype=jnp.int32)[None, :]
    ).astype(F32)
    pooled = POOL_TEMP * jnp.log(sums / doc_sizes)
    logits = jnp.dot(pooled, group, precision=FULL_PRECISION) / LOSS_TEMP
    logits = logits.reshape(3, NDOC, query_total)
    doc_numbers = chip * NDOC + jnp.arange(NDOC, dtype=jnp.int32)
    picked = (doc_numbers[:, None] == pairs).astype(F32)
    own_high = jnp.max(logits, axis=1)
    own_lse = own_high + jnp.log(jnp.sum(jnp.exp(logits - own_high[:, None]), axis=1))
    own_target = jnp.sum(logits * picked, axis=1)
    notes = jnp.pad(jnp.concatenate([own_lse, own_target], axis=1), ((0, 5), (0, 0)))
    notes = lax.all_to_all(
        jnp.broadcast_to(notes[None], (chip_count,) + notes.shape), chips, 0, 0
    )
    chip_lse = notes[:, :3, :query_total]
    high = jnp.max(chip_lse, axis=0)
    all_lse = high + jnp.log(jnp.sum(jnp.exp(chip_lse - high), axis=0))
    target = jnp.sum(notes[:, :3, query_total:], axis=0)
    losses = jnp.sum(all_lse - target, axis=0).reshape(chip_count, half_queries)
    grad_logits = (jnp.exp(logits - all_lse[:, None]) - picked) / LOSS_TEMP
    coefficient = (
        lax.dot_general(
            grad_logits.reshape(3 * NDOC, query_total),
            group,
            (((1,), (1,)), ((), ())),
            precision=FULL_PRECISION,
        )
        / sums
    )
    query_grad, doc_grad = pool_back(cuts, query_span, queries, row_embed, seg_row, coefficient)
    grad_blocks = lax.all_to_all(
        query_grad.reshape(chip_count, half_span, proj_width), chips, 0, 0
    )
    own_query_grad = jnp.sum(grad_blocks.astype(F32), axis=0)
    row_grad = jnp.concatenate([jnp.zeros((query_span, proj_width), F32), doc_grad], axis=0)
    row_grad = lax.dynamic_update_slice_in_dim(row_grad, own_query_grad, c * half_span, 0)
    grad_embed = rows_of(row_grad, own_start, share) + swap(
        rows_of(row_grad, other_start, share), "c"
    )

    proj_low = w_proj
    grad_embed_low = grad_embed.astype(BF)
    grad_embed_rest = (grad_embed - grad_embed_low.astype(F32)).astype(BF)
    grad_result = own_cot.astype(F32) + (
        contract_cols(grad_embed_low, proj_low) + contract_cols(grad_embed_rest, proj_low)
    )
    proj_grad = contract_rows(result_low, grad_embed_low) + contract_rows(
        result_low, grad_embed_rest
    )
    gain_two = jnp.sum(grad_result * unit_two, axis=0)
    shift_two = jnp.sum(grad_result, axis=0)
    grad_second = norm_backward(grad_result, unit_two, rstd_two, second_norm[0])
    grad_ffn = grad_second.astype(BF)
    down_bias = jnp.sum(grad_ffn.astype(F32), axis=0)
    other_ffn = swap(grad_ffn, "c")
    grad_ffn_all = jnp.concatenate([grad_ffn, other_ffn], axis=0)
    down_blocks = blocks_of(grad_ffn_all, activation)
    down_moved = exchange(*sum_moves(down_blocks, x, y))
    grad_up = (dot(grad_ffn_all, full_down) * slope.astype(F32)).astype(BF)
    up_bias = jnp.sum(grad_up.astype(F32), axis=0)
    up_blocks = blocks_of(normed_all, tie(grad_up, *down_moved))
    full_up = full_mid[:, :up_wide]
    grad_normed = (
        row_sum(lambda which: grad_up[which * share : (which + 1) * share], full_up, True)
        + grad_second
    )
    gain_one = jnp.sum(grad_normed * unit_one, axis=0)
    shift_one = jnp.sum(grad_normed, axis=0)
    grad_first = norm_backward(grad_normed, unit_one, rstd_one, gains[0])
    grad_attn = grad_first.astype(BF)
    out_bias = jnp.sum(grad_attn.astype(F32), axis=0)
    other_attn = swap(grad_attn, "c")
    grad_attn_all = jnp.where(
        c == 0,
        jnp.concatenate([grad_attn, other_attn], axis=0),
        jnp.concatenate([other_attn, grad_attn], axis=0),
    )
    grad_mixed = dot(grad_attn_all, full_out).astype(BF)
    out_blocks = blocks_of(grad_attn_all, mixed)
    down_parts = sum_parts(down_blocks, down_moved, x, y)
    moved = exchange(*line_moves(down_parts, x, y), *sum_moves(up_blocks, x, y))
    down_line = line_of(down_parts, moved, x, y)
    up_parts = sum_parts(up_blocks, moved[2:], x, y)
    grad_mixed, out_blocks, down_line, *up_parts = lax.optimization_barrier(
        (grad_mixed, out_blocks, down_line) + tuple(up_parts)
    )
    moved = exchange(
        near_move(down_line, z), *line_moves(up_parts, x, y), *sum_moves(out_blocks, x, y)
    )
    grads_one, sums_one = attend_back(bounds, 0, qkv, mixed, grad_mixed, lse, spans)
    down_pair = near_sum(down_line, moved[0], z)
    up_line = line_of(up_parts, moved[1:], x, y)
    out_parts = sum_parts(out_blocks, moved[3:], x, y)
    grad_mixed, down_pair, up_line, *out_parts = lax.optimization_barrier(
        (grad_mixed, down_pair, up_line) + tuple(out_parts)
    )
    up_line, y_given, losses = lax.optimization_barrier((up_line, result_low, losses))
    moved = exchange(
        far_move(down_pair, z),
        near_move(up_line, z),
        *line_moves(out_parts, x, y),
        (y_given, CORES, TURN),
    )
    other_losses = swap(losses, "c")
    proj_given, other_losses, grad_mixed = lax.optimization_barrier(
        (rows_of(proj_grad, other_start, share), other_losses, grad_mixed)
    )
    proj_half = rows_of(proj_grad, own_start, share)
    other_proj = swap(proj_given, "c")
    grad_mixed, other_proj = lax.optimization_barrier((grad_mixed, other_proj))
    proj_half = proj_half + other_proj
    losses = jnp.where(c == y, losses, other_losses)
    loss_out = rows_of(losses, 4 * z + 2 * x + c, 1)
    grads_two, sums_two = attend_back(bounds, 1, qkv, mixed, grad_mixed, lse, spans)
    y_out = moved[4]
    down_part = far_sum(down_pair, moved[0], z)
    up_pair = near_sum(up_line, moved[1], z)
    out_line = line_of(out_parts, moved[2:], x, y)
    grads_one, grads_two, down_part, up_pair, out_line = lax.optimization_barrier(
        (grads_one, grads_two, down_part, up_pair, out_line)
    )
    shared = jnp.stack([gain_one, gain_two, shift_one, shift_two, out_bias, down_bias])
    half_sums = jnp.concatenate(
        [
            sums_one[0],
            sums_two[0],
            sums_one[1],
            sums_two[1],
            up_bias,
        ]
    )
    small = jnp.concatenate([shared.reshape(-1, 128), half_sums.reshape(-1, 128), proj_half])

    qkv_blocks = jnp.concatenate(
        [blocks_of(row, grads_one), blocks_of(row, grads_two)], axis=4
    )
    qkv_blocks, up_pair, out_line, down_part, small = lax.optimization_barrier(
        (qkv_blocks, up_pair, out_line, down_part, small)
    )
    moved = exchange(
        *sum_moves(qkv_blocks, x, y),
        far_move(up_pair, z),
        near_move(out_line, z),
        (small.astype(BF), "y", SWAP),
    )
    qkv_parts = sum_parts(qkv_blocks, moved, x, y)
    up_part = far_sum(up_pair, moved[2], z)
    out_pair = near_sum(out_line, moved[3], z)
    small = small + moved[4].astype(F32)

    def input_terms(start):
        return contract_cols(
            rows_of(grads_one, start, share), full_qkv[:, : 3 * quarter]
        ) + contract_cols(rows_of(grads_two, start, share), full_qkv[:, 3 * quarter :])

    other_terms = swap(input_terms(other_start).astype(BF), "c")
    grad_input = (input_terms(own_start) + other_terms.astype(F32) + grad_first).astype(BF)
    moved = exchange(*line_moves(qkv_parts, x, y), far_move(out_pair, z), (small.astype(BF), "x", SWAP))
    qkv_line = line_of(qkv_parts, moved, x, y)
    out_part = far_sum(out_pair, moved[2], z)
    small = small + moved[3].astype(F32)
    moved = exchange(
        near_move(qkv_line, z),
        (small.astype(BF), "z", FAR),
        (tie(grad_input, qkv_line), CORES, TURN),
    )
    qkv_pair = near_sum(qkv_line, moved[0], z)
    small = small + moved[1].astype(F32)
    grad_input = moved[2]
    ffn_part = jnp.concatenate([down_part, up_part], axis=1).astype(BF)
    moved = exchange(
        far_move(qkv_pair, z), (small.astype(BF), "z", NEAR), (tie(ffn_part, qkv_pair), CORES, TURN)
    )
    attn_part = jnp.concatenate([far_sum(qkv_pair, moved[0], z), out_part], axis=1).astype(BF)
    small = small + moved[1].astype(F32)
    ffn_part = moved[2].astype(F32)
    down_part, up_part = ffn_part[:, :up_wide], ffn_part[:, up_wide:]
    attn_part, other_small = exchange((attn_part, CORES, TURN), (small.astype(BF), "c", SWAP))
    attn_part = attn_part.astype(F32)
    other_small = other_small.astype(F32)
    qkv_part, out_part = attn_part[:, : 3 * half_width], attn_part[:, 3 * half_width :]
    shared_rows = 6 * width // 128
    small_rows = small.shape[0] - share
    shared = (small[:shared_rows] + other_small[:shared_rows]).reshape(6, width)
    half_sums = jnp.where(
        c == y, small[shared_rows:small_rows], other_small[shared_rows:small_rows]
    ).reshape(-1)
    proj_sum = pair_up(small[small_rows:], other_small[small_rows:], c, 0).reshape(width, -1)
    qkv_part = qkv_part.reshape(64, 2, 3, quarter).transpose(2, 0, 1, 3).reshape(3, 64, half_width)
    return (
        y_out,
        loss_out,
        grad_input,
        qkv_part,
        half_sums[: 2 * half_width].reshape(2, half_width),
        out_part.T,
        shared[4],
        shared[0:2],
        shared[2:4],
        up_part,
        half_sums[2 * half_width :],
        down_part.T,
        shared[5],
        proj_sum,
    )


IN_SPECS = (
    P("dp", None),
    P(),
    P("dp", "tensor"),
    P(None, "dp", "tensor"),
    P(None, "tensor"),
    P("tensor", "dp"),
    P(),
    P(),
    P(),
    P("dp", "tensor"),
    P("tensor"),
    P("tensor", "dp"),
    P(),
    P(),
    P(("dp", "tensor"), None),
)
OUT_SPECS = (
    P(("dp", "tensor"), None),
    P("dp", "tensor"),
    P(("dp", "tensor"), None),
    P(None, "dp", "tensor"),
    P(None, "tensor"),
    P("tensor", "dp"),
    P(),
    P(),
    P(),
    P("dp", "tensor"),
    P("tensor"),
    P("tensor", "dp"),
    P(),
    P(),
)


def solution(mesh):
    if mesh.devices.shape != (16, 2):
        return jax.shard_map(
            local, mesh=mesh, in_specs=IN_SPECS, out_specs=OUT_SPECS, check_vma=False
        )
    names = {"dp": ("z", "x", "c"), "tensor": ("y",)}

    def respec(spec):
        parts = []
        for entry in spec:
            axes = () if entry is None else entry if isinstance(entry, tuple) else (entry,)
            parts.append(tuple(name for axis in axes for name in names[axis]) or None)
        return P(*parts)

    chips = Mesh(mesh.devices.reshape(4, 2, 2, 2), ("z", "x", "c", "y"))
    return jax.shard_map(
        local_chip,
        mesh=chips,
        in_specs=tuple(respec(spec) for spec in IN_SPECS),
        out_specs=tuple(respec(spec) for spec in OUT_SPECS),
        check_vma=False,
    )
```

profile of v0, /device:TPU:1, one launch (start us, length us, event | category | flops | bytes accessed | tf_op | source)
XLA Modules:
  0.0 514.0 jit_solution(6808770451807347149)
XLA Ops:
  1.7 4.5 collective-permute-start
  10.2 1.9 fusion.39
  13.6 3.3 collective-permute-start.3
  18.7 3.6 collective-permute-start.5
  23.8 3.2 collective-permute-start.4
  27.0 3.6 collective-permute-done.5
  30.8 4.6 collective-permute-done.4
  35.4 9.2 %collective-permute-done.6 = bf16[64,2688]{1,0:T(8,128)(2,1)S(1)} collective-permute-done((bf16[64,2688]{1,0:T(8,128)(2,1)S(1)}, bf16[64,2688]{1,0:T(8,128)(2,1)S(1)}, u32[]{:S(2)}, u32[]{:S(2)}) %collective-permute-start.6) | collective-permute-done | bytes 344096 | tf_op jit(solution)/shard_map/ppermute | solution.py:464
  47.9 5.9 %collective-permute-done.7 = bf16[4,32,1536]{2,1,0:T(8,128)(2,1)S(1)} collective-permute-done((bf16[4,32,1536]{2,1,0:T(8,128)(2,1)S(1)}, bf16[4,32,1536]{2,1,0:T(8,128)(2,1)S(1)}, u32[]{:S(2)}, u32[]{:S(2)}) %collective-permute-start.7) | collective-permute-done | bytes 393248 | tf_op jit(solution)/shard_map/ppermute | solution.py:464
  54.7 7.4 %collective-permute-done.9 = bf16[2,64,2688]{2,1,0:T(8,128)(2,1)S(1)} collective-permute-done((bf16[2,64,2688]{2,1,0:T(8,128)(2,1)S(1)}, bf16[2,64,2688]{2,1,0:T(8,128)(2,1)S(1)}, u32[]{:S(2)}, u32[]{:S(2)}) %collective-permute-start.9) | collective-permute-done | bytes 688160 | tf_op jit(solution)/shard_map/ppermute | solution.py:464
  63.5 2.7 collective-permute-start.12
  68.1 2.5 collective-permute-done.12
  70.6 5.8 %collective-permute-done.13 = bf16[4,32,2688]{2,1,0:T(8,128)(2,1)S(1)} collective-permute-done((bf16[4,32,2688]{2,1,0:T(8,128)(2,1)S(1)}, bf16[4,32,2688]{2,1,0:T(8,128)(2,1)S(1)}, u32[]{:S(2)}, u32[]{:S(2)}) %collective-permute-start.13) | collective-permute-done | bytes 688160 | tf_op jit(solution)/shard_map/ppermute | solution.py:464
  76.4 16.8 %collective-permute-done.11 = bf16[4,2,32,1536]{3,2,1,0:T(8,128)(2,1)S(1)} collective-permute-done((bf16[4,2,32,1536]{3,2,1,0:T(8,128)(2,1)S(1)}, bf16[4,2,32,1536]{3,2,1,0:T(8,128)(2,1)S(1)}, u32[]{:S(2)}, u32[]{:S(2)}) %collective-permute-start.11) | collective-permute-done | bytes 786464 | tf_op jit(solution)/shard_map/ppermute | solution.py:464
  97.4 3.6 add_convert_fusion.own_ref.qkv_ref
  105.4 10.4 %shard_map.254 = (bf16[1024,512]{1,0:T(8,128)(2,1)S(1)}, f32[8,1024]{1,0:T(8,128)S(1)}) custom-call(s32[2,4]{1,0:T(2,128)S(1)} %pad_add_fusion.1.bounds, bf16[1024,1536]{1,0:T(8,128)(2,1)S(1)} %add_convert_fusion.own_ref.qkv_ref, bf16[1024,1536]{1,0:T(8,128)(2,1)S(1)} %add_convert_fusion.own_ref.qkv_ref, s32[2,1024]{1,0:T(2,128)S(1)} %pad_add_fusion.spans), custom_call_target="tpu_custom_call" | custom-call | flops 2147483648 | bytes 12582912 | tf_op jit(solution)/shard_map/pallas_call | solution.py:678
  115.8 17.3 %collective-permute-done.18 = bf16[4,32,2048]{2,1,0:T(8,128)(2,1)S(1)} collective-permute-done((bf16[4,32,2048]{2,1,0:T(8,128)(2,1)S(1)}, bf16[4,32,2048]{2,1,0:T(8,128)(2,1)S(1)}, u32[]{:S(2)}, u32[]{:S(2)}) %collective-permute-start.18) | collective-permute-done | bytes 524320 | tf_op jit(solution)/shard_map/ppermute | solution.py:464
  136.8 2.4 copy-done.2
  140.9 5.9 %collective-permute-start.20 = (bf16[512,1024]{1,0:T(8,128)(2,1)}, bf16[512,1024]{1,0:T(8,128)(2,1)}, u32[]{:S(2)}, u32[]{:S(2)}) collective-permute-start(bf16[512,1024]{1,0:T(8,128)(2,1)} %convolution_convert_fusion.6), channel_id=1, source_target_pairs={{0,2},{2,0},{1,3},{3,1},{4,6},{6,4},{5,7},{7,5},{8,10},{10,8},{9,1... | collective-permute-start | bytes 3145736 | tf_op jit(solution)/shard_map/ppermute | solution.py:469
  146.8 2.0 fusion.31
  156.5 3.4 collective-permute-start.25
  161.1 17.9 %shard_map.255 = (bf16[1024,2048]{1,0:T(8,128)(2,1)S(1)}, bf16[1024,2048]{1,0:T(8,128)(2,1)S(1)}) custom-call(bf16[1024,1024]{1,0:T(8,128)(2,1)S(1)} %pad_maximum_fusion.5.x_ref, bf16[1024,2688]{1,0:T(8,128)(2,1)S(1)} %bitcast.282, f32[1,2048]{1,0:T(1,128)S(1)} %slice.503.b_ref), custom_call_target="tpu_custom_call" | custom-call | flops 4294967296 | bytes 14680064 | tf_op jit(solution)/shard_map/pallas_call | solution.py:848
  179.0 2.1 copy-done.7
  181.1 10.5 %collective-permute-done.25 = bf16[512,1024]{1,0:T(8,128)(2,1)S(1)} collective-permute-done((bf16[512,1024]{1,0:T(8,128)(2,1)S(1)}, bf16[512,1024]{1,0:T(8,128)(2,1)S(1)}, u32[]{:S(2)}, u32[]{:S(2)}) %collective-permute-start.25) | collective-permute-done | bytes 1048608 | tf_op jit(solution)/shard_map/ppermute | solution.py:464
  192.8 2.4 fusion.11
  195.3 2.6 collective-permute-done.26
  197.9 2.8 fusion.119
  205.3 7.4 %all-to-all-start = ((bf16[16,128,128]{2,1,0:T(8,128)(2,1)}), bf16[16,128,128]{2,1,0:T(8,128)(2,1)S(1)}, u32[]{:S(2)}, u32[]{:S(2)}) async-start(bf16[16,128,128]{2,1,0:T(8,128)(2,1)} %broadcast_in_dim.46), calls=%async_computation | async-start | bytes 1048576 | tf_op jit(solution)/shard_map/all_to_all | solution.py:1145
  213.9 11.4 %all-to-all-done = bf16[16,128,128]{2,1,0:T(8,128)(2,1)S(1)} async-done(((bf16[16,128,128]{2,1,0:T(8,128)(2,1)}), bf16[16,128,128]{2,1,0:T(8,128)(2,1)S(1)}, u32[]{:S(2)}, u32[]{:S(2)}) %all-to-all-start) | async-done | bytes 524320 | tf_op jit(solution)/shard_map/all_to_all | solution.py:1145
  225.4 9.1 %shard_map.256 = f32[24,2048]{1,0:T(8,128)S(1)} custom-call(bf16[2048,128]{1,0:T(8,128)(2,1)S(1)} %bitcast.287, bf16[1024,128]{1,0:T(8,128)(2,1)S(1)} %maximum_select_fusion.25.d_ref, s32[1,1024]{1,0:T(1,128)S(1)} %compare_select_fusion.seg_ref), custom_call_target="tpu_custom_call" | custom-call | flops 3221225472 | bytes 786432 | tf_op jit(solution)/shard_map/pallas_call | solution.py:903
  235.2 12.0 %all_to_all.15 = f32[16,8,128]{2,1,0:T(8,128)S(1)} all-to-all(f32[16,8,128]{2,1,0:T(8,128)S(1)} %broadcast_in_dim.47), channel_id=1, replica_groups=mesh['z'=4,'x'=2,'c'=2,'y'=2] {'z','x','y'}, dimensions={0} | all-to-all | bytes 131072 | tf_op jit(solution)/shard_map/all_to_all | solution.py:1165
  248.1 15.6 %shard_map.257 = (bf16[2048,128]{1,0:T(8,128)(2,1)}, f32[768,128]{1,0:T(8,128)S(1)}) custom-call(bf16[2048,128]{1,0:T(8,128)(2,1)S(1)} %bitcast.288, bf16[1024,128]{1,0:T(8,128)(2,1)S(1)} %maximum_select_fusion.25.d_ref, s32[1,1024]{1,0:T(1,128)S(1)} %compare_select_fusion.seg_ref, f32[24,2048]{1,0:T(8,128)S(1)} %convolution_divide_fusion.coef_ref), custom_call_target="tpu_custom_call" | custom-call | flops 4831838208 | bytes 1572864 | tf_op jit(solution)/shard_map/pallas_call | solution.py:979
  263.6 3.6 all-to-all-start.2
  267.3 10.4 %all-to-all-done.2 = bf16[16,128,128]{2,1,0:T(8,128)(2,1)S(1)} async-done(((bf16[16,128,128]{2,1,0:T(8,128)(2,1)}), bf16[16,128,128]{2,1,0:T(8,128)(2,1)S(1)}, u32[]{:S(2)}, u32[]{:S(2)}) %all-to-all-start.2) | async-done | bytes 524320 | tf_op jit(solution)/shard_map/all_to_all | solution.py:1184
  277.8 5.7 %collective-permute-start.28 = (f32[512,128]{1,0:T(8,128)S(1)}, f32[512,128]{1,0:T(8,128)S(1)}, u32[]{:S(2)}, u32[]{:S(2)}) collective-permute-start(f32[512,128]{1,0:T(8,128)S(1)} %constant_dynamic-slice_fusion.11), channel_id=1, source_target_pairs={{0,2},{2,0},{1,3},{3,1},{4,6},{6,4},{5,7},{7,5},{8,10},{10,8},{9,1... | collective-permute-start | bytes 786440 | tf_op jit(solution)/shard_map/ppermute | solution.py:469
  286.5 2.3 convert_reduce_fusion.1
  291.8 6.4 %convolution_convert_fusion.1 = bf16[1024,2048]{1,0:T(8,128)(2,1)S(1)} fusion(bf16[1024,2048]{1,0:T(8,128)(2,1)S(1)} %copy-done.6, bf16[512,1024]{1,0:T(8,128)(2,1)} %collective-permute-done.29, bf16[512,1024]{1,0:T(8,128)(2,1)} %get-tuple-element.241), kind=kOutput, calls=%fused_computation.6 | convolution fusion | flops 4301258752 | bytes 10485760 | tf_op jit(solution)/shard_map/dot_general | solution.py:33
  302.2 7.8 %convert_reduce_fusion = (f32[2048]{0:T(1024)S(1)}, bf16[1024,2048]{1,0:T(8,128)(2,1)}) fusion(bf16[1024,2048]{1,0:T(8,128)(2,1)S(1)} %copy-done.8, bf16[1024,2048]{1,0:T(8,128)(2,1)S(1)} %bitcast.298, bf16[512,1024]{1,0:T(8,128)(2,1)} %collective-permute-done.29, bf16[512,1024]{1,0:T(8,128)(2,1)} %get-tuple-element.241), kind=kOutput, calls=%fused_computation | convolution fusion | flops 4309645312 | bytes 14688256 | tf_op jit(solution)/shard_map/dot_general | solution.py:448
  310.1 4.1 fusion.14
  314.6 2.4 fusion.2
  317.0 6.3 %collective-permute-done.33 = bf16[4,2,32,2048]{3,2,0,1:T(8,128)(2,1)S(1)} collective-permute-done((bf16[4,2,32,2048]{3,2,0,1:T(8,128)(2,1)S(1)}, bf16[4,2,32,2048]{3,2,0,1:T(8,128)(2,1)S(1)}, u32[]{:S(2)}, u32[]{:S(2)}) %collective-permute-start.33) | collective-permute-done | bytes 1048608 | tf_op jit(solution)/shard_map/ppermute | solution.py:464
  323.6 5.3 %convolution_convert_fusion = bf16[1024,2048]{1,0:T(8,128)(2,1)S(1)} fusion(bf16[1024,2048]{1,0:T(8,128)(2,1)S(1)} %copy-done.50, bf16[512,1024]{1,0:T(8,128)(2,1)S(1)} %copy-done.38, bf16[512,1024]{1,0:T(8,128)(2,1)S(1)} %copy-done.28), kind=kOutput, calls=%fused_computation.5 | convolution fusion | flops 4301258752 | bytes 10485760 | tf_op jit(solution)/shard_map/dot_general | solution.py:33
  341.4 2.3 convert_reduce_fusion.2
  343.8 2.4 collective-permute-start.31
  346.2 22.2 %collective-permute-done.35 = bf16[4,32,2048]{2,1,0:T(8,128)(2,1)} collective-permute-done((bf16[4,32,2048]{2,1,0:T(8,128)(2,1)}, bf16[4,32,2048]{2,1,0:T(8,128)(2,1)}, u32[]{:S(2)}, u32[]{:S(2)}) %collective-permute-start.35) | collective-permute-done | bytes 524320 | tf_op jit(solution)/shard_map/ppermute | solution.py:464
  376.0 2.5 convolution_convert_fusion.5.grad_ref
  383.4 11.7 %shard_map.258 = (bf16[1024,768]{1,0:T(8,128)(2,1)S(1)}, f32[8,256]{1,0:T(8,128)S(1)}) custom-call(s32[2,4]{1,0:T(2,128)S(1)} %pad_add_fusion.1.bounds, bf16[1024,1536]{1,0:T(8,128)(2,1)S(1)} %copy-done.4, bf16[1024,1536]{1,0:T(8,128)(2,1)S(1)} %copy-done.4, bf16[1024,512]{1,0:T(8,128)(2,1)S(1)} %get-tuple-element.133.out_ref, ...), custom_call_target="tpu_custom_call" | custom-call | flops 2684354560 | bytes 12582912 | tf_op jit(solution)/shard_map/pallas_call | solution.py:781
  396.8 4.0 collective-permute-start.48
  401.0 2.2 collective-permute-start.44
  408.8 11.9 %shard_map.259 = (bf16[1024,768]{1,0:T(8,128)(2,1)S(1)}, f32[8,256]{1,0:T(8,128)S(1)}) custom-call(s32[2,4]{1,0:T(2,128)S(1)} %pad_add_fusion.1.bounds, bf16[1024,1536]{1,0:T(8,128)(2,1)S(1)} %copy-done.4, bf16[1024,1536]{1,0:T(8,128)(2,1)S(1)} %copy-done.4, bf16[1024,512]{1,0:T(8,128)(2,1)S(1)} %get-tuple-element.133.out_ref, ...), custom_call_target="tpu_custom_call" | custom-call | flops 2684354560 | bytes 12582912 | tf_op jit(solution)/shard_map/pallas_call | solution.py:781
  425.9 1.9 convolution_convert_fusion.2
  428.4 3.0 collective-permute-start.53
  433.2 2.0 collective-permute-start.52
  440.5 12.8 %collective-permute-done.54 = bf16[584,128]{1,0:T(8,128)(2,1)S(1)} collective-permute-done((bf16[584,128]{1,0:T(8,128)(2,1)S(1)}, bf16[584,128]{1,0:T(8,128)(2,1)S(1)}, u32[]{:S(2)}, u32[]{:S(2)}) %collective-permute-start.54) | collective-permute-done | bytes 149536 | tf_op jit(solution)/shard_map/ppermute | solution.py:464
  453.6 3.3 collective-permute-start.57
  459.9 4.5 collective-permute-start.62
  466.3 2.1 collective-permute-start.60
  469.2 3.2 collective-permute-done.60
  472.4 8.3 %collective-permute-done.59 = bf16[2,64,1536]{2,1,0:T(8,128)(2,1)S(1)} collective-permute-done((bf16[2,64,1536]{2,1,0:T(8,128)(2,1)S(1)}, bf16[2,64,1536]{2,1,0:T(8,128)(2,1)S(1)}, u32[]{:S(2)}, u32[]{:S(2)}) %collective-permute-start.59) | collective-permute-done | bytes 393248 | tf_op jit(solution)/shard_map/ppermute | solution.py:464
  480.8 4.4 collective-permute-start.65
  487.3 3.9 collective-permute-done.64
  491.2 3.3 collective-permute-done.63
  494.5 1.9 collective-permute-start.66
  499.7 2.5 collective-permute-done.66
  (455 shorter events, 126.5 us)
Async XLA Ops:
  1.7 10.5 %collective-permute-start = (bf16[64,1536]{1,0:T(8,128)(2,1)S(1)}, bf16[64,1536]{1,0:T(8,128)(2,1)}, u32[]{:S(2)}, u32[]{:S(2)}) collective-permute-start(bf16[64,1536]{1,0:T(8,128)(2,1)S(1)} %slice_dynamic-update-slice_fusion), channel_id=1, source_target_pairs={{0,0},{1,2},{2,1},{3,3},{4,4},{5,6},{6,5},{7,7},{8,8},{9,10},{10,9... | collective-permute-start | bytes 589832 | tf_op jit(solution)/shard_map/ppermute | solution.py:464
  7.6 4.6 collective-permute-start.2
  7.7 4.5 collective-permute-start.1
  13.6 8.9 %collective-permute-start.3 = (bf16[64,1536]{1,0:T(8,128)(2,1)}, bf16[64,1536]{1,0:T(8,128)(2,1)}, u32[]{:S(2)}, u32[]{:S(2)}) collective-permute-start(bf16[64,1536]{1,0:T(8,128)(2,1)} %collective-permute-done), channel_id=1, source_target_pairs={{0,24},{24,0},{8,16},{16,8},{1,25},{25,1},{9,17},{17,9},{2,26},{26... | collective-permute-start | bytes 589832 | tf_op jit(solution)/shard_map/ppermute | solution.py:464
  18.7 11.9 %collective-permute-start.5 = (bf16[64,4736]{1,0:T(8,128)(2,1)}, bf16[64,4736]{1,0:T(8,128)(2,1)S(1)}, u32[]{:S(2)}, u32[]{:S(2)}) collective-permute-start(bf16[64,4736]{1,0:T(8,128)(2,1)} %fusion.39), channel_id=1, source_target_pairs={{0,0},{1,2},{2,1},{3,3},{4,4},{5,6},{6,5},{7,7},{8,8},{9,10},{10,9... | collective-permute-start | bytes 1818632 | tf_op jit(solution)/shard_map/ppermute | solution.py:464
  23.8 11.6 %collective-permute-start.4 = (bf16[2,64,1536]{2,1,0:T(8,128)(2,1)S(1)}, bf16[2,64,1536]{2,1,0:T(8,128)(2,1)S(1)}, u32[]{:S(2)}, u32[]{:S(2)}) collective-permute-start(bf16[2,64,1536]{2,1,0:T(8,128)(2,1)S(1)} %maximum_select_fusion.22), channel_id=1, source_target_pairs={{0,8},{8,0},{16,24},{24,16},{1,9},{9,1},{17,25},{25,17},{2,10},{10... | collective-permute-start | bytes 1179656 | tf_op jit(solution)/shard_map/ppermute | solution.py:464
  30.6 14.0 %collective-permute-start.6 = (bf16[64,2688]{1,0:T(8,128)(2,1)S(1)}, bf16[64,2688]{1,0:T(8,128)(2,1)S(1)}, u32[]{:S(2)}, u32[]{:S(2)}) collective-permute-start(bf16[64,2688]{1,0:T(8,128)(2,1)S(1)} %get-tuple-element.298), channel_id=1, source_target_pairs={{0,24},{24,0},{8,16},{16,8},{1,25},{25,1},{9,17},{17,9},{2,26},{26... | collective-permute-start | bytes 1032200 | tf_op jit(solution)/shard_map/ppermute | solution.py:464
  45.1 8.7 %collective-permute-start.7 = (bf16[4,32,1536]{2,1,0:T(8,128)(2,1)S(1)}, bf16[4,32,1536]{2,1,0:T(8,128)(2,1)S(1)}, u32[]{:S(2)}, u32[]{:S(2)}) collective-permute-start(bf16[4,32,1536]{2,1,0:T(8,128)(2,1)S(1)} %get-tuple-element.288), channel_id=1, source_target_pairs={{0,4},{4,0},{1,5},{5,1},{2,6},{6,2},{3,7},{7,3},{8,12},{12,8},{9,1... | collective-permute-start | bytes 1179656 | tf_op jit(solution)/shard_map/ppermute | solution.py:464
  46.4 8.4 %collective-permute-start.8 = (bf16[4,32,1536]{2,1,0:T(8,128)(2,1)S(1)}, bf16[4,32,1536]{2,1,0:T(8,128)(2,1)S(1)}, u32[]{:S(2)}, u32[]{:S(2)}) collective-permute-start(bf16[4,32,1536]{2,1,0:T(8,128)(2,1)S(1)} %get-tuple-element.287), channel_id=1, source_target_pairs={{0,1},{1,0},{2,3},{3,2},{4,5},{5,4},{6,7},{7,6},{8,9},{9,8},{10,11... | collective-permute-start | bytes 1179656 | tf_op jit(solution)/shard_map/ppermute | solution.py:464
  47.7 14.4 %collective-permute-start.9 = (bf16[2,64,2688]{2,1,0:T(8,128)(2,1)S(1)}, bf16[2,64,2688]{2,1,0:T(8,128)(2,1)S(1)}, u32[]{:S(2)}, u32[]{:S(2)}) collective-permute-start(bf16[2,64,2688]{2,1,0:T(8,128)(2,1)S(1)} %maximum_select_fusion.19), channel_id=1, source_target_pairs={{0,8},{8,0},{16,24},{24,16},{1,9},{9,1},{17,25},{25,17},{2,10},{10... | collective-permute-start | bytes 2064392 | tf_op jit(solution)/shard_map/ppermute | solution.py:464
  62.9 13.5 %collective-permute-start.13 = (bf16[4,32,2688]{2,1,0:T(8,128)(2,1)S(1)}, bf16[4,32,2688]{2,1,0:T(8,128)(2,1)S(1)}, u32[]{:S(2)}, u32[]{:S(2)}) collective-permute-start(bf16[4,32,2688]{2,1,0:T(8,128)(2,1)S(1)} %get-tuple-element.278), channel_id=1, source_target_pairs={{0,4},{4,0},{1,5},{5,1},{2,6},{6,2},{3,7},{7,3},{8,12},{12,8},{9,1... | collective-permute-start | bytes 2064392 | tf_op jit(solution)/shard_map/ppermute | solution.py:464
  63.2 13.2 %collective-permute-start.14 = (bf16[4,32,2688]{2,1,0:T(8,128)(2,1)S(1)}, bf16[4,32,2688]{2,1,0:T(8,128)(2,1)S(1)}, u32[]{:S(2)}, u32[]{:S(2)}) collective-permute-start(bf16[4,32,2688]{2,1,0:T(8,128)(2,1)S(1)} %get-tuple-element.277), channel_id=1, source_target_pairs={{0,1},{1,0},{2,3},{3,2},{4,5},{5,4},{6,7},{7,6},{8,9},{9,8},{10,11... | collective-permute-start | bytes 2064392 | tf_op jit(solution)/shard_map/ppermute | solution.py:464
  63.5 7.1 %collective-permute-start.12 = (bf16[64,2048]{1,0:T(8,128)(2,1)S(1)}, bf16[64,2048]{1,0:T(8,128)(2,1)S(1)}, u32[]{:S(2)}, u32[]{:S(2)}) collective-permute-start(bf16[64,2048]{1,0:T(8,128)(2,1)S(1)} %get-tuple-element.127), channel_id=1, source_target_pairs={{0,24},{24,0},{8,16},{16,8},{1,25},{25,1},{9,17},{17,9},{2,26},{26... | collective-permute-start | bytes 786440 | tf_op jit(solution)/shard_map/ppermute | solution.py:464
  66.3 27.0 %collective-permute-start.11 = (bf16[4,2,32,1536]{3,2,1,0:T(8,128)(2,1)S(1)}, bf16[4,2,32,1536]{3,2,1,0:T(8,128)(2,1)S(1)}, u32[]{:S(2)}, u32[]{:S(2)}) collective-permute-start(bf16[4,2,32,1536]{3,2,1,0:T(8,128)(2,1)S(1)} %maximum_select_fusion.18), channel_id=1, source_target_pairs={{0,4},{4,0},{1,5},{5,1},{2,6},{6,2},{3,7},{7,3},{8,12},{12,8},{9,1... | collective-permute-start | bytes 2359304 | tf_op jit(solution)/shard_map/ppermute | solution.py:464
  67.7 25.6 %collective-permute-start.10 = (bf16[4,2,32,1536]{3,2,0,1:T(8,128)(2,1)S(1)}, bf16[4,2,32,1536]{3,2,0,1:T(8,128)(2,1)S(1)}, u32[]{:S(2)}, u32[]{:S(2)}) collective-permute-start(bf16[4,2,32,1536]{3,2,0,1:T(8,128)(2,1)S(1)} %maximum_select_fusion.17), channel_id=1, source_target_pairs={{0,1},{1,0},{2,3},{3,2},{4,5},{5,4},{6,7},{7,6},{8,9},{9,8},{10,11... | collective-permute-start | bytes 2359304 | tf_op jit(solution)/shard_map/ppermute | solution.py:464
  93.3 8.8 %collective-permute-start.15 = (bf16[2,64,2048]{2,1,0:T(8,128)(2,1)S(1)}, bf16[2,64,2048]{2,1,0:T(8,128)(2,1)S(1)}, u32[]{:S(2)}, u32[]{:S(2)}) collective-permute-start(bf16[2,64,2048]{2,1,0:T(8,128)(2,1)S(1)} %maximum_select_fusion.20), channel_id=1, source_target_pairs={{0,8},{8,0},{16,24},{24,16},{1,9},{9,1},{17,25},{25,17},{2,10},{10... | collective-permute-start | bytes 1572872 | tf_op jit(solution)/shard_map/ppermute | solution.py:464
  94.3 39.5 %collective-permute-start.17 = (bf16[4,2,32,2688]{3,2,0,1:T(8,128)(2,1)S(1)}, bf16[4,2,32,2688]{3,2,0,1:T(8,128)(2,1)S(1)}, u32[]{:S(2)}, u32[]{:S(2)}) collective-permute-start(bf16[4,2,32,2688]{3,2,0,1:T(8,128)(2,1)S(1)} %maximum_select_fusion.10), channel_id=1, source_target_pairs={{0,4},{4,0},{1,5},{5,1},{2,6},{6,2},{3,7},{7,3},{8,12},{12,8},{9,1... | collective-permute-start | bytes 4128776 | tf_op jit(solution)/shard_map/ppermute | solution.py:464
  95.8 38.0 %collective-permute-start.16 = (bf16[4,2,32,2688]{3,2,0,1:T(8,128)(2,1)S(1)}, bf16[4,2,32,2688]{3,2,0,1:T(8,128)(2,1)S(1)}, u32[]{:S(2)}, u32[]{:S(2)}) collective-permute-start(bf16[4,2,32,2688]{3,2,0,1:T(8,128)(2,1)S(1)} %maximum_select_fusion.9), channel_id=1, source_target_pairs={{0,1},{1,0},{2,3},{3,2},{4,5},{5,4},{6,7},{7,6},{8,9},{9,8},{10,11... | collective-permute-start | bytes 4128776 | tf_op jit(solution)/shard_map/ppermute | solution.py:464
  103.6 29.5 %collective-permute-start.18 = (bf16[4,32,2048]{2,1,0:T(8,128)(2,1)S(1)}, bf16[4,32,2048]{2,1,0:T(8,128)(2,1)S(1)}, u32[]{:S(2)}, u32[]{:S(2)}) collective-permute-start(bf16[4,32,2048]{2,1,0:T(8,128)(2,1)S(1)} %get-tuple-element.282), channel_id=1, source_target_pairs={{0,4},{4,0},{1,5},{5,1},{2,6},{6,2},{3,7},{7,3},{8,12},{12,8},{9,1... | collective-permute-start | bytes 1572872 | tf_op jit(solution)/shard_map/ppermute | solution.py:464
  104.8 29.0 %collective-permute-start.19 = (bf16[4,32,2048]{2,1,0:T(8,128)(2,1)S(1)}, bf16[4,32,2048]{2,1,0:T(8,128)(2,1)S(1)}, u32[]{:S(2)}, u32[]{:S(2)}) collective-permute-start(bf16[4,32,2048]{2,1,0:T(8,128)(2,1)S(1)} %get-tuple-element.281), channel_id=1, source_target_pairs={{0,1},{1,0},{2,3},{3,2},{4,5},{5,4},{6,7},{7,6},{8,9},{9,8},{10,11... | collective-permute-start | bytes 1572872 | tf_op jit(solution)/shard_map/ppermute | solution.py:464
  140.9 8.5 %collective-permute-start.20 = (bf16[512,1024]{1,0:T(8,128)(2,1)}, bf16[512,1024]{1,0:T(8,128)(2,1)}, u32[]{:S(2)}, u32[]{:S(2)}) collective-permute-start(bf16[512,1024]{1,0:T(8,128)(2,1)} %convolution_convert_fusion.6), channel_id=1, source_target_pairs={{0,2},{2,0},{1,3},{3,1},{4,6},{6,4},{5,7},{7,5},{8,10},{10,8},{9,1... | collective-permute-start | bytes 3145736 | tf_op jit(solution)/shard_map/ppermute | solution.py:469
  152.0 7.9 %collective-permute-start.21 = (bf16[512,1024]{1,0:T(8,128)(2,1)S(1)}, bf16[512,1024]{1,0:T(8,128)(2,1)S(1)}, u32[]{:S(2)}, u32[]{:S(2)}) collective-permute-start(bf16[512,1024]{1,0:T(8,128)(2,1)S(1)} %fusion.10), channel_id=1, source_target_pairs={{0,2},{2,0},{1,3},{3,1},{4,6},{6,4},{5,7},{7,5},{8,10},{10,8},{9,1... | collective-permute-start | bytes 3145736 | tf_op jit(solution)/shard_map/ppermute | solution.py:469
  155.4 25.6 %collective-permute-start.23 = (bf16[4,2,32,2048]{3,2,0,1:T(8,128)(2,1)S(1)}, bf16[4,2,32,2048]{3,2,0,1:T(8,128)(2,1)S(1)}, u32[]{:S(2)}, u32[]{:S(2)}) collective-permute-start(bf16[4,2,32,2048]{3,2,0,1:T(8,128)(2,1)S(1)} %maximum_select_fusion.13), channel_id=1, source_target_pairs={{0,1},{1,0},{2,3},{3,2},{4,5},{5,4},{6,7},{7,6},{8,9},{9,8},{10,11... | collective-permute-start | bytes 3145736 | tf_op jit(solution)/shard_map/ppermute | solution.py:464
  156.2 24.9 %collective-permute-start.24 = (bf16[4,2,32,2048]{3,2,1,0:T(8,128)(2,1)S(1)}, bf16[4,2,32,2048]{3,2,1,0:T(8,128)(2,1)S(1)}, u32[]{:S(2)}, u32[]{:S(2)}) collective-permute-start(bf16[4,2,32,2048]{3,2,1,0:T(8,128)(2,1)S(1)} %maximum_select_fusion.14), channel_id=1, source_target_pairs={{0,4},{4,0},{1,5},{5,1},{2,6},{6,2},{3,7},{7,3},{8,12},{12,8},{9,1... | collective-permute-start | bytes 3145736 | tf_op jit(solution)/shard_map/ppermute | solution.py:464
  156.5 35.1 %collective-permute-start.25 = (bf16[512,1024]{1,0:T(8,128)(2,1)S(1)}, bf16[512,1024]{1,0:T(8,128)(2,1)S(1)}, u32[]{:S(2)}, u32[]{:S(2)}) collective-permute-start(bf16[512,1024]{1,0:T(8,128)(2,1)S(1)} %copy-done.49), channel_id=1, source_target_pairs={{0,0},{1,2},{2,1},{3,3},{4,4},{5,6},{6,5},{7,7},{8,8},{9,10},{10,9... | collective-permute-start | bytes 3145736 | tf_op jit(solution)/shard_map/ppermute | solution.py:464
  205.3 20.0 %all-to-all-start = ((bf16[16,128,128]{2,1,0:T(8,128)(2,1)}), bf16[16,128,128]{2,1,0:T(8,128)(2,1)S(1)}, u32[]{:S(2)}, u32[]{:S(2)}) async-start(bf16[16,128,128]{2,1,0:T(8,128)(2,1)} %broadcast_in_dim.46), calls=%async_computation | async-start | bytes 1048576 | tf_op jit(solution)/shard_map/all_to_all | solution.py:1145
  263.6 14.0 %all-to-all-start.2 = ((bf16[16,128,128]{2,1,0:T(8,128)(2,1)}), bf16[16,128,128]{2,1,0:T(8,128)(2,1)S(1)}, u32[]{:S(2)}, u32[]{:S(2)}) async-start(bf16[16,128,128]{2,1,0:T(8,128)(2,1)} %bitcast.57), calls=%async_computation.2 | async-start | bytes 1048576 | tf_op jit(solution)/shard_map/all_to_all | solution.py:1184
  277.8 6.9 %collective-permute-start.28 = (f32[512,128]{1,0:T(8,128)S(1)}, f32[512,128]{1,0:T(8,128)S(1)}, u32[]{:S(2)}, u32[]{:S(2)}) collective-permute-start(f32[512,128]{1,0:T(8,128)S(1)} %constant_dynamic-slice_fusion.11), channel_id=1, source_target_pairs={{0,2},{2,0},{1,3},{3,1},{4,6},{6,4},{5,7},{7,5},{8,10},{10,8},{9,1... | collective-permute-start | bytes 786440 | tf_op jit(solution)/shard_map/ppermute | solution.py:469
  298.8 24.4 %collective-permute-start.33 = (bf16[4,2,32,2048]{3,2,0,1:T(8,128)(2,1)S(1)}, bf16[4,2,32,2048]{3,2,0,1:T(8,128)(2,1)S(1)}, u32[]{:S(2)}, u32[]{:S(2)}) collective-permute-start(bf16[4,2,32,2048]{3,2,0,1:T(8,128)(2,1)S(1)} %bitcast.318), channel_id=1, source_target_pairs={{0,1},{1,0},{2,3},{3,2},{4,5},{5,4},{6,7},{7,6},{8,9},{9,8},{10,11... | collective-permute-start | bytes 3145736 | tf_op jit(solution)/shard_map/ppermute | solution.py:464
  299.4 24.1 %collective-permute-start.32 = (bf16[4,2,32,2048]{3,2,0,1:T(8,128)(2,1)S(1)}, bf16[4,2,32,2048]{3,2,0,1:T(8,128)(2,1)S(1)}, u32[]{:S(2)}, u32[]{:S(2)}) collective-permute-start(bf16[4,2,32,2048]{3,2,0,1:T(8,128)(2,1)S(1)} %bitcast.319), channel_id=1, source_target_pairs={{0,4},{4,0},{1,5},{5,1},{2,6},{6,2},{3,7},{7,3},{8,12},{12,8},{9,1... | collective-permute-start | bytes 3145736 | tf_op jit(solution)/shard_map/ppermute | solution.py:464
  314.2 24.1 %collective-permute-start.30 = (bf16[512,1024]{1,0:T(8,128)(2,1)S(1)}, bf16[512,1024]{1,0:T(8,128)(2,1)S(1)}, u32[]{:S(2)}, u32[]{:S(2)}) collective-permute-start(bf16[512,1024]{1,0:T(8,128)(2,1)S(1)} %fusion.14), channel_id=1, source_target_pairs={{0,2},{2,0},{1,3},{3,1},{4,6},{6,4},{5,7},{7,5},{8,10},{10,8},{9,1... | collective-permute-start | bytes 3145736 | tf_op jit(solution)/shard_map/ppermute | solution.py:469
  330.4 37.9 %collective-permute-start.37 = (bf16[4,2,32,2048]{3,2,0,1:T(8,128)(2,1)}, bf16[4,2,32,2048]{3,2,0,1:T(8,128)(2,1)}, u32[]{:S(2)}, u32[]{:S(2)}) collective-permute-start(bf16[4,2,32,2048]{3,2,0,1:T(8,128)(2,1)} %bitcast.272), channel_id=1, source_target_pairs={{0,1},{1,0},{2,3},{3,2},{4,5},{5,4},{6,7},{7,6},{8,9},{9,8},{10,11... | collective-permute-start | bytes 3145736 | tf_op jit(solution)/shard_map/ppermute | solution.py:464
  334.0 34.4 %collective-permute-start.36 = (bf16[4,2,32,2048]{3,2,0,1:T(8,128)(2,1)}, bf16[4,2,32,2048]{3,2,0,1:T(8,128)(2,1)}, u32[]{:S(2)}, u32[]{:S(2)}) collective-permute-start(bf16[4,2,32,2048]{3,2,0,1:T(8,128)(2,1)} %bitcast.273), channel_id=1, source_target_pairs={{0,4},{4,0},{1,5},{5,1},{2,6},{6,2},{3,7},{7,3},{8,12},{12,8},{9,1... | collective-permute-start | bytes 3145736 | tf_op jit(solution)/shard_map/ppermute | solution.py:464
  336.3 32.1 %collective-permute-start.35 = (bf16[4,32,2048]{2,1,0:T(8,128)(2,1)}, bf16[4,32,2048]{2,1,0:T(8,128)(2,1)}, u32[]{:S(2)}, u32[]{:S(2)}) collective-permute-start(bf16[4,32,2048]{2,1,0:T(8,128)(2,1)} %fusion.41), channel_id=1, source_target_pairs={{0,4},{4,0},{1,5},{5,1},{2,6},{6,2},{3,7},{7,3},{8,12},{12,8},{9,1... | collective-permute-start | bytes 1572872 | tf_op jit(solution)/shard_map/ppermute | solution.py:464
  338.0 30.4 %collective-permute-start.34 = (bf16[4,32,2048]{2,1,0:T(8,128)(2,1)}, bf16[4,32,2048]{2,1,0:T(8,128)(2,1)}, u32[]{:S(2)}, u32[]{:S(2)}) collective-permute-start(bf16[4,32,2048]{2,1,0:T(8,128)(2,1)} %fusion.40), channel_id=1, source_target_pairs={{0,1},{1,0},{2,3},{3,2},{4,5},{5,4},{6,7},{7,6},{8,9},{9,8},{10,11... | collective-permute-start | bytes 1572872 | tf_op jit(solution)/shard_map/ppermute | solution.py:464
  343.8 30.9 %collective-permute-start.31 = (bf16[512,1024]{1,0:T(8,128)(2,1)}, bf16[512,1024]{1,0:T(8,128)(2,1)S(1)}, u32[]{:S(2)}, u32[]{:S(2)}) collective-permute-start(bf16[512,1024]{1,0:T(8,128)(2,1)} %get-tuple-element.244), channel_id=1, source_target_pairs={{0,2},{2,0},{1,3},{3,1},{4,6},{6,4},{5,7},{7,5},{8,10},{10,8},{9,1... | collective-permute-start | bytes 3145736 | tf_op jit(solution)/shard_map/ppermute | solution.py:469
  378.8 16.4 %collective-permute-start.41 = (bf16[4,2,32,512]{3,2,0,1:T(8,128)(2,1)S(1)}, bf16[4,2,32,512]{3,2,0,1:T(8,128)(2,1)S(1)}, u32[]{:S(2)}, u32[]{:S(2)}) collective-permute-start(bf16[4,2,32,512]{3,2,0,1:T(8,128)(2,1)S(1)} %dynamic-slice_bitcast_fusion.3), channel_id=1, source_target_pairs={{0,4},{4,0},{1,5},{5,1},{2,6},{6,2},{3,7},{7,3},{8,12},{12,8},{9,1... | collective-permute-start | bytes 786440 | tf_op jit(solution)/shard_map/ppermute | solution.py:464
  379.9 15.3 %collective-permute-start.42 = (bf16[4,2,32,512]{3,2,0,1:T(8,128)(2,1)S(1)}, bf16[4,2,32,512]{3,2,0,1:T(8,128)(2,1)S(1)}, u32[]{:S(2)}, u32[]{:S(2)}) collective-permute-start(bf16[4,2,32,512]{3,2,0,1:T(8,128)(2,1)S(1)} %dynamic-slice_bitcast_fusion.2), channel_id=1, source_target_pairs={{0,1},{1,0},{2,3},{3,2},{4,5},{5,4},{6,7},{7,6},{8,9},{9,8},{10,11... | collective-permute-start | bytes 786440 | tf_op jit(solution)/shard_map/ppermute | solution.py:464
  380.4 14.8 %collective-permute-start.38 = (bf16[2,64,2048]{2,1,0:T(8,128)(2,1)S(1)}, bf16[2,64,2048]{2,1,0:T(8,128)(2,1)S(1)}, u32[]{:S(2)}, u32[]{:S(2)}) collective-permute-start(bf16[2,64,2048]{2,1,0:T(8,128)(2,1)S(1)} %select_convert_fusion.1), channel_id=1, source_target_pairs={{0,8},{8,0},{16,24},{24,16},{1,9},{9,1},{17,25},{25,17},{2,10},{10... | collective-permute-start | bytes 1572872 | tf_op jit(solution)/shard_map/ppermute | solution.py:464
  381.6 13.7 %collective-permute-start.40 = (bf16[4,32,2048]{2,1,0:T(8,128)(2,1)S(1)}, bf16[4,32,2048]{2,1,0:T(8,128)(2,1)S(1)}, u32[]{:S(2)}, u32[]{:S(2)}) collective-permute-start(bf16[4,32,2048]{2,1,0:T(8,128)(2,1)S(1)} %fusion.43), channel_id=1, source_target_pairs={{0,4},{4,0},{1,5},{5,1},{2,6},{6,2},{3,7},{7,3},{8,12},{12,8},{9,1... | collective-permute-start | bytes 1572872 | tf_op jit(solution)/shard_map/ppermute | solution.py:464
  382.2 13.8 %collective-permute-start.39 = (bf16[4,32,2048]{2,1,0:T(8,128)(2,1)S(1)}, bf16[4,32,2048]{2,1,0:T(8,128)(2,1)S(1)}, u32[]{:S(2)}, u32[]{:S(2)}) collective-permute-start(bf16[4,32,2048]{2,1,0:T(8,128)(2,1)S(1)} %fusion.42), channel_id=1, source_target_pairs={{0,1},{1,0},{2,3},{3,2},{4,5},{5,4},{6,7},{7,6},{8,9},{9,8},{10,11... | collective-permute-start | bytes 1572872 | tf_op jit(solution)/shard_map/ppermute | solution.py:464
  396.8 9.6 %collective-permute-start.48 = (f32[16,4]{1,0:T(8,128)S(1)}, f32[16,4]{1,0:T(8,128)S(1)}, u32[]{:S(2)}, u32[]{:S(2)}) collective-permute-start(f32[16,4]{1,0:T(8,128)S(1)} %reshape.820), channel_id=1, source_target_pairs={{0,2},{2,0},{1,3},{3,1},{4,6},{6,4},{5,7},{7,5},{8,10},{10,8},{9,1... | collective-permute-start | bytes 776 | tf_op jit(solution)/shard_map/ppermute | solution.py:469
  401.0 20.1 %collective-permute-start.44 = (bf16[2,64,2048]{2,1,0:T(8,128)(2,1)S(1)}, bf16[2,64,2048]{2,1,0:T(8,128)(2,1)S(1)}, u32[]{:S(2)}, u32[]{:S(2)}) collective-permute-start(bf16[2,64,2048]{2,1,0:T(8,128)(2,1)S(1)} %select_convert_fusion), channel_id=1, source_target_pairs={{0,8},{8,0},{16,24},{24,16},{1,9},{9,1},{17,25},{25,17},{2,10},{10... | collective-permute-start | bytes 1572872 | tf_op jit(solution)/shard_map/ppermute | solution.py:464
  403.2 17.9 %collective-permute-start.47 = (bf16[512,1024]{1,0:T(8,128)(2,1)S(1)}, bf16[512,1024]{1,0:T(8,128)(2,1)S(1)}, u32[]{:S(2)}, u32[]{:S(2)}) collective-permute-start(bf16[512,1024]{1,0:T(8,128)(2,1)S(1)} %copy-done.14), channel_id=1, source_target_pairs={{0,0},{1,2},{2,1},{3,3},{4,4},{5,6},{6,5},{7,7},{8,8},{9,10},{10,9... | collective-permute-start | bytes 3145736 | tf_op jit(solution)/shard_map/ppermute | solution.py:464
  405.2 15.7 %collective-permute-start.43 = (bf16[64,2048]{1,0:T(8,128)(2,1)S(1)}, bf16[64,2048]{1,0:T(8,128)(2,1)S(1)}, u32[]{:S(2)}, u32[]{:S(2)}) collective-permute-start(bf16[64,2048]{1,0:T(8,128)(2,1)S(1)} %fusion.54), channel_id=1, source_target_pairs={{0,24},{24,0},{8,16},{16,8},{1,25},{25,1},{9,17},{17,9},{2,26},{26... | collective-permute-start | bytes 786440 | tf_op jit(solution)/shard_map/ppermute | solution.py:464
  406.5 14.3 %collective-permute-start.46 = (bf16[4,32,512]{2,1,0:T(8,128)(2,1)S(1)}, bf16[4,32,512]{2,1,0:T(8,128)(2,1)S(1)}, u32[]{:S(2)}, u32[]{:S(2)}) collective-permute-start(bf16[4,32,512]{2,1,0:T(8,128)(2,1)S(1)} %fusion.63), channel_id=1, source_target_pairs={{0,4},{4,0},{1,5},{5,1},{2,6},{6,2},{3,7},{7,3},{8,12},{12,8},{9,1... | collective-permute-start | bytes 393224 | tf_op jit(solution)/shard_map/ppermute | solution.py:464
  408.0 12.9 %collective-permute-start.45 = (bf16[4,32,512]{2,1,0:T(8,128)(2,1)S(1)}, bf16[4,32,512]{2,1,0:T(8,128)(2,1)S(1)}, u32[]{:S(2)}, u32[]{:S(2)}) collective-permute-start(bf16[4,32,512]{2,1,0:T(8,128)(2,1)S(1)} %fusion.62), channel_id=1, source_target_pairs={{0,1},{1,0},{2,3},{3,2},{4,5},{5,4},{6,7},{7,6},{8,9},{9,8},{10,11... | collective-permute-start | bytes 393224 | tf_op jit(solution)/shard_map/ppermute | solution.py:464
  428.4 10.3 %collective-permute-start.53 = (bf16[2,64,512]{2,1,0:T(8,128)(2,1)S(1)}, bf16[2,64,512]{2,1,0:T(8,128)(2,1)S(1)}, u32[]{:S(2)}, u32[]{:S(2)}) collective-permute-start(bf16[2,64,512]{2,1,0:T(8,128)(2,1)S(1)} %select_convert_fusion.6), channel_id=1, source_target_pairs={{0,8},{8,0},{16,24},{24,16},{1,9},{9,1},{17,25},{25,17},{2,10},{10... | collective-permute-start | bytes 393224 | tf_op jit(solution)/shard_map/ppermute | solution.py:464
  431.9 21.5 %collective-permute-start.51 = (bf16[4,2,32,1536]{3,2,0,1:T(8,128)(2,1)S(1)}, bf16[4,2,32,1536]{3,2,0,1:T(8,128)(2,1)S(1)}, u32[]{:S(2)}, u32[]{:S(2)}) collective-permute-start(bf16[4,2,32,1536]{3,2,0,1:T(8,128)(2,1)S(1)} %dynamic-slice_bitcast_fusion), channel_id=1, source_target_pairs={{0,1},{1,0},{2,3},{3,2},{4,5},{5,4},{6,7},{7,6},{8,9},{9,8},{10,11... | collective-permute-start | bytes 2359304 | tf_op jit(solution)/shard_map/ppermute | solution.py:464
  432.0 21.3 %collective-permute-start.50 = (bf16[4,2,32,1536]{3,2,0,1:T(8,128)(2,1)S(1)}, bf16[4,2,32,1536]{3,2,0,1:T(8,128)(2,1)S(1)}, u32[]{:S(2)}, u32[]{:S(2)}) collective-permute-start(bf16[4,2,32,1536]{3,2,0,1:T(8,128)(2,1)S(1)} %dynamic-slice_bitcast_fusion.1), channel_id=1, source_target_pairs={{0,4},{4,0},{1,5},{5,1},{2,6},{6,2},{3,7},{7,3},{8,12},{12,8},{9,1... | collective-permute-start | bytes 2359304 | tf_op jit(solution)/shard_map/ppermute | solution.py:464
  433.2 20.1 %collective-permute-start.52 = (bf16[64,2048]{1,0:T(8,128)(2,1)S(1)}, bf16[64,2048]{1,0:T(8,128)(2,1)S(1)}, u32[]{:S(2)}, u32[]{:S(2)}) collective-permute-start(bf16[64,2048]{1,0:T(8,128)(2,1)S(1)} %fusion.55), channel_id=1, source_target_pairs={{0,24},{24,0},{8,16},{16,8},{1,25},{25,1},{9,17},{17,9},{2,26},{26... | collective-permute-start | bytes 786440 | tf_op jit(solution)/shard_map/ppermute | solution.py:464
  435.2 18.1 %collective-permute-start.54 = (bf16[584,128]{1,0:T(8,128)(2,1)S(1)}, bf16[584,128]{1,0:T(8,128)(2,1)S(1)}, u32[]{:S(2)}, u32[]{:S(2)}) collective-permute-start(bf16[584,128]{1,0:T(8,128)(2,1)S(1)} %convert_element_type.481), channel_id=1, source_target_pairs={{0,1},{1,0},{2,3},{3,2},{4,5},{5,4},{6,7},{7,6},{8,9},{9,8},{10,11... | collective-permute-start | bytes 448520 | tf_op jit(solution)/shard_map/ppermute | solution.py:464
  438.7 19.3 %collective-permute-start.61 = (bf16[512,1024]{1,0:T(8,128)(2,1)S(1)}, bf16[512,1024]{1,0:T(8,128)(2,1)S(1)}, u32[]{:S(2)}, u32[]{:S(2)}) collective-permute-start(bf16[512,1024]{1,0:T(8,128)(2,1)S(1)} %add_convert_fusion.2), channel_id=1, source_target_pairs={{0,2},{2,0},{1,3},{3,1},{4,6},{6,4},{5,7},{7,5},{8,10},{10,8},{9,1... | collective-permute-start | bytes 3145736 | tf_op jit(solution)/shard_map/ppermute | solution.py:469
  453.4 11.1 %collective-permute-start.58 = (bf16[584,128]{1,0:T(8,128)(2,1)S(1)}, bf16[584,128]{1,0:T(8,128)(2,1)S(1)}, u32[]{:S(2)}, u32[]{:S(2)}) collective-permute-start(bf16[584,128]{1,0:T(8,128)(2,1)S(1)} %fusion.56), channel_id=1, source_target_pairs={{0,4},{4,0},{1,5},{5,1},{2,6},{6,2},{3,7},{7,3},{8,12},{12,8},{9,1... | collective-permute-start | bytes 448520 | tf_op jit(solution)/shard_map/ppermute | solution.py:464
  453.6 10.9 %collective-permute-start.57 = (bf16[64,512]{1,0:T(8,128)(2,1)S(1)}, bf16[64,512]{1,0:T(8,128)(2,1)S(1)}, u32[]{:S(2)}, u32[]{:S(2)}) collective-permute-start(bf16[64,512]{1,0:T(8,128)(2,1)S(1)} %fusion.68), channel_id=1, source_target_pairs={{0,24},{24,0},{8,16},{16,8},{1,25},{25,1},{9,17},{17,9},{2,26},{26... | collective-permute-start | bytes 196616 | tf_op jit(solution)/shard_map/ppermute | solution.py:464
  457.2 8.7 %collective-permute-start.56 = (bf16[4,32,1536]{2,1,0:T(8,128)(2,1)S(1)}, bf16[4,32,1536]{2,1,0:T(8,128)(2,1)S(1)}, u32[]{:S(2)}, u32[]{:S(2)}) collective-permute-start(bf16[4,32,1536]{2,1,0:T(8,128)(2,1)S(1)} %fusion.50), channel_id=1, source_target_pairs={{0,4},{4,0},{1,5},{5,1},{2,6},{6,2},{3,7},{7,3},{8,12},{12,8},{9,1... | collective-permute-start | bytes 1179656 | tf_op jit(solution)/shard_map/ppermute | solution.py:464
  457.6 8.7 %collective-permute-start.55 = (bf16[4,32,1536]{2,1,0:T(8,128)(2,1)S(1)}, bf16[4,32,1536]{2,1,0:T(8,128)(2,1)S(1)}, u32[]{:S(2)}, u32[]{:S(2)}) collective-permute-start(bf16[4,32,1536]{2,1,0:T(8,128)(2,1)S(1)} %fusion.49), channel_id=1, source_target_pairs={{0,1},{1,0},{2,3},{3,2},{4,5},{5,4},{6,7},{7,6},{8,9},{9,8},{10,11... | collective-permute-start | bytes 1179656 | tf_op jit(solution)/shard_map/ppermute | solution.py:464
  459.9 20.7 %collective-permute-start.62 = (bf16[512,1024]{1,0:T(8,128)(2,1)S(1)}, bf16[512,1024]{1,0:T(8,128)(2,1)S(1)}, u32[]{:S(2)}, u32[]{:S(2)}) collective-permute-start(bf16[512,1024]{1,0:T(8,128)(2,1)S(1)} %add_convert_fusion.1), channel_id=1, source_target_pairs={{0,0},{1,2},{2,1},{3,3},{4,4},{5,6},{6,5},{7,7},{8,8},{9,10},{10,9... | collective-permute-start | bytes 3145736 | tf_op jit(solution)/shard_map/ppermute | solution.py:464
  466.3 6.1 %collective-permute-start.60 = (bf16[584,128]{1,0:T(8,128)(2,1)S(1)}, bf16[584,128]{1,0:T(8,128)(2,1)S(1)}, u32[]{:S(2)}, u32[]{:S(2)}) collective-permute-start(bf16[584,128]{1,0:T(8,128)(2,1)S(1)} %fusion.97), channel_id=1, source_target_pairs={{0,24},{24,0},{8,16},{16,8},{1,25},{25,1},{9,17},{17,9},{2,26},{26... | collective-permute-start | bytes 448520 | tf_op jit(solution)/shard_map/ppermute | solution.py:464
  468.8 11.9 %collective-permute-start.59 = (bf16[2,64,1536]{2,1,0:T(8,128)(2,1)S(1)}, bf16[2,64,1536]{2,1,0:T(8,128)(2,1)S(1)}, u32[]{:S(2)}, u32[]{:S(2)}) collective-permute-start(bf16[2,64,1536]{2,1,0:T(8,128)(2,1)S(1)} %select_convert_fusion.2), channel_id=1, source_target_pairs={{0,8},{8,0},{16,24},{24,16},{1,9},{9,1},{17,25},{25,17},{2,10},{10... | collective-permute-start | bytes 1179656 | tf_op jit(solution)/shard_map/ppermute | solution.py:464
  480.8 13.6 %collective-permute-start.65 = (bf16[64,4096]{1,0:T(8,128)(2,1)S(1)}, bf16[64,4096]{1,0:T(8,128)(2,1)S(1)}, u32[]{:S(2)}, u32[]{:S(2)}) collective-permute-start(bf16[64,4096]{1,0:T(8,128)(2,1)S(1)} %pad_maximum_fusion.17), channel_id=1, source_target_pairs={{0,0},{1,2},{2,1},{3,3},{4,4},{5,6},{6,5},{7,7},{8,8},{9,10},{10,9... | collective-permute-start | bytes 1572872 | tf_op jit(solution)/shard_map/ppermute | solution.py:464
  485.3 5.8 %collective-permute-start.64 = (bf16[584,128]{1,0:T(8,128)(2,1)S(1)}, bf16[584,128]{1,0:T(8,128)(2,1)S(1)}, u32[]{:S(2)}, u32[]{:S(2)}) collective-permute-start(bf16[584,128]{1,0:T(8,128)(2,1)S(1)} %fusion.57), channel_id=1, source_target_pairs={{0,8},{8,0},{16,24},{24,16},{1,9},{9,1},{17,25},{25,17},{2,10},{10... | collective-permute-start | bytes 448520 | tf_op jit(solution)/shard_map/ppermute | solution.py:464
  485.9 8.5 %collective-permute-start.63 = (bf16[64,1536]{1,0:T(8,128)(2,1)S(1)}, bf16[64,1536]{1,0:T(8,128)(2,1)S(1)}, u32[]{:S(2)}, u32[]{:S(2)}) collective-permute-start(bf16[64,1536]{1,0:T(8,128)(2,1)S(1)} %fusion.58), channel_id=1, source_target_pairs={{0,24},{24,0},{8,16},{16,8},{1,25},{25,1},{9,17},{17,9},{2,26},{26... | collective-permute-start | bytes 589832 | tf_op jit(solution)/shard_map/ppermute | solution.py:464
  494.5 7.7 %collective-permute-start.66 = (bf16[64,2048]{1,0:T(8,128)(2,1)S(1)}, bf16[64,2048]{1,0:T(8,128)(2,1)S(1)}, u32[]{:S(2)}, u32[]{:S(2)}) collective-permute-start(bf16[64,2048]{1,0:T(8,128)(2,1)S(1)} %pad_maximum_fusion.20), channel_id=1, source_target_pairs={{0,0},{1,2},{2,1},{3,3},{4,4},{5,6},{6,5},{7,7},{8,8},{9,10},{10,9... | collective-permute-start | bytes 786440 | tf_op jit(solution)/shard_map/ppermute | solution.py:464
  (61 other events, 644.6 us)
where the time goes:
time: 519 us; the launch traced here: 514 us
  waiting for transfers between devices  182 us (35%)
  starting transfers between devices  106 us (20%)
  Pallas kernels  76.5 us (15%)
  matrix products  54.7 us (11%)
  local copies, waits for them, and re-layouts  43.4 us (8%)
  other arithmetic  36.7 us (7%)
  blocking collectives  12 us (2%)
    ppermute x56, waiting for transfers between devices, exchange(): lax.ppermute(value, axis, steps)  153 us
    ppermute x56, starting transfers between devices, exchange(): lax.ppermute(value, axis, steps)  73.3 us
    pallas_call x2, Pallas kernels, attend_back(): pl.pallas_call(partial(attend_back_kernel, group * heads), grid=(count //...  23.6 us
    ppermute x12, starting transfers between devices, swap(): return lax.ppermute(value, axis, SWAP)  21.7 us
    dot_general x12, matrix products, contract_cols(): lax.dot_general(left, right, (((1,), (1,)), ((), ())), precision=precisio...  21.2 us
    unnamed x131, local copies, waits for them, and re-layouts  21.1 us
    pallas_call x1, Pallas kernels, expand(): pl.pallas_call(expand_kernel, grid=(tiles,), in_specs=[pl.BlockSpec((coun...  17.9 us
    dot_general x7, matrix products, contract_rows(): lax.dot_general(left, right, (((0,), (0,)), ((), ())), precision=precisio...  17.7 us
  transfers between devices with their start and end apart: 70, of which 36 were waited for; matrix products, arithmetic and copies ran while one was open for 13% of the time, Pallas kernels for 10%

commit v1 on v0

--- a/solution.py
+++ b/solution.py
@@ -1108,11 +1108,8 @@
         (other_attn, jnp.stack([gains[1], shifts[1]]))
     )
     second_norm = swap(second_norm, "c")
-    second_norm, cot_given, *down_parts = lax.optimization_barrier(
-        (second_norm, cot) + tuple(down_parts)
-    )
-    down_got = exchange(*last_moves(down_parts), (cot_given, CORES, TURN))
-    own_cot = down_got[2]
+    second_norm, *down_parts = lax.optimization_barrier((second_norm,) + tuple(down_parts))
+    down_got = exchange(*last_moves(down_parts))
     attn_sum = contract_cols(mixed_half(0), full_out) + other_attn.astype(F32)
     own_tokens = rows_of(row, own_start, share).astype(F32)
     normed, unit_one, rstd_one = norm_forward(
@@ -1145,6 +1142,7 @@
     queries = lax.all_to_all(
         jnp.broadcast_to(own_queries[None], (chip_count,) + own_queries.shape), chips, 0, 0
     ).reshape(chip_count * half_span, -1)
+    queries, own_cot = lax.optimization_barrier((queries, lax.ppermute(cot, CORES, TURN)))
     proj_width = w_proj.shape[1]
     cuts = (proj_width, 3 * proj_width // 4, proj_width // 2)
     sums = pool(cuts, query_span, queries, row_embed, seg_row)
@@ -1181,6 +1179,9 @@
         / sums
     )
     query_grad, doc_grad = pool_back(cuts, query_span, queries, row_embed, seg_row, coefficient)
+    query_grad, y_out = lax.optimization_barrier(
+        (query_grad, lax.ppermute(result_low, CORES, TURN))
+    )
     grad_blocks = lax.all_to_all(
         query_grad.reshape(chip_count, half_span, proj_width), chips, 0, 0
     )
@@ -1247,12 +1248,9 @@
     grad_mixed, down_pair, up_line, *out_parts = lax.optimization_barrier(
         (grad_mixed, down_pair, up_line) + tuple(out_parts)
     )
-    up_line, y_given, losses = lax.optimization_barrier((up_line, result_low, losses))
+    up_line, losses = lax.optimization_barrier((up_line, losses))
     moved = exchange(
-        far_move(down_pair, z),
-        near_move(up_line, z),
-        *line_moves(out_parts, x, y),
-        (y_given, CORES, TURN),
+        far_move(down_pair, z), near_move(up_line, z), *line_moves(out_parts, x, y)
     )
     other_losses = swap(losses, "c")
     proj_given, other_losses, grad_mixed = lax.optimization_barrier(
@@ -1265,7 +1263,6 @@
     losses = jnp.where(c == y, losses, other_losses)
     loss_out = rows_of(losses, 4 * z + 2 * x + c, 1)
     grads_two, sums_two = attend_back(bounds, 1, qkv, mixed, grad_mixed, lse, spans)
-    y_out = moved[4]
     down_part = far_sum(down_pair, moved[0], z)
     up_pair = near_sum(up_line, moved[1], z)
     out_line = line_of(out_parts, moved[2:], x, y)

time: 519 us -> 516 us (level)
  waiting for transfers between devices: 182 us -> 163 us
  starting transfers between devices: 106 us -> 120 us
  blocking collectives: 12 us -> 0 us
  matrix products: 54.7 us -> 61.9 us
  Pallas kernels: 76.5 us -> 83.1 us
    ppermute x56 -> x54, waiting for transfers between devices: 153 us -> 135 us  [exchange(): lax.ppermute(value, axis, steps)]
    all_to_all x1 -> x0, blocking collectives: 12 us -> none  [local_chip(): lax.all_to_all(jnp.broadcast_to(notes[None], (chip_count,) + notes.shape)...]
    ppermute x0 -> x2, starting transfers between devices: none -> 7.96 us  [the longest x1 5.13 us: local_chip(): lax.ppermute(result_low, CORES, TURN)]
    all_to_all x1, starting transfers between devices: 3.57 us -> 9.44 us  [local_chip(): lax.all_to_all(query_grad.reshape(chip_count, half_span, proj_width), chi...]
    all_to_all x0 -> x1, starting transfers between devices: none -> 5.65 us  [local_chip(): lax.all_to_all(jnp.broadcast_to(notes[None], (chip_count,) + notes.shape)...]
    ppermute x56 -> x54, starting transfers between devices: 73.3 us -> 68.9 us  [exchange(): lax.ppermute(value, axis, steps)]
    unnamed x131 -> x129, local copies, waits for them, and re-layouts: 21.1 us -> 20.8 us
  transfers between devices with their start and end apart: 70 -> 71, of which waited for: 36 -> 29; matrix products, arithmetic and copies ran while one was open for 13% -> 15% of each run, Pallas kernels for 10% -> 15%
where the time goes in v1:
time: 516 us; the launch traced here: 510 us
  waiting for transfers between devices  163 us (32%)
  starting transfers between devices  120 us (23%)
  Pallas kernels  83.1 us (16%)
  matrix products  61.9 us (12%)
  local copies, waits for them, and re-layouts  43.2 us (8%)
  other arithmetic  34.7 us (7%)
    ppermute x54, waiting for transfers between devices, exchange(): lax.ppermute(value, axis, steps)  135 us
    ppermute x54, starting transfers between devices, exchange(): lax.ppermute(value, axis, steps)  68.9 us
    pallas_call x2, Pallas kernels, attend_back(): pl.pallas_call(partial(attend_back_kernel, group * heads), grid=(count //...  28.1 us
    dot_general x7, matrix products, contract_rows(): lax.dot_general(left, right, (((0,), (0,)), ((), ())), precision=precisio...  22.3 us
    dot_general x12, matrix products, contract_cols(): lax.dot_general(left, right, (((1,), (1,)), ((), ())), precision=precisio...  21.2 us
    unnamed x129, local copies, waits for them, and re-layouts  20.8 us
    ppermute x12, starting transfers between devices, swap(): return lax.ppermute(value, axis, SWAP)  20.5 us
    pallas_call x1, Pallas kernels, expand(): pl.pallas_call(expand_kernel, grid=(tiles,), in_specs=[pl.BlockSpec((coun...  17.5 us
  transfers between devices with their start and end apart: 71, of which 29 were waited for; matrix products, arithmetic and copies ran while one was open for 15% of the time, Pallas kernels for 15%

profile of v1, /device:TPU:1, one launch (start us, length us, event | category | flops | bytes accessed | tf_op | source)
XLA Modules:
  0.0 509.9 jit_solution(3169787384224298348)
XLA Ops:
  1.7 4.5 collective-permute-start
  10.0 1.9 fusion.39
  13.3 3.3 collective-permute-start.3
  18.5 4.2 collective-permute-start.5
  24.1 2.5 collective-permute-start.4
  26.6 4.3 collective-permute-done.5
  31.1 3.7 collective-permute-done.4
  34.8 9.2 %collective-permute-done.6 = bf16[64,2688]{1,0:T(8,128)(2,1)S(1)} collective-permute-done((bf16[64,2688]{1,0:T(8,128)(2,1)S(1)}, bf16[64,2688]{1,0:T(8,128)(2,1)S(1)}, u32[]{:S(2)}, u32[]{:S(2)}) %collective-permute-start.6) | collective-permute-done | bytes 344096 | tf_op jit(solution)/shard_map/ppermute | solution.py:464
  47.0 6.0 %collective-permute-done.7 = bf16[4,32,1536]{2,1,0:T(8,128)(2,1)S(1)} collective-permute-done((bf16[4,32,1536]{2,1,0:T(8,128)(2,1)S(1)}, bf16[4,32,1536]{2,1,0:T(8,128)(2,1)S(1)}, u32[]{:S(2)}, u32[]{:S(2)}) %collective-permute-start.7) | collective-permute-done | bytes 393248 | tf_op jit(solution)/shard_map/ppermute | solution.py:464
  53.9 6.4 %collective-permute-done.9 = bf16[2,64,2688]{2,1,0:T(8,128)(2,1)S(1)} collective-permute-done((bf16[2,64,2688]{2,1,0:T(8,128)(2,1)S(1)}, bf16[2,64,2688]{2,1,0:T(8,128)(2,1)S(1)}, u32[]{:S(2)}, u32[]{:S(2)}) %collective-permute-start.9) | collective-permute-done | bytes 688160 | tf_op jit(solution)/shard_map/ppermute | solution.py:464
  63.0 3.5 collective-permute-start.12
  68.1 2.3 collective-permute-done.12
  70.4 21.5 %collective-permute-done.13 = bf16[4,32,2688]{2,1,0:T(8,128)(2,1)S(1)} collective-permute-done((bf16[4,32,2688]{2,1,0:T(8,128)(2,1)S(1)}, bf16[4,32,2688]{2,1,0:T(8,128)(2,1)S(1)}, u32[]{:S(2)}, u32[]{:S(2)}) %collective-permute-start.13) | collective-permute-done | bytes 688160 | tf_op jit(solution)/shard_map/ppermute | solution.py:464
  93.1 3.5 collective-permute-start.15
  97.4 3.6 add_convert_fusion.own_ref.qkv_ref
  101.3 3.0 collective-permute-done.15
  108.5 12.5 %shard_map.254 = (bf16[1024,512]{1,0:T(8,128)(2,1)S(1)}, f32[8,1024]{1,0:T(8,128)S(1)}) custom-call(s32[2,4]{1,0:T(2,128)S(1)} %pad_add_fusion.1.bounds, bf16[1024,1536]{1,0:T(8,128)(2,1)S(1)} %add_convert_fusion.own_ref.qkv_ref, bf16[1024,1536]{1,0:T(8,128)(2,1)S(1)} %add_convert_fusion.own_ref.qkv_ref, s32[2,1024]{1,0:T(2,128)S(1)} %pad_add_fusion.spans), custom_call_target="tpu_custom_call" | custom-call | flops 2147483648 | bytes 12582912 | tf_op jit(solution)/shard_map/pallas_call | solution.py:678
  121.0 10.6 %collective-permute-done.18 = bf16[4,32,2048]{2,1,0:T(8,128)(2,1)S(1)} collective-permute-done((bf16[4,32,2048]{2,1,0:T(8,128)(2,1)S(1)}, bf16[4,32,2048]{2,1,0:T(8,128)(2,1)S(1)}, u32[]{:S(2)}, u32[]{:S(2)}) %collective-permute-start.18) | collective-permute-done | bytes 524320 | tf_op jit(solution)/shard_map/ppermute | solution.py:464
  134.8 2.4 copy-done.2
  138.9 5.8 %collective-permute-start.20 = (bf16[512,1024]{1,0:T(8,128)(2,1)}, bf16[512,1024]{1,0:T(8,128)(2,1)}, u32[]{:S(2)}, u32[]{:S(2)}) collective-permute-start(bf16[512,1024]{1,0:T(8,128)(2,1)} %convolution_convert_fusion.6), channel_id=1, source_target_pairs={{0,2},{2,0},{1,3},{3,1},{4,6},{6,4},{5,7},{7,5},{8,10},{10,8},{9,1... | collective-permute-start | bytes 3145736 | tf_op jit(solution)/shard_map/ppermute | solution.py:469
  144.8 2.0 fusion.31
  155.4 17.5 %shard_map.255 = (bf16[1024,2048]{1,0:T(8,128)(2,1)S(1)}, bf16[1024,2048]{1,0:T(8,128)(2,1)S(1)}) custom-call(bf16[1024,1024]{1,0:T(8,128)(2,1)S(1)} %pad_maximum_fusion.5.x_ref, bf16[1024,2688]{1,0:T(8,128)(2,1)S(1)} %bitcast.282, f32[1,2048]{1,0:T(1,128)S(1)} %slice.503.b_ref), custom_call_target="tpu_custom_call" | custom-call | flops 4294967296 | bytes 14680064 | tf_op jit(solution)/shard_map/pallas_call | solution.py:848
  172.9 2.1 copy-done.7
  175.0 2.9 collective-permute-done.23
  179.4 2.4 fusion.11
  183.4 2.8 collective-permute-start.27
  186.3 2.8 fusion.119
  194.9 7.8 %all-to-all-start = ((bf16[16,128,128]{2,1,0:T(8,128)(2,1)}), bf16[16,128,128]{2,1,0:T(8,128)(2,1)S(1)}, u32[]{:S(2)}, u32[]{:S(2)}) async-start(bf16[16,128,128]{2,1,0:T(8,128)(2,1)} %broadcast_in_dim.46), calls=%async_computation | async-start | bytes 1048576 | tf_op jit(solution)/shard_map/all_to_all | solution.py:1142
  204.0 11.4 %all-to-all-done = bf16[16,128,128]{2,1,0:T(8,128)(2,1)S(1)} async-done(((bf16[16,128,128]{2,1,0:T(8,128)(2,1)}), bf16[16,128,128]{2,1,0:T(8,128)(2,1)S(1)}, u32[]{:S(2)}, u32[]{:S(2)}) %all-to-all-start) | async-done | bytes 524320 | tf_op jit(solution)/shard_map/all_to_all | solution.py:1142
  215.4 9.1 %shard_map.256 = f32[24,2048]{1,0:T(8,128)S(1)} custom-call(bf16[2048,128]{1,0:T(8,128)(2,1)S(1)} %bitcast.287, bf16[1024,128]{1,0:T(8,128)(2,1)S(1)} %maximum_select_fusion.25.d_ref, s32[1,1024]{1,0:T(1,128)S(1)} %compare_select_fusion.seg_ref), custom_call_target="tpu_custom_call" | custom-call | flops 3221225472 | bytes 786432 | tf_op jit(solution)/shard_map/pallas_call | solution.py:903
  225.9 5.7 %all-to-all-start.1 = ((f32[16,8,128]{2,1,0:T(8,128)}), f32[16,8,128]{2,1,0:T(8,128)S(1)}, u32[]{:S(2)}, u32[]{:S(2)}) async-start(f32[16,8,128]{2,1,0:T(8,128)} %broadcast_in_dim.47), calls=%async_computation.1 | async-start | bytes 131072 | tf_op jit(solution)/shard_map/all_to_all | solution.py:1163
  231.5 5.1 %collective-permute-start.28 = (bf16[512,1024]{1,0:T(8,128)(2,1)}, bf16[512,1024]{1,0:T(8,128)(2,1)}, u32[]{:S(2)}, u32[]{:S(2)}) collective-permute-start(bf16[512,1024]{1,0:T(8,128)(2,1)} %add_convert_fusion.3), channel_id=1, source_target_pairs={{0,0},{1,2},{2,1},{3,3},{4,4},{5,6},{6,5},{7,7},{8,8},{9,10},{10,9... | collective-permute-start | bytes 3145736 | tf_op jit(solution)/shard_map/ppermute | solution.py:1183
  238.8 16.0 %shard_map.257 = (bf16[2048,128]{1,0:T(8,128)(2,1)}, f32[768,128]{1,0:T(8,128)S(1)}) custom-call(bf16[2048,128]{1,0:T(8,128)(2,1)S(1)} %bitcast.288, bf16[1024,128]{1,0:T(8,128)(2,1)S(1)} %maximum_select_fusion.25.d_ref, s32[1,1024]{1,0:T(1,128)S(1)} %compare_select_fusion.seg_ref, f32[24,2048]{1,0:T(8,128)S(1)} %convolution_divide_fusion.coef_ref), custom_call_target="tpu_custom_call" | custom-call | flops 4831838208 | bytes 1572864 | tf_op jit(solution)/shard_map/pallas_call | solution.py:979
  254.8 9.4 %all-to-all-start.2 = ((bf16[16,128,128]{2,1,0:T(8,128)(2,1)}), bf16[16,128,128]{2,1,0:T(8,128)(2,1)S(1)}, u32[]{:S(2)}, u32[]{:S(2)}) async-start(bf16[16,128,128]{2,1,0:T(8,128)(2,1)} %bitcast.57), calls=%async_computation.2 | async-start | bytes 1048576 | tf_op jit(solution)/shard_map/all_to_all | solution.py:1185
  264.3 12.1 %all-to-all-done.2 = bf16[16,128,128]{2,1,0:T(8,128)(2,1)S(1)} async-done(((bf16[16,128,128]{2,1,0:T(8,128)(2,1)}), bf16[16,128,128]{2,1,0:T(8,128)(2,1)S(1)}, u32[]{:S(2)}, u32[]{:S(2)}) %all-to-all-start.2) | async-done | bytes 524320 | tf_op jit(solution)/shard_map/all_to_all | solution.py:1185
  276.6 4.0 collective-permute-start.29
  290.1 6.4 %convolution_convert_fusion.1 = bf16[1024,2048]{1,0:T(8,128)(2,1)S(1)} fusion(bf16[1024,2048]{1,0:T(8,128)(2,1)S(1)} %copy-done.6, bf16[512,1024]{1,0:T(8,128)(2,1)} %collective-permute-done.30, bf16[512,1024]{1,0:T(8,128)(2,1)} %get-tuple-element.241), kind=kOutput, calls=%fused_computation.6 | convolution fusion | flops 4301258752 | bytes 10485760 | tf_op jit(solution)/shard_map/dot_general | solution.py:33
  300.5 7.9 %convert_reduce_fusion = (f32[2048]{0:T(1024)S(1)}, bf16[1024,2048]{1,0:T(8,128)(2,1)}) fusion(bf16[1024,2048]{1,0:T(8,128)(2,1)S(1)} %copy-done.8, bf16[1024,2048]{1,0:T(8,128)(2,1)S(1)} %bitcast.298, bf16[512,1024]{1,0:T(8,128)(2,1)} %collective-permute-done.30, bf16[512,1024]{1,0:T(8,128)(2,1)} %get-tuple-element.241), kind=kOutput, calls=%fused_computation | convolution fusion | flops 4309645312 | bytes 14688256 | tf_op jit(solution)/shard_map/dot_general | solution.py:448
  308.5 4.1 fusion.14
  312.8 2.4 fusion.2
  315.2 6.7 %collective-permute-done.33 = bf16[4,2,32,2048]{3,2,0,1:T(8,128)(2,1)S(1)} collective-permute-done((bf16[4,2,32,2048]{3,2,0,1:T(8,128)(2,1)S(1)}, bf16[4,2,32,2048]{3,2,0,1:T(8,128)(2,1)S(1)}, u32[]{:S(2)}, u32[]{:S(2)}) %collective-permute-start.33) | collective-permute-done | bytes 1048608 | tf_op jit(solution)/shard_map/ppermute | solution.py:464
  326.8 5.1 convolution_convert_fusion
  342.1 2.4 collective-permute-start.32
  344.6 16.5 %collective-permute-done.37 = bf16[4,2,32,2048]{3,2,0,1:T(8,128)(2,1)} collective-permute-done((bf16[4,2,32,2048]{3,2,0,1:T(8,128)(2,1)}, bf16[4,2,32,2048]{3,2,0,1:T(8,128)(2,1)}, u32[]{:S(2)}, u32[]{:S(2)}) %collective-permute-start.37) | collective-permute-done | bytes 1048608 | tf_op jit(solution)/shard_map/ppermute | solution.py:464
  368.2 3.8 convolution_convert_fusion.5.grad_ref
  372.1 3.5 convolution_convert_fusion.4
  380.5 13.9 %shard_map.258 = (bf16[1024,768]{1,0:T(8,128)(2,1)S(1)}, f32[8,256]{1,0:T(8,128)S(1)}) custom-call(s32[2,4]{1,0:T(2,128)S(1)} %pad_add_fusion.1.bounds, bf16[1024,1536]{1,0:T(8,128)(2,1)S(1)} %copy-done.4, bf16[1024,1536]{1,0:T(8,128)(2,1)S(1)} %copy-done.4, bf16[1024,512]{1,0:T(8,128)(2,1)S(1)} %get-tuple-element.133.out_ref, ...), custom_call_target="tpu_custom_call" | custom-call | flops 2684354560 | bytes 12582912 | tf_op jit(solution)/shard_map/pallas_call | solution.py:781
  395.4 4.1 collective-permute-start.44
  403.7 14.2 %shard_map.259 = (bf16[1024,768]{1,0:T(8,128)(2,1)S(1)}, f32[8,256]{1,0:T(8,128)S(1)}) custom-call(s32[2,4]{1,0:T(2,128)S(1)} %pad_add_fusion.1.bounds, bf16[1024,1536]{1,0:T(8,128)(2,1)S(1)} %copy-done.4, bf16[1024,1536]{1,0:T(8,128)(2,1)S(1)} %copy-done.4, bf16[1024,512]{1,0:T(8,128)(2,1)S(1)} %get-tuple-element.133.out_ref, ...), custom_call_target="tpu_custom_call" | custom-call | flops 2684354560 | bytes 12582912 | tf_op jit(solution)/shard_map/pallas_call | solution.py:781
  421.0 1.9 convolution_convert_fusion.3
  423.9 1.9 convolution_convert_fusion.2
  433.7 8.6 %collective-permute-done.53 = bf16[2,64,512]{2,1,0:T(8,128)(2,1)S(1)} collective-permute-done((bf16[2,64,512]{2,1,0:T(8,128)(2,1)S(1)}, bf16[2,64,512]{2,1,0:T(8,128)(2,1)S(1)}, u32[]{:S(2)}, u32[]{:S(2)}) %collective-permute-start.53) | collective-permute-done | bytes 131104 | tf_op jit(solution)/shard_map/ppermute | solution.py:464
  442.8 6.1 %collective-permute-done.54 = bf16[584,128]{1,0:T(8,128)(2,1)S(1)} collective-permute-done((bf16[584,128]{1,0:T(8,128)(2,1)S(1)}, bf16[584,128]{1,0:T(8,128)(2,1)S(1)}, u32[]{:S(2)}, u32[]{:S(2)}) %collective-permute-start.54) | collective-permute-done | bytes 149536 | tf_op jit(solution)/shard_map/ppermute | solution.py:464
  449.2 1.8 collective-permute-start.55
  451.7 2.5 collective-permute-start.57
  456.3 4.8 collective-permute-start.62
  461.2 1.9 collective-permute-done.58
  463.6 2.1 collective-permute-start.60
  465.8 9.1 %collective-permute-done.60 = bf16[584,128]{1,0:T(8,128)(2,1)S(1)} collective-permute-done((bf16[584,128]{1,0:T(8,128)(2,1)S(1)}, bf16[584,128]{1,0:T(8,128)(2,1)S(1)}, u32[]{:S(2)}, u32[]{:S(2)}) %collective-permute-start.60) | collective-permute-done | bytes 149536 | tf_op jit(solution)/shard_map/ppermute | solution.py:464
  475.0 6.0 %collective-permute-start.65 = (bf16[64,4096]{1,0:T(8,128)(2,1)S(1)}, bf16[64,4096]{1,0:T(8,128)(2,1)S(1)}, u32[]{:S(2)}, u32[]{:S(2)}) collective-permute-start(bf16[64,4096]{1,0:T(8,128)(2,1)S(1)} %pad_maximum_fusion.17), channel_id=1, source_target_pairs={{0,0},{1,2},{2,1},{3,3},{4,4},{5,6},{6,5},{7,7},{8,8},{9,10},{10,9... | collective-permute-start | bytes 1572872 | tf_op jit(solution)/shard_map/ppermute | solution.py:464
  482.8 9.3 %collective-permute-done.64 = bf16[584,128]{1,0:T(8,128)(2,1)S(1)} collective-permute-done((bf16[584,128]{1,0:T(8,128)(2,1)S(1)}, bf16[584,128]{1,0:T(8,128)(2,1)S(1)}, u32[]{:S(2)}, u32[]{:S(2)}) %collective-permute-start.64) | collective-permute-done | bytes 149536 | tf_op jit(solution)/shard_map/ppermute | solution.py:464
  492.2 1.9 collective-permute-start.66
  496.1 3.8 collective-permute-done.66
  506.2 2.3 copy.165
  (454 shorter events, 123.7 us)
Async XLA Ops:
  1.7 10.3 %collective-permute-start = (bf16[64,1536]{1,0:T(8,128)(2,1)S(1)}, bf16[64,1536]{1,0:T(8,128)(2,1)}, u32[]{:S(2)}, u32[]{:S(2)}) collective-permute-start(bf16[64,1536]{1,0:T(8,128)(2,1)S(1)} %slice_dynamic-update-slice_fusion), channel_id=1, source_target_pairs={{0,0},{1,2},{2,1},{3,3},{4,4},{5,6},{6,5},{7,7},{8,8},{9,10},{10,9... | collective-permute-start | bytes 589832 | tf_op jit(solution)/shard_map/ppermute | solution.py:464
  6.2 5.8 %collective-permute-start.1 = (bf16[1024,1024]{1,0:T(8,128)(2,1)}, bf16[1024,1024]{1,0:T(8,128)(2,1)S(1)}, u32[]{:S(2)}, u32[]{:S(2)}) collective-permute-start(bf16[1024,1024]{1,0:T(8,128)(2,1)} %param.15), channel_id=1, source_target_pairs={{0,2},{2,0},{1,3},{3,1},{4,6},{6,4},{5,7},{7,5},{8,10},{10,8},{9,1... | collective-permute-start | bytes 6291464 | tf_op jit(solution)/shard_map/ppermute | solution.py:464
  13.3 9.5 %collective-permute-start.3 = (bf16[64,1536]{1,0:T(8,128)(2,1)}, bf16[64,1536]{1,0:T(8,128)(2,1)}, u32[]{:S(2)}, u32[]{:S(2)}) collective-permute-start(bf16[64,1536]{1,0:T(8,128)(2,1)} %collective-permute-done), channel_id=1, source_target_pairs={{0,24},{24,0},{8,16},{16,8},{1,25},{25,1},{9,17},{17,9},{2,26},{26... | collective-permute-start | bytes 589832 | tf_op jit(solution)/shard_map/ppermute | solution.py:464
  18.5 12.4 %collective-permute-start.5 = (bf16[64,4736]{1,0:T(8,128)(2,1)}, bf16[64,4736]{1,0:T(8,128)(2,1)S(1)}, u32[]{:S(2)}, u32[]{:S(2)}) collective-permute-start(bf16[64,4736]{1,0:T(8,128)(2,1)} %fusion.39), channel_id=1, source_target_pairs={{0,0},{1,2},{2,1},{3,3},{4,4},{5,6},{6,5},{7,7},{8,8},{9,10},{10,9... | collective-permute-start | bytes 1818632 | tf_op jit(solution)/shard_map/ppermute | solution.py:464
  24.1 10.7 %collective-permute-start.4 = (bf16[2,64,1536]{2,1,0:T(8,128)(2,1)S(1)}, bf16[2,64,1536]{2,1,0:T(8,128)(2,1)S(1)}, u32[]{:S(2)}, u32[]{:S(2)}) collective-permute-start(bf16[2,64,1536]{2,1,0:T(8,128)(2,1)S(1)} %maximum_select_fusion.22), channel_id=1, source_target_pairs={{0,8},{8,0},{16,24},{24,16},{1,9},{9,1},{17,25},{25,17},{2,10},{10... | collective-permute-start | bytes 1179656 | tf_op jit(solution)/shard_map/ppermute | solution.py:464
  31.0 13.1 %collective-permute-start.6 = (bf16[64,2688]{1,0:T(8,128)(2,1)S(1)}, bf16[64,2688]{1,0:T(8,128)(2,1)S(1)}, u32[]{:S(2)}, u32[]{:S(2)}) collective-permute-start(bf16[64,2688]{1,0:T(8,128)(2,1)S(1)} %get-tuple-element.298), channel_id=1, source_target_pairs={{0,24},{24,0},{8,16},{16,8},{1,25},{25,1},{9,17},{17,9},{2,26},{26... | collective-permute-start | bytes 1032200 | tf_op jit(solution)/shard_map/ppermute | solution.py:464
  44.5 8.5 %collective-permute-start.7 = (bf16[4,32,1536]{2,1,0:T(8,128)(2,1)S(1)}, bf16[4,32,1536]{2,1,0:T(8,128)(2,1)S(1)}, u32[]{:S(2)}, u32[]{:S(2)}) collective-permute-start(bf16[4,32,1536]{2,1,0:T(8,128)(2,1)S(1)} %get-tuple-element.288), channel_id=1, source_target_pairs={{0,4},{4,0},{1,5},{5,1},{2,6},{6,2},{3,7},{7,3},{8,12},{12,8},{9,1... | collective-permute-start | bytes 1179656 | tf_op jit(solution)/shard_map/ppermute | solution.py:464
  45.8 8.2 %collective-permute-start.8 = (bf16[4,32,1536]{2,1,0:T(8,128)(2,1)S(1)}, bf16[4,32,1536]{2,1,0:T(8,128)(2,1)S(1)}, u32[]{:S(2)}, u32[]{:S(2)}) collective-permute-start(bf16[4,32,1536]{2,1,0:T(8,128)(2,1)S(1)} %get-tuple-element.287), channel_id=1, source_target_pairs={{0,1},{1,0},{2,3},{3,2},{4,5},{5,4},{6,7},{7,6},{8,9},{9,8},{10,11... | collective-permute-start | bytes 1179656 | tf_op jit(solution)/shard_map/ppermute | solution.py:464
  46.4 13.9 %collective-permute-start.9 = (bf16[2,64,2688]{2,1,0:T(8,128)(2,1)S(1)}, bf16[2,64,2688]{2,1,0:T(8,128)(2,1)S(1)}, u32[]{:S(2)}, u32[]{:S(2)}) collective-permute-start(bf16[2,64,2688]{2,1,0:T(8,128)(2,1)S(1)} %maximum_select_fusion.19), channel_id=1, source_target_pairs={{0,8},{8,0},{16,24},{24,16},{1,9},{9,1},{17,25},{25,17},{2,10},{10... | collective-permute-start | bytes 2064392 | tf_op jit(solution)/shard_map/ppermute | solution.py:464
  60.4 31.5 %collective-permute-start.10 = (bf16[4,2,32,1536]{3,2,0,1:T(8,128)(2,1)S(1)}, bf16[4,2,32,1536]{3,2,0,1:T(8,128)(2,1)S(1)}, u32[]{:S(2)}, u32[]{:S(2)}) collective-permute-start(bf16[4,2,32,1536]{3,2,0,1:T(8,128)(2,1)S(1)} %maximum_select_fusion.17), channel_id=1, source_target_pairs={{0,1},{1,0},{2,3},{3,2},{4,5},{5,4},{6,7},{7,6},{8,9},{9,8},{10,11... | collective-permute-start | bytes 2359304 | tf_op jit(solution)/shard_map/ppermute | solution.py:464
  62.0 30.0 %collective-permute-start.11 = (bf16[4,2,32,1536]{3,2,1,0:T(8,128)(2,1)S(1)}, bf16[4,2,32,1536]{3,2,1,0:T(8,128)(2,1)S(1)}, u32[]{:S(2)}, u32[]{:S(2)}) collective-permute-start(bf16[4,2,32,1536]{3,2,1,0:T(8,128)(2,1)S(1)} %maximum_select_fusion.18), channel_id=1, source_target_pairs={{0,4},{4,0},{1,5},{5,1},{2,6},{6,2},{3,7},{7,3},{8,12},{12,8},{9,1... | collective-permute-start | bytes 2359304 | tf_op jit(solution)/shard_map/ppermute | solution.py:464
  63.0 7.4 %collective-permute-start.12 = (bf16[64,2048]{1,0:T(8,128)(2,1)S(1)}, bf16[64,2048]{1,0:T(8,128)(2,1)S(1)}, u32[]{:S(2)}, u32[]{:S(2)}) collective-permute-start(bf16[64,2048]{1,0:T(8,128)(2,1)S(1)} %get-tuple-element.127), channel_id=1, source_target_pairs={{0,24},{24,0},{8,16},{16,8},{1,25},{25,1},{9,17},{17,9},{2,26},{26... | collective-permute-start | bytes 786440 | tf_op jit(solution)/shard_map/ppermute | solution.py:464
  66.5 25.4 %collective-permute-start.13 = (bf16[4,32,2688]{2,1,0:T(8,128)(2,1)S(1)}, bf16[4,32,2688]{2,1,0:T(8,128)(2,1)S(1)}, u32[]{:S(2)}, u32[]{:S(2)}) collective-permute-start(bf16[4,32,2688]{2,1,0:T(8,128)(2,1)S(1)} %get-tuple-element.278), channel_id=1, source_target_pairs={{0,4},{4,0},{1,5},{5,1},{2,6},{6,2},{3,7},{7,3},{8,12},{12,8},{9,1... | collective-permute-start | bytes 2064392 | tf_op jit(solution)/shard_map/ppermute | solution.py:464
  67.7 24.2 %collective-permute-start.14 = (bf16[4,32,2688]{2,1,0:T(8,128)(2,1)S(1)}, bf16[4,32,2688]{2,1,0:T(8,128)(2,1)S(1)}, u32[]{:S(2)}, u32[]{:S(2)}) collective-permute-start(bf16[4,32,2688]{2,1,0:T(8,128)(2,1)S(1)} %get-tuple-element.277), channel_id=1, source_target_pairs={{0,1},{1,0},{2,3},{3,2},{4,5},{5,4},{6,7},{7,6},{8,9},{9,8},{10,11... | collective-permute-start | bytes 2064392 | tf_op jit(solution)/shard_map/ppermute | solution.py:464
  92.2 39.4 %collective-permute-start.16 = (bf16[4,2,32,2688]{3,2,0,1:T(8,128)(2,1)S(1)}, bf16[4,2,32,2688]{3,2,0,1:T(8,128)(2,1)S(1)}, u32[]{:S(2)}, u32[]{:S(2)}) collective-permute-start(bf16[4,2,32,2688]{3,2,0,1:T(8,128)(2,1)S(1)} %maximum_select_fusion.9), channel_id=1, source_target_pairs={{0,1},{1,0},{2,3},{3,2},{4,5},{5,4},{6,7},{7,6},{8,9},{9,8},{10,11... | collective-permute-start | bytes 4128776 | tf_op jit(solution)/shard_map/ppermute | solution.py:464
  92.7 39.0 %collective-permute-start.17 = (bf16[4,2,32,2688]{3,2,0,1:T(8,128)(2,1)S(1)}, bf16[4,2,32,2688]{3,2,0,1:T(8,128)(2,1)S(1)}, u32[]{:S(2)}, u32[]{:S(2)}) collective-permute-start(bf16[4,2,32,2688]{3,2,0,1:T(8,128)(2,1)S(1)} %maximum_select_fusion.10), channel_id=1, source_target_pairs={{0,4},{4,0},{1,5},{5,1},{2,6},{6,2},{3,7},{7,3},{8,12},{12,8},{9,1... | collective-permute-start | bytes 4128776 | tf_op jit(solution)/shard_map/ppermute | solution.py:464
  93.1 11.3 %collective-permute-start.15 = (bf16[2,64,2048]{2,1,0:T(8,128)(2,1)S(1)}, bf16[2,64,2048]{2,1,0:T(8,128)(2,1)S(1)}, u32[]{:S(2)}, u32[]{:S(2)}) collective-permute-start(bf16[2,64,2048]{2,1,0:T(8,128)(2,1)S(1)} %maximum_select_fusion.20), channel_id=1, source_target_pairs={{0,8},{8,0},{16,24},{24,16},{1,9},{9,1},{17,25},{25,17},{2,10},{10... | collective-permute-start | bytes 1572872 | tf_op jit(solution)/shard_map/ppermute | solution.py:464
  105.8 25.8 %collective-permute-start.18 = (bf16[4,32,2048]{2,1,0:T(8,128)(2,1)S(1)}, bf16[4,32,2048]{2,1,0:T(8,128)(2,1)S(1)}, u32[]{:S(2)}, u32[]{:S(2)}) collective-permute-start(bf16[4,32,2048]{2,1,0:T(8,128)(2,1)S(1)} %get-tuple-element.282), channel_id=1, source_target_pairs={{0,4},{4,0},{1,5},{5,1},{2,6},{6,2},{3,7},{7,3},{8,12},{12,8},{9,1... | collective-permute-start | bytes 1572872 | tf_op jit(solution)/shard_map/ppermute | solution.py:464
  107.1 24.6 %collective-permute-start.19 = (bf16[4,32,2048]{2,1,0:T(8,128)(2,1)S(1)}, bf16[4,32,2048]{2,1,0:T(8,128)(2,1)S(1)}, u32[]{:S(2)}, u32[]{:S(2)}) collective-permute-start(bf16[4,32,2048]{2,1,0:T(8,128)(2,1)S(1)} %get-tuple-element.281), channel_id=1, source_target_pairs={{0,1},{1,0},{2,3},{3,2},{4,5},{5,4},{6,7},{7,6},{8,9},{9,8},{10,11... | collective-permute-start | bytes 1572872 | tf_op jit(solution)/shard_map/ppermute | solution.py:464
  138.9 8.5 %collective-permute-start.20 = (bf16[512,1024]{1,0:T(8,128)(2,1)}, bf16[512,1024]{1,0:T(8,128)(2,1)}, u32[]{:S(2)}, u32[]{:S(2)}) collective-permute-start(bf16[512,1024]{1,0:T(8,128)(2,1)} %convolution_convert_fusion.6), channel_id=1, source_target_pairs={{0,2},{2,0},{1,3},{3,1},{4,6},{6,4},{5,7},{7,5},{8,10},{10,8},{9,1... | collective-permute-start | bytes 3145736 | tf_op jit(solution)/shard_map/ppermute | solution.py:469
  153.5 24.4 %collective-permute-start.23 = (bf16[4,2,32,2048]{3,2,0,1:T(8,128)(2,1)S(1)}, bf16[4,2,32,2048]{3,2,0,1:T(8,128)(2,1)S(1)}, u32[]{:S(2)}, u32[]{:S(2)}) collective-permute-start(bf16[4,2,32,2048]{3,2,0,1:T(8,128)(2,1)S(1)} %maximum_select_fusion.13), channel_id=1, source_target_pairs={{0,1},{1,0},{2,3},{3,2},{4,5},{5,4},{6,7},{7,6},{8,9},{9,8},{10,11... | collective-permute-start | bytes 3145736 | tf_op jit(solution)/shard_map/ppermute | solution.py:464
  153.9 24.1 %collective-permute-start.24 = (bf16[4,2,32,2048]{3,2,1,0:T(8,128)(2,1)S(1)}, bf16[4,2,32,2048]{3,2,1,0:T(8,128)(2,1)S(1)}, u32[]{:S(2)}, u32[]{:S(2)}) collective-permute-start(bf16[4,2,32,2048]{3,2,1,0:T(8,128)(2,1)S(1)} %maximum_select_fusion.14), channel_id=1, source_target_pairs={{0,4},{4,0},{1,5},{5,1},{2,6},{6,2},{3,7},{7,3},{8,12},{12,8},{9,1... | collective-permute-start | bytes 3145736 | tf_op jit(solution)/shard_map/ppermute | solution.py:464
  183.4 20.6 %collective-permute-start.27 = (bf16[512,1024]{1,0:T(8,128)(2,1)}, bf16[512,1024]{1,0:T(8,128)(2,1)S(1)}, u32[]{:S(2)}, u32[]{:S(2)}) collective-permute-start(bf16[512,1024]{1,0:T(8,128)(2,1)} %param.29), channel_id=1, source_target_pairs={{0,0},{1,2},{2,1},{3,3},{4,4},{5,6},{6,5},{7,7},{8,8},{9,10},{10,9... | collective-permute-start | bytes 3145736 | tf_op jit(solution)/shard_map/ppermute | solution.py:1145
  194.9 20.5 %all-to-all-start = ((bf16[16,128,128]{2,1,0:T(8,128)(2,1)}), bf16[16,128,128]{2,1,0:T(8,128)(2,1)S(1)}, u32[]{:S(2)}, u32[]{:S(2)}) async-start(bf16[16,128,128]{2,1,0:T(8,128)(2,1)} %broadcast_in_dim.46), calls=%async_computation | async-start | bytes 1048576 | tf_op jit(solution)/shard_map/all_to_all | solution.py:1142
  225.9 12.0 %all-to-all-start.1 = ((f32[16,8,128]{2,1,0:T(8,128)}), f32[16,8,128]{2,1,0:T(8,128)S(1)}, u32[]{:S(2)}, u32[]{:S(2)}) async-start(f32[16,8,128]{2,1,0:T(8,128)} %broadcast_in_dim.47), calls=%async_computation.1 | async-start | bytes 131072 | tf_op jit(solution)/shard_map/all_to_all | solution.py:1163
  231.5 23.2 %collective-permute-start.28 = (bf16[512,1024]{1,0:T(8,128)(2,1)}, bf16[512,1024]{1,0:T(8,128)(2,1)}, u32[]{:S(2)}, u32[]{:S(2)}) collective-permute-start(bf16[512,1024]{1,0:T(8,128)(2,1)} %add_convert_fusion.3), channel_id=1, source_target_pairs={{0,0},{1,2},{2,1},{3,3},{4,4},{5,6},{6,5},{7,7},{8,8},{9,10},{10,9... | collective-permute-start | bytes 3145736 | tf_op jit(solution)/shard_map/ppermute | solution.py:1183
  254.8 21.6 %all-to-all-start.2 = ((bf16[16,128,128]{2,1,0:T(8,128)(2,1)}), bf16[16,128,128]{2,1,0:T(8,128)(2,1)S(1)}, u32[]{:S(2)}, u32[]{:S(2)}) async-start(bf16[16,128,128]{2,1,0:T(8,128)(2,1)} %bitcast.57), calls=%async_computation.2 | async-start | bytes 1048576 | tf_op jit(solution)/shard_map/all_to_all | solution.py:1185
  276.6 5.1 %collective-permute-start.29 = (f32[512,128]{1,0:T(8,128)S(1)}, f32[512,128]{1,0:T(8,128)S(1)}, u32[]{:S(2)}, u32[]{:S(2)}) collective-permute-start(f32[512,128]{1,0:T(8,128)S(1)} %constant_dynamic-slice_fusion.11), channel_id=1, source_target_pairs={{0,2},{2,0},{1,3},{3,1},{4,6},{6,4},{5,7},{7,5},{8,10},{10,8},{9,1... | collective-permute-start | bytes 786440 | tf_op jit(solution)/shard_map/ppermute | solution.py:469
  285.2 4.9 collective-permute-start.30
  297.1 24.7 %collective-permute-start.33 = (bf16[4,2,32,2048]{3,2,0,1:T(8,128)(2,1)S(1)}, bf16[4,2,32,2048]{3,2,0,1:T(8,128)(2,1)S(1)}, u32[]{:S(2)}, u32[]{:S(2)}) collective-permute-start(bf16[4,2,32,2048]{3,2,0,1:T(8,128)(2,1)S(1)} %bitcast.318), channel_id=1, source_target_pairs={{0,4},{4,0},{1,5},{5,1},{2,6},{6,2},{3,7},{7,3},{8,12},{12,8},{9,1... | collective-permute-start | bytes 3145736 | tf_op jit(solution)/shard_map/ppermute | solution.py:464
  298.4 24.4 %collective-permute-start.34 = (bf16[4,2,32,2048]{3,2,0,1:T(8,128)(2,1)S(1)}, bf16[4,2,32,2048]{3,2,0,1:T(8,128)(2,1)S(1)}, u32[]{:S(2)}, u32[]{:S(2)}) collective-permute-start(bf16[4,2,32,2048]{3,2,0,1:T(8,128)(2,1)S(1)} %bitcast.319), channel_id=1, source_target_pairs={{0,1},{1,0},{2,3},{3,2},{4,5},{5,4},{6,7},{7,6},{8,9},{9,8},{10,11... | collective-permute-start | bytes 3145736 | tf_op jit(solution)/shard_map/ppermute | solution.py:464
  312.6 26.4 %collective-permute-start.31 = (bf16[512,1024]{1,0:T(8,128)(2,1)S(1)}, bf16[512,1024]{1,0:T(8,128)(2,1)S(1)}, u32[]{:S(2)}, u32[]{:S(2)}) collective-permute-start(bf16[512,1024]{1,0:T(8,128)(2,1)S(1)} %fusion.14), channel_id=1, source_target_pairs={{0,2},{2,0},{1,3},{3,1},{4,6},{6,4},{5,7},{7,5},{8,10},{10,8},{9,1... | collective-permute-start | bytes 3145736 | tf_op jit(solution)/shard_map/ppermute | solution.py:469
  324.2 20.4 %collective-permute-start.35 = (bf16[4,32,2048]{2,1,0:T(8,128)(2,1)}, bf16[4,32,2048]{2,1,0:T(8,128)(2,1)}, u32[]{:S(2)}, u32[]{:S(2)}) collective-permute-start(bf16[4,32,2048]{2,1,0:T(8,128)(2,1)} %fusion.40), channel_id=1, source_target_pairs={{0,1},{1,0},{2,3},{3,2},{4,5},{5,4},{6,7},{7,6},{8,9},{9,8},{10,11... | collective-permute-start | bytes 1572872 | tf_op jit(solution)/shard_map/ppermute | solution.py:464
  326.4 18.2 %collective-permute-start.36 = (bf16[4,32,2048]{2,1,0:T(8,128)(2,1)}, bf16[4,32,2048]{2,1,0:T(8,128)(2,1)}, u32[]{:S(2)}, u32[]{:S(2)}) collective-permute-start(bf16[4,32,2048]{2,1,0:T(8,128)(2,1)} %fusion.41), channel_id=1, source_target_pairs={{0,4},{4,0},{1,5},{5,1},{2,6},{6,2},{3,7},{7,3},{8,12},{12,8},{9,1... | collective-permute-start | bytes 1572872 | tf_op jit(solution)/shard_map/ppermute | solution.py:464
  334.6 26.4 %collective-permute-start.37 = (bf16[4,2,32,2048]{3,2,0,1:T(8,128)(2,1)}, bf16[4,2,32,2048]{3,2,0,1:T(8,128)(2,1)}, u32[]{:S(2)}, u32[]{:S(2)}) collective-permute-start(bf16[4,2,32,2048]{3,2,0,1:T(8,128)(2,1)} %bitcast.273), channel_id=1, source_target_pairs={{0,4},{4,0},{1,5},{5,1},{2,6},{6,2},{3,7},{7,3},{8,12},{12,8},{9,1... | collective-permute-start | bytes 3145736 | tf_op jit(solution)/shard_map/ppermute | solution.py:464
  337.8 23.2 %collective-permute-start.38 = (bf16[4,2,32,2048]{3,2,0,1:T(8,128)(2,1)}, bf16[4,2,32,2048]{3,2,0,1:T(8,128)(2,1)}, u32[]{:S(2)}, u32[]{:S(2)}) collective-permute-start(bf16[4,2,32,2048]{3,2,0,1:T(8,128)(2,1)} %bitcast.272), channel_id=1, source_target_pairs={{0,1},{1,0},{2,3},{3,2},{4,5},{5,4},{6,7},{7,6},{8,9},{9,8},{10,11... | collective-permute-start | bytes 3145736 | tf_op jit(solution)/shard_map/ppermute | solution.py:464
  342.1 26.2 %collective-permute-start.32 = (bf16[512,1024]{1,0:T(8,128)(2,1)}, bf16[512,1024]{1,0:T(8,128)(2,1)}, u32[]{:S(2)}, u32[]{:S(2)}) collective-permute-start(bf16[512,1024]{1,0:T(8,128)(2,1)} %get-tuple-element.244), channel_id=1, source_target_pairs={{0,2},{2,0},{1,3},{3,1},{4,6},{6,4},{5,7},{7,5},{8,10},{10,8},{9,1... | collective-permute-start | bytes 3145736 | tf_op jit(solution)/shard_map/ppermute | solution.py:469
  376.0 18.5 %collective-permute-start.39 = (bf16[2,64,2048]{2,1,0:T(8,128)(2,1)S(1)}, bf16[2,64,2048]{2,1,0:T(8,128)(2,1)S(1)}, u32[]{:S(2)}, u32[]{:S(2)}) collective-permute-start(bf16[2,64,2048]{2,1,0:T(8,128)(2,1)S(1)} %select_convert_fusion.1), channel_id=1, source_target_pairs={{0,8},{8,0},{16,24},{24,16},{1,9},{9,1},{17,25},{25,17},{2,10},{10... | collective-permute-start | bytes 1572872 | tf_op jit(solution)/shard_map/ppermute | solution.py:464
  377.1 17.4 %collective-permute-start.40 = (bf16[4,32,2048]{2,1,0:T(8,128)(2,1)S(1)}, bf16[4,32,2048]{2,1,0:T(8,128)(2,1)S(1)}, u32[]{:S(2)}, u32[]{:S(2)}) collective-permute-start(bf16[4,32,2048]{2,1,0:T(8,128)(2,1)S(1)} %fusion.42), channel_id=1, source_target_pairs={{0,1},{1,0},{2,3},{3,2},{4,5},{5,4},{6,7},{7,6},{8,9},{9,8},{10,11... | collective-permute-start | bytes 1572872 | tf_op jit(solution)/shard_map/ppermute | solution.py:464
  378.4 16.1 %collective-permute-start.41 = (bf16[4,32,2048]{2,1,0:T(8,128)(2,1)S(1)}, bf16[4,32,2048]{2,1,0:T(8,128)(2,1)S(1)}, u32[]{:S(2)}, u32[]{:S(2)}) collective-permute-start(bf16[4,32,2048]{2,1,0:T(8,128)(2,1)S(1)} %fusion.43), channel_id=1, source_target_pairs={{0,4},{4,0},{1,5},{5,1},{2,6},{6,2},{3,7},{7,3},{8,12},{12,8},{9,1... | collective-permute-start | bytes 1572872 | tf_op jit(solution)/shard_map/ppermute | solution.py:464
  379.1 15.4 %collective-permute-start.42 = (bf16[4,2,32,512]{3,2,0,1:T(8,128)(2,1)S(1)}, bf16[4,2,32,512]{3,2,0,1:T(8,128)(2,1)S(1)}, u32[]{:S(2)}, u32[]{:S(2)}) collective-permute-start(bf16[4,2,32,512]{3,2,0,1:T(8,128)(2,1)S(1)} %dynamic-slice_bitcast_fusion.3), channel_id=1, source_target_pairs={{0,4},{4,0},{1,5},{5,1},{2,6},{6,2},{3,7},{7,3},{8,12},{12,8},{9,1... | collective-permute-start | bytes 786440 | tf_op jit(solution)/shard_map/ppermute | solution.py:464
  380.2 14.3 %collective-permute-start.43 = (bf16[4,2,32,512]{3,2,0,1:T(8,128)(2,1)S(1)}, bf16[4,2,32,512]{3,2,0,1:T(8,128)(2,1)S(1)}, u32[]{:S(2)}, u32[]{:S(2)}) collective-permute-start(bf16[4,2,32,512]{3,2,0,1:T(8,128)(2,1)S(1)} %dynamic-slice_bitcast_fusion.2), channel_id=1, source_target_pairs={{0,1},{1,0},{2,3},{3,2},{4,5},{5,4},{6,7},{7,6},{8,9},{9,8},{10,11... | collective-permute-start | bytes 786440 | tf_op jit(solution)/shard_map/ppermute | solution.py:464
  395.4 5.5 %collective-permute-start.44 = (f32[16,4]{1,0:T(8,128)S(1)}, f32[16,4]{1,0:T(8,128)S(1)}, u32[]{:S(2)}, u32[]{:S(2)}) collective-permute-start(f32[16,4]{1,0:T(8,128)S(1)} %reshape.820), channel_id=1, source_target_pairs={{0,2},{2,0},{1,3},{3,1},{4,6},{6,4},{5,7},{7,5},{8,10},{10,8},{9,1... | collective-permute-start | bytes 776 | tf_op jit(solution)/shard_map/ppermute | solution.py:469
  399.5 18.5 %collective-permute-start.46 = (bf16[64,2048]{1,0:T(8,128)(2,1)S(1)}, bf16[64,2048]{1,0:T(8,128)(2,1)S(1)}, u32[]{:S(2)}, u32[]{:S(2)}) collective-permute-start(bf16[64,2048]{1,0:T(8,128)(2,1)S(1)} %fusion.54), channel_id=1, source_target_pairs={{0,24},{24,0},{8,16},{16,8},{1,25},{25,1},{9,17},{17,9},{2,26},{26... | collective-permute-start | bytes 786440 | tf_op jit(solution)/shard_map/ppermute | solution.py:464
  400.3 18.9 %collective-permute-start.47 = (bf16[2,64,2048]{2,1,0:T(8,128)(2,1)S(1)}, bf16[2,64,2048]{2,1,0:T(8,128)(2,1)S(1)}, u32[]{:S(2)}, u32[]{:S(2)}) collective-permute-start(bf16[2,64,2048]{2,1,0:T(8,128)(2,1)S(1)} %select_convert_fusion), channel_id=1, source_target_pairs={{0,8},{8,0},{16,24},{24,16},{1,9},{9,1},{17,25},{25,17},{2,10},{10... | collective-permute-start | bytes 1572872 | tf_op jit(solution)/shard_map/ppermute | solution.py:464
  401.5 16.6 %collective-permute-start.48 = (bf16[4,32,512]{2,1,0:T(8,128)(2,1)S(1)}, bf16[4,32,512]{2,1,0:T(8,128)(2,1)S(1)}, u32[]{:S(2)}, u32[]{:S(2)}) collective-permute-start(bf16[4,32,512]{2,1,0:T(8,128)(2,1)S(1)} %fusion.62), channel_id=1, source_target_pairs={{0,1},{1,0},{2,3},{3,2},{4,5},{5,4},{6,7},{7,6},{8,9},{9,8},{10,11... | collective-permute-start | bytes 393224 | tf_op jit(solution)/shard_map/ppermute | solution.py:464
  401.9 16.2 %collective-permute-start.49 = (bf16[4,32,512]{2,1,0:T(8,128)(2,1)S(1)}, bf16[4,32,512]{2,1,0:T(8,128)(2,1)S(1)}, u32[]{:S(2)}, u32[]{:S(2)}) collective-permute-start(bf16[4,32,512]{2,1,0:T(8,128)(2,1)S(1)} %fusion.63), channel_id=1, source_target_pairs={{0,4},{4,0},{1,5},{5,1},{2,6},{6,2},{3,7},{7,3},{8,12},{12,8},{9,1... | collective-permute-start | bytes 393224 | tf_op jit(solution)/shard_map/ppermute | solution.py:464
  426.8 22.0 %collective-permute-start.50 = (bf16[4,2,32,1536]{3,2,0,1:T(8,128)(2,1)S(1)}, bf16[4,2,32,1536]{3,2,0,1:T(8,128)(2,1)S(1)}, u32[]{:S(2)}, u32[]{:S(2)}) collective-permute-start(bf16[4,2,32,1536]{3,2,0,1:T(8,128)(2,1)S(1)} %dynamic-slice_bitcast_fusion.1), channel_id=1, source_target_pairs={{0,4},{4,0},{1,5},{5,1},{2,6},{6,2},{3,7},{7,3},{8,12},{12,8},{9,1... | collective-permute-start | bytes 2359304 | tf_op jit(solution)/shard_map/ppermute | solution.py:464
  427.5 21.3 %collective-permute-start.51 = (bf16[4,2,32,1536]{3,2,0,1:T(8,128)(2,1)S(1)}, bf16[4,2,32,1536]{3,2,0,1:T(8,128)(2,1)S(1)}, u32[]{:S(2)}, u32[]{:S(2)}) collective-permute-start(bf16[4,2,32,1536]{3,2,0,1:T(8,128)(2,1)S(1)} %dynamic-slice_bitcast_fusion), channel_id=1, source_target_pairs={{0,1},{1,0},{2,3},{3,2},{4,5},{5,4},{6,7},{7,6},{8,9},{9,8},{10,11... | collective-permute-start | bytes 2359304 | tf_op jit(solution)/shard_map/ppermute | solution.py:464
  429.3 19.5 %collective-permute-start.52 = (bf16[64,2048]{1,0:T(8,128)(2,1)S(1)}, bf16[64,2048]{1,0:T(8,128)(2,1)S(1)}, u32[]{:S(2)}, u32[]{:S(2)}) collective-permute-start(bf16[64,2048]{1,0:T(8,128)(2,1)S(1)} %fusion.55), channel_id=1, source_target_pairs={{0,24},{24,0},{8,16},{16,8},{1,25},{25,1},{9,17},{17,9},{2,26},{26... | collective-permute-start | bytes 786440 | tf_op jit(solution)/shard_map/ppermute | solution.py:464
  431.2 11.1 %collective-permute-start.53 = (bf16[2,64,512]{2,1,0:T(8,128)(2,1)S(1)}, bf16[2,64,512]{2,1,0:T(8,128)(2,1)S(1)}, u32[]{:S(2)}, u32[]{:S(2)}) collective-permute-start(bf16[2,64,512]{2,1,0:T(8,128)(2,1)S(1)} %select_convert_fusion.6), channel_id=1, source_target_pairs={{0,8},{8,0},{16,24},{24,16},{1,9},{9,1},{17,25},{25,17},{2,10},{10... | collective-permute-start | bytes 393224 | tf_op jit(solution)/shard_map/ppermute | solution.py:464
  431.3 17.5 %collective-permute-start.54 = (bf16[584,128]{1,0:T(8,128)(2,1)S(1)}, bf16[584,128]{1,0:T(8,128)(2,1)S(1)}, u32[]{:S(2)}, u32[]{:S(2)}) collective-permute-start(bf16[584,128]{1,0:T(8,128)(2,1)S(1)} %convert_element_type.481), channel_id=1, source_target_pairs={{0,1},{1,0},{2,3},{3,2},{4,5},{5,4},{6,7},{7,6},{8,9},{9,8},{10,11... | collective-permute-start | bytes 448520 | tf_op jit(solution)/shard_map/ppermute | solution.py:464
  442.3 12.9 %collective-permute-start.61 = (bf16[512,1024]{1,0:T(8,128)(2,1)S(1)}, bf16[512,1024]{1,0:T(8,128)(2,1)S(1)}, u32[]{:S(2)}, u32[]{:S(2)}) collective-permute-start(bf16[512,1024]{1,0:T(8,128)(2,1)S(1)} %add_convert_fusion.2), channel_id=1, source_target_pairs={{0,2},{2,0},{1,3},{3,1},{4,6},{6,4},{5,7},{7,5},{8,10},{10,8},{9,1... | collective-permute-start | bytes 3145736 | tf_op jit(solution)/shard_map/ppermute | solution.py:469
  449.2 14.0 %collective-permute-start.55 = (bf16[4,32,1536]{2,1,0:T(8,128)(2,1)S(1)}, bf16[4,32,1536]{2,1,0:T(8,128)(2,1)S(1)}, u32[]{:S(2)}, u32[]{:S(2)}) collective-permute-start(bf16[4,32,1536]{2,1,0:T(8,128)(2,1)S(1)} %fusion.49), channel_id=1, source_target_pairs={{0,1},{1,0},{2,3},{3,2},{4,5},{5,4},{6,7},{7,6},{8,9},{9,8},{10,11... | collective-permute-start | bytes 1179656 | tf_op jit(solution)/shard_map/ppermute | solution.py:464
  451.3 11.8 %collective-permute-start.56 = (bf16[4,32,1536]{2,1,0:T(8,128)(2,1)S(1)}, bf16[4,32,1536]{2,1,0:T(8,128)(2,1)S(1)}, u32[]{:S(2)}, u32[]{:S(2)}) collective-permute-start(bf16[4,32,1536]{2,1,0:T(8,128)(2,1)S(1)} %fusion.50), channel_id=1, source_target_pairs={{0,4},{4,0},{1,5},{5,1},{2,6},{6,2},{3,7},{7,3},{8,12},{12,8},{9,1... | collective-permute-start | bytes 1179656 | tf_op jit(solution)/shard_map/ppermute | solution.py:464
  451.7 9.5 %collective-permute-start.57 = (bf16[64,512]{1,0:T(8,128)(2,1)S(1)}, bf16[64,512]{1,0:T(8,128)(2,1)S(1)}, u32[]{:S(2)}, u32[]{:S(2)}) collective-permute-start(bf16[64,512]{1,0:T(8,128)(2,1)S(1)} %fusion.68), channel_id=1, source_target_pairs={{0,24},{24,0},{8,16},{16,8},{1,25},{25,1},{9,17},{17,9},{2,26},{26... | collective-permute-start | bytes 196616 | tf_op jit(solution)/shard_map/ppermute | solution.py:464
  454.2 9.0 %collective-permute-start.58 = (bf16[584,128]{1,0:T(8,128)(2,1)S(1)}, bf16[584,128]{1,0:T(8,128)(2,1)S(1)}, u32[]{:S(2)}, u32[]{:S(2)}) collective-permute-start(bf16[584,128]{1,0:T(8,128)(2,1)S(1)} %fusion.56), channel_id=1, source_target_pairs={{0,4},{4,0},{1,5},{5,1},{2,6},{6,2},{3,7},{7,3},{8,12},{12,8},{9,1... | collective-permute-start | bytes 448520 | tf_op jit(solution)/shard_map/ppermute | solution.py:464
  456.3 18.6 %collective-permute-start.62 = (bf16[512,1024]{1,0:T(8,128)(2,1)S(1)}, bf16[512,1024]{1,0:T(8,128)(2,1)S(1)}, u32[]{:S(2)}, u32[]{:S(2)}) collective-permute-start(bf16[512,1024]{1,0:T(8,128)(2,1)S(1)} %add_convert_fusion.1), channel_id=1, source_target_pairs={{0,0},{1,2},{2,1},{3,3},{4,4},{5,6},{6,5},{7,7},{8,8},{9,10},{10,9... | collective-permute-start | bytes 3145736 | tf_op jit(solution)/shard_map/ppermute | solution.py:464
  463.5 11.4 %collective-permute-start.59 = (bf16[2,64,1536]{2,1,0:T(8,128)(2,1)S(1)}, bf16[2,64,1536]{2,1,0:T(8,128)(2,1)S(1)}, u32[]{:S(2)}, u32[]{:S(2)}) collective-permute-start(bf16[2,64,1536]{2,1,0:T(8,128)(2,1)S(1)} %select_convert_fusion.2), channel_id=1, source_target_pairs={{0,8},{8,0},{16,24},{24,16},{1,9},{9,1},{17,25},{25,17},{2,10},{10... | collective-permute-start | bytes 1179656 | tf_op jit(solution)/shard_map/ppermute | solution.py:464
  463.6 11.3 %collective-permute-start.60 = (bf16[584,128]{1,0:T(8,128)(2,1)S(1)}, bf16[584,128]{1,0:T(8,128)(2,1)S(1)}, u32[]{:S(2)}, u32[]{:S(2)}) collective-permute-start(bf16[584,128]{1,0:T(8,128)(2,1)S(1)} %fusion.97), channel_id=1, source_target_pairs={{0,24},{24,0},{8,16},{16,8},{1,25},{25,1},{9,17},{17,9},{2,26},{26... | collective-permute-start | bytes 448520 | tf_op jit(solution)/shard_map/ppermute | solution.py:464
  475.0 17.1 %collective-permute-start.65 = (bf16[64,4096]{1,0:T(8,128)(2,1)S(1)}, bf16[64,4096]{1,0:T(8,128)(2,1)S(1)}, u32[]{:S(2)}, u32[]{:S(2)}) collective-permute-start(bf16[64,4096]{1,0:T(8,128)(2,1)S(1)} %pad_maximum_fusion.17), channel_id=1, source_target_pairs={{0,0},{1,2},{2,1},{3,3},{4,4},{5,6},{6,5},{7,7},{8,8},{9,10},{10,9... | collective-permute-start | bytes 1572872 | tf_op jit(solution)/shard_map/ppermute | solution.py:464
  481.1 11.0 %collective-permute-start.63 = (bf16[64,1536]{1,0:T(8,128)(2,1)S(1)}, bf16[64,1536]{1,0:T(8,128)(2,1)S(1)}, u32[]{:S(2)}, u32[]{:S(2)}) collective-permute-start(bf16[64,1536]{1,0:T(8,128)(2,1)S(1)} %fusion.58), channel_id=1, source_target_pairs={{0,24},{24,0},{8,16},{16,8},{1,25},{25,1},{9,17},{17,9},{2,26},{26... | collective-permute-start | bytes 589832 | tf_op jit(solution)/shard_map/ppermute | solution.py:464
  482.7 9.4 %collective-permute-start.64 = (bf16[584,128]{1,0:T(8,128)(2,1)S(1)}, bf16[584,128]{1,0:T(8,128)(2,1)S(1)}, u32[]{:S(2)}, u32[]{:S(2)}) collective-permute-start(bf16[584,128]{1,0:T(8,128)(2,1)S(1)} %fusion.57), channel_id=1, source_target_pairs={{0,8},{8,0},{16,24},{24,16},{1,9},{9,1},{17,25},{25,17},{2,10},{10... | collective-permute-start | bytes 448520 | tf_op jit(solution)/shard_map/ppermute | solution.py:464
  492.2 7.7 %collective-permute-start.66 = (bf16[64,2048]{1,0:T(8,128)(2,1)S(1)}, bf16[64,2048]{1,0:T(8,128)(2,1)S(1)}, u32[]{:S(2)}, u32[]{:S(2)}) collective-permute-start(bf16[64,2048]{1,0:T(8,128)(2,1)S(1)} %pad_maximum_fusion.20), channel_id=1, source_target_pairs={{0,0},{1,2},{2,1},{3,3},{4,4},{5,6},{6,5},{7,7},{8,8},{9,10},{10,9... | collective-permute-start | bytes 786440 | tf_op jit(solution)/shard_map/ppermute | solution.py:464
  (61 other events, 603.8 us)

commit v2 on v1

--- a/solution.py
+++ b/solution.py
@@ -599,6 +599,7 @@
 
 TILE = 256
 KEYS = 256
+LOSS_TILE = 512
 NEG = -1e30
 
 
@@ -831,7 +832,7 @@
 
 def expand_kernel(x_ref, w_ref, b_ref, *refs):
     act_ref, slope_ref = refs[-2:]
-    rows = 256
+    rows = 128
     for start in range(0, x_ref.shape[0], rows):
         part = slice(start, start + rows)
         value = exact(x_ref[part, :], w_ref[...], ((1,), (0,))) + b_ref[...]
@@ -902,13 +903,13 @@
     whole = lambda shape: pl.BlockSpec(shape, lambda i: (0, 0))
     return pl.pallas_call(
         partial(pool_kernel, cuts, span),
-        grid=(count // TILE,),
+        grid=(count // LOSS_TILE,),
         in_specs=[
-            pl.BlockSpec((TILE, width), lambda i: (i, 0)),
+            pl.BlockSpec((LOSS_TILE, width), lambda i: (i, 0)),
             whole((tokens, width)),
             whole((1, tokens)),
         ],
-        out_specs=pl.BlockSpec((len(cuts) * NDOC, TILE), lambda i: (0, i)),
+        out_specs=pl.BlockSpec((len(cuts) * NDOC, LOSS_TILE), lambda i: (0, i)),
         out_shape=jax.ShapeDtypeStruct((len(cuts) * NDOC, count), F32),
         scratch_shapes=[
             pltpu.VMEM((len(cuts), tokens - span, width), BF),
@@ -978,14 +979,14 @@
     whole = lambda shape: pl.BlockSpec(shape, lambda i: (0, 0))
     return pl.pallas_call(
         partial(pool_back_kernel, cuts, span),
-        grid=(count // TILE,),
+        grid=(count // LOSS_TILE,),
         in_specs=[
-            pl.BlockSpec((TILE, width), lambda i: (i, 0)),
+            pl.BlockSpec((LOSS_TILE, width), lambda i: (i, 0)),
             whole((tokens, width)),
             whole((1, tokens)),
-            pl.BlockSpec((len(cuts) * NDOC, TILE), lambda i: (0, i)),
+            pl.BlockSpec((len(cuts) * NDOC, LOSS_TILE), lambda i: (0, i)),
         ],
-        out_specs=[pl.BlockSpec((TILE, width), lambda i: (i, 0)), whole((docs, width))],
+        out_specs=[pl.BlockSpec((LOSS_TILE, width), lambda i: (i, 0)), whole((docs, width))],
         out_shape=[
             jax.ShapeDtypeStruct((count, width), BF),
             jax.ShapeDtypeStruct((docs, width), F32),
@@ -1039,7 +1040,8 @@
         [w_qkv[k][:, g * quarter : (g + 1) * quarter] for g in range(2) for k in range(3)], axis=1
     )
     pair_rows = jnp.pad(pairing.astype(BF), ((0, 63), (0, 128 - half_queries)))
-    mid_rows = jnp.concatenate([w_up, w_out.T, pair_rows], axis=1)
+    qkv_rows = jnp.concatenate([qkv_rows, w_out.T], axis=1)
+    mid_rows = jnp.concatenate([w_up, pair_rows], axis=1)
     bias = jnp.concatenate([b_qv.reshape(-1), b_up])[None].astype(F32)
     got = exchange(
         (qkv_rows, CORES, TURN), (tokens, "c", SWAP), (bias, "y", SWAP)
@@ -1068,12 +1070,7 @@
     mid_parts = first_parts(mid_line, got[3:], x, y)
     (near,) = exchange((down_pair, "z", NEAR))
     down_line = whole_line(down_pair, near, z)
-    got = exchange(*last_moves(mid_parts), *first_moves(down_line))
-    full_mid = full_rows(mid_parts, got, x, y)
-    down_parts = first_parts(down_line, got[2:], x, y)
-    full_out = full_mid[:, up_wide : up_wide + half_width]
-    pairs = full_mid[:, up_wide + half_width :].reshape(chip_count, 64, 128)
-    pairs = pairs[:, 0, :half_queries].astype(jnp.int32).reshape(1, query_total)
+    full_qkv, full_out = full_qkv[:, : 3 * half_width], full_qkv[:, 3 * half_width :]
     row_lengths = lax.dynamic_index_in_dim(lengths, chip, 0, keepdims=False)
     segments = segments_of(row_lengths, token_count)
     seg_row, spans = segments[None, :], token_spans(row_lengths, token_count)
@@ -1093,7 +1090,16 @@
         axis=1,
     )
     qkv = (dot(row, full_qkv) + qkv_bias).astype(BF)
-    mixed, lse = attend(bounds, tie(qkv, down_line), spans)
+    down_line, qkv, first_norm = lax.optimization_barrier(
+        (down_line, qkv, jnp.stack([gains[0], shifts[0]]))
+    )
+    first_norm = swap(first_norm, "c")
+    first_norm, qkv = lax.optimization_barrier((first_norm, qkv))
+    full_mid = full_rows(mid_parts, exchange(*last_moves(mid_parts)), x, y)
+    down_parts = first_parts(down_line, exchange(*first_moves(down_line)), x, y)
+    pairs = full_mid[:, up_wide:].reshape(chip_count, 64, 128)
+    pairs = pairs[:, 0, :half_queries].astype(jnp.int32).reshape(1, query_total)
+    mixed, lse = attend(bounds, qkv, spans)
 
     def row_sum(left, weight_t, transposed):
         times = contract_cols if transposed else dot
@@ -1104,19 +1110,20 @@
         return rows_of(mixed, other_start if which else own_start, share)
 
     other_attn = swap(contract_cols(mixed_half(1), full_out).astype(BF), "c")
-    other_attn, second_norm = lax.optimization_barrier(
-        (other_attn, jnp.stack([gains[1], shifts[1]]))
+    attn_sum = contract_cols(mixed_half(0), full_out) + other_attn.astype(F32)
+    own_tokens = rows_of(row, own_start, share).astype(F32)
+    normed, unit_one, rstd_one = norm_forward(
+        own_tokens + attn_sum + b_out.astype(F32), first_norm[0], first_norm[1]
+    )
+    normed_low = normed.astype(BF)
+    other_normed = swap(normed_low, "c")
+    other_normed, second_norm = lax.optimization_barrier(
+        (other_normed, jnp.stack([gains[1], shifts[1]]))
     )
     second_norm = swap(second_norm, "c")
     second_norm, *down_parts = lax.optimization_barrier((second_norm,) + tuple(down_parts))
     down_got = exchange(*last_moves(down_parts))
-    attn_sum = contract_cols(mixed_half(0), full_out) + other_attn.astype(F32)
-    own_tokens = rows_of(row, own_start, share).astype(F32)
-    normed, unit_one, rstd_one = norm_forward(
-        own_tokens + attn_sum + b_out.astype(F32), gains[0], shifts[0]
-    )
-    normed_low = normed.astype(BF)
-    normed_all = jnp.concatenate([normed_low, swap(normed_low, "c")], axis=0)
+    normed_all = jnp.concatenate([normed_low, other_normed], axis=0)
     activation, slope = expand(
         normed_all, full_mid, bias[:, 2 * half_width :], 0, up_wide // 256
     )
@@ -1220,7 +1227,7 @@
     )
     gain_one = jnp.sum(grad_normed * unit_one, axis=0)
     shift_one = jnp.sum(grad_normed, axis=0)
-    grad_first = norm_backward(grad_normed, unit_one, rstd_one, gains[0])
+    grad_first = norm_backward(grad_normed, unit_one, rstd_one, first_norm[0])
     grad_attn = grad_first.astype(BF)
     out_bias = jnp.sum(grad_attn.astype(F32), axis=0)
     other_attn = swap(grad_attn, "c")

time: 516 us -> 526 us (1.019)
  waiting for transfers between devices: 163 us -> 192 us
  Pallas kernels: 83.1 us -> 65.6 us
  matrix products: 61.9 us -> 55.2 us
    ppermute x54, waiting for transfers between devices: 135 us -> 165 us  [exchange(): lax.ppermute(value, axis, steps)]
    pallas_call x2, Pallas kernels: 28.1 us -> 19.2 us  [attend_back(): pl.pallas_call(partial(attend_back_kernel, group * heads), grid=(count //...]
    ppermute x12 -> x13, starting transfers between devices: 20.5 us -> 23 us  [swap(): return lax.ppermute(value, axis, SWAP)]
    unnamed x129 -> x120, local copies, waits for them, and re-layouts: 20.8 us -> 21.8 us
  transfers between devices with their start and end apart: 71 -> 72, of which waited for: 29 -> 39; matrix products, arithmetic and copies ran while one was open for 15% -> 16% of each run, Pallas kernels for 15% -> 11%
where the time goes in v2:
time: 526 us; the launch traced here: 519 us
  waiting for transfers between devices  192 us (37%)
  starting transfers between devices  121 us (23%)
  Pallas kernels  65.6 us (12%)
  matrix products  55.2 us (10%)
  local copies, waits for them, and re-layouts  46 us (9%)
  other arithmetic  35.6 us (7%)
    ppermute x54, waiting for transfers between devices, exchange(): lax.ppermute(value, axis, steps)  165 us
    ppermute x54, starting transfers between devices, exchange(): lax.ppermute(value, axis, steps)  69.4 us
    ppermute x13, starting transfers between devices, swap(): return lax.ppermute(value, axis, SWAP)  23 us
    unnamed x120, local copies, waits for them, and re-layouts  21.8 us
    dot_general x7, matrix products, contract_rows(): lax.dot_general(left, right, (((0,), (0,)), ((), ())), precision=precisio...  20.3 us
    dot_general x12, matrix products, contract_cols(): lax.dot_general(left, right, (((1,), (1,)), ((), ())), precision=precisio...  19.2 us
    pallas_call x2, Pallas kernels, attend_back(): pl.pallas_call(partial(attend_back_kernel, group * heads), grid=(count //...  19.2 us
    pallas_call x1, Pallas kernels, expand(): pl.pallas_call(expand_kernel, grid=(tiles,), in_specs=[pl.BlockSpec((coun...  16.6 us
  transfers between devices with their start and end apart: 72, of which 39 were waited for; matrix products, arithmetic and copies ran while one was open for 16% of the time, Pallas kernels for 11%

profile of v2, /device:TPU:1, one launch (start us, length us, event | category | flops | bytes accessed | tf_op | source)
XLA Modules:
  0.0 518.6 jit_solution(16007857163613736349)
XLA Ops:
  2.2 2.1 collective-permute-start.2
  10.5 2.5 collective-permute-start
  18.4 3.3 broadcast_select_fusion
  21.7 3.4 collective-permute-start.4
  25.1 3.2 collective-permute-start.3
  30.3 5.3 %collective-permute-start.5 = (bf16[2,64,2048]{2,1,0:T(8,128)(2,1)S(1)}, bf16[2,64,2048]{2,1,0:T(8,128)(2,1)S(1)}, u32[]{:S(2)}, u32[]{:S(2)}) collective-permute-start(bf16[2,64,2048]{2,1,0:T(8,128)(2,1)S(1)} %maximum_select_fusion.20), channel_id=1, source_target_pairs={{0,8},{8,0},{16,24},{24,16},{1,9},{9,1},{17,25},{25,17},{2,10},{10... | collective-permute-start | bytes 1572872 | tf_op jit(solution)/shard_map/ppermute | solution.py:464
  35.8 2.1 collective-permute-start.6
  38.0 9.9 %collective-permute-done.5 = bf16[2,64,2048]{2,1,0:T(8,128)(2,1)S(1)} collective-permute-done((bf16[2,64,2048]{2,1,0:T(8,128)(2,1)S(1)}, bf16[2,64,2048]{2,1,0:T(8,128)(2,1)S(1)}, u32[]{:S(2)}, u32[]{:S(2)}) %collective-permute-start.5) | collective-permute-done | bytes 524320 | tf_op jit(solution)/shard_map/ppermute | solution.py:464
  47.9 8.0 %collective-permute-done.6 = bf16[64,2176]{1,0:T(8,128)(2,1)S(1)} collective-permute-done((bf16[64,2176]{1,0:T(8,128)(2,1)S(1)}, bf16[64,2176]{1,0:T(8,128)(2,1)S(1)}, u32[]{:S(2)}, u32[]{:S(2)}) %collective-permute-start.6) | collective-permute-done | bytes 278560 | tf_op jit(solution)/shard_map/ppermute | solution.py:464
  58.0 11.8 %collective-permute-done.8 = bf16[4,32,2048]{2,1,0:T(8,128)(2,1)S(1)} collective-permute-done((bf16[4,32,2048]{2,1,0:T(8,128)(2,1)S(1)}, bf16[4,32,2048]{2,1,0:T(8,128)(2,1)S(1)}, u32[]{:S(2)}, u32[]{:S(2)}) %collective-permute-start.8) | collective-permute-done | bytes 524320 | tf_op jit(solution)/shard_map/ppermute | solution.py:464
  75.2 3.9 collective-permute-done.12
  79.0 27.1 %collective-permute-done.14 = bf16[4,32,2176]{2,1,0:T(8,128)(2,1)S(1)} collective-permute-done((bf16[4,32,2176]{2,1,0:T(8,128)(2,1)S(1)}, bf16[4,32,2176]{2,1,0:T(8,128)(2,1)S(1)}, u32[]{:S(2)}, u32[]{:S(2)}) %collective-permute-start.14) | collective-permute-done | bytes 557088 | tf_op jit(solution)/shard_map/ppermute | solution.py:464
  110.2 3.6 add_convert_fusion.own_ref.qkv_ref
  113.9 3.1 collective-permute-done.15
  117.2 4.4 collective-permute-start.16
  123.5 8.3 %shard_map.254 = (bf16[1024,512]{1,0:T(8,128)(2,1)S(1)}, f32[8,1024]{1,0:T(8,128)S(1)}) custom-call(s32[2,4]{1,0:T(2,128)S(1)} %pad_add_fusion.1.bounds, bf16[1024,1536]{1,0:T(8,128)(2,1)S(1)} %add_convert_fusion.own_ref.qkv_ref, bf16[1024,1536]{1,0:T(8,128)(2,1)S(1)} %add_convert_fusion.own_ref.qkv_ref, s32[2,1024]{1,0:T(2,128)S(1)} %pad_add_fusion.spans), custom_call_target="tpu_custom_call" | custom-call | flops 2147483648 | bytes 12582912 | tf_op jit(solution)/shard_map/pallas_call | solution.py:679
  133.3 2.9 collective-permute-start.23
  139.6 8.8 %collective-permute-done.23 = bf16[4,32,2048]{2,1,0:T(8,128)(2,1)S(1)} collective-permute-done((bf16[4,32,2048]{2,1,0:T(8,128)(2,1)S(1)}, bf16[4,32,2048]{2,1,0:T(8,128)(2,1)S(1)}, u32[]{:S(2)}, u32[]{:S(2)}) %collective-permute-start.23) | collective-permute-done | bytes 524320 | tf_op jit(solution)/shard_map/ppermute | solution.py:464
  148.4 11.1 %collective-permute-done.22 = bf16[4,32,2048]{2,1,0:T(8,128)(2,1)S(1)} collective-permute-done((bf16[4,32,2048]{2,1,0:T(8,128)(2,1)S(1)}, bf16[4,32,2048]{2,1,0:T(8,128)(2,1)S(1)}, u32[]{:S(2)}, u32[]{:S(2)}) %collective-permute-start.22) | collective-permute-done | bytes 524320 | tf_op jit(solution)/shard_map/ppermute | solution.py:464
  165.3 16.6 %shard_map.255 = (bf16[1024,2048]{1,0:T(8,128)(2,1)S(1)}, bf16[1024,2048]{1,0:T(8,128)(2,1)S(1)}) custom-call(bf16[1024,1024]{1,0:T(8,128)(2,1)S(1)} %pad_maximum_fusion.5.x_ref, bf16[1024,2176]{1,0:T(8,128)(2,1)S(1)} %bitcast.276, f32[1,2048]{1,0:T(1,128)S(1)} %slice.516.b_ref), custom_call_target="tpu_custom_call" | custom-call | flops 4294967296 | bytes 14680064 | tf_op jit(solution)/shard_map/pallas_call | solution.py:849
  182.0 2.1 copy-done.2
  184.1 2.1 copy-done.7
  188.6 2.4 fusion.12
  192.5 2.5 collective-permute-start.28
  195.1 2.8 fusion.123
  203.7 5.8 %all-to-all-start = ((bf16[16,128,128]{2,1,0:T(8,128)(2,1)}), bf16[16,128,128]{2,1,0:T(8,128)(2,1)S(1)}, u32[]{:S(2)}, u32[]{:S(2)}) async-start(bf16[16,128,128]{2,1,0:T(8,128)(2,1)} %broadcast_in_dim.46), calls=%async_computation | async-start | bytes 1048576 | tf_op jit(solution)/shard_map/all_to_all | solution.py:1149
  210.7 11.4 %all-to-all-done = bf16[16,128,128]{2,1,0:T(8,128)(2,1)S(1)} async-done(((bf16[16,128,128]{2,1,0:T(8,128)(2,1)}), bf16[16,128,128]{2,1,0:T(8,128)(2,1)S(1)}, u32[]{:S(2)}, u32[]{:S(2)}) %all-to-all-start) | async-done | bytes 524320 | tf_op jit(solution)/shard_map/all_to_all | solution.py:1149
  222.1 8.3 %shard_map.256 = f32[24,2048]{1,0:T(8,128)S(1)} custom-call(bf16[2048,128]{1,0:T(8,128)(2,1)S(1)} %bitcast.282, bf16[1024,128]{1,0:T(8,128)(2,1)S(1)} %maximum_select_fusion.25.d_ref, s32[1,1024]{1,0:T(1,128)S(1)} %compare_select_fusion.seg_ref), custom_call_target="tpu_custom_call" | custom-call | flops 3221225472 | bytes 786432 | tf_op jit(solution)/shard_map/pallas_call | solution.py:904
  231.9 5.7 %all-to-all-start.1 = ((f32[16,8,128]{2,1,0:T(8,128)}), f32[16,8,128]{2,1,0:T(8,128)S(1)}, u32[]{:S(2)}, u32[]{:S(2)}) async-start(f32[16,8,128]{2,1,0:T(8,128)} %broadcast_in_dim.47), calls=%async_computation.1 | async-start | bytes 131072 | tf_op jit(solution)/shard_map/all_to_all | solution.py:1170
  237.5 5.1 collective-permute-start.29
  244.8 13.2 %shard_map.257 = (bf16[2048,128]{1,0:T(8,128)(2,1)}, f32[768,128]{1,0:T(8,128)S(1)}) custom-call(bf16[2048,128]{1,0:T(8,128)(2,1)S(1)} %bitcast.283, bf16[1024,128]{1,0:T(8,128)(2,1)S(1)} %maximum_select_fusion.25.d_ref, s32[1,1024]{1,0:T(1,128)S(1)} %compare_select_fusion.seg_ref, f32[24,2048]{1,0:T(8,128)S(1)} %convolution_divide_fusion.coef_ref), custom_call_target="tpu_custom_call" | custom-call | flops 4831838208 | bytes 1572864 | tf_op jit(solution)/shard_map/pallas_call | solution.py:980
  258.0 9.4 %all-to-all-start.2 = ((bf16[16,128,128]{2,1,0:T(8,128)(2,1)}), bf16[16,128,128]{2,1,0:T(8,128)(2,1)S(1)}, u32[]{:S(2)}, u32[]{:S(2)}) async-start(bf16[16,128,128]{2,1,0:T(8,128)(2,1)} %bitcast.57), calls=%async_computation.2 | async-start | bytes 1048576 | tf_op jit(solution)/shard_map/all_to_all | solution.py:1192
  267.4 12.1 %all-to-all-done.2 = bf16[16,128,128]{2,1,0:T(8,128)(2,1)S(1)} async-done(((bf16[16,128,128]{2,1,0:T(8,128)(2,1)}), bf16[16,128,128]{2,1,0:T(8,128)(2,1)S(1)}, u32[]{:S(2)}, u32[]{:S(2)}) %all-to-all-start.2) | async-done | bytes 524320 | tf_op jit(solution)/shard_map/all_to_all | solution.py:1192
  279.7 4.0 collective-permute-start.30
  288.9 1.8 fusion.125
  293.3 6.4 %convolution_convert_fusion.1 = bf16[1024,2048]{1,0:T(8,128)(2,1)S(1)} fusion(bf16[1024,2048]{1,0:T(8,128)(2,1)S(1)} %copy-done.6, bf16[512,1024]{1,0:T(8,128)(2,1)} %collective-permute-done.31, bf16[512,1024]{1,0:T(8,128)(2,1)} %get-tuple-element.249), kind=kOutput, calls=%fused_computation.7 | convolution fusion | flops 4301258752 | bytes 10485760 | tf_op jit(solution)/shard_map/dot_general | solution.py:33
  303.7 7.8 %convert_reduce_fusion = (f32[2048]{0:T(1024)S(1)}, bf16[1024,2048]{1,0:T(8,128)(2,1)}) fusion(bf16[1024,2048]{1,0:T(8,128)(2,1)S(1)} %copy-done.8, bf16[1024,2048]{1,0:T(8,128)(2,1)S(1)} %bitcast.296, bf16[512,1024]{1,0:T(8,128)(2,1)} %collective-permute-done.31, bf16[512,1024]{1,0:T(8,128)(2,1)} %get-tuple-element.249), kind=kOutput, calls=%fused_computation | convolution fusion | flops 4309645312 | bytes 14688256 | tf_op jit(solution)/shard_map/dot_general | solution.py:448
  311.5 4.1 fusion.15
  315.8 2.4 fusion.2
  318.2 6.8 %collective-permute-done.35 = bf16[4,2,32,2048]{3,2,0,1:T(8,128)(2,1)S(1)} collective-permute-done((bf16[4,2,32,2048]{3,2,0,1:T(8,128)(2,1)S(1)}, bf16[4,2,32,2048]{3,2,0,1:T(8,128)(2,1)S(1)}, u32[]{:S(2)}, u32[]{:S(2)}) %collective-permute-start.35) | collective-permute-done | bytes 1048608 | tf_op jit(solution)/shard_map/ppermute | solution.py:464
  325.3 5.2 %convolution_convert_fusion = bf16[1024,2048]{1,0:T(8,128)(2,1)S(1)} fusion(bf16[1024,2048]{1,0:T(8,128)(2,1)S(1)} %copy-done.46, bf16[512,1024]{1,0:T(8,128)(2,1)S(1)} %copy-done.37, bf16[512,1024]{1,0:T(8,128)(2,1)S(1)} %copy-done.23), kind=kOutput, calls=%fused_computation.6 | convolution fusion | flops 4301258752 | bytes 10485760 | tf_op jit(solution)/shard_map/dot_general | solution.py:33
  344.4 2.3 collective-permute-start.33
  346.7 20.1 %collective-permute-done.39 = bf16[4,2,32,2048]{3,2,0,1:T(8,128)(2,1)} collective-permute-done((bf16[4,2,32,2048]{3,2,0,1:T(8,128)(2,1)}, bf16[4,2,32,2048]{3,2,0,1:T(8,128)(2,1)}, u32[]{:S(2)}, u32[]{:S(2)}) %collective-permute-start.39) | collective-permute-done | bytes 1048608 | tf_op jit(solution)/shard_map/ppermute | solution.py:464
  366.8 2.3 collective-permute-done.38
  384.7 9.5 %shard_map.258 = (bf16[1024,768]{1,0:T(8,128)(2,1)S(1)}, f32[8,256]{1,0:T(8,128)S(1)}) custom-call(s32[2,4]{1,0:T(2,128)S(1)} %pad_add_fusion.1.bounds, bf16[1024,1536]{1,0:T(8,128)(2,1)S(1)} %copy-done.4, bf16[1024,1536]{1,0:T(8,128)(2,1)S(1)} %copy-done.4, bf16[1024,512]{1,0:T(8,128)(2,1)S(1)} %get-tuple-element.139.out_ref, ...), custom_call_target="tpu_custom_call" | custom-call | flops 2684354560 | bytes 12582912 | tf_op jit(solution)/shard_map/pallas_call | solution.py:782
  394.2 3.4 collective-permute-done.44
  403.3 3.7 collective-permute-start.45
  411.8 9.7 %shard_map.259 = (bf16[1024,768]{1,0:T(8,128)(2,1)S(1)}, f32[8,256]{1,0:T(8,128)S(1)}) custom-call(s32[2,4]{1,0:T(2,128)S(1)} %pad_add_fusion.1.bounds, bf16[1024,1536]{1,0:T(8,128)(2,1)S(1)} %copy-done.4, bf16[1024,1536]{1,0:T(8,128)(2,1)S(1)} %copy-done.4, bf16[1024,512]{1,0:T(8,128)(2,1)S(1)} %get-tuple-element.139.out_ref, ...), custom_call_target="tpu_custom_call" | custom-call | flops 2684354560 | bytes 12582912 | tf_op jit(solution)/shard_map/pallas_call | solution.py:782
  421.6 7.7 %collective-permute-done.48 = bf16[2,64,2048]{2,1,0:T(8,128)(2,1)S(1)} collective-permute-done((bf16[2,64,2048]{2,1,0:T(8,128)(2,1)S(1)}, bf16[2,64,2048]{2,1,0:T(8,128)(2,1)S(1)}, u32[]{:S(2)}, u32[]{:S(2)}) %collective-permute-start.48) | collective-permute-done | bytes 524320 | tf_op jit(solution)/shard_map/ppermute | solution.py:464
  431.2 1.9 convolution_convert_fusion.3
  434.2 1.9 convolution_convert_fusion.2
  444.0 3.4 collective-permute-start.62
  447.4 2.7 collective-permute-done.53
  450.2 6.7 %collective-permute-done.51 = bf16[4,2,32,1536]{3,2,0,1:T(8,128)(2,1)S(1)} collective-permute-done((bf16[4,2,32,1536]{3,2,0,1:T(8,128)(2,1)S(1)}, bf16[4,2,32,1536]{3,2,0,1:T(8,128)(2,1)S(1)}, u32[]{:S(2)}, u32[]{:S(2)}) %collective-permute-start.51) | collective-permute-done | bytes 786464 | tf_op jit(solution)/shard_map/ppermute | solution.py:464
  456.9 1.9 collective-permute-done.52
  465.1 4.7 collective-permute-start.63
  470.9 2.8 collective-permute-done.57
  473.9 2.0 collective-permute-start.61
  476.2 3.9 collective-permute-done.61
  480.0 8.9 %collective-permute-done.60 = bf16[2,64,1536]{2,1,0:T(8,128)(2,1)S(1)} collective-permute-done((bf16[2,64,1536]{2,1,0:T(8,128)(2,1)S(1)}, bf16[2,64,1536]{2,1,0:T(8,128)(2,1)S(1)}, u32[]{:S(2)}, u32[]{:S(2)}) %collective-permute-start.60) | collective-permute-done | bytes 393248 | tf_op jit(solution)/shard_map/ppermute | solution.py:464
  489.2 4.7 collective-permute-start.66
  495.8 5.3 %collective-permute-done.64 = bf16[64,1536]{1,0:T(8,128)(2,1)S(1)} collective-permute-done((bf16[64,1536]{1,0:T(8,128)(2,1)S(1)}, bf16[64,1536]{1,0:T(8,128)(2,1)S(1)}, u32[]{:S(2)}, u32[]{:S(2)}) %collective-permute-start.64) | collective-permute-done | bytes 196640 | tf_op jit(solution)/shard_map/ppermute | solution.py:464
  501.1 3.3 collective-permute-start.67
  515.1 2.3 copy.183
  (449 shorter events, 137.5 us)
Async XLA Ops:
  2.2 15.0 %collective-permute-start.2 = (f32[1,3072]{1,0:T(1,128)S(1)}, f32[1,3072]{1,0:T(1,128)S(1)}, u32[]{:S(2)}, u32[]{:S(2)}) collective-permute-start(f32[1,3072]{1,0:T(1,128)S(1)} %maximum_convert_fusion), channel_id=1, source_target_pairs={{0,1},{1,0},{2,3},{3,2},{4,5},{5,4},{6,7},{7,6},{8,9},{9,8},{10,11... | collective-permute-start | bytes 36872 | tf_op jit(solution)/shard_map/ppermute | solution.py:464
  10.5 7.9 %collective-permute-start = (bf16[64,2048]{1,0:T(8,128)(2,1)}, bf16[64,2048]{1,0:T(8,128)(2,1)S(1)}, u32[]{:S(2)}, u32[]{:S(2)}) collective-permute-start(bf16[64,2048]{1,0:T(8,128)(2,1)} %bitcast_dynamic-update-slice_fusion), channel_id=1, source_target_pairs={{0,0},{1,2},{2,1},{3,3},{4,4},{5,6},{6,5},{7,7},{8,8},{9,10},{10,9... | collective-permute-start | bytes 786440 | tf_op jit(solution)/shard_map/ppermute | solution.py:464
  13.0 5.4 %collective-permute-start.1 = (bf16[1024,1024]{1,0:T(8,128)(2,1)}, bf16[1024,1024]{1,0:T(8,128)(2,1)}, u32[]{:S(2)}, u32[]{:S(2)}) collective-permute-start(bf16[1024,1024]{1,0:T(8,128)(2,1)} %param.15), channel_id=1, source_target_pairs={{0,2},{2,0},{1,3},{3,1},{4,6},{6,4},{5,7},{7,5},{8,10},{10,8},{9,1... | collective-permute-start | bytes 6291464 | tf_op jit(solution)/shard_map/ppermute | solution.py:464
  21.7 8.5 %collective-permute-start.4 = (bf16[64,2048]{1,0:T(8,128)(2,1)S(1)}, bf16[64,2048]{1,0:T(8,128)(2,1)S(1)}, u32[]{:S(2)}, u32[]{:S(2)}) collective-permute-start(bf16[64,2048]{1,0:T(8,128)(2,1)S(1)} %collective-permute-done), channel_id=1, source_target_pairs={{0,24},{24,0},{8,16},{16,8},{1,25},{25,1},{9,17},{17,9},{2,26},{26... | collective-permute-start | bytes 786440 | tf_op jit(solution)/shard_map/ppermute | solution.py:464
  25.1 10.7 %collective-permute-start.3 = (bf16[64,4224]{1,0:T(8,128)(2,1)S(1)}, bf16[64,4224]{1,0:T(8,128)(2,1)S(1)}, u32[]{:S(2)}, u32[]{:S(2)}) collective-permute-start(bf16[64,4224]{1,0:T(8,128)(2,1)S(1)} %fusion.42), channel_id=1, source_target_pairs={{0,0},{1,2},{2,1},{3,3},{4,4},{5,6},{6,5},{7,7},{8,8},{9,10},{10,9... | collective-permute-start | bytes 1622024 | tf_op jit(solution)/shard_map/ppermute | solution.py:464
  30.3 17.6 %collective-permute-start.5 = (bf16[2,64,2048]{2,1,0:T(8,128)(2,1)S(1)}, bf16[2,64,2048]{2,1,0:T(8,128)(2,1)S(1)}, u32[]{:S(2)}, u32[]{:S(2)}) collective-permute-start(bf16[2,64,2048]{2,1,0:T(8,128)(2,1)S(1)} %maximum_select_fusion.20), channel_id=1, source_target_pairs={{0,8},{8,0},{16,24},{24,16},{1,9},{9,1},{17,25},{25,17},{2,10},{10... | collective-permute-start | bytes 1572872 | tf_op jit(solution)/shard_map/ppermute | solution.py:464
  35.8 20.0 %collective-permute-start.6 = (bf16[64,2176]{1,0:T(8,128)(2,1)S(1)}, bf16[64,2176]{1,0:T(8,128)(2,1)S(1)}, u32[]{:S(2)}, u32[]{:S(2)}) collective-permute-start(bf16[64,2176]{1,0:T(8,128)(2,1)S(1)} %get-tuple-element.304), channel_id=1, source_target_pairs={{0,24},{24,0},{8,16},{16,8},{1,25},{25,1},{9,17},{17,9},{2,26},{26... | collective-permute-start | bytes 835592 | tf_op jit(solution)/shard_map/ppermute | solution.py:464
  56.0 13.9 %collective-permute-start.9 = (bf16[2,64,2176]{2,1,0:T(8,128)(2,1)S(1)}, bf16[2,64,2176]{2,1,0:T(8,128)(2,1)S(1)}, u32[]{:S(2)}, u32[]{:S(2)}) collective-permute-start(bf16[2,64,2176]{2,1,0:T(8,128)(2,1)S(1)} %maximum_select_fusion.19), channel_id=1, source_target_pairs={{0,8},{8,0},{16,24},{24,16},{1,9},{9,1},{17,25},{25,17},{2,10},{10... | collective-permute-start | bytes 1671176 | tf_op jit(solution)/shard_map/ppermute | solution.py:464
  56.6 13.2 %collective-permute-start.8 = (bf16[4,32,2048]{2,1,0:T(8,128)(2,1)S(1)}, bf16[4,32,2048]{2,1,0:T(8,128)(2,1)S(1)}, u32[]{:S(2)}, u32[]{:S(2)}) collective-permute-start(bf16[4,32,2048]{2,1,0:T(8,128)(2,1)S(1)} %get-tuple-element.293), channel_id=1, source_target_pairs={{0,1},{1,0},{2,3},{3,2},{4,5},{5,4},{6,7},{7,6},{8,9},{9,8},{10,11... | collective-permute-start | bytes 1572872 | tf_op jit(solution)/shard_map/ppermute | solution.py:464
  56.7 13.2 %collective-permute-start.7 = (bf16[4,32,2048]{2,1,0:T(8,128)(2,1)S(1)}, bf16[4,32,2048]{2,1,0:T(8,128)(2,1)S(1)}, u32[]{:S(2)}, u32[]{:S(2)}) collective-permute-start(bf16[4,32,2048]{2,1,0:T(8,128)(2,1)S(1)} %get-tuple-element.294), channel_id=1, source_target_pairs={{0,4},{4,0},{1,5},{5,1},{2,6},{6,2},{3,7},{7,3},{8,12},{12,8},{9,1... | collective-permute-start | bytes 1572872 | tf_op jit(solution)/shard_map/ppermute | solution.py:464
  70.5 8.5 %collective-permute-start.12 = (bf16[64,2048]{1,0:T(8,128)(2,1)S(1)}, bf16[64,2048]{1,0:T(8,128)(2,1)S(1)}, u32[]{:S(2)}, u32[]{:S(2)}) collective-permute-start(bf16[64,2048]{1,0:T(8,128)(2,1)S(1)} %get-tuple-element.131), channel_id=1, source_target_pairs={{0,24},{24,0},{8,16},{16,8},{1,25},{25,1},{9,17},{17,9},{2,26},{26... | collective-permute-start | bytes 786440 | tf_op jit(solution)/shard_map/ppermute | solution.py:464
  71.4 35.4 %collective-permute-start.10 = (bf16[4,2,32,2048]{3,2,0,1:T(8,128)(2,1)S(1)}, bf16[4,2,32,2048]{3,2,0,1:T(8,128)(2,1)S(1)}, u32[]{:S(2)}, u32[]{:S(2)}) collective-permute-start(bf16[4,2,32,2048]{3,2,0,1:T(8,128)(2,1)S(1)} %maximum_select_fusion.13), channel_id=1, source_target_pairs={{0,1},{1,0},{2,3},{3,2},{4,5},{5,4},{6,7},{7,6},{8,9},{9,8},{10,11... | collective-permute-start | bytes 3145736 | tf_op jit(solution)/shard_map/ppermute | solution.py:464
  72.6 34.2 %collective-permute-start.11 = (bf16[4,2,32,2048]{3,2,1,0:T(8,128)(2,1)S(1)}, bf16[4,2,32,2048]{3,2,1,0:T(8,128)(2,1)S(1)}, u32[]{:S(2)}, u32[]{:S(2)}) collective-permute-start(bf16[4,2,32,2048]{3,2,1,0:T(8,128)(2,1)S(1)} %maximum_select_fusion.14), channel_id=1, source_target_pairs={{0,4},{4,0},{1,5},{5,1},{2,6},{6,2},{3,7},{7,3},{8,12},{12,8},{9,1... | collective-permute-start | bytes 3145736 | tf_op jit(solution)/shard_map/ppermute | solution.py:464
  74.1 32.0 %collective-permute-start.14 = (bf16[4,32,2176]{2,1,0:T(8,128)(2,1)S(1)}, bf16[4,32,2176]{2,1,0:T(8,128)(2,1)S(1)}, u32[]{:S(2)}, u32[]{:S(2)}) collective-permute-start(bf16[4,32,2176]{2,1,0:T(8,128)(2,1)S(1)} %get-tuple-element.283), channel_id=1, source_target_pairs={{0,1},{1,0},{2,3},{3,2},{4,5},{5,4},{6,7},{7,6},{8,9},{9,8},{10,11... | collective-permute-start | bytes 1671176 | tf_op jit(solution)/shard_map/ppermute | solution.py:464
  74.6 32.2 %collective-permute-start.13 = (bf16[4,32,2176]{2,1,0:T(8,128)(2,1)S(1)}, bf16[4,32,2176]{2,1,0:T(8,128)(2,1)S(1)}, u32[]{:S(2)}, u32[]{:S(2)}) collective-permute-start(bf16[4,32,2176]{2,1,0:T(8,128)(2,1)S(1)} %get-tuple-element.284), channel_id=1, source_target_pairs={{0,4},{4,0},{1,5},{5,1},{2,6},{6,2},{3,7},{7,3},{8,12},{12,8},{9,1... | collective-permute-start | bytes 1671176 | tf_op jit(solution)/shard_map/ppermute | solution.py:464
  106.9 10.1 %collective-permute-start.15 = (bf16[2,64,2048]{2,1,0:T(8,128)(2,1)S(1)}, bf16[2,64,2048]{2,1,0:T(8,128)(2,1)S(1)}, u32[]{:S(2)}, u32[]{:S(2)}) collective-permute-start(bf16[2,64,2048]{2,1,0:T(8,128)(2,1)S(1)} %maximum_select_fusion.21), channel_id=1, source_target_pairs={{0,8},{8,0},{16,24},{24,16},{1,9},{9,1},{17,25},{25,17},{2,10},{10... | collective-permute-start | bytes 1572872 | tf_op jit(solution)/shard_map/ppermute | solution.py:464
  107.5 52.4 %collective-permute-start.19 = (bf16[4,2,32,2176]{3,2,0,1:T(8,128)(2,1)S(1)}, bf16[4,2,32,2176]{3,2,0,1:T(8,128)(2,1)S(1)}, u32[]{:S(2)}, u32[]{:S(2)}) collective-permute-start(bf16[4,2,32,2176]{3,2,0,1:T(8,128)(2,1)S(1)} %maximum_select_fusion.9), channel_id=1, source_target_pairs={{0,1},{1,0},{2,3},{3,2},{4,5},{5,4},{6,7},{7,6},{8,9},{9,8},{10,11... | collective-permute-start | bytes 3342344 | tf_op jit(solution)/shard_map/ppermute | solution.py:464
  117.2 6.2 %collective-permute-start.16 = (f32[2,1024]{1,0:T(2,128)S(1)}, f32[2,1024]{1,0:T(2,128)S(1)}, u32[]{:S(2)}, u32[]{:S(2)}) collective-permute-start(f32[2,1024]{1,0:T(2,128)S(1)} %pad_maximum_fusion.21), channel_id=1, source_target_pairs={{0,2},{2,0},{1,3},{3,1},{4,6},{6,4},{5,7},{7,5},{8,10},{10,8},{9,1... | collective-permute-start | bytes 24584 | tf_op jit(solution)/shard_map/ppermute | solution.py:469
  121.8 38.1 %collective-permute-start.20 = (bf16[4,2,32,2176]{3,2,0,1:T(8,128)(2,1)S(1)}, bf16[4,2,32,2176]{3,2,0,1:T(8,128)(2,1)S(1)}, u32[]{:S(2)}, u32[]{:S(2)}) collective-permute-start(bf16[4,2,32,2176]{3,2,0,1:T(8,128)(2,1)S(1)} %maximum_select_fusion.10), channel_id=1, source_target_pairs={{0,4},{4,0},{1,5},{5,1},{2,6},{6,2},{3,7},{7,3},{8,12},{12,8},{9,1... | collective-permute-start | bytes 3342344 | tf_op jit(solution)/shard_map/ppermute | solution.py:464
  133.3 15.1 %collective-permute-start.23 = (bf16[4,32,2048]{2,1,0:T(8,128)(2,1)S(1)}, bf16[4,32,2048]{2,1,0:T(8,128)(2,1)S(1)}, u32[]{:S(2)}, u32[]{:S(2)}) collective-permute-start(bf16[4,32,2048]{2,1,0:T(8,128)(2,1)S(1)} %get-tuple-element.287), channel_id=1, source_target_pairs={{0,1},{1,0},{2,3},{3,2},{4,5},{5,4},{6,7},{7,6},{8,9},{9,8},{10,11... | collective-permute-start | bytes 1572872 | tf_op jit(solution)/shard_map/ppermute | solution.py:464
  136.2 23.3 %collective-permute-start.22 = (bf16[4,32,2048]{2,1,0:T(8,128)(2,1)S(1)}, bf16[4,32,2048]{2,1,0:T(8,128)(2,1)S(1)}, u32[]{:S(2)}, u32[]{:S(2)}) collective-permute-start(bf16[4,32,2048]{2,1,0:T(8,128)(2,1)S(1)} %get-tuple-element.288), channel_id=1, source_target_pairs={{0,4},{4,0},{1,5},{5,1},{2,6},{6,2},{3,7},{7,3},{8,12},{12,8},{9,1... | collective-permute-start | bytes 1572872 | tf_op jit(solution)/shard_map/ppermute | solution.py:464
  138.7 21.6 %collective-permute-start.18 = (bf16[512,1024]{1,0:T(8,128)(2,1)S(1)}, bf16[512,1024]{1,0:T(8,128)(2,1)S(1)}, u32[]{:S(2)}, u32[]{:S(2)}) collective-permute-start(bf16[512,1024]{1,0:T(8,128)(2,1)S(1)} %fusion.11), channel_id=1, source_target_pairs={{0,2},{2,0},{1,3},{3,1},{4,6},{6,4},{5,7},{7,5},{8,10},{10,8},{9,1... | collective-permute-start | bytes 3145736 | tf_op jit(solution)/shard_map/ppermute | solution.py:469
  161.9 24.4 %collective-permute-start.24 = (bf16[4,2,32,2048]{3,2,0,1:T(8,128)(2,1)S(1)}, bf16[4,2,32,2048]{3,2,0,1:T(8,128)(2,1)S(1)}, u32[]{:S(2)}, u32[]{:S(2)}) collective-permute-start(bf16[4,2,32,2048]{3,2,0,1:T(8,128)(2,1)S(1)} %maximum_select_fusion.17), channel_id=1, source_target_pairs={{0,1},{1,0},{2,3},{3,2},{4,5},{5,4},{6,7},{7,6},{8,9},{9,8},{10,11... | collective-permute-start | bytes 3145736 | tf_op jit(solution)/shard_map/ppermute | solution.py:464
  162.7 24.1 %collective-permute-start.25 = (bf16[4,2,32,2048]{3,2,0,1:T(8,128)(2,1)S(1)}, bf16[4,2,32,2048]{3,2,0,1:T(8,128)(2,1)S(1)}, u32[]{:S(2)}, u32[]{:S(2)}) collective-permute-start(bf16[4,2,32,2048]{3,2,0,1:T(8,128)(2,1)S(1)} %maximum_select_fusion.18), channel_id=1, source_target_pairs={{0,4},{4,0},{1,5},{5,1},{2,6},{6,2},{3,7},{7,3},{8,12},{12,8},{9,1... | collective-permute-start | bytes 3145736 | tf_op jit(solution)/shard_map/ppermute | solution.py:464
  192.5 18.2 %collective-permute-start.28 = (bf16[512,1024]{1,0:T(8,128)(2,1)}, bf16[512,1024]{1,0:T(8,128)(2,1)S(1)}, u32[]{:S(2)}, u32[]{:S(2)}) collective-permute-start(bf16[512,1024]{1,0:T(8,128)(2,1)} %param.29), channel_id=1, source_target_pairs={{0,0},{1,2},{2,1},{3,3},{4,4},{5,6},{6,5},{7,7},{8,8},{9,10},{10,9... | collective-permute-start | bytes 3145736 | tf_op jit(solution)/shard_map/ppermute | solution.py:1152
  203.7 18.4 %all-to-all-start = ((bf16[16,128,128]{2,1,0:T(8,128)(2,1)}), bf16[16,128,128]{2,1,0:T(8,128)(2,1)S(1)}, u32[]{:S(2)}, u32[]{:S(2)}) async-start(bf16[16,128,128]{2,1,0:T(8,128)(2,1)} %broadcast_in_dim.46), calls=%async_computation | async-start | bytes 1048576 | tf_op jit(solution)/shard_map/all_to_all | solution.py:1149
  231.9 12.0 %all-to-all-start.1 = ((f32[16,8,128]{2,1,0:T(8,128)}), f32[16,8,128]{2,1,0:T(8,128)S(1)}, u32[]{:S(2)}, u32[]{:S(2)}) async-start(f32[16,8,128]{2,1,0:T(8,128)} %broadcast_in_dim.47), calls=%async_computation.1 | async-start | bytes 131072 | tf_op jit(solution)/shard_map/all_to_all | solution.py:1170
  237.5 20.5 %collective-permute-start.29 = (bf16[512,1024]{1,0:T(8,128)(2,1)}, bf16[512,1024]{1,0:T(8,128)(2,1)}, u32[]{:S(2)}, u32[]{:S(2)}) collective-permute-start(bf16[512,1024]{1,0:T(8,128)(2,1)} %add_convert_fusion.3), channel_id=1, source_target_pairs={{0,0},{1,2},{2,1},{3,3},{4,4},{5,6},{6,5},{7,7},{8,8},{9,10},{10,9... | collective-permute-start | bytes 3145736 | tf_op jit(solution)/shard_map/ppermute | solution.py:1190
  258.0 21.6 %all-to-all-start.2 = ((bf16[16,128,128]{2,1,0:T(8,128)(2,1)}), bf16[16,128,128]{2,1,0:T(8,128)(2,1)S(1)}, u32[]{:S(2)}, u32[]{:S(2)}) async-start(bf16[16,128,128]{2,1,0:T(8,128)(2,1)} %bitcast.57), calls=%async_computation.2 | async-start | bytes 1048576 | tf_op jit(solution)/shard_map/all_to_all | solution.py:1192
  279.7 5.1 collective-permute-start.30
  300.3 24.7 %collective-permute-start.35 = (bf16[4,2,32,2048]{3,2,0,1:T(8,128)(2,1)S(1)}, bf16[4,2,32,2048]{3,2,0,1:T(8,128)(2,1)S(1)}, u32[]{:S(2)}, u32[]{:S(2)}) collective-permute-start(bf16[4,2,32,2048]{3,2,0,1:T(8,128)(2,1)S(1)} %bitcast.318), channel_id=1, source_target_pairs={{0,1},{1,0},{2,3},{3,2},{4,5},{5,4},{6,7},{7,6},{8,9},{9,8},{10,11... | collective-permute-start | bytes 3145736 | tf_op jit(solution)/shard_map/ppermute | solution.py:464
  300.9 24.4 %collective-permute-start.34 = (bf16[4,2,32,2048]{3,2,0,1:T(8,128)(2,1)S(1)}, bf16[4,2,32,2048]{3,2,0,1:T(8,128)(2,1)S(1)}, u32[]{:S(2)}, u32[]{:S(2)}) collective-permute-start(bf16[4,2,32,2048]{3,2,0,1:T(8,128)(2,1)S(1)} %bitcast.319), channel_id=1, source_target_pairs={{0,4},{4,0},{1,5},{5,1},{2,6},{6,2},{3,7},{7,3},{8,12},{12,8},{9,1... | collective-permute-start | bytes 3145736 | tf_op jit(solution)/shard_map/ppermute | solution.py:464
  315.6 25.5 %collective-permute-start.32 = (bf16[512,1024]{1,0:T(8,128)(2,1)S(1)}, bf16[512,1024]{1,0:T(8,128)(2,1)S(1)}, u32[]{:S(2)}, u32[]{:S(2)}) collective-permute-start(bf16[512,1024]{1,0:T(8,128)(2,1)S(1)} %fusion.15), channel_id=1, source_target_pairs={{0,2},{2,0},{1,3},{3,1},{4,6},{6,4},{5,7},{7,5},{8,10},{10,8},{9,1... | collective-permute-start | bytes 3145736 | tf_op jit(solution)/shard_map/ppermute | solution.py:469
  331.9 14.8 %collective-permute-start.36 = (bf16[4,32,2048]{2,1,0:T(8,128)(2,1)}, bf16[4,32,2048]{2,1,0:T(8,128)(2,1)}, u32[]{:S(2)}, u32[]{:S(2)}) collective-permute-start(bf16[4,32,2048]{2,1,0:T(8,128)(2,1)} %fusion.43), channel_id=1, source_target_pairs={{0,1},{1,0},{2,3},{3,2},{4,5},{5,4},{6,7},{7,6},{8,9},{9,8},{10,11... | collective-permute-start | bytes 1572872 | tf_op jit(solution)/shard_map/ppermute | solution.py:464
  334.4 12.3 %collective-permute-start.37 = (bf16[4,32,2048]{2,1,0:T(8,128)(2,1)}, bf16[4,32,2048]{2,1,0:T(8,128)(2,1)}, u32[]{:S(2)}, u32[]{:S(2)}) collective-permute-start(bf16[4,32,2048]{2,1,0:T(8,128)(2,1)} %fusion.44), channel_id=1, source_target_pairs={{0,4},{4,0},{1,5},{5,1},{2,6},{6,2},{3,7},{7,3},{8,12},{12,8},{9,1... | collective-permute-start | bytes 1572872 | tf_op jit(solution)/shard_map/ppermute | solution.py:464
  340.3 26.6 %collective-permute-start.39 = (bf16[4,2,32,2048]{3,2,0,1:T(8,128)(2,1)}, bf16[4,2,32,2048]{3,2,0,1:T(8,128)(2,1)}, u32[]{:S(2)}, u32[]{:S(2)}) collective-permute-start(bf16[4,2,32,2048]{3,2,0,1:T(8,128)(2,1)} %bitcast.272), channel_id=1, source_target_pairs={{0,1},{1,0},{2,3},{3,2},{4,5},{5,4},{6,7},{7,6},{8,9},{9,8},{10,11... | collective-permute-start | bytes 3145736 | tf_op jit(solution)/shard_map/ppermute | solution.py:464
  340.6 28.5 %collective-permute-start.38 = (bf16[4,2,32,2048]{3,2,0,1:T(8,128)(2,1)}, bf16[4,2,32,2048]{3,2,0,1:T(8,128)(2,1)}, u32[]{:S(2)}, u32[]{:S(2)}) collective-permute-start(bf16[4,2,32,2048]{3,2,0,1:T(8,128)(2,1)} %bitcast.273), channel_id=1, source_target_pairs={{0,4},{4,0},{1,5},{5,1},{2,6},{6,2},{3,7},{7,3},{8,12},{12,8},{9,1... | collective-permute-start | bytes 3145736 | tf_op jit(solution)/shard_map/ppermute | solution.py:464
  344.4 32.0 %collective-permute-start.33 = (bf16[512,1024]{1,0:T(8,128)(2,1)}, bf16[512,1024]{1,0:T(8,128)(2,1)S(1)}, u32[]{:S(2)}, u32[]{:S(2)}) collective-permute-start(bf16[512,1024]{1,0:T(8,128)(2,1)} %get-tuple-element.252), channel_id=1, source_target_pairs={{0,2},{2,0},{1,3},{3,1},{4,6},{6,4},{5,7},{7,5},{8,10},{10,8},{9,1... | collective-permute-start | bytes 3145736 | tf_op jit(solution)/shard_map/ppermute | solution.py:469
  380.2 17.4 %collective-permute-start.42 = (bf16[4,32,2048]{2,1,0:T(8,128)(2,1)S(1)}, bf16[4,32,2048]{2,1,0:T(8,128)(2,1)}, u32[]{:S(2)}, u32[]{:S(2)}) collective-permute-start(bf16[4,32,2048]{2,1,0:T(8,128)(2,1)S(1)} %fusion.46), channel_id=1, source_target_pairs={{0,4},{4,0},{1,5},{5,1},{2,6},{6,2},{3,7},{7,3},{8,12},{12,8},{9,1... | collective-permute-start | bytes 1572872 | tf_op jit(solution)/shard_map/ppermute | solution.py:464
  381.2 16.4 %collective-permute-start.41 = (bf16[4,32,2048]{2,1,0:T(8,128)(2,1)S(1)}, bf16[4,32,2048]{2,1,0:T(8,128)(2,1)S(1)}, u32[]{:S(2)}, u32[]{:S(2)}) collective-permute-start(bf16[4,32,2048]{2,1,0:T(8,128)(2,1)S(1)} %fusion.45), channel_id=1, source_target_pairs={{0,1},{1,0},{2,3},{3,2},{4,5},{5,4},{6,7},{7,6},{8,9},{9,8},{10,11... | collective-permute-start | bytes 1572872 | tf_op jit(solution)/shard_map/ppermute | solution.py:464
  381.7 15.9 %collective-permute-start.44 = (bf16[4,2,32,512]{3,2,0,1:T(8,128)(2,1)S(1)}, bf16[4,2,32,512]{3,2,0,1:T(8,128)(2,1)}, u32[]{:S(2)}, u32[]{:S(2)}) collective-permute-start(bf16[4,2,32,512]{3,2,0,1:T(8,128)(2,1)S(1)} %dynamic-slice_bitcast_fusion.2), channel_id=1, source_target_pairs={{0,1},{1,0},{2,3},{3,2},{4,5},{5,4},{6,7},{7,6},{8,9},{9,8},{10,11... | collective-permute-start | bytes 786440 | tf_op jit(solution)/shard_map/ppermute | solution.py:464
  382.9 14.7 %collective-permute-start.43 = (bf16[4,2,32,512]{3,2,0,1:T(8,128)(2,1)S(1)}, bf16[4,2,32,512]{3,2,0,1:T(8,128)(2,1)}, u32[]{:S(2)}, u32[]{:S(2)}) collective-permute-start(bf16[4,2,32,512]{3,2,0,1:T(8,128)(2,1)S(1)} %dynamic-slice_bitcast_fusion.3), channel_id=1, source_target_pairs={{0,4},{4,0},{1,5},{5,1},{2,6},{6,2},{3,7},{7,3},{8,12},{12,8},{9,1... | collective-permute-start | bytes 786440 | tf_op jit(solution)/shard_map/ppermute | solution.py:464
  383.6 14.0 %collective-permute-start.40 = (bf16[2,64,2048]{2,1,0:T(8,128)(2,1)S(1)}, bf16[2,64,2048]{2,1,0:T(8,128)(2,1)S(1)}, u32[]{:S(2)}, u32[]{:S(2)}) collective-permute-start(bf16[2,64,2048]{2,1,0:T(8,128)(2,1)S(1)} %select_convert_fusion.1), channel_id=1, source_target_pairs={{0,8},{8,0},{16,24},{24,16},{1,9},{9,1},{17,25},{25,17},{2,10},{10... | collective-permute-start | bytes 1572872 | tf_op jit(solution)/shard_map/ppermute | solution.py:464
  403.3 6.2 %collective-permute-start.45 = (f32[16,4]{1,0:T(8,128)S(1)}, f32[16,4]{1,0:T(8,128)S(1)}, u32[]{:S(2)}, u32[]{:S(2)}) collective-permute-start(f32[16,4]{1,0:T(8,128)S(1)} %reshape.820), channel_id=1, source_target_pairs={{0,2},{2,0},{1,3},{3,1},{4,6},{6,4},{5,7},{7,5},{8,10},{10,8},{9,1... | collective-permute-start | bytes 776 | tf_op jit(solution)/shard_map/ppermute | solution.py:469
  407.1 14.5 %collective-permute-start.50 = (bf16[4,32,512]{2,1,0:T(8,128)(2,1)S(1)}, bf16[4,32,512]{2,1,0:T(8,128)(2,1)S(1)}, u32[]{:S(2)}, u32[]{:S(2)}) collective-permute-start(bf16[4,32,512]{2,1,0:T(8,128)(2,1)S(1)} %fusion.66), channel_id=1, source_target_pairs={{0,4},{4,0},{1,5},{5,1},{2,6},{6,2},{3,7},{7,3},{8,12},{12,8},{9,1... | collective-permute-start | bytes 393224 | tf_op jit(solution)/shard_map/ppermute | solution.py:464
  407.7 13.9 %collective-permute-start.49 = (bf16[4,32,512]{2,1,0:T(8,128)(2,1)S(1)}, bf16[4,32,512]{2,1,0:T(8,128)(2,1)S(1)}, u32[]{:S(2)}, u32[]{:S(2)}) collective-permute-start(bf16[4,32,512]{2,1,0:T(8,128)(2,1)S(1)} %fusion.65), channel_id=1, source_target_pairs={{0,1},{1,0},{2,3},{3,2},{4,5},{5,4},{6,7},{7,6},{8,9},{9,8},{10,11... | collective-permute-start | bytes 393224 | tf_op jit(solution)/shard_map/ppermute | solution.py:464
  408.0 13.6 %collective-permute-start.47 = (bf16[64,2048]{1,0:T(8,128)(2,1)S(1)}, bf16[64,2048]{1,0:T(8,128)(2,1)S(1)}, u32[]{:S(2)}, u32[]{:S(2)}) collective-permute-start(bf16[64,2048]{1,0:T(8,128)(2,1)S(1)} %fusion.57), channel_id=1, source_target_pairs={{0,24},{24,0},{8,16},{16,8},{1,25},{25,1},{9,17},{17,9},{2,26},{26... | collective-permute-start | bytes 786440 | tf_op jit(solution)/shard_map/ppermute | solution.py:464
  410.6 18.8 %collective-permute-start.48 = (bf16[2,64,2048]{2,1,0:T(8,128)(2,1)S(1)}, bf16[2,64,2048]{2,1,0:T(8,128)(2,1)S(1)}, u32[]{:S(2)}, u32[]{:S(2)}) collective-permute-start(bf16[2,64,2048]{2,1,0:T(8,128)(2,1)S(1)} %select_convert_fusion), channel_id=1, source_target_pairs={{0,8},{8,0},{16,24},{24,16},{1,9},{9,1},{17,25},{25,17},{2,10},{10... | collective-permute-start | bytes 1572872 | tf_op jit(solution)/shard_map/ppermute | solution.py:464
  436.9 10.5 %collective-permute-start.55 = (bf16[584,128]{1,0:T(8,128)(2,1)S(1)}, bf16[584,128]{1,0:T(8,128)(2,1)S(1)}, u32[]{:S(2)}, u32[]{:S(2)}) collective-permute-start(bf16[584,128]{1,0:T(8,128)(2,1)S(1)} %convert_element_type.481), channel_id=1, source_target_pairs={{0,1},{1,0},{2,3},{3,2},{4,5},{5,4},{6,7},{7,6},{8,9},{9,8},{10,11... | collective-permute-start | bytes 448520 | tf_op jit(solution)/shard_map/ppermute | solution.py:464
  438.5 18.4 %collective-permute-start.51 = (bf16[4,2,32,1536]{3,2,0,1:T(8,128)(2,1)S(1)}, bf16[4,2,32,1536]{3,2,0,1:T(8,128)(2,1)S(1)}, u32[]{:S(2)}, u32[]{:S(2)}) collective-permute-start(bf16[4,2,32,1536]{3,2,0,1:T(8,128)(2,1)S(1)} %dynamic-slice_bitcast_fusion.1), channel_id=1, source_target_pairs={{0,4},{4,0},{1,5},{5,1},{2,6},{6,2},{3,7},{7,3},{8,12},{12,8},{9,1... | collective-permute-start | bytes 2359304 | tf_op jit(solution)/shard_map/ppermute | solution.py:464
  439.5 19.3 %collective-permute-start.52 = (bf16[4,2,32,1536]{3,2,0,1:T(8,128)(2,1)S(1)}, bf16[4,2,32,1536]{3,2,0,1:T(8,128)(2,1)S(1)}, u32[]{:S(2)}, u32[]{:S(2)}) collective-permute-start(bf16[4,2,32,1536]{3,2,0,1:T(8,128)(2,1)S(1)} %dynamic-slice_bitcast_fusion), channel_id=1, source_target_pairs={{0,1},{1,0},{2,3},{3,2},{4,5},{5,4},{6,7},{7,6},{8,9},{9,8},{10,11... | collective-permute-start | bytes 2359304 | tf_op jit(solution)/shard_map/ppermute | solution.py:464
  439.9 10.2 %collective-permute-start.53 = (bf16[64,2048]{1,0:T(8,128)(2,1)S(1)}, bf16[64,2048]{1,0:T(8,128)(2,1)S(1)}, u32[]{:S(2)}, u32[]{:S(2)}) collective-permute-start(bf16[64,2048]{1,0:T(8,128)(2,1)S(1)} %fusion.58), channel_id=1, source_target_pairs={{0,24},{24,0},{8,16},{16,8},{1,25},{25,1},{9,17},{17,9},{2,26},{26... | collective-permute-start | bytes 786440 | tf_op jit(solution)/shard_map/ppermute | solution.py:464
  444.0 19.9 %collective-permute-start.62 = (bf16[512,1024]{1,0:T(8,128)(2,1)S(1)}, bf16[512,1024]{1,0:T(8,128)(2,1)S(1)}, u32[]{:S(2)}, u32[]{:S(2)}) collective-permute-start(bf16[512,1024]{1,0:T(8,128)(2,1)S(1)} %add_convert_fusion.2), channel_id=1, source_target_pairs={{0,2},{2,0},{1,3},{3,1},{4,6},{6,4},{5,7},{7,5},{8,10},{10,8},{9,1... | collective-permute-start | bytes 3145736 | tf_op jit(solution)/shard_map/ppermute | solution.py:469
  459.2 10.7 %collective-permute-start.58 = (bf16[64,512]{1,0:T(8,128)(2,1)S(1)}, bf16[64,512]{1,0:T(8,128)(2,1)S(1)}, u32[]{:S(2)}, u32[]{:S(2)}) collective-permute-start(bf16[64,512]{1,0:T(8,128)(2,1)S(1)} %fusion.71), channel_id=1, source_target_pairs={{0,24},{24,0},{8,16},{16,8},{1,25},{25,1},{9,17},{17,9},{2,26},{26... | collective-permute-start | bytes 196616 | tf_op jit(solution)/shard_map/ppermute | solution.py:464
  460.6 9.2 %collective-permute-start.59 = (bf16[584,128]{1,0:T(8,128)(2,1)S(1)}, bf16[584,128]{1,0:T(8,128)(2,1)S(1)}, u32[]{:S(2)}, u32[]{:S(2)}) collective-permute-start(bf16[584,128]{1,0:T(8,128)(2,1)S(1)} %fusion.59), channel_id=1, source_target_pairs={{0,4},{4,0},{1,5},{5,1},{2,6},{6,2},{3,7},{7,3},{8,12},{12,8},{9,1... | collective-permute-start | bytes 448520 | tf_op jit(solution)/shard_map/ppermute | solution.py:464
  462.0 8.8 %collective-permute-start.56 = (bf16[4,32,1536]{2,1,0:T(8,128)(2,1)S(1)}, bf16[4,32,1536]{2,1,0:T(8,128)(2,1)S(1)}, u32[]{:S(2)}, u32[]{:S(2)}) collective-permute-start(bf16[4,32,1536]{2,1,0:T(8,128)(2,1)S(1)} %fusion.52), channel_id=1, source_target_pairs={{0,1},{1,0},{2,3},{3,2},{4,5},{5,4},{6,7},{7,6},{8,9},{9,8},{10,11... | collective-permute-start | bytes 1179656 | tf_op jit(solution)/shard_map/ppermute | solution.py:464
  463.5 10.2 %collective-permute-start.57 = (bf16[4,32,1536]{2,1,0:T(8,128)(2,1)S(1)}, bf16[4,32,1536]{2,1,0:T(8,128)(2,1)S(1)}, u32[]{:S(2)}, u32[]{:S(2)}) collective-permute-start(bf16[4,32,1536]{2,1,0:T(8,128)(2,1)S(1)} %fusion.53), channel_id=1, source_target_pairs={{0,4},{4,0},{1,5},{5,1},{2,6},{6,2},{3,7},{7,3},{8,12},{12,8},{9,1... | collective-permute-start | bytes 1179656 | tf_op jit(solution)/shard_map/ppermute | solution.py:464
  465.1 23.8 %collective-permute-start.63 = (bf16[512,1024]{1,0:T(8,128)(2,1)S(1)}, bf16[512,1024]{1,0:T(8,128)(2,1)S(1)}, u32[]{:S(2)}, u32[]{:S(2)}) collective-permute-start(bf16[512,1024]{1,0:T(8,128)(2,1)S(1)} %add_convert_fusion.1), channel_id=1, source_target_pairs={{0,0},{1,2},{2,1},{3,3},{4,4},{5,6},{6,5},{7,7},{8,8},{9,10},{10,9... | collective-permute-start | bytes 3145736 | tf_op jit(solution)/shard_map/ppermute | solution.py:464
  473.9 6.1 %collective-permute-start.61 = (bf16[584,128]{1,0:T(8,128)(2,1)S(1)}, bf16[584,128]{1,0:T(8,128)(2,1)S(1)}, u32[]{:S(2)}, u32[]{:S(2)}) collective-permute-start(bf16[584,128]{1,0:T(8,128)(2,1)S(1)} %fusion.100), channel_id=1, source_target_pairs={{0,24},{24,0},{8,16},{16,8},{1,25},{25,1},{9,17},{17,9},{2,26},{26... | collective-permute-start | bytes 448520 | tf_op jit(solution)/shard_map/ppermute | solution.py:464
  476.0 12.8 %collective-permute-start.60 = (bf16[2,64,1536]{2,1,0:T(8,128)(2,1)S(1)}, bf16[2,64,1536]{2,1,0:T(8,128)(2,1)S(1)}, u32[]{:S(2)}, u32[]{:S(2)}) collective-permute-start(bf16[2,64,1536]{2,1,0:T(8,128)(2,1)S(1)} %select_convert_fusion.2), channel_id=1, source_target_pairs={{0,8},{8,0},{16,24},{24,16},{1,9},{9,1},{17,25},{25,17},{2,10},{10... | collective-permute-start | bytes 1179656 | tf_op jit(solution)/shard_map/ppermute | solution.py:464
  489.1 6.7 %collective-permute-start.65 = (bf16[584,128]{1,0:T(8,128)(2,1)S(1)}, bf16[584,128]{1,0:T(8,128)(2,1)S(1)}, u32[]{:S(2)}, u32[]{:S(2)}) collective-permute-start(bf16[584,128]{1,0:T(8,128)(2,1)S(1)} %fusion.60), channel_id=1, source_target_pairs={{0,8},{8,0},{16,24},{24,16},{1,9},{9,1},{17,25},{25,17},{2,10},{10... | collective-permute-start | bytes 448520 | tf_op jit(solution)/shard_map/ppermute | solution.py:464
  489.2 11.9 %collective-permute-start.66 = (bf16[64,4096]{1,0:T(8,128)(2,1)S(1)}, bf16[64,4096]{1,0:T(8,128)(2,1)S(1)}, u32[]{:S(2)}, u32[]{:S(2)}) collective-permute-start(bf16[64,4096]{1,0:T(8,128)(2,1)S(1)} %pad_maximum_fusion.17), channel_id=1, source_target_pairs={{0,0},{1,2},{2,1},{3,3},{4,4},{5,6},{6,5},{7,7},{8,8},{9,10},{10,9... | collective-permute-start | bytes 1572872 | tf_op jit(solution)/shard_map/ppermute | solution.py:464
  493.9 7.1 %collective-permute-start.64 = (bf16[64,1536]{1,0:T(8,128)(2,1)S(1)}, bf16[64,1536]{1,0:T(8,128)(2,1)S(1)}, u32[]{:S(2)}, u32[]{:S(2)}) collective-permute-start(bf16[64,1536]{1,0:T(8,128)(2,1)S(1)} %fusion.61), channel_id=1, source_target_pairs={{0,24},{24,0},{8,16},{16,8},{1,25},{25,1},{9,17},{17,9},{2,26},{26... | collective-permute-start | bytes 589832 | tf_op jit(solution)/shard_map/ppermute | solution.py:464
  501.1 7.7 %collective-permute-start.67 = (bf16[64,2048]{1,0:T(8,128)(2,1)S(1)}, bf16[64,2048]{1,0:T(8,128)(2,1)S(1)}, u32[]{:S(2)}, u32[]{:S(2)}) collective-permute-start(bf16[64,2048]{1,0:T(8,128)(2,1)S(1)} %pad_maximum_fusion.20), channel_id=1, source_target_pairs={{0,0},{1,2},{2,1},{3,3},{4,4},{5,6},{6,5},{7,7},{8,8},{9,10},{10,9... | collective-permute-start | bytes 786440 | tf_op jit(solution)/shard_map/ppermute | solution.py:464
  (57 other events, 569.0 us)

commit v3 on v1

--- a/solution.py
+++ b/solution.py
@@ -599,6 +599,7 @@
 
 TILE = 256
 KEYS = 256
+LOSS_TILE = 1024
 NEG = -1e30
 
 
@@ -831,7 +832,7 @@
 
 def expand_kernel(x_ref, w_ref, b_ref, *refs):
     act_ref, slope_ref = refs[-2:]
-    rows = 256
+    rows = 128
     for start in range(0, x_ref.shape[0], rows):
         part = slice(start, start + rows)
         value = exact(x_ref[part, :], w_ref[...], ((1,), (0,))) + b_ref[...]
@@ -902,13 +903,13 @@
     whole = lambda shape: pl.BlockSpec(shape, lambda i: (0, 0))
     return pl.pallas_call(
         partial(pool_kernel, cuts, span),
-        grid=(count // TILE,),
+        grid=(count // LOSS_TILE,),
         in_specs=[
-            pl.BlockSpec((TILE, width), lambda i: (i, 0)),
+            pl.BlockSpec((LOSS_TILE, width), lambda i: (i, 0)),
             whole((tokens, width)),
             whole((1, tokens)),
         ],
-        out_specs=pl.BlockSpec((len(cuts) * NDOC, TILE), lambda i: (0, i)),
+        out_specs=pl.BlockSpec((len(cuts) * NDOC, LOSS_TILE), lambda i: (0, i)),
         out_shape=jax.ShapeDtypeStruct((len(cuts) * NDOC, count), F32),
         scratch_shapes=[
             pltpu.VMEM((len(cuts), tokens - span, width), BF),
@@ -978,14 +979,14 @@
     whole = lambda shape: pl.BlockSpec(shape, lambda i: (0, 0))
     return pl.pallas_call(
         partial(pool_back_kernel, cuts, span),
-        grid=(count // TILE,),
+        grid=(count // LOSS_TILE,),
         in_specs=[
-            pl.BlockSpec((TILE, width), lambda i: (i, 0)),
+            pl.BlockSpec((LOSS_TILE, width), lambda i: (i, 0)),
             whole((tokens, width)),
             whole((1, tokens)),
-            pl.BlockSpec((len(cuts) * NDOC, TILE), lambda i: (0, i)),
+            pl.BlockSpec((len(cuts) * NDOC, LOSS_TILE), lambda i: (0, i)),
         ],
-        out_specs=[pl.BlockSpec((TILE, width), lambda i: (i, 0)), whole((docs, width))],
+        out_specs=[pl.BlockSpec((LOSS_TILE, width), lambda i: (i, 0)), whole((docs, width))],
         out_shape=[
             jax.ShapeDtypeStruct((count, width), BF),
             jax.ShapeDtypeStruct((docs, width), F32),

time: 516 us -> 510 us (0.988)
  Pallas kernels: 83.1 us -> 76.2 us
    pallas_call x2, Pallas kernels: 25 us -> 19.5 us  [the longest x1 12.5 us: pool_back(): pl.pallas_call(partial(pool_back_kernel, cuts, span), grid=(count // LOSS...]
  transfers between devices with their start and end apart: 71 -> 71, of which waited for: 29 -> 29; matrix products, arithmetic and copies ran while one was open for 15% -> 15% of each run, Pallas kernels for 15% -> 14%
where the time goes in v3:
time: 510 us; the launch traced here: 504 us
  waiting for transfers between devices  166 us (33%)
  starting transfers between devices  119 us (23%)
  Pallas kernels  76.2 us (15%)
  matrix products  62.2 us (12%)
  local copies, waits for them, and re-layouts  43.2 us (8%)
  other arithmetic  34.7 us (7%)
    ppermute x54, waiting for transfers between devices, exchange(): lax.ppermute(value, axis, steps)  137 us
    ppermute x54, starting transfers between devices, exchange(): lax.ppermute(value, axis, steps)  67.6 us
    pallas_call x2, Pallas kernels, attend_back(): pl.pallas_call(partial(attend_back_kernel, group * heads), grid=(count //...  28 us
    dot_general x7, matrix products, contract_rows(): lax.dot_general(left, right, (((0,), (0,)), ((), ())), precision=precisio...  22.5 us
    dot_general x12, matrix products, contract_cols(): lax.dot_general(left, right, (((1,), (1,)), ((), ())), precision=precisio...  21.2 us
    unnamed x129, local copies, waits for them, and re-layouts  20.8 us
    ppermute x12, starting transfers between devices, swap(): return lax.ppermute(value, axis, SWAP)  20.7 us
    dot_general x4, matrix products, dot(): return jnp.dot(left, right, preferred_element_type=F32)  17.1 us
  transfers between devices with their start and end apart: 71, of which 29 were waited for; matrix products, arithmetic and copies ran while one was open for 15% of the time, Pallas kernels for 14%

profile of v3, /device:TPU:1, one launch (start us, length us, event | category | flops | bytes accessed | tf_op | source)
XLA Modules:
  0.0 504.4 jit_solution(3475078430093743304)
XLA Ops:
  1.7 4.5 collective-permute-start
  10.0 1.9 fusion.39
  13.3 3.3 collective-permute-start.3
  18.5 4.2 collective-permute-start.5
  24.1 2.5 collective-permute-start.4
  26.6 4.3 collective-permute-done.5
  31.1 3.7 collective-permute-done.4
  34.8 9.2 %collective-permute-done.6 = bf16[64,2688]{1,0:T(8,128)(2,1)S(1)} collective-permute-done((bf16[64,2688]{1,0:T(8,128)(2,1)S(1)}, bf16[64,2688]{1,0:T(8,128)(2,1)S(1)}, u32[]{:S(2)}, u32[]{:S(2)}) %collective-permute-start.6) | collective-permute-done | bytes 344096 | tf_op jit(solution)/shard_map/ppermute | solution.py:464
  47.0 6.0 %collective-permute-done.7 = bf16[4,32,1536]{2,1,0:T(8,128)(2,1)S(1)} collective-permute-done((bf16[4,32,1536]{2,1,0:T(8,128)(2,1)S(1)}, bf16[4,32,1536]{2,1,0:T(8,128)(2,1)S(1)}, u32[]{:S(2)}, u32[]{:S(2)}) %collective-permute-start.7) | collective-permute-done | bytes 393248 | tf_op jit(solution)/shard_map/ppermute | solution.py:464
  53.9 6.4 %collective-permute-done.9 = bf16[2,64,2688]{2,1,0:T(8,128)(2,1)S(1)} collective-permute-done((bf16[2,64,2688]{2,1,0:T(8,128)(2,1)S(1)}, bf16[2,64,2688]{2,1,0:T(8,128)(2,1)S(1)}, u32[]{:S(2)}, u32[]{:S(2)}) %collective-permute-start.9) | collective-permute-done | bytes 688160 | tf_op jit(solution)/shard_map/ppermute | solution.py:464
  63.0 3.5 collective-permute-start.12
  68.1 2.3 collective-permute-done.12
  70.4 21.5 %collective-permute-done.13 = bf16[4,32,2688]{2,1,0:T(8,128)(2,1)S(1)} collective-permute-done((bf16[4,32,2688]{2,1,0:T(8,128)(2,1)S(1)}, bf16[4,32,2688]{2,1,0:T(8,128)(2,1)S(1)}, u32[]{:S(2)}, u32[]{:S(2)}) %collective-permute-start.13) | collective-permute-done | bytes 688160 | tf_op jit(solution)/shard_map/ppermute | solution.py:464
  93.1 3.5 collective-permute-start.15
  97.4 3.6 add_convert_fusion.own_ref.qkv_ref
  101.3 3.0 collective-permute-done.15
  108.5 12.5 %shard_map.254 = (bf16[1024,512]{1,0:T(8,128)(2,1)S(1)}, f32[8,1024]{1,0:T(8,128)S(1)}) custom-call(s32[2,4]{1,0:T(2,128)S(1)} %pad_add_fusion.1.bounds, bf16[1024,1536]{1,0:T(8,128)(2,1)S(1)} %add_convert_fusion.own_ref.qkv_ref, bf16[1024,1536]{1,0:T(8,128)(2,1)S(1)} %add_convert_fusion.own_ref.qkv_ref, s32[2,1024]{1,0:T(2,128)S(1)} %pad_add_fusion.spans), custom_call_target="tpu_custom_call" | custom-call | flops 2147483648 | bytes 12582912 | tf_op jit(solution)/shard_map/pallas_call | solution.py:679
  121.0 10.6 %collective-permute-done.18 = bf16[4,32,2048]{2,1,0:T(8,128)(2,1)S(1)} collective-permute-done((bf16[4,32,2048]{2,1,0:T(8,128)(2,1)S(1)}, bf16[4,32,2048]{2,1,0:T(8,128)(2,1)S(1)}, u32[]{:S(2)}, u32[]{:S(2)}) %collective-permute-start.18) | collective-permute-done | bytes 524320 | tf_op jit(solution)/shard_map/ppermute | solution.py:464
  134.8 2.4 copy-done.2
  138.9 5.8 %collective-permute-start.20 = (bf16[512,1024]{1,0:T(8,128)(2,1)}, bf16[512,1024]{1,0:T(8,128)(2,1)}, u32[]{:S(2)}, u32[]{:S(2)}) collective-permute-start(bf16[512,1024]{1,0:T(8,128)(2,1)} %convolution_convert_fusion.6), channel_id=1, source_target_pairs={{0,2},{2,0},{1,3},{3,1},{4,6},{6,4},{5,7},{7,5},{8,10},{10,8},{9,1... | collective-permute-start | bytes 3145736 | tf_op jit(solution)/shard_map/ppermute | solution.py:469
  144.8 2.0 fusion.31
  155.4 16.2 %shard_map.255 = (bf16[1024,2048]{1,0:T(8,128)(2,1)S(1)}, bf16[1024,2048]{1,0:T(8,128)(2,1)S(1)}) custom-call(bf16[1024,1024]{1,0:T(8,128)(2,1)S(1)} %pad_maximum_fusion.5.x_ref, bf16[1024,2688]{1,0:T(8,128)(2,1)S(1)} %bitcast.282, f32[1,2048]{1,0:T(1,128)S(1)} %slice.503.b_ref), custom_call_target="tpu_custom_call" | custom-call | flops 4294967296 | bytes 14680064 | tf_op jit(solution)/shard_map/pallas_call | solution.py:849
  171.6 2.1 copy-done.7
  173.7 4.2 collective-permute-done.23
  179.4 2.4 fusion.11
  183.4 2.8 collective-permute-start.27
  186.3 2.8 fusion.119
  194.9 7.8 %all-to-all-start = ((bf16[16,128,128]{2,1,0:T(8,128)(2,1)}), bf16[16,128,128]{2,1,0:T(8,128)(2,1)S(1)}, u32[]{:S(2)}, u32[]{:S(2)}) async-start(bf16[16,128,128]{2,1,0:T(8,128)(2,1)} %broadcast_in_dim.46), calls=%async_computation | async-start | bytes 1048576 | tf_op jit(solution)/shard_map/all_to_all | solution.py:1143
  204.0 11.4 %all-to-all-done = bf16[16,128,128]{2,1,0:T(8,128)(2,1)S(1)} async-done(((bf16[16,128,128]{2,1,0:T(8,128)(2,1)}), bf16[16,128,128]{2,1,0:T(8,128)(2,1)S(1)}, u32[]{:S(2)}, u32[]{:S(2)}) %all-to-all-start) | async-done | bytes 524320 | tf_op jit(solution)/shard_map/all_to_all | solution.py:1143
  215.4 7.0 %shard_map.256 = f32[24,2048]{1,0:T(8,128)S(1)} custom-call(bf16[2048,128]{1,0:T(8,128)(2,1)S(1)} %bitcast.287, bf16[1024,128]{1,0:T(8,128)(2,1)S(1)} %maximum_select_fusion.25.d_ref, s32[1,1024]{1,0:T(1,128)S(1)} %compare_select_fusion.seg_ref), custom_call_target="tpu_custom_call" | custom-call | flops 3221225472 | bytes 786432 | tf_op jit(solution)/shard_map/pallas_call | solution.py:904
  223.8 5.7 %all-to-all-start.1 = ((f32[16,8,128]{2,1,0:T(8,128)}), f32[16,8,128]{2,1,0:T(8,128)S(1)}, u32[]{:S(2)}, u32[]{:S(2)}) async-start(f32[16,8,128]{2,1,0:T(8,128)} %broadcast_in_dim.47), calls=%async_computation.1 | async-start | bytes 131072 | tf_op jit(solution)/shard_map/all_to_all | solution.py:1164
  229.5 5.1 %collective-permute-start.28 = (bf16[512,1024]{1,0:T(8,128)(2,1)}, bf16[512,1024]{1,0:T(8,128)(2,1)}, u32[]{:S(2)}, u32[]{:S(2)}) collective-permute-start(bf16[512,1024]{1,0:T(8,128)(2,1)} %add_convert_fusion.3), channel_id=1, source_target_pairs={{0,0},{1,2},{2,1},{3,3},{4,4},{5,6},{6,5},{7,7},{8,8},{9,10},{10,9... | collective-permute-start | bytes 3145736 | tf_op jit(solution)/shard_map/ppermute | solution.py:1184
  236.7 12.5 %shard_map.257 = (bf16[2048,128]{1,0:T(8,128)(2,1)}, f32[768,128]{1,0:T(8,128)S(1)}) custom-call(bf16[2048,128]{1,0:T(8,128)(2,1)S(1)} %bitcast.288, bf16[1024,128]{1,0:T(8,128)(2,1)S(1)} %maximum_select_fusion.25.d_ref, s32[1,1024]{1,0:T(1,128)S(1)} %compare_select_fusion.seg_ref, f32[24,2048]{1,0:T(8,128)S(1)} %convolution_divide_fusion.coef_ref), custom_call_target="tpu_custom_call" | custom-call | flops 4831838208 | bytes 1572864 | tf_op jit(solution)/shard_map/pallas_call | solution.py:980
  249.3 9.6 %all-to-all-start.2 = ((bf16[16,128,128]{2,1,0:T(8,128)(2,1)}), bf16[16,128,128]{2,1,0:T(8,128)(2,1)S(1)}, u32[]{:S(2)}, u32[]{:S(2)}) async-start(bf16[16,128,128]{2,1,0:T(8,128)(2,1)} %bitcast.57), calls=%async_computation.2 | async-start | bytes 1048576 | tf_op jit(solution)/shard_map/all_to_all | solution.py:1186
  258.9 12.1 %all-to-all-done.2 = bf16[16,128,128]{2,1,0:T(8,128)(2,1)S(1)} async-done(((bf16[16,128,128]{2,1,0:T(8,128)(2,1)}), bf16[16,128,128]{2,1,0:T(8,128)(2,1)S(1)}, u32[]{:S(2)}, u32[]{:S(2)}) %all-to-all-start.2) | async-done | bytes 524320 | tf_op jit(solution)/shard_map/all_to_all | solution.py:1186
  271.2 4.0 collective-permute-start.29
  280.3 1.8 fusion.121
  284.8 6.4 %convolution_convert_fusion.1 = bf16[1024,2048]{1,0:T(8,128)(2,1)S(1)} fusion(bf16[1024,2048]{1,0:T(8,128)(2,1)S(1)} %copy-done.6, bf16[512,1024]{1,0:T(8,128)(2,1)} %collective-permute-done.30, bf16[512,1024]{1,0:T(8,128)(2,1)} %get-tuple-element.241), kind=kOutput, calls=%fused_computation.6 | convolution fusion | flops 4301258752 | bytes 10485760 | tf_op jit(solution)/shard_map/dot_general | solution.py:33
  295.2 8.0 %convert_reduce_fusion = (f32[2048]{0:T(1024)S(1)}, bf16[1024,2048]{1,0:T(8,128)(2,1)}) fusion(bf16[1024,2048]{1,0:T(8,128)(2,1)S(1)} %copy-done.8, bf16[1024,2048]{1,0:T(8,128)(2,1)S(1)} %bitcast.298, bf16[512,1024]{1,0:T(8,128)(2,1)} %collective-permute-done.30, bf16[512,1024]{1,0:T(8,128)(2,1)} %get-tuple-element.241), kind=kOutput, calls=%fused_computation | convolution fusion | flops 4309645312 | bytes 14688256 | tf_op jit(solution)/shard_map/dot_general | solution.py:448
  303.2 4.1 fusion.14
  307.5 2.4 fusion.2
  309.9 6.6 %collective-permute-done.33 = bf16[4,2,32,2048]{3,2,0,1:T(8,128)(2,1)S(1)} collective-permute-done((bf16[4,2,32,2048]{3,2,0,1:T(8,128)(2,1)S(1)}, bf16[4,2,32,2048]{3,2,0,1:T(8,128)(2,1)S(1)}, u32[]{:S(2)}, u32[]{:S(2)}) %collective-permute-start.33) | collective-permute-done | bytes 1048608 | tf_op jit(solution)/shard_map/ppermute | solution.py:464
  321.5 5.3 %convolution_convert_fusion = bf16[1024,2048]{1,0:T(8,128)(2,1)S(1)} fusion(bf16[1024,2048]{1,0:T(8,128)(2,1)S(1)} %copy-done.49, bf16[512,1024]{1,0:T(8,128)(2,1)S(1)} %copy-done.38, bf16[512,1024]{1,0:T(8,128)(2,1)S(1)} %copy-done.25), kind=kOutput, calls=%fused_computation.5 | convolution fusion | flops 4301258752 | bytes 10485760 | tf_op jit(solution)/shard_map/dot_general | solution.py:33
  336.9 2.4 collective-permute-start.32
  339.4 16.2 %collective-permute-done.37 = bf16[4,2,32,2048]{3,2,0,1:T(8,128)(2,1)} collective-permute-done((bf16[4,2,32,2048]{3,2,0,1:T(8,128)(2,1)}, bf16[4,2,32,2048]{3,2,0,1:T(8,128)(2,1)}, u32[]{:S(2)}, u32[]{:S(2)}) %collective-permute-start.37) | collective-permute-done | bytes 1048608 | tf_op jit(solution)/shard_map/ppermute | solution.py:464
  362.9 3.8 convolution_convert_fusion.5.grad_ref
  366.7 3.5 convolution_convert_fusion.4
  375.2 13.9 %shard_map.258 = (bf16[1024,768]{1,0:T(8,128)(2,1)S(1)}, f32[8,256]{1,0:T(8,128)S(1)}) custom-call(s32[2,4]{1,0:T(2,128)S(1)} %pad_add_fusion.1.bounds, bf16[1024,1536]{1,0:T(8,128)(2,1)S(1)} %copy-done.4, bf16[1024,1536]{1,0:T(8,128)(2,1)S(1)} %copy-done.4, bf16[1024,512]{1,0:T(8,128)(2,1)S(1)} %get-tuple-element.133.out_ref, ...), custom_call_target="tpu_custom_call" | custom-call | flops 2684354560 | bytes 12582912 | tf_op jit(solution)/shard_map/pallas_call | solution.py:782
  390.0 4.3 collective-permute-start.44
  397.8 14.1 %shard_map.259 = (bf16[1024,768]{1,0:T(8,128)(2,1)S(1)}, f32[8,256]{1,0:T(8,128)S(1)}) custom-call(s32[2,4]{1,0:T(2,128)S(1)} %pad_add_fusion.1.bounds, bf16[1024,1536]{1,0:T(8,128)(2,1)S(1)} %copy-done.4, bf16[1024,1536]{1,0:T(8,128)(2,1)S(1)} %copy-done.4, bf16[1024,512]{1,0:T(8,128)(2,1)S(1)} %get-tuple-element.133.out_ref, ...), custom_call_target="tpu_custom_call" | custom-call | flops 2684354560 | bytes 12582912 | tf_op jit(solution)/shard_map/pallas_call | solution.py:782
  415.7 1.9 convolution_convert_fusion.3
  418.6 1.9 convolution_convert_fusion.2
  428.3 8.5 %collective-permute-done.53 = bf16[2,64,512]{2,1,0:T(8,128)(2,1)S(1)} collective-permute-done((bf16[2,64,512]{2,1,0:T(8,128)(2,1)S(1)}, bf16[2,64,512]{2,1,0:T(8,128)(2,1)S(1)}, u32[]{:S(2)}, u32[]{:S(2)}) %collective-permute-start.53) | collective-permute-done | bytes 131104 | tf_op jit(solution)/shard_map/ppermute | solution.py:464
  437.4 6.2 %collective-permute-done.54 = bf16[584,128]{1,0:T(8,128)(2,1)S(1)} collective-permute-done((bf16[584,128]{1,0:T(8,128)(2,1)S(1)}, bf16[584,128]{1,0:T(8,128)(2,1)S(1)}, u32[]{:S(2)}, u32[]{:S(2)}) %collective-permute-start.54) | collective-permute-done | bytes 149536 | tf_op jit(solution)/shard_map/ppermute | solution.py:464
  446.4 2.4 collective-permute-start.57
  451.0 4.8 collective-permute-start.62
  455.8 2.1 collective-permute-done.58
  458.5 2.0 collective-permute-start.60
  460.5 9.3 %collective-permute-done.60 = bf16[584,128]{1,0:T(8,128)(2,1)S(1)} collective-permute-done((bf16[584,128]{1,0:T(8,128)(2,1)S(1)}, bf16[584,128]{1,0:T(8,128)(2,1)S(1)}, u32[]{:S(2)}, u32[]{:S(2)}) %collective-permute-start.60) | collective-permute-done | bytes 149536 | tf_op jit(solution)/shard_map/ppermute | solution.py:464
  469.9 5.9 %collective-permute-start.65 = (bf16[64,4096]{1,0:T(8,128)(2,1)S(1)}, bf16[64,4096]{1,0:T(8,128)(2,1)S(1)}, u32[]{:S(2)}, u32[]{:S(2)}) collective-permute-start(bf16[64,4096]{1,0:T(8,128)(2,1)S(1)} %pad_maximum_fusion.17), channel_id=1, source_target_pairs={{0,0},{1,2},{2,1},{3,3},{4,4},{5,6},{6,5},{7,7},{8,8},{9,10},{10,9... | collective-permute-start | bytes 1572872 | tf_op jit(solution)/shard_map/ppermute | solution.py:464
  477.5 9.4 %collective-permute-done.64 = bf16[584,128]{1,0:T(8,128)(2,1)S(1)} collective-permute-done((bf16[584,128]{1,0:T(8,128)(2,1)S(1)}, bf16[584,128]{1,0:T(8,128)(2,1)S(1)}, u32[]{:S(2)}, u32[]{:S(2)}) %collective-permute-start.64) | collective-permute-done | bytes 149536 | tf_op jit(solution)/shard_map/ppermute | solution.py:464
  487.0 1.9 collective-permute-start.66
  490.9 3.8 collective-permute-done.66
  500.9 2.3 copy.165
  (454 shorter events, 123.5 us)
Async XLA Ops:
  1.7 10.3 %collective-permute-start = (bf16[64,1536]{1,0:T(8,128)(2,1)S(1)}, bf16[64,1536]{1,0:T(8,128)(2,1)}, u32[]{:S(2)}, u32[]{:S(2)}) collective-permute-start(bf16[64,1536]{1,0:T(8,128)(2,1)S(1)} %slice_dynamic-update-slice_fusion), channel_id=1, source_target_pairs={{0,0},{1,2},{2,1},{3,3},{4,4},{5,6},{6,5},{7,7},{8,8},{9,10},{10,9... | collective-permute-start | bytes 589832 | tf_op jit(solution)/shard_map/ppermute | solution.py:464
  6.2 5.8 %collective-permute-start.1 = (bf16[1024,1024]{1,0:T(8,128)(2,1)}, bf16[1024,1024]{1,0:T(8,128)(2,1)S(1)}, u32[]{:S(2)}, u32[]{:S(2)}) collective-permute-start(bf16[1024,1024]{1,0:T(8,128)(2,1)} %param.15), channel_id=1, source_target_pairs={{0,2},{2,0},{1,3},{3,1},{4,6},{6,4},{5,7},{7,5},{8,10},{10,8},{9,1... | collective-permute-start | bytes 6291464 | tf_op jit(solution)/shard_map/ppermute | solution.py:464
  13.3 9.5 %collective-permute-start.3 = (bf16[64,1536]{1,0:T(8,128)(2,1)}, bf16[64,1536]{1,0:T(8,128)(2,1)}, u32[]{:S(2)}, u32[]{:S(2)}) collective-permute-start(bf16[64,1536]{1,0:T(8,128)(2,1)} %collective-permute-done), channel_id=1, source_target_pairs={{0,24},{24,0},{8,16},{16,8},{1,25},{25,1},{9,17},{17,9},{2,26},{26... | collective-permute-start | bytes 589832 | tf_op jit(solution)/shard_map/ppermute | solution.py:464
  18.5 12.4 %collective-permute-start.5 = (bf16[64,4736]{1,0:T(8,128)(2,1)}, bf16[64,4736]{1,0:T(8,128)(2,1)S(1)}, u32[]{:S(2)}, u32[]{:S(2)}) collective-permute-start(bf16[64,4736]{1,0:T(8,128)(2,1)} %fusion.39), channel_id=1, source_target_pairs={{0,0},{1,2},{2,1},{3,3},{4,4},{5,6},{6,5},{7,7},{8,8},{9,10},{10,9... | collective-permute-start | bytes 1818632 | tf_op jit(solution)/shard_map/ppermute | solution.py:464
  24.1 10.7 %collective-permute-start.4 = (bf16[2,64,1536]{2,1,0:T(8,128)(2,1)S(1)}, bf16[2,64,1536]{2,1,0:T(8,128)(2,1)S(1)}, u32[]{:S(2)}, u32[]{:S(2)}) collective-permute-start(bf16[2,64,1536]{2,1,0:T(8,128)(2,1)S(1)} %maximum_select_fusion.22), channel_id=1, source_target_pairs={{0,8},{8,0},{16,24},{24,16},{1,9},{9,1},{17,25},{25,17},{2,10},{10... | collective-permute-start | bytes 1179656 | tf_op jit(solution)/shard_map/ppermute | solution.py:464
  31.0 13.1 %collective-permute-start.6 = (bf16[64,2688]{1,0:T(8,128)(2,1)S(1)}, bf16[64,2688]{1,0:T(8,128)(2,1)S(1)}, u32[]{:S(2)}, u32[]{:S(2)}) collective-permute-start(bf16[64,2688]{1,0:T(8,128)(2,1)S(1)} %get-tuple-element.298), channel_id=1, source_target_pairs={{0,24},{24,0},{8,16},{16,8},{1,25},{25,1},{9,17},{17,9},{2,26},{26... | collective-permute-start | bytes 1032200 | tf_op jit(solution)/shard_map/ppermute | solution.py:464
  44.5 8.5 %collective-permute-start.7 = (bf16[4,32,1536]{2,1,0:T(8,128)(2,1)S(1)}, bf16[4,32,1536]{2,1,0:T(8,128)(2,1)S(1)}, u32[]{:S(2)}, u32[]{:S(2)}) collective-permute-start(bf16[4,32,1536]{2,1,0:T(8,128)(2,1)S(1)} %get-tuple-element.288), channel_id=1, source_target_pairs={{0,4},{4,0},{1,5},{5,1},{2,6},{6,2},{3,7},{7,3},{8,12},{12,8},{9,1... | collective-permute-start | bytes 1179656 | tf_op jit(solution)/shard_map/ppermute | solution.py:464
  45.8 8.2 %collective-permute-start.8 = (bf16[4,32,1536]{2,1,0:T(8,128)(2,1)S(1)}, bf16[4,32,1536]{2,1,0:T(8,128)(2,1)S(1)}, u32[]{:S(2)}, u32[]{:S(2)}) collective-permute-start(bf16[4,32,1536]{2,1,0:T(8,128)(2,1)S(1)} %get-tuple-element.287), channel_id=1, source_target_pairs={{0,1},{1,0},{2,3},{3,2},{4,5},{5,4},{6,7},{7,6},{8,9},{9,8},{10,11... | collective-permute-start | bytes 1179656 | tf_op jit(solution)/shard_map/ppermute | solution.py:464
  46.4 13.9 %collective-permute-start.9 = (bf16[2,64,2688]{2,1,0:T(8,128)(2,1)S(1)}, bf16[2,64,2688]{2,1,0:T(8,128)(2,1)S(1)}, u32[]{:S(2)}, u32[]{:S(2)}) collective-permute-start(bf16[2,64,2688]{2,1,0:T(8,128)(2,1)S(1)} %maximum_select_fusion.19), channel_id=1, source_target_pairs={{0,8},{8,0},{16,24},{24,16},{1,9},{9,1},{17,25},{25,17},{2,10},{10... | collective-permute-start | bytes 2064392 | tf_op jit(solution)/shard_map/ppermute | solution.py:464
  60.4 31.5 %collective-permute-start.10 = (bf16[4,2,32,1536]{3,2,0,1:T(8,128)(2,1)S(1)}, bf16[4,2,32,1536]{3,2,0,1:T(8,128)(2,1)S(1)}, u32[]{:S(2)}, u32[]{:S(2)}) collective-permute-start(bf16[4,2,32,1536]{3,2,0,1:T(8,128)(2,1)S(1)} %maximum_select_fusion.17), channel_id=1, source_target_pairs={{0,1},{1,0},{2,3},{3,2},{4,5},{5,4},{6,7},{7,6},{8,9},{9,8},{10,11... | collective-permute-start | bytes 2359304 | tf_op jit(solution)/shard_map/ppermute | solution.py:464
  62.0 30.0 %collective-permute-start.11 = (bf16[4,2,32,1536]{3,2,1,0:T(8,128)(2,1)S(1)}, bf16[4,2,32,1536]{3,2,1,0:T(8,128)(2,1)S(1)}, u32[]{:S(2)}, u32[]{:S(2)}) collective-permute-start(bf16[4,2,32,1536]{3,2,1,0:T(8,128)(2,1)S(1)} %maximum_select_fusion.18), channel_id=1, source_target_pairs={{0,4},{4,0},{1,5},{5,1},{2,6},{6,2},{3,7},{7,3},{8,12},{12,8},{9,1... | collective-permute-start | bytes 2359304 | tf_op jit(solution)/shard_map/ppermute | solution.py:464
  63.0 7.4 %collective-permute-start.12 = (bf16[64,2048]{1,0:T(8,128)(2,1)S(1)}, bf16[64,2048]{1,0:T(8,128)(2,1)S(1)}, u32[]{:S(2)}, u32[]{:S(2)}) collective-permute-start(bf16[64,2048]{1,0:T(8,128)(2,1)S(1)} %get-tuple-element.127), channel_id=1, source_target_pairs={{0,24},{24,0},{8,16},{16,8},{1,25},{25,1},{9,17},{17,9},{2,26},{26... | collective-permute-start | bytes 786440 | tf_op jit(solution)/shard_map/ppermute | solution.py:464
  66.5 25.4 %collective-permute-start.13 = (bf16[4,32,2688]{2,1,0:T(8,128)(2,1)S(1)}, bf16[4,32,2688]{2,1,0:T(8,128)(2,1)S(1)}, u32[]{:S(2)}, u32[]{:S(2)}) collective-permute-start(bf16[4,32,2688]{2,1,0:T(8,128)(2,1)S(1)} %get-tuple-element.278), channel_id=1, source_target_pairs={{0,4},{4,0},{1,5},{5,1},{2,6},{6,2},{3,7},{7,3},{8,12},{12,8},{9,1... | collective-permute-start | bytes 2064392 | tf_op jit(solution)/shard_map/ppermute | solution.py:464
  67.7 24.2 %collective-permute-start.14 = (bf16[4,32,2688]{2,1,0:T(8,128)(2,1)S(1)}, bf16[4,32,2688]{2,1,0:T(8,128)(2,1)S(1)}, u32[]{:S(2)}, u32[]{:S(2)}) collective-permute-start(bf16[4,32,2688]{2,1,0:T(8,128)(2,1)S(1)} %get-tuple-element.277), channel_id=1, source_target_pairs={{0,1},{1,0},{2,3},{3,2},{4,5},{5,4},{6,7},{7,6},{8,9},{9,8},{10,11... | collective-permute-start | bytes 2064392 | tf_op jit(solution)/shard_map/ppermute | solution.py:464
  92.2 39.4 %collective-permute-start.16 = (bf16[4,2,32,2688]{3,2,0,1:T(8,128)(2,1)S(1)}, bf16[4,2,32,2688]{3,2,0,1:T(8,128)(2,1)S(1)}, u32[]{:S(2)}, u32[]{:S(2)}) collective-permute-start(bf16[4,2,32,2688]{3,2,0,1:T(8,128)(2,1)S(1)} %maximum_select_fusion.9), channel_id=1, source_target_pairs={{0,1},{1,0},{2,3},{3,2},{4,5},{5,4},{6,7},{7,6},{8,9},{9,8},{10,11... | collective-permute-start | bytes 4128776 | tf_op jit(solution)/shard_map/ppermute | solution.py:464
  92.7 39.0 %collective-permute-start.17 = (bf16[4,2,32,2688]{3,2,0,1:T(8,128)(2,1)S(1)}, bf16[4,2,32,2688]{3,2,0,1:T(8,128)(2,1)S(1)}, u32[]{:S(2)}, u32[]{:S(2)}) collective-permute-start(bf16[4,2,32,2688]{3,2,0,1:T(8,128)(2,1)S(1)} %maximum_select_fusion.10), channel_id=1, source_target_pairs={{0,4},{4,0},{1,5},{5,1},{2,6},{6,2},{3,7},{7,3},{8,12},{12,8},{9,1... | collective-permute-start | bytes 4128776 | tf_op jit(solution)/shard_map/ppermute | solution.py:464
  93.1 11.3 %collective-permute-start.15 = (bf16[2,64,2048]{2,1,0:T(8,128)(2,1)S(1)}, bf16[2,64,2048]{2,1,0:T(8,128)(2,1)S(1)}, u32[]{:S(2)}, u32[]{:S(2)}) collective-permute-start(bf16[2,64,2048]{2,1,0:T(8,128)(2,1)S(1)} %maximum_select_fusion.20), channel_id=1, source_target_pairs={{0,8},{8,0},{16,24},{24,16},{1,9},{9,1},{17,25},{25,17},{2,10},{10... | collective-permute-start | bytes 1572872 | tf_op jit(solution)/shard_map/ppermute | solution.py:464
  105.8 25.8 %collective-permute-start.18 = (bf16[4,32,2048]{2,1,0:T(8,128)(2,1)S(1)}, bf16[4,32,2048]{2,1,0:T(8,128)(2,1)S(1)}, u32[]{:S(2)}, u32[]{:S(2)}) collective-permute-start(bf16[4,32,2048]{2,1,0:T(8,128)(2,1)S(1)} %get-tuple-element.282), channel_id=1, source_target_pairs={{0,4},{4,0},{1,5},{5,1},{2,6},{6,2},{3,7},{7,3},{8,12},{12,8},{9,1... | collective-permute-start | bytes 1572872 | tf_op jit(solution)/shard_map/ppermute | solution.py:464
  107.1 24.6 %collective-permute-start.19 = (bf16[4,32,2048]{2,1,0:T(8,128)(2,1)S(1)}, bf16[4,32,2048]{2,1,0:T(8,128)(2,1)S(1)}, u32[]{:S(2)}, u32[]{:S(2)}) collective-permute-start(bf16[4,32,2048]{2,1,0:T(8,128)(2,1)S(1)} %get-tuple-element.281), channel_id=1, source_target_pairs={{0,1},{1,0},{2,3},{3,2},{4,5},{5,4},{6,7},{7,6},{8,9},{9,8},{10,11... | collective-permute-start | bytes 1572872 | tf_op jit(solution)/shard_map/ppermute | solution.py:464
  138.9 8.5 %collective-permute-start.20 = (bf16[512,1024]{1,0:T(8,128)(2,1)}, bf16[512,1024]{1,0:T(8,128)(2,1)}, u32[]{:S(2)}, u32[]{:S(2)}) collective-permute-start(bf16[512,1024]{1,0:T(8,128)(2,1)} %convolution_convert_fusion.6), channel_id=1, source_target_pairs={{0,2},{2,0},{1,3},{3,1},{4,6},{6,4},{5,7},{7,5},{8,10},{10,8},{9,1... | collective-permute-start | bytes 3145736 | tf_op jit(solution)/shard_map/ppermute | solution.py:469
  153.5 24.4 %collective-permute-start.23 = (bf16[4,2,32,2048]{3,2,0,1:T(8,128)(2,1)S(1)}, bf16[4,2,32,2048]{3,2,0,1:T(8,128)(2,1)S(1)}, u32[]{:S(2)}, u32[]{:S(2)}) collective-permute-start(bf16[4,2,32,2048]{3,2,0,1:T(8,128)(2,1)S(1)} %maximum_select_fusion.13), channel_id=1, source_target_pairs={{0,1},{1,0},{2,3},{3,2},{4,5},{5,4},{6,7},{7,6},{8,9},{9,8},{10,11... | collective-permute-start | bytes 3145736 | tf_op jit(solution)/shard_map/ppermute | solution.py:464
  153.9 24.1 %collective-permute-start.24 = (bf16[4,2,32,2048]{3,2,1,0:T(8,128)(2,1)S(1)}, bf16[4,2,32,2048]{3,2,1,0:T(8,128)(2,1)S(1)}, u32[]{:S(2)}, u32[]{:S(2)}) collective-permute-start(bf16[4,2,32,2048]{3,2,1,0:T(8,128)(2,1)S(1)} %maximum_select_fusion.14), channel_id=1, source_target_pairs={{0,4},{4,0},{1,5},{5,1},{2,6},{6,2},{3,7},{7,3},{8,12},{12,8},{9,1... | collective-permute-start | bytes 3145736 | tf_op jit(solution)/shard_map/ppermute | solution.py:464
  183.4 20.6 %collective-permute-start.27 = (bf16[512,1024]{1,0:T(8,128)(2,1)}, bf16[512,1024]{1,0:T(8,128)(2,1)S(1)}, u32[]{:S(2)}, u32[]{:S(2)}) collective-permute-start(bf16[512,1024]{1,0:T(8,128)(2,1)} %param.29), channel_id=1, source_target_pairs={{0,0},{1,2},{2,1},{3,3},{4,4},{5,6},{6,5},{7,7},{8,8},{9,10},{10,9... | collective-permute-start | bytes 3145736 | tf_op jit(solution)/shard_map/ppermute | solution.py:1146
  194.9 20.5 %all-to-all-start = ((bf16[16,128,128]{2,1,0:T(8,128)(2,1)}), bf16[16,128,128]{2,1,0:T(8,128)(2,1)S(1)}, u32[]{:S(2)}, u32[]{:S(2)}) async-start(bf16[16,128,128]{2,1,0:T(8,128)(2,1)} %broadcast_in_dim.46), calls=%async_computation | async-start | bytes 1048576 | tf_op jit(solution)/shard_map/all_to_all | solution.py:1143
  223.8 12.1 %all-to-all-start.1 = ((f32[16,8,128]{2,1,0:T(8,128)}), f32[16,8,128]{2,1,0:T(8,128)S(1)}, u32[]{:S(2)}, u32[]{:S(2)}) async-start(f32[16,8,128]{2,1,0:T(8,128)} %broadcast_in_dim.47), calls=%async_computation.1 | async-start | bytes 131072 | tf_op jit(solution)/shard_map/all_to_all | solution.py:1164
  229.5 19.8 %collective-permute-start.28 = (bf16[512,1024]{1,0:T(8,128)(2,1)}, bf16[512,1024]{1,0:T(8,128)(2,1)}, u32[]{:S(2)}, u32[]{:S(2)}) collective-permute-start(bf16[512,1024]{1,0:T(8,128)(2,1)} %add_convert_fusion.3), channel_id=1, source_target_pairs={{0,0},{1,2},{2,1},{3,3},{4,4},{5,6},{6,5},{7,7},{8,8},{9,10},{10,9... | collective-permute-start | bytes 3145736 | tf_op jit(solution)/shard_map/ppermute | solution.py:1184
  249.3 21.8 %all-to-all-start.2 = ((bf16[16,128,128]{2,1,0:T(8,128)(2,1)}), bf16[16,128,128]{2,1,0:T(8,128)(2,1)S(1)}, u32[]{:S(2)}, u32[]{:S(2)}) async-start(bf16[16,128,128]{2,1,0:T(8,128)(2,1)} %bitcast.57), calls=%async_computation.2 | async-start | bytes 1048576 | tf_op jit(solution)/shard_map/all_to_all | solution.py:1186
  271.2 5.1 %collective-permute-start.29 = (f32[512,128]{1,0:T(8,128)S(1)}, f32[512,128]{1,0:T(8,128)S(1)}, u32[]{:S(2)}, u32[]{:S(2)}) collective-permute-start(f32[512,128]{1,0:T(8,128)S(1)} %constant_dynamic-slice_fusion.11), channel_id=1, source_target_pairs={{0,2},{2,0},{1,3},{3,1},{4,6},{6,4},{5,7},{7,5},{8,10},{10,8},{9,1... | collective-permute-start | bytes 786440 | tf_op jit(solution)/shard_map/ppermute | solution.py:469
  279.9 4.9 collective-permute-start.30
  291.8 24.7 %collective-permute-start.33 = (bf16[4,2,32,2048]{3,2,0,1:T(8,128)(2,1)S(1)}, bf16[4,2,32,2048]{3,2,0,1:T(8,128)(2,1)S(1)}, u32[]{:S(2)}, u32[]{:S(2)}) collective-permute-start(bf16[4,2,32,2048]{3,2,0,1:T(8,128)(2,1)S(1)} %bitcast.318), channel_id=1, source_target_pairs={{0,4},{4,0},{1,5},{5,1},{2,6},{6,2},{3,7},{7,3},{8,12},{12,8},{9,1... | collective-permute-start | bytes 3145736 | tf_op jit(solution)/shard_map/ppermute | solution.py:464
  293.1 24.4 %collective-permute-start.34 = (bf16[4,2,32,2048]{3,2,0,1:T(8,128)(2,1)S(1)}, bf16[4,2,32,2048]{3,2,0,1:T(8,128)(2,1)S(1)}, u32[]{:S(2)}, u32[]{:S(2)}) collective-permute-start(bf16[4,2,32,2048]{3,2,0,1:T(8,128)(2,1)S(1)} %bitcast.319), channel_id=1, source_target_pairs={{0,1},{1,0},{2,3},{3,2},{4,5},{5,4},{6,7},{7,6},{8,9},{9,8},{10,11... | collective-permute-start | bytes 3145736 | tf_op jit(solution)/shard_map/ppermute | solution.py:464
  307.3 26.5 %collective-permute-start.31 = (bf16[512,1024]{1,0:T(8,128)(2,1)S(1)}, bf16[512,1024]{1,0:T(8,128)(2,1)S(1)}, u32[]{:S(2)}, u32[]{:S(2)}) collective-permute-start(bf16[512,1024]{1,0:T(8,128)(2,1)S(1)} %fusion.14), channel_id=1, source_target_pairs={{0,2},{2,0},{1,3},{3,1},{4,6},{6,4},{5,7},{7,5},{8,10},{10,8},{9,1... | collective-permute-start | bytes 3145736 | tf_op jit(solution)/shard_map/ppermute | solution.py:469
  318.8 20.6 %collective-permute-start.35 = (bf16[4,32,2048]{2,1,0:T(8,128)(2,1)}, bf16[4,32,2048]{2,1,0:T(8,128)(2,1)}, u32[]{:S(2)}, u32[]{:S(2)}) collective-permute-start(bf16[4,32,2048]{2,1,0:T(8,128)(2,1)} %fusion.40), channel_id=1, source_target_pairs={{0,1},{1,0},{2,3},{3,2},{4,5},{5,4},{6,7},{7,6},{8,9},{9,8},{10,11... | collective-permute-start | bytes 1572872 | tf_op jit(solution)/shard_map/ppermute | solution.py:464
  321.0 18.4 %collective-permute-start.36 = (bf16[4,32,2048]{2,1,0:T(8,128)(2,1)}, bf16[4,32,2048]{2,1,0:T(8,128)(2,1)}, u32[]{:S(2)}, u32[]{:S(2)}) collective-permute-start(bf16[4,32,2048]{2,1,0:T(8,128)(2,1)} %fusion.41), channel_id=1, source_target_pairs={{0,4},{4,0},{1,5},{5,1},{2,6},{6,2},{3,7},{7,3},{8,12},{12,8},{9,1... | collective-permute-start | bytes 1572872 | tf_op jit(solution)/shard_map/ppermute | solution.py:464
  329.4 26.2 %collective-permute-start.37 = (bf16[4,2,32,2048]{3,2,0,1:T(8,128)(2,1)}, bf16[4,2,32,2048]{3,2,0,1:T(8,128)(2,1)}, u32[]{:S(2)}, u32[]{:S(2)}) collective-permute-start(bf16[4,2,32,2048]{3,2,0,1:T(8,128)(2,1)} %bitcast.273), channel_id=1, source_target_pairs={{0,4},{4,0},{1,5},{5,1},{2,6},{6,2},{3,7},{7,3},{8,12},{12,8},{9,1... | collective-permute-start | bytes 3145736 | tf_op jit(solution)/shard_map/ppermute | solution.py:464
  332.6 23.0 %collective-permute-start.38 = (bf16[4,2,32,2048]{3,2,0,1:T(8,128)(2,1)}, bf16[4,2,32,2048]{3,2,0,1:T(8,128)(2,1)}, u32[]{:S(2)}, u32[]{:S(2)}) collective-permute-start(bf16[4,2,32,2048]{3,2,0,1:T(8,128)(2,1)} %bitcast.272), channel_id=1, source_target_pairs={{0,1},{1,0},{2,3},{3,2},{4,5},{5,4},{6,7},{7,6},{8,9},{9,8},{10,11... | collective-permute-start | bytes 3145736 | tf_op jit(solution)/shard_map/ppermute | solution.py:464
  336.9 26.0 %collective-permute-start.32 = (bf16[512,1024]{1,0:T(8,128)(2,1)}, bf16[512,1024]{1,0:T(8,128)(2,1)}, u32[]{:S(2)}, u32[]{:S(2)}) collective-permute-start(bf16[512,1024]{1,0:T(8,128)(2,1)} %get-tuple-element.244), channel_id=1, source_target_pairs={{0,2},{2,0},{1,3},{3,1},{4,6},{6,4},{5,7},{7,5},{8,10},{10,8},{9,1... | collective-permute-start | bytes 3145736 | tf_op jit(solution)/shard_map/ppermute | solution.py:469
  370.6 18.5 %collective-permute-start.39 = (bf16[2,64,2048]{2,1,0:T(8,128)(2,1)S(1)}, bf16[2,64,2048]{2,1,0:T(8,128)(2,1)S(1)}, u32[]{:S(2)}, u32[]{:S(2)}) collective-permute-start(bf16[2,64,2048]{2,1,0:T(8,128)(2,1)S(1)} %select_convert_fusion.1), channel_id=1, source_target_pairs={{0,8},{8,0},{16,24},{24,16},{1,9},{9,1},{17,25},{25,17},{2,10},{10... | collective-permute-start | bytes 1572872 | tf_op jit(solution)/shard_map/ppermute | solution.py:464
  371.7 17.4 %collective-permute-start.40 = (bf16[4,32,2048]{2,1,0:T(8,128)(2,1)S(1)}, bf16[4,32,2048]{2,1,0:T(8,128)(2,1)S(1)}, u32[]{:S(2)}, u32[]{:S(2)}) collective-permute-start(bf16[4,32,2048]{2,1,0:T(8,128)(2,1)S(1)} %fusion.42), channel_id=1, source_target_pairs={{0,1},{1,0},{2,3},{3,2},{4,5},{5,4},{6,7},{7,6},{8,9},{9,8},{10,11... | collective-permute-start | bytes 1572872 | tf_op jit(solution)/shard_map/ppermute | solution.py:464
  373.1 16.1 %collective-permute-start.41 = (bf16[4,32,2048]{2,1,0:T(8,128)(2,1)S(1)}, bf16[4,32,2048]{2,1,0:T(8,128)(2,1)S(1)}, u32[]{:S(2)}, u32[]{:S(2)}) collective-permute-start(bf16[4,32,2048]{2,1,0:T(8,128)(2,1)S(1)} %fusion.43), channel_id=1, source_target_pairs={{0,4},{4,0},{1,5},{5,1},{2,6},{6,2},{3,7},{7,3},{8,12},{12,8},{9,1... | collective-permute-start | bytes 1572872 | tf_op jit(solution)/shard_map/ppermute | solution.py:464
  373.7 15.4 %collective-permute-start.42 = (bf16[4,2,32,512]{3,2,0,1:T(8,128)(2,1)S(1)}, bf16[4,2,32,512]{3,2,0,1:T(8,128)(2,1)S(1)}, u32[]{:S(2)}, u32[]{:S(2)}) collective-permute-start(bf16[4,2,32,512]{3,2,0,1:T(8,128)(2,1)S(1)} %dynamic-slice_bitcast_fusion.3), channel_id=1, source_target_pairs={{0,4},{4,0},{1,5},{5,1},{2,6},{6,2},{3,7},{7,3},{8,12},{12,8},{9,1... | collective-permute-start | bytes 786440 | tf_op jit(solution)/shard_map/ppermute | solution.py:464
  374.8 14.3 %collective-permute-start.43 = (bf16[4,2,32,512]{3,2,0,1:T(8,128)(2,1)S(1)}, bf16[4,2,32,512]{3,2,0,1:T(8,128)(2,1)S(1)}, u32[]{:S(2)}, u32[]{:S(2)}) collective-permute-start(bf16[4,2,32,512]{3,2,0,1:T(8,128)(2,1)S(1)} %dynamic-slice_bitcast_fusion.2), channel_id=1, source_target_pairs={{0,1},{1,0},{2,3},{3,2},{4,5},{5,4},{6,7},{7,6},{8,9},{9,8},{10,11... | collective-permute-start | bytes 786440 | tf_op jit(solution)/shard_map/ppermute | solution.py:464
  390.0 5.5 %collective-permute-start.44 = (f32[16,4]{1,0:T(8,128)S(1)}, f32[16,4]{1,0:T(8,128)S(1)}, u32[]{:S(2)}, u32[]{:S(2)}) collective-permute-start(f32[16,4]{1,0:T(8,128)S(1)} %reshape.820), channel_id=1, source_target_pairs={{0,2},{2,0},{1,3},{3,1},{4,6},{6,4},{5,7},{7,5},{8,10},{10,8},{9,1... | collective-permute-start | bytes 776 | tf_op jit(solution)/shard_map/ppermute | solution.py:469
  394.4 17.7 %collective-permute-start.46 = (bf16[64,2048]{1,0:T(8,128)(2,1)S(1)}, bf16[64,2048]{1,0:T(8,128)(2,1)S(1)}, u32[]{:S(2)}, u32[]{:S(2)}) collective-permute-start(bf16[64,2048]{1,0:T(8,128)(2,1)S(1)} %fusion.54), channel_id=1, source_target_pairs={{0,24},{24,0},{8,16},{16,8},{1,25},{25,1},{9,17},{17,9},{2,26},{26... | collective-permute-start | bytes 786440 | tf_op jit(solution)/shard_map/ppermute | solution.py:464
  394.9 18.9 %collective-permute-start.47 = (bf16[2,64,2048]{2,1,0:T(8,128)(2,1)S(1)}, bf16[2,64,2048]{2,1,0:T(8,128)(2,1)S(1)}, u32[]{:S(2)}, u32[]{:S(2)}) collective-permute-start(bf16[2,64,2048]{2,1,0:T(8,128)(2,1)S(1)} %select_convert_fusion), channel_id=1, source_target_pairs={{0,8},{8,0},{16,24},{24,16},{1,9},{9,1},{17,25},{25,17},{2,10},{10... | collective-permute-start | bytes 1572872 | tf_op jit(solution)/shard_map/ppermute | solution.py:464
  396.1 15.9 %collective-permute-start.48 = (bf16[4,32,512]{2,1,0:T(8,128)(2,1)S(1)}, bf16[4,32,512]{2,1,0:T(8,128)(2,1)S(1)}, u32[]{:S(2)}, u32[]{:S(2)}) collective-permute-start(bf16[4,32,512]{2,1,0:T(8,128)(2,1)S(1)} %fusion.62), channel_id=1, source_target_pairs={{0,1},{1,0},{2,3},{3,2},{4,5},{5,4},{6,7},{7,6},{8,9},{9,8},{10,11... | collective-permute-start | bytes 393224 | tf_op jit(solution)/shard_map/ppermute | solution.py:464
  396.5 15.6 %collective-permute-start.49 = (bf16[4,32,512]{2,1,0:T(8,128)(2,1)S(1)}, bf16[4,32,512]{2,1,0:T(8,128)(2,1)S(1)}, u32[]{:S(2)}, u32[]{:S(2)}) collective-permute-start(bf16[4,32,512]{2,1,0:T(8,128)(2,1)S(1)} %fusion.63), channel_id=1, source_target_pairs={{0,4},{4,0},{1,5},{5,1},{2,6},{6,2},{3,7},{7,3},{8,12},{12,8},{9,1... | collective-permute-start | bytes 393224 | tf_op jit(solution)/shard_map/ppermute | solution.py:464
  421.5 22.2 %collective-permute-start.50 = (bf16[4,2,32,1536]{3,2,0,1:T(8,128)(2,1)S(1)}, bf16[4,2,32,1536]{3,2,0,1:T(8,128)(2,1)S(1)}, u32[]{:S(2)}, u32[]{:S(2)}) collective-permute-start(bf16[4,2,32,1536]{3,2,0,1:T(8,128)(2,1)S(1)} %dynamic-slice_bitcast_fusion.1), channel_id=1, source_target_pairs={{0,4},{4,0},{1,5},{5,1},{2,6},{6,2},{3,7},{7,3},{8,12},{12,8},{9,1... | collective-permute-start | bytes 2359304 | tf_op jit(solution)/shard_map/ppermute | solution.py:464
  422.1 21.5 %collective-permute-start.51 = (bf16[4,2,32,1536]{3,2,0,1:T(8,128)(2,1)S(1)}, bf16[4,2,32,1536]{3,2,0,1:T(8,128)(2,1)S(1)}, u32[]{:S(2)}, u32[]{:S(2)}) collective-permute-start(bf16[4,2,32,1536]{3,2,0,1:T(8,128)(2,1)S(1)} %dynamic-slice_bitcast_fusion), channel_id=1, source_target_pairs={{0,1},{1,0},{2,3},{3,2},{4,5},{5,4},{6,7},{7,6},{8,9},{9,8},{10,11... | collective-permute-start | bytes 2359304 | tf_op jit(solution)/shard_map/ppermute | solution.py:464
  424.0 19.6 %collective-permute-start.52 = (bf16[64,2048]{1,0:T(8,128)(2,1)S(1)}, bf16[64,2048]{1,0:T(8,128)(2,1)S(1)}, u32[]{:S(2)}, u32[]{:S(2)}) collective-permute-start(bf16[64,2048]{1,0:T(8,128)(2,1)S(1)} %fusion.55), channel_id=1, source_target_pairs={{0,24},{24,0},{8,16},{16,8},{1,25},{25,1},{9,17},{17,9},{2,26},{26... | collective-permute-start | bytes 786440 | tf_op jit(solution)/shard_map/ppermute | solution.py:464
  425.9 11.0 %collective-permute-start.53 = (bf16[2,64,512]{2,1,0:T(8,128)(2,1)S(1)}, bf16[2,64,512]{2,1,0:T(8,128)(2,1)S(1)}, u32[]{:S(2)}, u32[]{:S(2)}) collective-permute-start(bf16[2,64,512]{2,1,0:T(8,128)(2,1)S(1)} %select_convert_fusion.6), channel_id=1, source_target_pairs={{0,8},{8,0},{16,24},{24,16},{1,9},{9,1},{17,25},{25,17},{2,10},{10... | collective-permute-start | bytes 393224 | tf_op jit(solution)/shard_map/ppermute | solution.py:464
  426.0 17.7 %collective-permute-start.54 = (bf16[584,128]{1,0:T(8,128)(2,1)S(1)}, bf16[584,128]{1,0:T(8,128)(2,1)S(1)}, u32[]{:S(2)}, u32[]{:S(2)}) collective-permute-start(bf16[584,128]{1,0:T(8,128)(2,1)S(1)} %convert_element_type.481), channel_id=1, source_target_pairs={{0,1},{1,0},{2,3},{3,2},{4,5},{5,4},{6,7},{7,6},{8,9},{9,8},{10,11... | collective-permute-start | bytes 448520 | tf_op jit(solution)/shard_map/ppermute | solution.py:464
  436.9 12.9 %collective-permute-start.61 = (bf16[512,1024]{1,0:T(8,128)(2,1)S(1)}, bf16[512,1024]{1,0:T(8,128)(2,1)S(1)}, u32[]{:S(2)}, u32[]{:S(2)}) collective-permute-start(bf16[512,1024]{1,0:T(8,128)(2,1)S(1)} %add_convert_fusion.2), channel_id=1, source_target_pairs={{0,2},{2,0},{1,3},{3,1},{4,6},{6,4},{5,7},{7,5},{8,10},{10,8},{9,1... | collective-permute-start | bytes 3145736 | tf_op jit(solution)/shard_map/ppermute | solution.py:469
  444.0 14.0 %collective-permute-start.55 = (bf16[4,32,1536]{2,1,0:T(8,128)(2,1)S(1)}, bf16[4,32,1536]{2,1,0:T(8,128)(2,1)S(1)}, u32[]{:S(2)}, u32[]{:S(2)}) collective-permute-start(bf16[4,32,1536]{2,1,0:T(8,128)(2,1)S(1)} %fusion.49), channel_id=1, source_target_pairs={{0,1},{1,0},{2,3},{3,2},{4,5},{5,4},{6,7},{7,6},{8,9},{9,8},{10,11... | collective-permute-start | bytes 1179656 | tf_op jit(solution)/shard_map/ppermute | solution.py:464
  446.1 11.9 %collective-permute-start.56 = (bf16[4,32,1536]{2,1,0:T(8,128)(2,1)S(1)}, bf16[4,32,1536]{2,1,0:T(8,128)(2,1)S(1)}, u32[]{:S(2)}, u32[]{:S(2)}) collective-permute-start(bf16[4,32,1536]{2,1,0:T(8,128)(2,1)S(1)} %fusion.50), channel_id=1, source_target_pairs={{0,4},{4,0},{1,5},{5,1},{2,6},{6,2},{3,7},{7,3},{8,12},{12,8},{9,1... | collective-permute-start | bytes 1179656 | tf_op jit(solution)/shard_map/ppermute | solution.py:464
  446.4 9.4 %collective-permute-start.57 = (bf16[64,512]{1,0:T(8,128)(2,1)S(1)}, bf16[64,512]{1,0:T(8,128)(2,1)S(1)}, u32[]{:S(2)}, u32[]{:S(2)}) collective-permute-start(bf16[64,512]{1,0:T(8,128)(2,1)S(1)} %fusion.68), channel_id=1, source_target_pairs={{0,24},{24,0},{8,16},{16,8},{1,25},{25,1},{9,17},{17,9},{2,26},{26... | collective-permute-start | bytes 196616 | tf_op jit(solution)/shard_map/ppermute | solution.py:464
  448.8 9.2 %collective-permute-start.58 = (bf16[584,128]{1,0:T(8,128)(2,1)S(1)}, bf16[584,128]{1,0:T(8,128)(2,1)S(1)}, u32[]{:S(2)}, u32[]{:S(2)}) collective-permute-start(bf16[584,128]{1,0:T(8,128)(2,1)S(1)} %fusion.56), channel_id=1, source_target_pairs={{0,4},{4,0},{1,5},{5,1},{2,6},{6,2},{3,7},{7,3},{8,12},{12,8},{9,1... | collective-permute-start | bytes 448520 | tf_op jit(solution)/shard_map/ppermute | solution.py:464
  451.0 18.8 %collective-permute-start.62 = (bf16[512,1024]{1,0:T(8,128)(2,1)S(1)}, bf16[512,1024]{1,0:T(8,128)(2,1)S(1)}, u32[]{:S(2)}, u32[]{:S(2)}) collective-permute-start(bf16[512,1024]{1,0:T(8,128)(2,1)S(1)} %add_convert_fusion.1), channel_id=1, source_target_pairs={{0,0},{1,2},{2,1},{3,3},{4,4},{5,6},{6,5},{7,7},{8,8},{9,10},{10,9... | collective-permute-start | bytes 3145736 | tf_op jit(solution)/shard_map/ppermute | solution.py:464
  458.3 11.5 %collective-permute-start.59 = (bf16[2,64,1536]{2,1,0:T(8,128)(2,1)S(1)}, bf16[2,64,1536]{2,1,0:T(8,128)(2,1)S(1)}, u32[]{:S(2)}, u32[]{:S(2)}) collective-permute-start(bf16[2,64,1536]{2,1,0:T(8,128)(2,1)S(1)} %select_convert_fusion.2), channel_id=1, source_target_pairs={{0,8},{8,0},{16,24},{24,16},{1,9},{9,1},{17,25},{25,17},{2,10},{10... | collective-permute-start | bytes 1179656 | tf_op jit(solution)/shard_map/ppermute | solution.py:464
  458.5 11.3 %collective-permute-start.60 = (bf16[584,128]{1,0:T(8,128)(2,1)S(1)}, bf16[584,128]{1,0:T(8,128)(2,1)S(1)}, u32[]{:S(2)}, u32[]{:S(2)}) collective-permute-start(bf16[584,128]{1,0:T(8,128)(2,1)S(1)} %fusion.97), channel_id=1, source_target_pairs={{0,24},{24,0},{8,16},{16,8},{1,25},{25,1},{9,17},{17,9},{2,26},{26... | collective-permute-start | bytes 448520 | tf_op jit(solution)/shard_map/ppermute | solution.py:464
  469.9 16.9 %collective-permute-start.65 = (bf16[64,4096]{1,0:T(8,128)(2,1)S(1)}, bf16[64,4096]{1,0:T(8,128)(2,1)S(1)}, u32[]{:S(2)}, u32[]{:S(2)}) collective-permute-start(bf16[64,4096]{1,0:T(8,128)(2,1)S(1)} %pad_maximum_fusion.17), channel_id=1, source_target_pairs={{0,0},{1,2},{2,1},{3,3},{4,4},{5,6},{6,5},{7,7},{8,8},{9,10},{10,9... | collective-permute-start | bytes 1572872 | tf_op jit(solution)/shard_map/ppermute | solution.py:464
  475.9 11.0 %collective-permute-start.63 = (bf16[64,1536]{1,0:T(8,128)(2,1)S(1)}, bf16[64,1536]{1,0:T(8,128)(2,1)S(1)}, u32[]{:S(2)}, u32[]{:S(2)}) collective-permute-start(bf16[64,1536]{1,0:T(8,128)(2,1)S(1)} %fusion.58), channel_id=1, source_target_pairs={{0,24},{24,0},{8,16},{16,8},{1,25},{25,1},{9,17},{17,9},{2,26},{26... | collective-permute-start | bytes 589832 | tf_op jit(solution)/shard_map/ppermute | solution.py:464
  477.4 9.5 %collective-permute-start.64 = (bf16[584,128]{1,0:T(8,128)(2,1)S(1)}, bf16[584,128]{1,0:T(8,128)(2,1)S(1)}, u32[]{:S(2)}, u32[]{:S(2)}) collective-permute-start(bf16[584,128]{1,0:T(8,128)(2,1)S(1)} %fusion.57), channel_id=1, source_target_pairs={{0,8},{8,0},{16,24},{24,16},{1,9},{9,1},{17,25},{25,17},{2,10},{10... | collective-permute-start | bytes 448520 | tf_op jit(solution)/shard_map/ppermute | solution.py:464
  487.0 7.7 %collective-permute-start.66 = (bf16[64,2048]{1,0:T(8,128)(2,1)S(1)}, bf16[64,2048]{1,0:T(8,128)(2,1)S(1)}, u32[]{:S(2)}, u32[]{:S(2)}) collective-permute-start(bf16[64,2048]{1,0:T(8,128)(2,1)S(1)} %pad_maximum_fusion.20), channel_id=1, source_target_pairs={{0,0},{1,2},{2,1},{3,3},{4,4},{5,6},{6,5},{7,7},{8,8},{9,10},{10,9... | collective-permute-start | bytes 786440 | tf_op jit(solution)/shard_map/ppermute | solution.py:464
  (61 other events, 604.1 us)

commit v4 on v3

--- a/solution.py
+++ b/solution.py
@@ -1292,7 +1292,7 @@
         *sum_moves(qkv_blocks, x, y),
         far_move(up_pair, z),
         near_move(out_line, z),
-        (small.astype(BF), "y", SWAP),
+        (small.astype(BF), "z", NEAR),
     )
     qkv_parts = sum_parts(qkv_blocks, moved, x, y)
     up_part = far_sum(up_pair, moved[2], z)
@@ -1306,13 +1306,13 @@
 
     other_terms = swap(input_terms(other_start).astype(BF), "c")
     grad_input = (input_terms(own_start) + other_terms.astype(F32) + grad_first).astype(BF)
-    moved = exchange(*line_moves(qkv_parts, x, y), far_move(out_pair, z), (small.astype(BF), "x", SWAP))
+    moved = exchange(*line_moves(qkv_parts, x, y), far_move(out_pair, z), (small.astype(BF), "z", FAR))
     qkv_line = line_of(qkv_parts, moved, x, y)
     out_part = far_sum(out_pair, moved[2], z)
     small = small + moved[3].astype(F32)
     moved = exchange(
         near_move(qkv_line, z),
-        (small.astype(BF), "z", FAR),
+        (small.astype(BF), "x", SWAP),
         (tie(grad_input, qkv_line), CORES, TURN),
     )
     qkv_pair = near_sum(qkv_line, moved[0], z)
@@ -1320,7 +1320,7 @@
     grad_input = moved[2]
     ffn_part = jnp.concatenate([down_part, up_part], axis=1).astype(BF)
     moved = exchange(
-        far_move(qkv_pair, z), (small.astype(BF), "z", NEAR), (tie(ffn_part, qkv_pair), CORES, TURN)
+        far_move(qkv_pair, z), (small.astype(BF), "y", SWAP), (tie(ffn_part, qkv_pair), CORES, TURN)
     )
     attn_part = jnp.concatenate([far_sum(qkv_pair, moved[0], z), out_part], axis=1).astype(BF)
     small = small + moved[1].astype(F32)

time: 510 us -> 502 us (0.984)
  Pallas kernels: 76.2 us -> 69.7 us
  transfers between devices with their start and end apart: 71 -> 71, of which waited for: 29 -> 32; matrix products, arithmetic and copies ran while one was open for 15% -> 16% of each run, Pallas kernels for 14% -> 13%
where the time goes in v4:
time: 502 us; the launch traced here: 497 us
  waiting for transfers between devices  165 us (33%)
  starting transfers between devices  119 us (24%)
  Pallas kernels  69.7 us (14%)
  matrix products  62.2 us (12%)
  local copies, waits for them, and re-layouts  43.2 us (9%)
  other arithmetic  34.7 us (7%)
    ppermute x54, waiting for transfers between devices, exchange(): lax.ppermute(value, axis, steps)  137 us
    ppermute x54, starting transfers between devices, exchange(): lax.ppermute(value, axis, steps)  67.4 us
    pallas_call x2, Pallas kernels, attend_back(): pl.pallas_call(partial(attend_back_kernel, group * heads), grid=(count //...  23.6 us
    dot_general x7, matrix products, contract_rows(): lax.dot_general(left, right, (((0,), (0,)), ((), ())), precision=precisio...  22.5 us
    dot_general x12, matrix products, contract_cols(): lax.dot_general(left, right, (((1,), (1,)), ((), ())), precision=precisio...  21.3 us
    unnamed x129, local copies, waits for them, and re-layouts  20.8 us
    ppermute x12, starting transfers between devices, swap(): return lax.ppermute(value, axis, SWAP)  20.7 us
    dot_general x4, matrix products, dot(): return jnp.dot(left, right, preferred_element_type=F32)  17.1 us
  transfers between devices with their start and end apart: 71, of which 32 were waited for; matrix products, arithmetic and copies ran while one was open for 16% of the time, Pallas kernels for 13%

profile of v4, /device:TPU:1, one launch (start us, length us, event | category | flops | bytes accessed | tf_op | source)
XLA Modules:
  0.0 497.1 jit_solution(13652951864802936783)
XLA Ops:
  1.7 4.5 collective-permute-start
  10.0 1.9 fusion.39
  13.3 3.3 collective-permute-start.3
  18.5 4.2 collective-permute-start.5
  24.1 2.5 collective-permute-start.4
  26.6 4.3 collective-permute-done.5
  31.1 3.7 collective-permute-done.4
  34.8 9.2 %collective-permute-done.6 = bf16[64,2688]{1,0:T(8,128)(2,1)S(1)} collective-permute-done((bf16[64,2688]{1,0:T(8,128)(2,1)S(1)}, bf16[64,2688]{1,0:T(8,128)(2,1)S(1)}, u32[]{:S(2)}, u32[]{:S(2)}) %collective-permute-start.6) | collective-permute-done | bytes 344096 | tf_op jit(solution)/shard_map/ppermute | solution.py:464
  47.0 6.0 %collective-permute-done.7 = bf16[4,32,1536]{2,1,0:T(8,128)(2,1)S(1)} collective-permute-done((bf16[4,32,1536]{2,1,0:T(8,128)(2,1)S(1)}, bf16[4,32,1536]{2,1,0:T(8,128)(2,1)S(1)}, u32[]{:S(2)}, u32[]{:S(2)}) %collective-permute-start.7) | collective-permute-done | bytes 393248 | tf_op jit(solution)/shard_map/ppermute | solution.py:464
  53.9 6.4 %collective-permute-done.9 = bf16[2,64,2688]{2,1,0:T(8,128)(2,1)S(1)} collective-permute-done((bf16[2,64,2688]{2,1,0:T(8,128)(2,1)S(1)}, bf16[2,64,2688]{2,1,0:T(8,128)(2,1)S(1)}, u32[]{:S(2)}, u32[]{:S(2)}) %collective-permute-start.9) | collective-permute-done | bytes 688160 | tf_op jit(solution)/shard_map/ppermute | solution.py:464
  63.0 3.5 collective-permute-start.12
  68.1 2.3 collective-permute-done.12
  70.4 21.5 %collective-permute-done.13 = bf16[4,32,2688]{2,1,0:T(8,128)(2,1)S(1)} collective-permute-done((bf16[4,32,2688]{2,1,0:T(8,128)(2,1)S(1)}, bf16[4,32,2688]{2,1,0:T(8,128)(2,1)S(1)}, u32[]{:S(2)}, u32[]{:S(2)}) %collective-permute-start.13) | collective-permute-done | bytes 688160 | tf_op jit(solution)/shard_map/ppermute | solution.py:464
  93.1 3.5 collective-permute-start.15
  97.4 3.6 add_convert_fusion.own_ref.qkv_ref
  101.3 3.0 collective-permute-done.15
  108.5 10.4 %shard_map.254 = (bf16[1024,512]{1,0:T(8,128)(2,1)S(1)}, f32[8,1024]{1,0:T(8,128)S(1)}) custom-call(s32[2,4]{1,0:T(2,128)S(1)} %pad_add_fusion.1.bounds, bf16[1024,1536]{1,0:T(8,128)(2,1)S(1)} %add_convert_fusion.own_ref.qkv_ref, bf16[1024,1536]{1,0:T(8,128)(2,1)S(1)} %add_convert_fusion.own_ref.qkv_ref, s32[2,1024]{1,0:T(2,128)S(1)} %pad_add_fusion.spans), custom_call_target="tpu_custom_call" | custom-call | flops 2147483648 | bytes 12582912 | tf_op jit(solution)/shard_map/pallas_call | solution.py:679
  118.9 12.7 %collective-permute-done.18 = bf16[4,32,2048]{2,1,0:T(8,128)(2,1)S(1)} collective-permute-done((bf16[4,32,2048]{2,1,0:T(8,128)(2,1)S(1)}, bf16[4,32,2048]{2,1,0:T(8,128)(2,1)S(1)}, u32[]{:S(2)}, u32[]{:S(2)}) %collective-permute-start.18) | collective-permute-done | bytes 524320 | tf_op jit(solution)/shard_map/ppermute | solution.py:464
  134.8 2.4 copy-done.2
  138.9 5.8 %collective-permute-start.20 = (bf16[512,1024]{1,0:T(8,128)(2,1)}, bf16[512,1024]{1,0:T(8,128)(2,1)}, u32[]{:S(2)}, u32[]{:S(2)}) collective-permute-start(bf16[512,1024]{1,0:T(8,128)(2,1)} %convolution_convert_fusion.6), channel_id=1, source_target_pairs={{0,2},{2,0},{1,3},{3,1},{4,6},{6,4},{5,7},{7,5},{8,10},{10,8},{9,1... | collective-permute-start | bytes 3145736 | tf_op jit(solution)/shard_map/ppermute | solution.py:469
  144.8 2.0 fusion.31
  155.4 16.2 %shard_map.255 = (bf16[1024,2048]{1,0:T(8,128)(2,1)S(1)}, bf16[1024,2048]{1,0:T(8,128)(2,1)S(1)}) custom-call(bf16[1024,1024]{1,0:T(8,128)(2,1)S(1)} %pad_maximum_fusion.5.x_ref, bf16[1024,2688]{1,0:T(8,128)(2,1)S(1)} %bitcast.282, f32[1,2048]{1,0:T(1,128)S(1)} %slice.503.b_ref), custom_call_target="tpu_custom_call" | custom-call | flops 4294967296 | bytes 14680064 | tf_op jit(solution)/shard_map/pallas_call | solution.py:849
  171.6 2.1 copy-done.7
  173.7 4.2 collective-permute-done.23
  179.4 2.4 fusion.11
  183.4 2.8 collective-permute-start.27
  186.3 2.8 fusion.119
  194.9 7.8 %all-to-all-start = ((bf16[16,128,128]{2,1,0:T(8,128)(2,1)}), bf16[16,128,128]{2,1,0:T(8,128)(2,1)S(1)}, u32[]{:S(2)}, u32[]{:S(2)}) async-start(bf16[16,128,128]{2,1,0:T(8,128)(2,1)} %broadcast_in_dim.46), calls=%async_computation | async-start | bytes 1048576 | tf_op jit(solution)/shard_map/all_to_all | solution.py:1143
  204.0 11.4 %all-to-all-done = bf16[16,128,128]{2,1,0:T(8,128)(2,1)S(1)} async-done(((bf16[16,128,128]{2,1,0:T(8,128)(2,1)}), bf16[16,128,128]{2,1,0:T(8,128)(2,1)S(1)}, u32[]{:S(2)}, u32[]{:S(2)}) %all-to-all-start) | async-done | bytes 524320 | tf_op jit(solution)/shard_map/all_to_all | solution.py:1143
  215.4 7.0 %shard_map.256 = f32[24,2048]{1,0:T(8,128)S(1)} custom-call(bf16[2048,128]{1,0:T(8,128)(2,1)S(1)} %bitcast.287, bf16[1024,128]{1,0:T(8,128)(2,1)S(1)} %maximum_select_fusion.25.d_ref, s32[1,1024]{1,0:T(1,128)S(1)} %compare_select_fusion.seg_ref), custom_call_target="tpu_custom_call" | custom-call | flops 3221225472 | bytes 786432 | tf_op jit(solution)/shard_map/pallas_call | solution.py:904
  223.8 5.7 %all-to-all-start.1 = ((f32[16,8,128]{2,1,0:T(8,128)}), f32[16,8,128]{2,1,0:T(8,128)S(1)}, u32[]{:S(2)}, u32[]{:S(2)}) async-start(f32[16,8,128]{2,1,0:T(8,128)} %broadcast_in_dim.47), calls=%async_computation.1 | async-start | bytes 131072 | tf_op jit(solution)/shard_map/all_to_all | solution.py:1164
  229.5 5.1 %collective-permute-start.28 = (bf16[512,1024]{1,0:T(8,128)(2,1)}, bf16[512,1024]{1,0:T(8,128)(2,1)}, u32[]{:S(2)}, u32[]{:S(2)}) collective-permute-start(bf16[512,1024]{1,0:T(8,128)(2,1)} %add_convert_fusion.3), channel_id=1, source_target_pairs={{0,0},{1,2},{2,1},{3,3},{4,4},{5,6},{6,5},{7,7},{8,8},{9,10},{10,9... | collective-permute-start | bytes 3145736 | tf_op jit(solution)/shard_map/ppermute | solution.py:1184
  236.7 12.5 %shard_map.257 = (bf16[2048,128]{1,0:T(8,128)(2,1)}, f32[768,128]{1,0:T(8,128)S(1)}) custom-call(bf16[2048,128]{1,0:T(8,128)(2,1)S(1)} %bitcast.288, bf16[1024,128]{1,0:T(8,128)(2,1)S(1)} %maximum_select_fusion.25.d_ref, s32[1,1024]{1,0:T(1,128)S(1)} %compare_select_fusion.seg_ref, f32[24,2048]{1,0:T(8,128)S(1)} %convolution_divide_fusion.coef_ref), custom_call_target="tpu_custom_call" | custom-call | flops 4831838208 | bytes 1572864 | tf_op jit(solution)/shard_map/pallas_call | solution.py:980
  249.3 9.6 %all-to-all-start.2 = ((bf16[16,128,128]{2,1,0:T(8,128)(2,1)}), bf16[16,128,128]{2,1,0:T(8,128)(2,1)S(1)}, u32[]{:S(2)}, u32[]{:S(2)}) async-start(bf16[16,128,128]{2,1,0:T(8,128)(2,1)} %bitcast.57), calls=%async_computation.2 | async-start | bytes 1048576 | tf_op jit(solution)/shard_map/all_to_all | solution.py:1186
  258.9 12.1 %all-to-all-done.2 = bf16[16,128,128]{2,1,0:T(8,128)(2,1)S(1)} async-done(((bf16[16,128,128]{2,1,0:T(8,128)(2,1)}), bf16[16,128,128]{2,1,0:T(8,128)(2,1)S(1)}, u32[]{:S(2)}, u32[]{:S(2)}) %all-to-all-start.2) | async-done | bytes 524320 | tf_op jit(solution)/shard_map/all_to_all | solution.py:1186
  271.2 4.0 collective-permute-start.29
  284.8 6.4 %convolution_convert_fusion.1 = bf16[1024,2048]{1,0:T(8,128)(2,1)S(1)} fusion(bf16[1024,2048]{1,0:T(8,128)(2,1)S(1)} %copy-done.6, bf16[512,1024]{1,0:T(8,128)(2,1)} %collective-permute-done.30, bf16[512,1024]{1,0:T(8,128)(2,1)} %get-tuple-element.241), kind=kOutput, calls=%fused_computation.6 | convolution fusion | flops 4301258752 | bytes 10485760 | tf_op jit(solution)/shard_map/dot_general | solution.py:33
  295.2 8.0 %convert_reduce_fusion = (f32[2048]{0:T(1024)S(1)}, bf16[1024,2048]{1,0:T(8,128)(2,1)}) fusion(bf16[1024,2048]{1,0:T(8,128)(2,1)S(1)} %copy-done.8, bf16[1024,2048]{1,0:T(8,128)(2,1)S(1)} %bitcast.298, bf16[512,1024]{1,0:T(8,128)(2,1)} %collective-permute-done.30, bf16[512,1024]{1,0:T(8,128)(2,1)} %get-tuple-element.241), kind=kOutput, calls=%fused_computation | convolution fusion | flops 4309645312 | bytes 14688256 | tf_op jit(solution)/shard_map/dot_general | solution.py:448
  303.2 4.1 fusion.14
  307.5 2.4 fusion.2
  309.9 6.6 %collective-permute-done.33 = bf16[4,2,32,2048]{3,2,0,1:T(8,128)(2,1)S(1)} collective-permute-done((bf16[4,2,32,2048]{3,2,0,1:T(8,128)(2,1)S(1)}, bf16[4,2,32,2048]{3,2,0,1:T(8,128)(2,1)S(1)}, u32[]{:S(2)}, u32[]{:S(2)}) %collective-permute-start.33) | collective-permute-done | bytes 1048608 | tf_op jit(solution)/shard_map/ppermute | solution.py:464
  321.5 5.3 %convolution_convert_fusion = bf16[1024,2048]{1,0:T(8,128)(2,1)S(1)} fusion(bf16[1024,2048]{1,0:T(8,128)(2,1)S(1)} %copy-done.49, bf16[512,1024]{1,0:T(8,128)(2,1)S(1)} %copy-done.38, bf16[512,1024]{1,0:T(8,128)(2,1)S(1)} %copy-done.25), kind=kOutput, calls=%fused_computation.5 | convolution fusion | flops 4301258752 | bytes 10485760 | tf_op jit(solution)/shard_map/dot_general | solution.py:33
  336.9 2.4 collective-permute-start.32
  339.4 16.2 %collective-permute-done.37 = bf16[4,2,32,2048]{3,2,0,1:T(8,128)(2,1)} collective-permute-done((bf16[4,2,32,2048]{3,2,0,1:T(8,128)(2,1)}, bf16[4,2,32,2048]{3,2,0,1:T(8,128)(2,1)}, u32[]{:S(2)}, u32[]{:S(2)}) %collective-permute-start.37) | collective-permute-done | bytes 1048608 | tf_op jit(solution)/shard_map/ppermute | solution.py:464
  362.9 3.8 convolution_convert_fusion.5.grad_ref
  366.7 3.5 convolution_convert_fusion.4
  375.2 11.7 %shard_map.258 = (bf16[1024,768]{1,0:T(8,128)(2,1)S(1)}, f32[8,256]{1,0:T(8,128)S(1)}) custom-call(s32[2,4]{1,0:T(2,128)S(1)} %pad_add_fusion.1.bounds, bf16[1024,1536]{1,0:T(8,128)(2,1)S(1)} %copy-done.4, bf16[1024,1536]{1,0:T(8,128)(2,1)S(1)} %copy-done.4, bf16[1024,512]{1,0:T(8,128)(2,1)S(1)} %get-tuple-element.133.out_ref, ...), custom_call_target="tpu_custom_call" | custom-call | flops 2684354560 | bytes 12582912 | tf_op jit(solution)/shard_map/pallas_call | solution.py:782
  389.6 4.4 collective-permute-start.44
  398.6 11.9 %shard_map.259 = (bf16[1024,768]{1,0:T(8,128)(2,1)S(1)}, f32[8,256]{1,0:T(8,128)S(1)}) custom-call(s32[2,4]{1,0:T(2,128)S(1)} %pad_add_fusion.1.bounds, bf16[1024,1536]{1,0:T(8,128)(2,1)S(1)} %copy-done.4, bf16[1024,1536]{1,0:T(8,128)(2,1)S(1)} %copy-done.4, bf16[1024,512]{1,0:T(8,128)(2,1)S(1)} %get-tuple-element.133.out_ref, ...), custom_call_target="tpu_custom_call" | custom-call | flops 2684354560 | bytes 12582912 | tf_op jit(solution)/shard_map/pallas_call | solution.py:782
  410.6 4.1 collective-permute-done.47
  423.5 2.4 collective-permute-start.52
  429.5 6.9 %collective-permute-done.53 = bf16[2,64,512]{2,1,0:T(8,128)(2,1)S(1)} collective-permute-done((bf16[2,64,512]{2,1,0:T(8,128)(2,1)S(1)}, bf16[2,64,512]{2,1,0:T(8,128)(2,1)S(1)}, u32[]{:S(2)}, u32[]{:S(2)}) %collective-permute-start.53) | collective-permute-done | bytes 131104 | tf_op jit(solution)/shard_map/ppermute | solution.py:464
  437.0 2.6 collective-permute-done.54
  442.9 2.7 collective-permute-start.57
  447.6 6.4 %collective-permute-start.62 = (bf16[512,1024]{1,0:T(8,128)(2,1)S(1)}, bf16[512,1024]{1,0:T(8,128)(2,1)S(1)}, u32[]{:S(2)}, u32[]{:S(2)}) collective-permute-start(bf16[512,1024]{1,0:T(8,128)(2,1)S(1)} %add_convert_fusion.1), channel_id=1, source_target_pairs={{0,0},{1,2},{2,1},{3,3},{4,4},{5,6},{6,5},{7,7},{8,8},{9,10},{10,9... | collective-permute-start | bytes 3145736 | tf_op jit(solution)/shard_map/ppermute | solution.py:464
  454.7 4.3 collective-permute-done.60
  458.9 5.0 %collective-permute-done.59 = bf16[2,64,1536]{2,1,0:T(8,128)(2,1)S(1)} collective-permute-done((bf16[2,64,1536]{2,1,0:T(8,128)(2,1)S(1)}, bf16[2,64,1536]{2,1,0:T(8,128)(2,1)S(1)}, u32[]{:S(2)}, u32[]{:S(2)}) %collective-permute-start.59) | collective-permute-done | bytes 393248 | tf_op jit(solution)/shard_map/ppermute | solution.py:464
  463.9 2.6 collective-permute-done.62
  466.6 3.6 collective-permute-start.65
  470.3 2.0 collective-permute-start.63
  472.5 7.0 %collective-permute-done.64 = bf16[584,128]{1,0:T(8,128)(2,1)S(1)} collective-permute-done((bf16[584,128]{1,0:T(8,128)(2,1)S(1)}, bf16[584,128]{1,0:T(8,128)(2,1)S(1)}, u32[]{:S(2)}, u32[]{:S(2)}) %collective-permute-start.64) | collective-permute-done | bytes 149536 | tf_op jit(solution)/shard_map/ppermute | solution.py:464
  479.7 2.8 collective-permute-start.66
  484.4 2.9 collective-permute-done.66
  493.6 2.3 copy.165
  (454 shorter events, 127.2 us)
Async XLA Ops:
  1.7 10.3 %collective-permute-start = (bf16[64,1536]{1,0:T(8,128)(2,1)S(1)}, bf16[64,1536]{1,0:T(8,128)(2,1)}, u32[]{:S(2)}, u32[]{:S(2)}) collective-permute-start(bf16[64,1536]{1,0:T(8,128)(2,1)S(1)} %slice_dynamic-update-slice_fusion), channel_id=1, source_target_pairs={{0,0},{1,2},{2,1},{3,3},{4,4},{5,6},{6,5},{7,7},{8,8},{9,10},{10,9... | collective-permute-start | bytes 589832 | tf_op jit(solution)/shard_map/ppermute | solution.py:464
  6.2 5.8 %collective-permute-start.1 = (bf16[1024,1024]{1,0:T(8,128)(2,1)}, bf16[1024,1024]{1,0:T(8,128)(2,1)S(1)}, u32[]{:S(2)}, u32[]{:S(2)}) collective-permute-start(bf16[1024,1024]{1,0:T(8,128)(2,1)} %param.15), channel_id=1, source_target_pairs={{0,2},{2,0},{1,3},{3,1},{4,6},{6,4},{5,7},{7,5},{8,10},{10,8},{9,1... | collective-permute-start | bytes 6291464 | tf_op jit(solution)/shard_map/ppermute | solution.py:464
  13.3 9.5 %collective-permute-start.3 = (bf16[64,1536]{1,0:T(8,128)(2,1)}, bf16[64,1536]{1,0:T(8,128)(2,1)}, u32[]{:S(2)}, u32[]{:S(2)}) collective-permute-start(bf16[64,1536]{1,0:T(8,128)(2,1)} %collective-permute-done), channel_id=1, source_target_pairs={{0,24},{24,0},{8,16},{16,8},{1,25},{25,1},{9,17},{17,9},{2,26},{26... | collective-permute-start | bytes 589832 | tf_op jit(solution)/shard_map/ppermute | solution.py:464
  18.5 12.4 %collective-permute-start.5 = (bf16[64,4736]{1,0:T(8,128)(2,1)}, bf16[64,4736]{1,0:T(8,128)(2,1)S(1)}, u32[]{:S(2)}, u32[]{:S(2)}) collective-permute-start(bf16[64,4736]{1,0:T(8,128)(2,1)} %fusion.39), channel_id=1, source_target_pairs={{0,0},{1,2},{2,1},{3,3},{4,4},{5,6},{6,5},{7,7},{8,8},{9,10},{10,9... | collective-permute-start | bytes 1818632 | tf_op jit(solution)/shard_map/ppermute | solution.py:464
  24.1 10.7 %collective-permute-start.4 = (bf16[2,64,1536]{2,1,0:T(8,128)(2,1)S(1)}, bf16[2,64,1536]{2,1,0:T(8,128)(2,1)S(1)}, u32[]{:S(2)}, u32[]{:S(2)}) collective-permute-start(bf16[2,64,1536]{2,1,0:T(8,128)(2,1)S(1)} %maximum_select_fusion.22), channel_id=1, source_target_pairs={{0,8},{8,0},{16,24},{24,16},{1,9},{9,1},{17,25},{25,17},{2,10},{10... | collective-permute-start | bytes 1179656 | tf_op jit(solution)/shard_map/ppermute | solution.py:464
  31.0 13.1 %collective-permute-start.6 = (bf16[64,2688]{1,0:T(8,128)(2,1)S(1)}, bf16[64,2688]{1,0:T(8,128)(2,1)S(1)}, u32[]{:S(2)}, u32[]{:S(2)}) collective-permute-start(bf16[64,2688]{1,0:T(8,128)(2,1)S(1)} %get-tuple-element.298), channel_id=1, source_target_pairs={{0,24},{24,0},{8,16},{16,8},{1,25},{25,1},{9,17},{17,9},{2,26},{26... | collective-permute-start | bytes 1032200 | tf_op jit(solution)/shard_map/ppermute | solution.py:464
  44.5 8.5 %collective-permute-start.7 = (bf16[4,32,1536]{2,1,0:T(8,128)(2,1)S(1)}, bf16[4,32,1536]{2,1,0:T(8,128)(2,1)S(1)}, u32[]{:S(2)}, u32[]{:S(2)}) collective-permute-start(bf16[4,32,1536]{2,1,0:T(8,128)(2,1)S(1)} %get-tuple-element.288), channel_id=1, source_target_pairs={{0,4},{4,0},{1,5},{5,1},{2,6},{6,2},{3,7},{7,3},{8,12},{12,8},{9,1... | collective-permute-start | bytes 1179656 | tf_op jit(solution)/shard_map/ppermute | solution.py:464
  45.8 8.2 %collective-permute-start.8 = (bf16[4,32,1536]{2,1,0:T(8,128)(2,1)S(1)}, bf16[4,32,1536]{2,1,0:T(8,128)(2,1)S(1)}, u32[]{:S(2)}, u32[]{:S(2)}) collective-permute-start(bf16[4,32,1536]{2,1,0:T(8,128)(2,1)S(1)} %get-tuple-element.287), channel_id=1, source_target_pairs={{0,1},{1,0},{2,3},{3,2},{4,5},{5,4},{6,7},{7,6},{8,9},{9,8},{10,11... | collective-permute-start | bytes 1179656 | tf_op jit(solution)/shard_map/ppermute | solution.py:464
  46.4 13.9 %collective-permute-start.9 = (bf16[2,64,2688]{2,1,0:T(8,128)(2,1)S(1)}, bf16[2,64,2688]{2,1,0:T(8,128)(2,1)S(1)}, u32[]{:S(2)}, u32[]{:S(2)}) collective-permute-start(bf16[2,64,2688]{2,1,0:T(8,128)(2,1)S(1)} %maximum_select_fusion.19), channel_id=1, source_target_pairs={{0,8},{8,0},{16,24},{24,16},{1,9},{9,1},{17,25},{25,17},{2,10},{10... | collective-permute-start | bytes 2064392 | tf_op jit(solution)/shard_map/ppermute | solution.py:464
  60.4 31.5 %collective-permute-start.10 = (bf16[4,2,32,1536]{3,2,0,1:T(8,128)(2,1)S(1)}, bf16[4,2,32,1536]{3,2,0,1:T(8,128)(2,1)S(1)}, u32[]{:S(2)}, u32[]{:S(2)}) collective-permute-start(bf16[4,2,32,1536]{3,2,0,1:T(8,128)(2,1)S(1)} %maximum_select_fusion.17), channel_id=1, source_target_pairs={{0,1},{1,0},{2,3},{3,2},{4,5},{5,4},{6,7},{7,6},{8,9},{9,8},{10,11... | collective-permute-start | bytes 2359304 | tf_op jit(solution)/shard_map/ppermute | solution.py:464
  62.0 30.0 %collective-permute-start.11 = (bf16[4,2,32,1536]{3,2,1,0:T(8,128)(2,1)S(1)}, bf16[4,2,32,1536]{3,2,1,0:T(8,128)(2,1)S(1)}, u32[]{:S(2)}, u32[]{:S(2)}) collective-permute-start(bf16[4,2,32,1536]{3,2,1,0:T(8,128)(2,1)S(1)} %maximum_select_fusion.18), channel_id=1, source_target_pairs={{0,4},{4,0},{1,5},{5,1},{2,6},{6,2},{3,7},{7,3},{8,12},{12,8},{9,1... | collective-permute-start | bytes 2359304 | tf_op jit(solution)/shard_map/ppermute | solution.py:464
  63.0 7.4 %collective-permute-start.12 = (bf16[64,2048]{1,0:T(8,128)(2,1)S(1)}, bf16[64,2048]{1,0:T(8,128)(2,1)S(1)}, u32[]{:S(2)}, u32[]{:S(2)}) collective-permute-start(bf16[64,2048]{1,0:T(8,128)(2,1)S(1)} %get-tuple-element.127), channel_id=1, source_target_pairs={{0,24},{24,0},{8,16},{16,8},{1,25},{25,1},{9,17},{17,9},{2,26},{26... | collective-permute-start | bytes 786440 | tf_op jit(solution)/shard_map/ppermute | solution.py:464
  66.5 25.4 %collective-permute-start.13 = (bf16[4,32,2688]{2,1,0:T(8,128)(2,1)S(1)}, bf16[4,32,2688]{2,1,0:T(8,128)(2,1)S(1)}, u32[]{:S(2)}, u32[]{:S(2)}) collective-permute-start(bf16[4,32,2688]{2,1,0:T(8,128)(2,1)S(1)} %get-tuple-element.278), channel_id=1, source_target_pairs={{0,4},{4,0},{1,5},{5,1},{2,6},{6,2},{3,7},{7,3},{8,12},{12,8},{9,1... | collective-permute-start | bytes 2064392 | tf_op jit(solution)/shard_map/ppermute | solution.py:464
  67.7 24.2 %collective-permute-start.14 = (bf16[4,32,2688]{2,1,0:T(8,128)(2,1)S(1)}, bf16[4,32,2688]{2,1,0:T(8,128)(2,1)S(1)}, u32[]{:S(2)}, u32[]{:S(2)}) collective-permute-start(bf16[4,32,2688]{2,1,0:T(8,128)(2,1)S(1)} %get-tuple-element.277), channel_id=1, source_target_pairs={{0,1},{1,0},{2,3},{3,2},{4,5},{5,4},{6,7},{7,6},{8,9},{9,8},{10,11... | collective-permute-start | bytes 2064392 | tf_op jit(solution)/shard_map/ppermute | solution.py:464
  92.2 39.4 %collective-permute-start.16 = (bf16[4,2,32,2688]{3,2,0,1:T(8,128)(2,1)S(1)}, bf16[4,2,32,2688]{3,2,0,1:T(8,128)(2,1)S(1)}, u32[]{:S(2)}, u32[]{:S(2)}) collective-permute-start(bf16[4,2,32,2688]{3,2,0,1:T(8,128)(2,1)S(1)} %maximum_select_fusion.9), channel_id=1, source_target_pairs={{0,1},{1,0},{2,3},{3,2},{4,5},{5,4},{6,7},{7,6},{8,9},{9,8},{10,11... | collective-permute-start | bytes 4128776 | tf_op jit(solution)/shard_map/ppermute | solution.py:464
  92.7 39.0 %collective-permute-start.17 = (bf16[4,2,32,2688]{3,2,0,1:T(8,128)(2,1)S(1)}, bf16[4,2,32,2688]{3,2,0,1:T(8,128)(2,1)S(1)}, u32[]{:S(2)}, u32[]{:S(2)}) collective-permute-start(bf16[4,2,32,2688]{3,2,0,1:T(8,128)(2,1)S(1)} %maximum_select_fusion.10), channel_id=1, source_target_pairs={{0,4},{4,0},{1,5},{5,1},{2,6},{6,2},{3,7},{7,3},{8,12},{12,8},{9,1... | collective-permute-start | bytes 4128776 | tf_op jit(solution)/shard_map/ppermute | solution.py:464
  93.1 11.3 %collective-permute-start.15 = (bf16[2,64,2048]{2,1,0:T(8,128)(2,1)S(1)}, bf16[2,64,2048]{2,1,0:T(8,128)(2,1)S(1)}, u32[]{:S(2)}, u32[]{:S(2)}) collective-permute-start(bf16[2,64,2048]{2,1,0:T(8,128)(2,1)S(1)} %maximum_select_fusion.20), channel_id=1, source_target_pairs={{0,8},{8,0},{16,24},{24,16},{1,9},{9,1},{17,25},{25,17},{2,10},{10... | collective-permute-start | bytes 1572872 | tf_op jit(solution)/shard_map/ppermute | solution.py:464
  105.8 25.8 %collective-permute-start.18 = (bf16[4,32,2048]{2,1,0:T(8,128)(2,1)S(1)}, bf16[4,32,2048]{2,1,0:T(8,128)(2,1)S(1)}, u32[]{:S(2)}, u32[]{:S(2)}) collective-permute-start(bf16[4,32,2048]{2,1,0:T(8,128)(2,1)S(1)} %get-tuple-element.282), channel_id=1, source_target_pairs={{0,4},{4,0},{1,5},{5,1},{2,6},{6,2},{3,7},{7,3},{8,12},{12,8},{9,1... | collective-permute-start | bytes 1572872 | tf_op jit(solution)/shard_map/ppermute | solution.py:464
  107.1 24.6 %collective-permute-start.19 = (bf16[4,32,2048]{2,1,0:T(8,128)(2,1)S(1)}, bf16[4,32,2048]{2,1,0:T(8,128)(2,1)S(1)}, u32[]{:S(2)}, u32[]{:S(2)}) collective-permute-start(bf16[4,32,2048]{2,1,0:T(8,128)(2,1)S(1)} %get-tuple-element.281), channel_id=1, source_target_pairs={{0,1},{1,0},{2,3},{3,2},{4,5},{5,4},{6,7},{7,6},{8,9},{9,8},{10,11... | collective-permute-start | bytes 1572872 | tf_op jit(solution)/shard_map/ppermute | solution.py:464
  138.9 8.5 %collective-permute-start.20 = (bf16[512,1024]{1,0:T(8,128)(2,1)}, bf16[512,1024]{1,0:T(8,128)(2,1)}, u32[]{:S(2)}, u32[]{:S(2)}) collective-permute-start(bf16[512,1024]{1,0:T(8,128)(2,1)} %convolution_convert_fusion.6), channel_id=1, source_target_pairs={{0,2},{2,0},{1,3},{3,1},{4,6},{6,4},{5,7},{7,5},{8,10},{10,8},{9,1... | collective-permute-start | bytes 3145736 | tf_op jit(solution)/shard_map/ppermute | solution.py:469
  153.5 24.4 %collective-permute-start.23 = (bf16[4,2,32,2048]{3,2,0,1:T(8,128)(2,1)S(1)}, bf16[4,2,32,2048]{3,2,0,1:T(8,128)(2,1)S(1)}, u32[]{:S(2)}, u32[]{:S(2)}) collective-permute-start(bf16[4,2,32,2048]{3,2,0,1:T(8,128)(2,1)S(1)} %maximum_select_fusion.13), channel_id=1, source_target_pairs={{0,1},{1,0},{2,3},{3,2},{4,5},{5,4},{6,7},{7,6},{8,9},{9,8},{10,11... | collective-permute-start | bytes 3145736 | tf_op jit(solution)/shard_map/ppermute | solution.py:464
  153.9 24.1 %collective-permute-start.24 = (bf16[4,2,32,2048]{3,2,1,0:T(8,128)(2,1)S(1)}, bf16[4,2,32,2048]{3,2,1,0:T(8,128)(2,1)S(1)}, u32[]{:S(2)}, u32[]{:S(2)}) collective-permute-start(bf16[4,2,32,2048]{3,2,1,0:T(8,128)(2,1)S(1)} %maximum_select_fusion.14), channel_id=1, source_target_pairs={{0,4},{4,0},{1,5},{5,1},{2,6},{6,2},{3,7},{7,3},{8,12},{12,8},{9,1... | collective-permute-start | bytes 3145736 | tf_op jit(solution)/shard_map/ppermute | solution.py:464
  181.8 4.4 collective-permute-start.25
  183.4 20.6 %collective-permute-start.27 = (bf16[512,1024]{1,0:T(8,128)(2,1)}, bf16[512,1024]{1,0:T(8,128)(2,1)S(1)}, u32[]{:S(2)}, u32[]{:S(2)}) collective-permute-start(bf16[512,1024]{1,0:T(8,128)(2,1)} %param.29), channel_id=1, source_target_pairs={{0,0},{1,2},{2,1},{3,3},{4,4},{5,6},{6,5},{7,7},{8,8},{9,10},{10,9... | collective-permute-start | bytes 3145736 | tf_op jit(solution)/shard_map/ppermute | solution.py:1146
  194.9 20.5 %all-to-all-start = ((bf16[16,128,128]{2,1,0:T(8,128)(2,1)}), bf16[16,128,128]{2,1,0:T(8,128)(2,1)S(1)}, u32[]{:S(2)}, u32[]{:S(2)}) async-start(bf16[16,128,128]{2,1,0:T(8,128)(2,1)} %broadcast_in_dim.46), calls=%async_computation | async-start | bytes 1048576 | tf_op jit(solution)/shard_map/all_to_all | solution.py:1143
  223.8 12.1 %all-to-all-start.1 = ((f32[16,8,128]{2,1,0:T(8,128)}), f32[16,8,128]{2,1,0:T(8,128)S(1)}, u32[]{:S(2)}, u32[]{:S(2)}) async-start(f32[16,8,128]{2,1,0:T(8,128)} %broadcast_in_dim.47), calls=%async_computation.1 | async-start | bytes 131072 | tf_op jit(solution)/shard_map/all_to_all | solution.py:1164
  229.5 19.8 %collective-permute-start.28 = (bf16[512,1024]{1,0:T(8,128)(2,1)}, bf16[512,1024]{1,0:T(8,128)(2,1)}, u32[]{:S(2)}, u32[]{:S(2)}) collective-permute-start(bf16[512,1024]{1,0:T(8,128)(2,1)} %add_convert_fusion.3), channel_id=1, source_target_pairs={{0,0},{1,2},{2,1},{3,3},{4,4},{5,6},{6,5},{7,7},{8,8},{9,10},{10,9... | collective-permute-start | bytes 3145736 | tf_op jit(solution)/shard_map/ppermute | solution.py:1184
  249.3 21.8 %all-to-all-start.2 = ((bf16[16,128,128]{2,1,0:T(8,128)(2,1)}), bf16[16,128,128]{2,1,0:T(8,128)(2,1)S(1)}, u32[]{:S(2)}, u32[]{:S(2)}) async-start(bf16[16,128,128]{2,1,0:T(8,128)(2,1)} %bitcast.57), calls=%async_computation.2 | async-start | bytes 1048576 | tf_op jit(solution)/shard_map/all_to_all | solution.py:1186
  271.2 5.1 %collective-permute-start.29 = (f32[512,128]{1,0:T(8,128)S(1)}, f32[512,128]{1,0:T(8,128)S(1)}, u32[]{:S(2)}, u32[]{:S(2)}) collective-permute-start(f32[512,128]{1,0:T(8,128)S(1)} %constant_dynamic-slice_fusion.11), channel_id=1, source_target_pairs={{0,2},{2,0},{1,3},{3,1},{4,6},{6,4},{5,7},{7,5},{8,10},{10,8},{9,1... | collective-permute-start | bytes 786440 | tf_op jit(solution)/shard_map/ppermute | solution.py:469
  279.9 4.9 collective-permute-start.30
  291.8 24.7 %collective-permute-start.33 = (bf16[4,2,32,2048]{3,2,0,1:T(8,128)(2,1)S(1)}, bf16[4,2,32,2048]{3,2,0,1:T(8,128)(2,1)S(1)}, u32[]{:S(2)}, u32[]{:S(2)}) collective-permute-start(bf16[4,2,32,2048]{3,2,0,1:T(8,128)(2,1)S(1)} %bitcast.318), channel_id=1, source_target_pairs={{0,4},{4,0},{1,5},{5,1},{2,6},{6,2},{3,7},{7,3},{8,12},{12,8},{9,1... | collective-permute-start | bytes 3145736 | tf_op jit(solution)/shard_map/ppermute | solution.py:464
  293.1 24.4 %collective-permute-start.34 = (bf16[4,2,32,2048]{3,2,0,1:T(8,128)(2,1)S(1)}, bf16[4,2,32,2048]{3,2,0,1:T(8,128)(2,1)S(1)}, u32[]{:S(2)}, u32[]{:S(2)}) collective-permute-start(bf16[4,2,32,2048]{3,2,0,1:T(8,128)(2,1)S(1)} %bitcast.319), channel_id=1, source_target_pairs={{0,1},{1,0},{2,3},{3,2},{4,5},{5,4},{6,7},{7,6},{8,9},{9,8},{10,11... | collective-permute-start | bytes 3145736 | tf_op jit(solution)/shard_map/ppermute | solution.py:464
  307.3 26.5 %collective-permute-start.31 = (bf16[512,1024]{1,0:T(8,128)(2,1)S(1)}, bf16[512,1024]{1,0:T(8,128)(2,1)S(1)}, u32[]{:S(2)}, u32[]{:S(2)}) collective-permute-start(bf16[512,1024]{1,0:T(8,128)(2,1)S(1)} %fusion.14), channel_id=1, source_target_pairs={{0,2},{2,0},{1,3},{3,1},{4,6},{6,4},{5,7},{7,5},{8,10},{10,8},{9,1... | collective-permute-start | bytes 3145736 | tf_op jit(solution)/shard_map/ppermute | solution.py:469
  318.8 20.6 %collective-permute-start.35 = (bf16[4,32,2048]{2,1,0:T(8,128)(2,1)}, bf16[4,32,2048]{2,1,0:T(8,128)(2,1)}, u32[]{:S(2)}, u32[]{:S(2)}) collective-permute-start(bf16[4,32,2048]{2,1,0:T(8,128)(2,1)} %fusion.40), channel_id=1, source_target_pairs={{0,1},{1,0},{2,3},{3,2},{4,5},{5,4},{6,7},{7,6},{8,9},{9,8},{10,11... | collective-permute-start | bytes 1572872 | tf_op jit(solution)/shard_map/ppermute | solution.py:464
  321.0 18.4 %collective-permute-start.36 = (bf16[4,32,2048]{2,1,0:T(8,128)(2,1)}, bf16[4,32,2048]{2,1,0:T(8,128)(2,1)}, u32[]{:S(2)}, u32[]{:S(2)}) collective-permute-start(bf16[4,32,2048]{2,1,0:T(8,128)(2,1)} %fusion.41), channel_id=1, source_target_pairs={{0,4},{4,0},{1,5},{5,1},{2,6},{6,2},{3,7},{7,3},{8,12},{12,8},{9,1... | collective-permute-start | bytes 1572872 | tf_op jit(solution)/shard_map/ppermute | solution.py:464
  329.4 26.2 %collective-permute-start.37 = (bf16[4,2,32,2048]{3,2,0,1:T(8,128)(2,1)}, bf16[4,2,32,2048]{3,2,0,1:T(8,128)(2,1)}, u32[]{:S(2)}, u32[]{:S(2)}) collective-permute-start(bf16[4,2,32,2048]{3,2,0,1:T(8,128)(2,1)} %bitcast.273), channel_id=1, source_target_pairs={{0,4},{4,0},{1,5},{5,1},{2,6},{6,2},{3,7},{7,3},{8,12},{12,8},{9,1... | collective-permute-start | bytes 3145736 | tf_op jit(solution)/shard_map/ppermute | solution.py:464
  332.6 23.0 %collective-permute-start.38 = (bf16[4,2,32,2048]{3,2,0,1:T(8,128)(2,1)}, bf16[4,2,32,2048]{3,2,0,1:T(8,128)(2,1)}, u32[]{:S(2)}, u32[]{:S(2)}) collective-permute-start(bf16[4,2,32,2048]{3,2,0,1:T(8,128)(2,1)} %bitcast.272), channel_id=1, source_target_pairs={{0,1},{1,0},{2,3},{3,2},{4,5},{5,4},{6,7},{7,6},{8,9},{9,8},{10,11... | collective-permute-start | bytes 3145736 | tf_op jit(solution)/shard_map/ppermute | solution.py:464
  336.9 26.0 %collective-permute-start.32 = (bf16[512,1024]{1,0:T(8,128)(2,1)}, bf16[512,1024]{1,0:T(8,128)(2,1)}, u32[]{:S(2)}, u32[]{:S(2)}) collective-permute-start(bf16[512,1024]{1,0:T(8,128)(2,1)} %get-tuple-element.244), channel_id=1, source_target_pairs={{0,2},{2,0},{1,3},{3,1},{4,6},{6,4},{5,7},{7,5},{8,10},{10,8},{9,1... | collective-permute-start | bytes 3145736 | tf_op jit(solution)/shard_map/ppermute | solution.py:469
  370.6 18.2 %collective-permute-start.39 = (bf16[2,64,2048]{2,1,0:T(8,128)(2,1)S(1)}, bf16[2,64,2048]{2,1,0:T(8,128)(2,1)S(1)}, u32[]{:S(2)}, u32[]{:S(2)}) collective-permute-start(bf16[2,64,2048]{2,1,0:T(8,128)(2,1)S(1)} %select_convert_fusion.1), channel_id=1, source_target_pairs={{0,8},{8,0},{16,24},{24,16},{1,9},{9,1},{17,25},{25,17},{2,10},{10... | collective-permute-start | bytes 1572872 | tf_op jit(solution)/shard_map/ppermute | solution.py:464
  371.7 17.0 %collective-permute-start.40 = (bf16[4,32,2048]{2,1,0:T(8,128)(2,1)S(1)}, bf16[4,32,2048]{2,1,0:T(8,128)(2,1)S(1)}, u32[]{:S(2)}, u32[]{:S(2)}) collective-permute-start(bf16[4,32,2048]{2,1,0:T(8,128)(2,1)S(1)} %fusion.42), channel_id=1, source_target_pairs={{0,1},{1,0},{2,3},{3,2},{4,5},{5,4},{6,7},{7,6},{8,9},{9,8},{10,11... | collective-permute-start | bytes 1572872 | tf_op jit(solution)/shard_map/ppermute | solution.py:464
  373.1 15.7 %collective-permute-start.41 = (bf16[4,32,2048]{2,1,0:T(8,128)(2,1)S(1)}, bf16[4,32,2048]{2,1,0:T(8,128)(2,1)S(1)}, u32[]{:S(2)}, u32[]{:S(2)}) collective-permute-start(bf16[4,32,2048]{2,1,0:T(8,128)(2,1)S(1)} %fusion.43), channel_id=1, source_target_pairs={{0,4},{4,0},{1,5},{5,1},{2,6},{6,2},{3,7},{7,3},{8,12},{12,8},{9,1... | collective-permute-start | bytes 1572872 | tf_op jit(solution)/shard_map/ppermute | solution.py:464
  373.7 15.1 %collective-permute-start.42 = (bf16[4,2,32,512]{3,2,0,1:T(8,128)(2,1)S(1)}, bf16[4,2,32,512]{3,2,0,1:T(8,128)(2,1)S(1)}, u32[]{:S(2)}, u32[]{:S(2)}) collective-permute-start(bf16[4,2,32,512]{3,2,0,1:T(8,128)(2,1)S(1)} %dynamic-slice_bitcast_fusion.3), channel_id=1, source_target_pairs={{0,4},{4,0},{1,5},{5,1},{2,6},{6,2},{3,7},{7,3},{8,12},{12,8},{9,1... | collective-permute-start | bytes 786440 | tf_op jit(solution)/shard_map/ppermute | solution.py:464
  374.8 13.9 %collective-permute-start.43 = (bf16[4,2,32,512]{3,2,0,1:T(8,128)(2,1)S(1)}, bf16[4,2,32,512]{3,2,0,1:T(8,128)(2,1)S(1)}, u32[]{:S(2)}, u32[]{:S(2)}) collective-permute-start(bf16[4,2,32,512]{3,2,0,1:T(8,128)(2,1)S(1)} %dynamic-slice_bitcast_fusion.2), channel_id=1, source_target_pairs={{0,1},{1,0},{2,3},{3,2},{4,5},{5,4},{6,7},{7,6},{8,9},{9,8},{10,11... | collective-permute-start | bytes 786440 | tf_op jit(solution)/shard_map/ppermute | solution.py:464
  389.6 6.0 %collective-permute-start.44 = (f32[16,4]{1,0:T(8,128)S(1)}, f32[16,4]{1,0:T(8,128)S(1)}, u32[]{:S(2)}, u32[]{:S(2)}) collective-permute-start(f32[16,4]{1,0:T(8,128)S(1)} %reshape.820), channel_id=1, source_target_pairs={{0,2},{2,0},{1,3},{3,1},{4,6},{6,4},{5,7},{7,5},{8,10},{10,8},{9,1... | collective-permute-start | bytes 776 | tf_op jit(solution)/shard_map/ppermute | solution.py:469
  394.1 16.6 %collective-permute-start.46 = (bf16[64,2048]{1,0:T(8,128)(2,1)S(1)}, bf16[64,2048]{1,0:T(8,128)(2,1)S(1)}, u32[]{:S(2)}, u32[]{:S(2)}) collective-permute-start(bf16[64,2048]{1,0:T(8,128)(2,1)S(1)} %fusion.54), channel_id=1, source_target_pairs={{0,24},{24,0},{8,16},{16,8},{1,25},{25,1},{9,17},{17,9},{2,26},{26... | collective-permute-start | bytes 786440 | tf_op jit(solution)/shard_map/ppermute | solution.py:464
  395.6 19.2 %collective-permute-start.47 = (bf16[2,64,2048]{2,1,0:T(8,128)(2,1)S(1)}, bf16[2,64,2048]{2,1,0:T(8,128)(2,1)S(1)}, u32[]{:S(2)}, u32[]{:S(2)}) collective-permute-start(bf16[2,64,2048]{2,1,0:T(8,128)(2,1)S(1)} %select_convert_fusion), channel_id=1, source_target_pairs={{0,8},{8,0},{16,24},{24,16},{1,9},{9,1},{17,25},{25,17},{2,10},{10... | collective-permute-start | bytes 1572872 | tf_op jit(solution)/shard_map/ppermute | solution.py:464
  396.1 14.5 %collective-permute-start.48 = (bf16[4,32,512]{2,1,0:T(8,128)(2,1)S(1)}, bf16[4,32,512]{2,1,0:T(8,128)(2,1)S(1)}, u32[]{:S(2)}, u32[]{:S(2)}) collective-permute-start(bf16[4,32,512]{2,1,0:T(8,128)(2,1)S(1)} %fusion.62), channel_id=1, source_target_pairs={{0,1},{1,0},{2,3},{3,2},{4,5},{5,4},{6,7},{7,6},{8,9},{9,8},{10,11... | collective-permute-start | bytes 393224 | tf_op jit(solution)/shard_map/ppermute | solution.py:464
  396.8 13.8 %collective-permute-start.49 = (bf16[4,32,512]{2,1,0:T(8,128)(2,1)S(1)}, bf16[4,32,512]{2,1,0:T(8,128)(2,1)S(1)}, u32[]{:S(2)}, u32[]{:S(2)}) collective-permute-start(bf16[4,32,512]{2,1,0:T(8,128)(2,1)S(1)} %fusion.63), channel_id=1, source_target_pairs={{0,4},{4,0},{1,5},{5,1},{2,6},{6,2},{3,7},{7,3},{8,12},{12,8},{9,1... | collective-permute-start | bytes 393224 | tf_op jit(solution)/shard_map/ppermute | solution.py:464
  422.4 18.3 %collective-permute-start.50 = (bf16[4,2,32,1536]{3,2,0,1:T(8,128)(2,1)S(1)}, bf16[4,2,32,1536]{3,2,0,1:T(8,128)(2,1)S(1)}, u32[]{:S(2)}, u32[]{:S(2)}) collective-permute-start(bf16[4,2,32,1536]{3,2,0,1:T(8,128)(2,1)S(1)} %dynamic-slice_bitcast_fusion.1), channel_id=1, source_target_pairs={{0,4},{4,0},{1,5},{5,1},{2,6},{6,2},{3,7},{7,3},{8,12},{12,8},{9,1... | collective-permute-start | bytes 2359304 | tf_op jit(solution)/shard_map/ppermute | solution.py:464
  422.6 18.2 %collective-permute-start.51 = (bf16[4,2,32,1536]{3,2,0,1:T(8,128)(2,1)S(1)}, bf16[4,2,32,1536]{3,2,0,1:T(8,128)(2,1)S(1)}, u32[]{:S(2)}, u32[]{:S(2)}) collective-permute-start(bf16[4,2,32,1536]{3,2,0,1:T(8,128)(2,1)S(1)} %dynamic-slice_bitcast_fusion), channel_id=1, source_target_pairs={{0,1},{1,0},{2,3},{3,2},{4,5},{5,4},{6,7},{7,6},{8,9},{9,8},{10,11... | collective-permute-start | bytes 2359304 | tf_op jit(solution)/shard_map/ppermute | solution.py:464
  423.5 16.2 %collective-permute-start.52 = (bf16[64,2048]{1,0:T(8,128)(2,1)S(1)}, bf16[64,2048]{1,0:T(8,128)(2,1)S(1)}, u32[]{:S(2)}, u32[]{:S(2)}) collective-permute-start(bf16[64,2048]{1,0:T(8,128)(2,1)S(1)} %fusion.55), channel_id=1, source_target_pairs={{0,24},{24,0},{8,16},{16,8},{1,25},{25,1},{9,17},{17,9},{2,26},{26... | collective-permute-start | bytes 786440 | tf_op jit(solution)/shard_map/ppermute | solution.py:464
  425.9 10.6 %collective-permute-start.53 = (bf16[2,64,512]{2,1,0:T(8,128)(2,1)S(1)}, bf16[2,64,512]{2,1,0:T(8,128)(2,1)S(1)}, u32[]{:S(2)}, u32[]{:S(2)}) collective-permute-start(bf16[2,64,512]{2,1,0:T(8,128)(2,1)S(1)} %select_convert_fusion.6), channel_id=1, source_target_pairs={{0,8},{8,0},{16,24},{24,16},{1,9},{9,1},{17,25},{25,17},{2,10},{10... | collective-permute-start | bytes 393224 | tf_op jit(solution)/shard_map/ppermute | solution.py:464
  426.0 13.7 %collective-permute-start.54 = (bf16[584,128]{1,0:T(8,128)(2,1)S(1)}, bf16[584,128]{1,0:T(8,128)(2,1)S(1)}, u32[]{:S(2)}, u32[]{:S(2)}) collective-permute-start(bf16[584,128]{1,0:T(8,128)(2,1)S(1)} %convert_element_type.481), channel_id=1, source_target_pairs={{0,8},{8,0},{16,24},{24,16},{1,9},{9,1},{17,25},{25,17},{2,10},{10... | collective-permute-start | bytes 448520 | tf_op jit(solution)/shard_map/ppermute | solution.py:464
  436.5 9.9 %collective-permute-start.61 = (bf16[512,1024]{1,0:T(8,128)(2,1)S(1)}, bf16[512,1024]{1,0:T(8,128)(2,1)S(1)}, u32[]{:S(2)}, u32[]{:S(2)}) collective-permute-start(bf16[512,1024]{1,0:T(8,128)(2,1)S(1)} %add_convert_fusion.2), channel_id=1, source_target_pairs={{0,2},{2,0},{1,3},{3,1},{4,6},{6,4},{5,7},{7,5},{8,10},{10,8},{9,1... | collective-permute-start | bytes 3145736 | tf_op jit(solution)/shard_map/ppermute | solution.py:469
  441.1 13.0 %collective-permute-start.55 = (bf16[4,32,1536]{2,1,0:T(8,128)(2,1)S(1)}, bf16[4,32,1536]{2,1,0:T(8,128)(2,1)S(1)}, u32[]{:S(2)}, u32[]{:S(2)}) collective-permute-start(bf16[4,32,1536]{2,1,0:T(8,128)(2,1)S(1)} %fusion.49), channel_id=1, source_target_pairs={{0,1},{1,0},{2,3},{3,2},{4,5},{5,4},{6,7},{7,6},{8,9},{9,8},{10,11... | collective-permute-start | bytes 1179656 | tf_op jit(solution)/shard_map/ppermute | solution.py:464
  441.7 12.3 %collective-permute-start.56 = (bf16[4,32,1536]{2,1,0:T(8,128)(2,1)S(1)}, bf16[4,32,1536]{2,1,0:T(8,128)(2,1)S(1)}, u32[]{:S(2)}, u32[]{:S(2)}) collective-permute-start(bf16[4,32,1536]{2,1,0:T(8,128)(2,1)S(1)} %fusion.50), channel_id=1, source_target_pairs={{0,4},{4,0},{1,5},{5,1},{2,6},{6,2},{3,7},{7,3},{8,12},{12,8},{9,1... | collective-permute-start | bytes 1179656 | tf_op jit(solution)/shard_map/ppermute | solution.py:464
  442.9 11.1 %collective-permute-start.57 = (bf16[64,512]{1,0:T(8,128)(2,1)S(1)}, bf16[64,512]{1,0:T(8,128)(2,1)S(1)}, u32[]{:S(2)}, u32[]{:S(2)}) collective-permute-start(bf16[64,512]{1,0:T(8,128)(2,1)S(1)} %fusion.68), channel_id=1, source_target_pairs={{0,24},{24,0},{8,16},{16,8},{1,25},{25,1},{9,17},{17,9},{2,26},{26... | collective-permute-start | bytes 196616 | tf_op jit(solution)/shard_map/ppermute | solution.py:464
  445.6 8.4 %collective-permute-start.58 = (bf16[584,128]{1,0:T(8,128)(2,1)S(1)}, bf16[584,128]{1,0:T(8,128)(2,1)S(1)}, u32[]{:S(2)}, u32[]{:S(2)}) collective-permute-start(bf16[584,128]{1,0:T(8,128)(2,1)S(1)} %fusion.56), channel_id=1, source_target_pairs={{0,24},{24,0},{8,16},{16,8},{1,25},{25,1},{9,17},{17,9},{2,26},{26... | collective-permute-start | bytes 448520 | tf_op jit(solution)/shard_map/ppermute | solution.py:464
  447.6 18.9 %collective-permute-start.62 = (bf16[512,1024]{1,0:T(8,128)(2,1)S(1)}, bf16[512,1024]{1,0:T(8,128)(2,1)S(1)}, u32[]{:S(2)}, u32[]{:S(2)}) collective-permute-start(bf16[512,1024]{1,0:T(8,128)(2,1)S(1)} %add_convert_fusion.1), channel_id=1, source_target_pairs={{0,0},{1,2},{2,1},{3,3},{4,4},{5,6},{6,5},{7,7},{8,8},{9,10},{10,9... | collective-permute-start | bytes 3145736 | tf_op jit(solution)/shard_map/ppermute | solution.py:464
  454.4 9.5 %collective-permute-start.59 = (bf16[2,64,1536]{2,1,0:T(8,128)(2,1)S(1)}, bf16[2,64,1536]{2,1,0:T(8,128)(2,1)S(1)}, u32[]{:S(2)}, u32[]{:S(2)}) collective-permute-start(bf16[2,64,1536]{2,1,0:T(8,128)(2,1)S(1)} %select_convert_fusion.2), channel_id=1, source_target_pairs={{0,8},{8,0},{16,24},{24,16},{1,9},{9,1},{17,25},{25,17},{2,10},{10... | collective-permute-start | bytes 1179656 | tf_op jit(solution)/shard_map/ppermute | solution.py:464
  466.6 13.0 %collective-permute-start.65 = (bf16[64,4096]{1,0:T(8,128)(2,1)S(1)}, bf16[64,4096]{1,0:T(8,128)(2,1)S(1)}, u32[]{:S(2)}, u32[]{:S(2)}) collective-permute-start(bf16[64,4096]{1,0:T(8,128)(2,1)S(1)} %pad_maximum_fusion.17), channel_id=1, source_target_pairs={{0,0},{1,2},{2,1},{3,3},{4,4},{5,6},{6,5},{7,7},{8,8},{9,10},{10,9... | collective-permute-start | bytes 1572872 | tf_op jit(solution)/shard_map/ppermute | solution.py:464
  470.3 9.3 %collective-permute-start.63 = (bf16[64,1536]{1,0:T(8,128)(2,1)S(1)}, bf16[64,1536]{1,0:T(8,128)(2,1)S(1)}, u32[]{:S(2)}, u32[]{:S(2)}) collective-permute-start(bf16[64,1536]{1,0:T(8,128)(2,1)S(1)} %fusion.58), channel_id=1, source_target_pairs={{0,24},{24,0},{8,16},{16,8},{1,25},{25,1},{9,17},{17,9},{2,26},{26... | collective-permute-start | bytes 589832 | tf_op jit(solution)/shard_map/ppermute | solution.py:464
  472.4 7.1 %collective-permute-start.64 = (bf16[584,128]{1,0:T(8,128)(2,1)S(1)}, bf16[584,128]{1,0:T(8,128)(2,1)S(1)}, u32[]{:S(2)}, u32[]{:S(2)}) collective-permute-start(bf16[584,128]{1,0:T(8,128)(2,1)S(1)} %fusion.57), channel_id=1, source_target_pairs={{0,1},{1,0},{2,3},{3,2},{4,5},{5,4},{6,7},{7,6},{8,9},{9,8},{10,11... | collective-permute-start | bytes 448520 | tf_op jit(solution)/shard_map/ppermute | solution.py:464
  479.7 7.7 %collective-permute-start.66 = (bf16[64,2048]{1,0:T(8,128)(2,1)S(1)}, bf16[64,2048]{1,0:T(8,128)(2,1)S(1)}, u32[]{:S(2)}, u32[]{:S(2)}) collective-permute-start(bf16[64,2048]{1,0:T(8,128)(2,1)S(1)} %pad_maximum_fusion.20), channel_id=1, source_target_pairs={{0,0},{1,2},{2,1},{3,3},{4,4},{5,6},{6,5},{7,7},{8,8},{9,10},{10,9... | collective-permute-start | bytes 786440 | tf_op jit(solution)/shard_map/ppermute | solution.py:464
  (61 other events, 602.9 us)

commit v5 on v4

--- a/solution.py
+++ b/solution.py
@@ -1056,17 +1056,18 @@
     mid_wide = mid_rows.shape[1]
     rest_rows = tie(rest_rows, qkv_pair)
     mid_rows, down_rows = rest_rows[:, :mid_wide], rest_rows[:, mid_wide:]
-    got = exchange((qkv_pair, "z", NEAR), (mid_rows, "z", FAR))
-    qkv_line = whole_line(qkv_pair, got[0], z)
-    mid_pair = far_pair(mid_rows, got[1], z)
-    got = exchange(*first_moves(qkv_line), (mid_pair, "z", NEAR))
-    qkv_parts = first_parts(qkv_line, got, x, y)
-    mid_line = whole_line(mid_pair, got[2], z)
-    last = last_moves(qkv_parts)
-    got = exchange(*last, (tie(down_rows, mid_line), "z", FAR), *first_moves(mid_line))
-    full_qkv = full_rows(qkv_parts, got, x, y)
-    down_pair = far_pair(down_rows, got[2], z)
-    mid_parts = first_parts(mid_line, got[3:], x, y)
+    (near,) = exchange((qkv_pair, "z", NEAR))
+    qkv_line = whole_line(qkv_pair, near, z)
+    (far,) = exchange((mid_rows, "z", FAR))
+    mid_pair = far_pair(mid_rows, far, z)
+    qkv_parts = first_parts(qkv_line, exchange(*first_moves(qkv_line)), x, y)
+    (near,) = exchange((mid_pair, "z", NEAR))
+    mid_line = whole_line(mid_pair, near, z)
+    full_qkv = full_rows(qkv_parts, exchange(*last_moves(qkv_parts)), x, y)
+    down_rows, mid_line = lax.optimization_barrier((down_rows, mid_line))
+    got = exchange((down_rows, "z", FAR), *first_moves(mid_line))
+    down_pair = far_pair(down_rows, got[0], z)
+    mid_parts = first_parts(mid_line, got[1:], x, y)
     (near,) = exchange((down_pair, "z", NEAR))
     down_line = whole_line(down_pair, near, z)
     got = exchange(*last_moves(mid_parts), *first_moves(down_line))

time: 502 us -> 497 us (0.990)
    ppermute x54, starting transfers between devices: 67.4 us -> 73.3 us  [exchange(): lax.ppermute(value, axis, steps)]
    unnamed x129 -> x127, local copies, waits for them, and re-layouts: 20.8 us -> 19.5 us
  transfers between devices with their start and end apart: 71 -> 71, of which waited for: 32 -> 32; matrix products, arithmetic and copies ran while one was open for 16% -> 15% of each run, Pallas kernels for 13% -> 13%
where the time goes in v5:
time: 497 us; the launch traced here: 492 us
  waiting for transfers between devices  161 us (32%)
  starting transfers between devices  119 us (24%)
  Pallas kernels  69.7 us (14%)
  matrix products  62.2 us (13%)
  local copies, waits for them, and re-layouts  43.9 us (9%)
  other arithmetic  32.6 us (7%)
    ppermute x54, waiting for transfers between devices, exchange(): lax.ppermute(value, axis, steps)  133 us
    ppermute x54, starting transfers between devices, exchange(): lax.ppermute(value, axis, steps)  73.3 us
    pallas_call x2, Pallas kernels, attend_back(): pl.pallas_call(partial(attend_back_kernel, group * heads), grid=(count //...  23.6 us
    dot_general x7, matrix products, contract_rows(): lax.dot_general(left, right, (((0,), (0,)), ((), ())), precision=precisio...  22.5 us
    dot_general x12, matrix products, contract_cols(): lax.dot_general(left, right, (((1,), (1,)), ((), ())), precision=precisio...  21.2 us
    unnamed x127, local copies, waits for them, and re-layouts  19.5 us
    ppermute x12, starting transfers between devices, swap(): return lax.ppermute(value, axis, SWAP)  19 us
    dot_general x4, matrix products, dot(): return jnp.dot(left, right, preferred_element_type=F32)  17.1 us
  transfers between devices with their start and end apart: 71, of which 32 were waited for; matrix products, arithmetic and copies ran while one was open for 15% of the time, Pallas kernels for 13%

profile of v5, /device:TPU:1, one launch (start us, length us, event | category | flops | bytes accessed | tf_op | source)
XLA Modules:
  0.0 491.8 jit_solution(2508699322251295587)
XLA Ops:
  1.7 4.5 collective-permute-start
  13.1 3.9 collective-permute-start.9
  17.0 3.4 collective-permute-start.3
  20.5 3.8 collective-permute-done.3
  24.4 3.7 collective-permute-start.4
  28.1 9.5 %collective-permute-done.4 = bf16[2,64,1536]{2,1,0:T(8,128)(2,1)S(1)} collective-permute-done((bf16[2,64,1536]{2,1,0:T(8,128)(2,1)S(1)}, bf16[2,64,1536]{2,1,0:T(8,128)(2,1)S(1)}, u32[]{:S(2)}, u32[]{:S(2)}) %collective-permute-start.4) | collective-permute-done | bytes 393248 | tf_op jit(solution)/shard_map/ppermute | solution.py:464
  43.0 7.0 %collective-permute-done.10 = bf16[64,2688]{1,0:T(8,128)(2,1)S(1)} collective-permute-done((bf16[64,2688]{1,0:T(8,128)(2,1)S(1)}, bf16[64,2688]{1,0:T(8,128)(2,1)S(1)}, u32[]{:S(2)}, u32[]{:S(2)}) %collective-permute-start.10) | collective-permute-done | bytes 344096 | tf_op jit(solution)/shard_map/ppermute | solution.py:464
  50.1 6.9 %collective-permute-start.11 = (bf16[2,64,2688]{2,1,0:T(8,128)(2,1)S(1)}, bf16[2,64,2688]{2,1,0:T(8,128)(2,1)S(1)}, u32[]{:S(2)}, u32[]{:S(2)}) collective-permute-start(bf16[2,64,2688]{2,1,0:T(8,128)(2,1)S(1)} %maximum_select_fusion.19), channel_id=1, source_target_pairs={{0,8},{8,0},{16,24},{24,16},{1,9},{9,1},{17,25},{25,17},{2,10},{10... | collective-permute-start | bytes 2064392 | tf_op jit(solution)/shard_map/ppermute | solution.py:464
  59.1 12.5 %collective-permute-done.11 = bf16[2,64,2688]{2,1,0:T(8,128)(2,1)S(1)} collective-permute-done((bf16[2,64,2688]{2,1,0:T(8,128)(2,1)S(1)}, bf16[2,64,2688]{2,1,0:T(8,128)(2,1)S(1)}, u32[]{:S(2)}, u32[]{:S(2)}) %collective-permute-start.11) | collective-permute-done | bytes 688160 | tf_op jit(solution)/shard_map/ppermute | solution.py:464
  72.0 3.3 collective-permute-start.12
  77.8 3.6 add_convert_fusion.own_ref.qkv_ref
  81.5 9.6 %collective-permute-done.13 = bf16[4,32,2688]{2,1,0:T(8,128)(2,1)S(1)} collective-permute-done((bf16[4,32,2688]{2,1,0:T(8,128)(2,1)S(1)}, bf16[4,32,2688]{2,1,0:T(8,128)(2,1)S(1)}, u32[]{:S(2)}, u32[]{:S(2)}) %collective-permute-start.13) | collective-permute-done | bytes 688160 | tf_op jit(solution)/shard_map/ppermute | solution.py:464
  93.6 10.1 %collective-permute-done.15 = bf16[2,64,2048]{2,1,0:T(8,128)(2,1)S(1)} collective-permute-done((bf16[2,64,2048]{2,1,0:T(8,128)(2,1)S(1)}, bf16[2,64,2048]{2,1,0:T(8,128)(2,1)S(1)}, u32[]{:S(2)}, u32[]{:S(2)}) %collective-permute-start.15) | collective-permute-done | bytes 524320 | tf_op jit(solution)/shard_map/ppermute | solution.py:464
  107.6 10.4 %shard_map.254 = (bf16[1024,512]{1,0:T(8,128)(2,1)S(1)}, f32[8,1024]{1,0:T(8,128)S(1)}) custom-call(s32[2,4]{1,0:T(2,128)S(1)} %pad_add_fusion.1.bounds, bf16[1024,1536]{1,0:T(8,128)(2,1)S(1)} %add_convert_fusion.own_ref.qkv_ref, bf16[1024,1536]{1,0:T(8,128)(2,1)S(1)} %add_convert_fusion.own_ref.qkv_ref, s32[2,1024]{1,0:T(2,128)S(1)} %pad_add_fusion.spans), custom_call_target="tpu_custom_call" | custom-call | flops 2147483648 | bytes 12582912 | tf_op jit(solution)/shard_map/pallas_call | solution.py:679
  118.0 15.1 %collective-permute-done.18 = bf16[4,32,2048]{2,1,0:T(8,128)(2,1)S(1)} collective-permute-done((bf16[4,32,2048]{2,1,0:T(8,128)(2,1)S(1)}, bf16[4,32,2048]{2,1,0:T(8,128)(2,1)S(1)}, u32[]{:S(2)}, u32[]{:S(2)}) %collective-permute-start.18) | collective-permute-done | bytes 524320 | tf_op jit(solution)/shard_map/ppermute | solution.py:464
  136.3 2.3 copy-done.2
  140.3 3.7 collective-permute-start.20
  144.1 2.0 fusion.31
  155.5 16.2 %shard_map.255 = (bf16[1024,2048]{1,0:T(8,128)(2,1)S(1)}, bf16[1024,2048]{1,0:T(8,128)(2,1)S(1)}) custom-call(bf16[1024,1024]{1,0:T(8,128)(2,1)S(1)} %pad_maximum_fusion.5.x_ref, bf16[1024,2688]{1,0:T(8,128)(2,1)S(1)} %bitcast.281, f32[1,2048]{1,0:T(1,128)S(1)} %slice.505.b_ref), custom_call_target="tpu_custom_call" | custom-call | flops 4294967296 | bytes 14680064 | tf_op jit(solution)/shard_map/pallas_call | solution.py:849
  171.7 2.1 copy-done.7
  173.8 3.4 collective-permute-done.23
  179.5 2.4 fusion.11
  183.4 2.1 collective-permute-start.27
  185.7 2.8 fusion.119
  194.3 4.1 all-to-all-start
  199.7 11.3 %all-to-all-done = bf16[16,128,128]{2,1,0:T(8,128)(2,1)S(1)} async-done(((bf16[16,128,128]{2,1,0:T(8,128)(2,1)}), bf16[16,128,128]{2,1,0:T(8,128)(2,1)S(1)}, u32[]{:S(2)}, u32[]{:S(2)}) %all-to-all-start) | async-done | bytes 524320 | tf_op jit(solution)/shard_map/all_to_all | solution.py:1144
  211.1 7.0 %shard_map.256 = f32[24,2048]{1,0:T(8,128)S(1)} custom-call(bf16[2048,128]{1,0:T(8,128)(2,1)S(1)} %bitcast.286, bf16[1024,128]{1,0:T(8,128)(2,1)S(1)} %maximum_select_fusion.25.d_ref, s32[1,1024]{1,0:T(1,128)S(1)} %compare_select_fusion.seg_ref), custom_call_target="tpu_custom_call" | custom-call | flops 3221225472 | bytes 786432 | tf_op jit(solution)/shard_map/pallas_call | solution.py:904
  219.5 5.7 %all-to-all-start.1 = ((f32[16,8,128]{2,1,0:T(8,128)}), f32[16,8,128]{2,1,0:T(8,128)S(1)}, u32[]{:S(2)}, u32[]{:S(2)}) async-start(f32[16,8,128]{2,1,0:T(8,128)} %broadcast_in_dim.47), calls=%async_computation.1 | async-start | bytes 131072 | tf_op jit(solution)/shard_map/all_to_all | solution.py:1165
  225.1 5.1 %collective-permute-start.28 = (bf16[512,1024]{1,0:T(8,128)(2,1)}, bf16[512,1024]{1,0:T(8,128)(2,1)}, u32[]{:S(2)}, u32[]{:S(2)}) collective-permute-start(bf16[512,1024]{1,0:T(8,128)(2,1)} %add_convert_fusion.3), channel_id=1, source_target_pairs={{0,0},{1,2},{2,1},{3,3},{4,4},{5,6},{6,5},{7,7},{8,8},{9,10},{10,9... | collective-permute-start | bytes 3145736 | tf_op jit(solution)/shard_map/ppermute | solution.py:1185
  232.4 12.5 %shard_map.257 = (bf16[2048,128]{1,0:T(8,128)(2,1)}, f32[768,128]{1,0:T(8,128)S(1)}) custom-call(bf16[2048,128]{1,0:T(8,128)(2,1)S(1)} %bitcast.287, bf16[1024,128]{1,0:T(8,128)(2,1)S(1)} %maximum_select_fusion.25.d_ref, s32[1,1024]{1,0:T(1,128)S(1)} %compare_select_fusion.seg_ref, f32[24,2048]{1,0:T(8,128)S(1)} %convolution_divide_fusion.coef_ref), custom_call_target="tpu_custom_call" | custom-call | flops 4831838208 | bytes 1572864 | tf_op jit(solution)/shard_map/pallas_call | solution.py:980
  244.9 9.6 %all-to-all-start.2 = ((bf16[16,128,128]{2,1,0:T(8,128)(2,1)}), bf16[16,128,128]{2,1,0:T(8,128)(2,1)S(1)}, u32[]{:S(2)}, u32[]{:S(2)}) async-start(bf16[16,128,128]{2,1,0:T(8,128)(2,1)} %bitcast.57), calls=%async_computation.2 | async-start | bytes 1048576 | tf_op jit(solution)/shard_map/all_to_all | solution.py:1187
  254.6 12.1 %all-to-all-done.2 = bf16[16,128,128]{2,1,0:T(8,128)(2,1)S(1)} async-done(((bf16[16,128,128]{2,1,0:T(8,128)(2,1)}), bf16[16,128,128]{2,1,0:T(8,128)(2,1)S(1)}, u32[]{:S(2)}, u32[]{:S(2)}) %all-to-all-start.2) | async-done | bytes 524320 | tf_op jit(solution)/shard_map/all_to_all | solution.py:1187
  266.9 4.0 collective-permute-start.29
  280.5 6.4 %convolution_convert_fusion.1 = bf16[1024,2048]{1,0:T(8,128)(2,1)S(1)} fusion(bf16[1024,2048]{1,0:T(8,128)(2,1)S(1)} %copy-done.6, bf16[512,1024]{1,0:T(8,128)(2,1)} %collective-permute-done.30, bf16[512,1024]{1,0:T(8,128)(2,1)} %get-tuple-element.237), kind=kOutput, calls=%fused_computation.6 | convolution fusion | flops 4301258752 | bytes 10485760 | tf_op jit(solution)/shard_map/dot_general | solution.py:33
  290.9 8.0 %convert_reduce_fusion = (f32[2048]{0:T(1024)S(1)}, bf16[1024,2048]{1,0:T(8,128)(2,1)}) fusion(bf16[1024,2048]{1,0:T(8,128)(2,1)S(1)} %copy-done.8, bf16[1024,2048]{1,0:T(8,128)(2,1)S(1)} %bitcast.297, bf16[512,1024]{1,0:T(8,128)(2,1)} %collective-permute-done.30, bf16[512,1024]{1,0:T(8,128)(2,1)} %get-tuple-element.237), kind=kOutput, calls=%fused_computation | convolution fusion | flops 4309645312 | bytes 14688256 | tf_op jit(solution)/shard_map/dot_general | solution.py:448
  298.9 4.1 fusion.14
  303.2 2.4 fusion.2
  305.6 6.6 %collective-permute-done.33 = bf16[4,2,32,2048]{3,2,0,1:T(8,128)(2,1)S(1)} collective-permute-done((bf16[4,2,32,2048]{3,2,0,1:T(8,128)(2,1)S(1)}, bf16[4,2,32,2048]{3,2,0,1:T(8,128)(2,1)S(1)}, u32[]{:S(2)}, u32[]{:S(2)}) %collective-permute-start.33) | collective-permute-done | bytes 1048608 | tf_op jit(solution)/shard_map/ppermute | solution.py:464
  317.2 5.2 %convolution_convert_fusion = bf16[1024,2048]{1,0:T(8,128)(2,1)S(1)} fusion(bf16[1024,2048]{1,0:T(8,128)(2,1)S(1)} %copy-done.48, bf16[512,1024]{1,0:T(8,128)(2,1)S(1)} %copy-done.37, bf16[512,1024]{1,0:T(8,128)(2,1)S(1)} %copy-done.25), kind=kOutput, calls=%fused_computation.5 | convolution fusion | flops 4301258752 | bytes 10485760 | tf_op jit(solution)/shard_map/dot_general | solution.py:33
  332.7 2.4 collective-permute-start.32
  335.1 16.2 %collective-permute-done.37 = bf16[4,2,32,2048]{3,2,0,1:T(8,128)(2,1)} collective-permute-done((bf16[4,2,32,2048]{3,2,0,1:T(8,128)(2,1)}, bf16[4,2,32,2048]{3,2,0,1:T(8,128)(2,1)}, u32[]{:S(2)}, u32[]{:S(2)}) %collective-permute-start.37) | collective-permute-done | bytes 1048608 | tf_op jit(solution)/shard_map/ppermute | solution.py:464
  358.6 3.8 convolution_convert_fusion.5.grad_ref
  362.4 3.5 convolution_convert_fusion.4
  370.9 11.7 %shard_map.258 = (bf16[1024,768]{1,0:T(8,128)(2,1)S(1)}, f32[8,256]{1,0:T(8,128)S(1)}) custom-call(s32[2,4]{1,0:T(2,128)S(1)} %pad_add_fusion.1.bounds, bf16[1024,1536]{1,0:T(8,128)(2,1)S(1)} %copy-done.4, bf16[1024,1536]{1,0:T(8,128)(2,1)S(1)} %copy-done.4, bf16[1024,512]{1,0:T(8,128)(2,1)S(1)} %get-tuple-element.129.out_ref, ...), custom_call_target="tpu_custom_call" | custom-call | flops 2684354560 | bytes 12582912 | tf_op jit(solution)/shard_map/pallas_call | solution.py:782
  382.7 1.9 collective-permute-done.42
  385.4 4.4 collective-permute-start.44
  393.6 11.9 %shard_map.259 = (bf16[1024,768]{1,0:T(8,128)(2,1)S(1)}, f32[8,256]{1,0:T(8,128)S(1)}) custom-call(s32[2,4]{1,0:T(2,128)S(1)} %pad_add_fusion.1.bounds, bf16[1024,1536]{1,0:T(8,128)(2,1)S(1)} %copy-done.4, bf16[1024,1536]{1,0:T(8,128)(2,1)S(1)} %copy-done.4, bf16[1024,512]{1,0:T(8,128)(2,1)S(1)} %get-tuple-element.129.out_ref, ...), custom_call_target="tpu_custom_call" | custom-call | flops 2684354560 | bytes 12582912 | tf_op jit(solution)/shard_map/pallas_call | solution.py:782
  405.6 3.9 collective-permute-done.47
  411.4 1.9 convolution_convert_fusion.3
  414.3 1.9 convolution_convert_fusion.2
  419.2 2.3 collective-permute-start.52
  425.2 6.9 %collective-permute-done.53 = bf16[2,64,512]{2,1,0:T(8,128)(2,1)S(1)} collective-permute-done((bf16[2,64,512]{2,1,0:T(8,128)(2,1)S(1)}, bf16[2,64,512]{2,1,0:T(8,128)(2,1)S(1)}, u32[]{:S(2)}, u32[]{:S(2)}) %collective-permute-start.53) | collective-permute-done | bytes 131104 | tf_op jit(solution)/shard_map/ppermute | solution.py:464
  432.8 2.6 collective-permute-done.54
  438.9 2.4 collective-permute-start.57
  443.6 5.1 %collective-permute-start.62 = (bf16[512,1024]{1,0:T(8,128)(2,1)S(1)}, bf16[512,1024]{1,0:T(8,128)(2,1)S(1)}, u32[]{:S(2)}, u32[]{:S(2)}) collective-permute-start(bf16[512,1024]{1,0:T(8,128)(2,1)S(1)} %add_convert_fusion.1), channel_id=1, source_target_pairs={{0,0},{1,2},{2,1},{3,3},{4,4},{5,6},{6,5},{7,7},{8,8},{9,10},{10,9... | collective-permute-start | bytes 3145736 | tf_op jit(solution)/shard_map/ppermute | solution.py:464
  450.0 3.4 collective-permute-done.60
  453.4 4.3 collective-permute-done.59
  457.7 3.5 collective-permute-done.62
  461.4 3.6 collective-permute-start.65
  465.1 2.3 collective-permute-start.63
  467.6 6.7 %collective-permute-done.64 = bf16[584,128]{1,0:T(8,128)(2,1)S(1)} collective-permute-done((bf16[584,128]{1,0:T(8,128)(2,1)S(1)}, bf16[584,128]{1,0:T(8,128)(2,1)S(1)}, u32[]{:S(2)}, u32[]{:S(2)}) %collective-permute-start.64) | collective-permute-done | bytes 149536 | tf_op jit(solution)/shard_map/ppermute | solution.py:464
  474.4 2.8 collective-permute-start.66
  479.2 2.9 collective-permute-done.66
  488.4 2.3 copy.165
  (452 shorter events, 125.2 us)
Async XLA Ops:
  1.7 9.5 %collective-permute-start = (bf16[64,1536]{1,0:T(8,128)(2,1)S(1)}, bf16[64,1536]{1,0:T(8,128)(2,1)S(1)}, u32[]{:S(2)}, u32[]{:S(2)}) collective-permute-start(bf16[64,1536]{1,0:T(8,128)(2,1)S(1)} %slice_dynamic-update-slice_fusion), channel_id=1, source_target_pairs={{0,0},{1,2},{2,1},{3,3},{4,4},{5,6},{6,5},{7,7},{8,8},{9,10},{10,9... | collective-permute-start | bytes 589832 | tf_op jit(solution)/shard_map/ppermute | solution.py:464
  6.2 5.0 %collective-permute-start.1 = (bf16[1024,1024]{1,0:T(8,128)(2,1)}, bf16[1024,1024]{1,0:T(8,128)(2,1)}, u32[]{:S(2)}, u32[]{:S(2)}) collective-permute-start(bf16[1024,1024]{1,0:T(8,128)(2,1)} %param.15), channel_id=1, source_target_pairs={{0,2},{2,0},{1,3},{3,1},{4,6},{6,4},{5,7},{7,5},{8,10},{10,8},{9,1... | collective-permute-start | bytes 6291464 | tf_op jit(solution)/shard_map/ppermute | solution.py:464
  13.1 24.7 %collective-permute-start.9 = (bf16[64,4736]{1,0:T(8,128)(2,1)S(1)}, bf16[64,4736]{1,0:T(8,128)(2,1)}, u32[]{:S(2)}, u32[]{:S(2)}) collective-permute-start(bf16[64,4736]{1,0:T(8,128)(2,1)S(1)} %fusion.39), channel_id=1, source_target_pairs={{0,0},{1,2},{2,1},{3,3},{4,4},{5,6},{6,5},{7,7},{8,8},{9,10},{10,9... | collective-permute-start | bytes 1818632 | tf_op jit(solution)/shard_map/ppermute | solution.py:464
  17.0 7.3 %collective-permute-start.3 = (bf16[64,1536]{1,0:T(8,128)(2,1)S(1)}, bf16[64,1536]{1,0:T(8,128)(2,1)S(1)}, u32[]{:S(2)}, u32[]{:S(2)}) collective-permute-start(bf16[64,1536]{1,0:T(8,128)(2,1)S(1)} %collective-permute-done), channel_id=1, source_target_pairs={{0,24},{24,0},{8,16},{16,8},{1,25},{25,1},{9,17},{17,9},{2,26},{26... | collective-permute-start | bytes 589832 | tf_op jit(solution)/shard_map/ppermute | solution.py:464
  24.4 13.2 %collective-permute-start.4 = (bf16[2,64,1536]{2,1,0:T(8,128)(2,1)S(1)}, bf16[2,64,1536]{2,1,0:T(8,128)(2,1)S(1)}, u32[]{:S(2)}, u32[]{:S(2)}) collective-permute-start(bf16[2,64,1536]{2,1,0:T(8,128)(2,1)S(1)} %maximum_select_fusion.22), channel_id=1, source_target_pairs={{0,8},{8,0},{16,24},{24,16},{1,9},{9,1},{17,25},{25,17},{2,10},{10... | collective-permute-start | bytes 1179656 | tf_op jit(solution)/shard_map/ppermute | solution.py:464
  38.8 11.2 %collective-permute-start.10 = (bf16[64,2688]{1,0:T(8,128)(2,1)S(1)}, bf16[64,2688]{1,0:T(8,128)(2,1)S(1)}, u32[]{:S(2)}, u32[]{:S(2)}) collective-permute-start(bf16[64,2688]{1,0:T(8,128)(2,1)S(1)} %get-tuple-element.292), channel_id=1, source_target_pairs={{0,24},{24,0},{8,16},{16,8},{1,25},{25,1},{9,17},{17,9},{2,26},{26... | collective-permute-start | bytes 1032200 | tf_op jit(solution)/shard_map/ppermute | solution.py:464
  40.7 16.4 %collective-permute-start.5 = (bf16[4,32,1536]{2,1,0:T(8,128)(2,1)S(1)}, bf16[4,32,1536]{2,1,0:T(8,128)(2,1)S(1)}, u32[]{:S(2)}, u32[]{:S(2)}) collective-permute-start(bf16[4,32,1536]{2,1,0:T(8,128)(2,1)S(1)} %get-tuple-element.284), channel_id=1, source_target_pairs={{0,4},{4,0},{1,5},{5,1},{2,6},{6,2},{3,7},{7,3},{8,12},{12,8},{9,1... | collective-permute-start | bytes 1179656 | tf_op jit(solution)/shard_map/ppermute | solution.py:464
  42.0 15.1 %collective-permute-start.6 = (bf16[4,32,1536]{2,1,0:T(8,128)(2,1)S(1)}, bf16[4,32,1536]{2,1,0:T(8,128)(2,1)S(1)}, u32[]{:S(2)}, u32[]{:S(2)}) collective-permute-start(bf16[4,32,1536]{2,1,0:T(8,128)(2,1)S(1)} %get-tuple-element.283), channel_id=1, source_target_pairs={{0,1},{1,0},{2,3},{3,2},{4,5},{5,4},{6,7},{7,6},{8,9},{9,8},{10,11... | collective-permute-start | bytes 1179656 | tf_op jit(solution)/shard_map/ppermute | solution.py:464
  50.1 21.5 %collective-permute-start.11 = (bf16[2,64,2688]{2,1,0:T(8,128)(2,1)S(1)}, bf16[2,64,2688]{2,1,0:T(8,128)(2,1)S(1)}, u32[]{:S(2)}, u32[]{:S(2)}) collective-permute-start(bf16[2,64,2688]{2,1,0:T(8,128)(2,1)S(1)} %maximum_select_fusion.19), channel_id=1, source_target_pairs={{0,8},{8,0},{16,24},{24,16},{1,9},{9,1},{17,25},{25,17},{2,10},{10... | collective-permute-start | bytes 2064392 | tf_op jit(solution)/shard_map/ppermute | solution.py:464
  57.3 19.7 %collective-permute-start.7 = (bf16[4,2,32,1536]{3,2,0,1:T(8,128)(2,1)S(1)}, bf16[4,2,32,1536]{3,2,0,1:T(8,128)(2,1)S(1)}, u32[]{:S(2)}, u32[]{:S(2)}) collective-permute-start(bf16[4,2,32,1536]{3,2,0,1:T(8,128)(2,1)S(1)} %maximum_select_fusion.17), channel_id=1, source_target_pairs={{0,1},{1,0},{2,3},{3,2},{4,5},{5,4},{6,7},{7,6},{8,9},{9,8},{10,11... | collective-permute-start | bytes 2359304 | tf_op jit(solution)/shard_map/ppermute | solution.py:464
  57.4 19.5 %collective-permute-start.8 = (bf16[4,2,32,1536]{3,2,1,0:T(8,128)(2,1)S(1)}, bf16[4,2,32,1536]{3,2,1,0:T(8,128)(2,1)S(1)}, u32[]{:S(2)}, u32[]{:S(2)}) collective-permute-start(bf16[4,2,32,1536]{3,2,1,0:T(8,128)(2,1)S(1)} %maximum_select_fusion.18), channel_id=1, source_target_pairs={{0,4},{4,0},{1,5},{5,1},{2,6},{6,2},{3,7},{7,3},{8,12},{12,8},{9,1... | collective-permute-start | bytes 2359304 | tf_op jit(solution)/shard_map/ppermute | solution.py:464
  72.0 9.5 %collective-permute-start.12 = (bf16[64,2048]{1,0:T(8,128)(2,1)S(1)}, bf16[64,2048]{1,0:T(8,128)(2,1)S(1)}, u32[]{:S(2)}, u32[]{:S(2)}) collective-permute-start(bf16[64,2048]{1,0:T(8,128)(2,1)S(1)} %slice.390), channel_id=1, source_target_pairs={{0,24},{24,0},{8,16},{16,8},{1,25},{25,1},{9,17},{17,9},{2,26},{26... | collective-permute-start | bytes 786440 | tf_op jit(solution)/shard_map/ppermute | solution.py:464
  75.7 15.4 %collective-permute-start.13 = (bf16[4,32,2688]{2,1,0:T(8,128)(2,1)S(1)}, bf16[4,32,2688]{2,1,0:T(8,128)(2,1)S(1)}, u32[]{:S(2)}, u32[]{:S(2)}) collective-permute-start(bf16[4,32,2688]{2,1,0:T(8,128)(2,1)S(1)} %get-tuple-element.274), channel_id=1, source_target_pairs={{0,4},{4,0},{1,5},{5,1},{2,6},{6,2},{3,7},{7,3},{8,12},{12,8},{9,1... | collective-permute-start | bytes 2064392 | tf_op jit(solution)/shard_map/ppermute | solution.py:464
  76.9 15.1 %collective-permute-start.14 = (bf16[4,32,2688]{2,1,0:T(8,128)(2,1)S(1)}, bf16[4,32,2688]{2,1,0:T(8,128)(2,1)S(1)}, u32[]{:S(2)}, u32[]{:S(2)}) collective-permute-start(bf16[4,32,2688]{2,1,0:T(8,128)(2,1)S(1)} %get-tuple-element.273), channel_id=1, source_target_pairs={{0,1},{1,0},{2,3},{3,2},{4,5},{5,4},{6,7},{7,6},{8,9},{9,8},{10,11... | collective-permute-start | bytes 2064392 | tf_op jit(solution)/shard_map/ppermute | solution.py:464
  92.3 40.8 %collective-permute-start.16 = (bf16[4,2,32,2688]{3,2,0,1:T(8,128)(2,1)S(1)}, bf16[4,2,32,2688]{3,2,0,1:T(8,128)(2,1)S(1)}, u32[]{:S(2)}, u32[]{:S(2)}) collective-permute-start(bf16[4,2,32,2688]{3,2,0,1:T(8,128)(2,1)S(1)} %maximum_select_fusion.9), channel_id=1, source_target_pairs={{0,1},{1,0},{2,3},{3,2},{4,5},{5,4},{6,7},{7,6},{8,9},{9,8},{10,11... | collective-permute-start | bytes 4128776 | tf_op jit(solution)/shard_map/ppermute | solution.py:464
  92.9 40.2 %collective-permute-start.17 = (bf16[4,2,32,2688]{3,2,0,1:T(8,128)(2,1)S(1)}, bf16[4,2,32,2688]{3,2,0,1:T(8,128)(2,1)S(1)}, u32[]{:S(2)}, u32[]{:S(2)}) collective-permute-start(bf16[4,2,32,2688]{3,2,0,1:T(8,128)(2,1)S(1)} %maximum_select_fusion.10), channel_id=1, source_target_pairs={{0,4},{4,0},{1,5},{5,1},{2,6},{6,2},{3,7},{7,3},{8,12},{12,8},{9,1... | collective-permute-start | bytes 4128776 | tf_op jit(solution)/shard_map/ppermute | solution.py:464
  93.3 10.5 %collective-permute-start.15 = (bf16[2,64,2048]{2,1,0:T(8,128)(2,1)S(1)}, bf16[2,64,2048]{2,1,0:T(8,128)(2,1)S(1)}, u32[]{:S(2)}, u32[]{:S(2)}) collective-permute-start(bf16[2,64,2048]{2,1,0:T(8,128)(2,1)S(1)} %maximum_select_fusion.20), channel_id=1, source_target_pairs={{0,8},{8,0},{16,24},{24,16},{1,9},{9,1},{17,25},{25,17},{2,10},{10... | collective-permute-start | bytes 1572872 | tf_op jit(solution)/shard_map/ppermute | solution.py:464
  105.2 27.9 %collective-permute-start.18 = (bf16[4,32,2048]{2,1,0:T(8,128)(2,1)S(1)}, bf16[4,32,2048]{2,1,0:T(8,128)(2,1)S(1)}, u32[]{:S(2)}, u32[]{:S(2)}) collective-permute-start(bf16[4,32,2048]{2,1,0:T(8,128)(2,1)S(1)} %get-tuple-element.278), channel_id=1, source_target_pairs={{0,4},{4,0},{1,5},{5,1},{2,6},{6,2},{3,7},{7,3},{8,12},{12,8},{9,1... | collective-permute-start | bytes 1572872 | tf_op jit(solution)/shard_map/ppermute | solution.py:464
  106.4 26.7 %collective-permute-start.19 = (bf16[4,32,2048]{2,1,0:T(8,128)(2,1)S(1)}, bf16[4,32,2048]{2,1,0:T(8,128)(2,1)S(1)}, u32[]{:S(2)}, u32[]{:S(2)}) collective-permute-start(bf16[4,32,2048]{2,1,0:T(8,128)(2,1)S(1)} %get-tuple-element.277), channel_id=1, source_target_pairs={{0,1},{1,0},{2,3},{3,2},{4,5},{5,4},{6,7},{7,6},{8,9},{9,8},{10,11... | collective-permute-start | bytes 1572872 | tf_op jit(solution)/shard_map/ppermute | solution.py:464
  140.3 6.3 %collective-permute-start.20 = (bf16[512,1024]{1,0:T(8,128)(2,1)}, bf16[512,1024]{1,0:T(8,128)(2,1)}, u32[]{:S(2)}, u32[]{:S(2)}) collective-permute-start(bf16[512,1024]{1,0:T(8,128)(2,1)} %convolution_convert_fusion.6), channel_id=1, source_target_pairs={{0,2},{2,0},{1,3},{3,1},{4,6},{6,4},{5,7},{7,5},{8,10},{10,8},{9,1... | collective-permute-start | bytes 3145736 | tf_op jit(solution)/shard_map/ppermute | solution.py:469
  149.3 5.0 %collective-permute-start.21 = (bf16[512,1024]{1,0:T(8,128)(2,1)S(1)}, bf16[512,1024]{1,0:T(8,128)(2,1)S(1)}, u32[]{:S(2)}, u32[]{:S(2)}) collective-permute-start(bf16[512,1024]{1,0:T(8,128)(2,1)S(1)} %fusion.10), channel_id=1, source_target_pairs={{0,2},{2,0},{1,3},{3,1},{4,6},{6,4},{5,7},{7,5},{8,10},{10,8},{9,1... | collective-permute-start | bytes 3145736 | tf_op jit(solution)/shard_map/ppermute | solution.py:469
  152.8 24.4 %collective-permute-start.23 = (bf16[4,2,32,2048]{3,2,0,1:T(8,128)(2,1)S(1)}, bf16[4,2,32,2048]{3,2,0,1:T(8,128)(2,1)S(1)}, u32[]{:S(2)}, u32[]{:S(2)}) collective-permute-start(bf16[4,2,32,2048]{3,2,0,1:T(8,128)(2,1)S(1)} %maximum_select_fusion.13), channel_id=1, source_target_pairs={{0,1},{1,0},{2,3},{3,2},{4,5},{5,4},{6,7},{7,6},{8,9},{9,8},{10,11... | collective-permute-start | bytes 3145736 | tf_op jit(solution)/shard_map/ppermute | solution.py:464
  154.0 24.1 %collective-permute-start.24 = (bf16[4,2,32,2048]{3,2,1,0:T(8,128)(2,1)S(1)}, bf16[4,2,32,2048]{3,2,1,0:T(8,128)(2,1)S(1)}, u32[]{:S(2)}, u32[]{:S(2)}) collective-permute-start(bf16[4,2,32,2048]{3,2,1,0:T(8,128)(2,1)S(1)} %maximum_select_fusion.14), channel_id=1, source_target_pairs={{0,4},{4,0},{1,5},{5,1},{2,6},{6,2},{3,7},{7,3},{8,12},{12,8},{9,1... | collective-permute-start | bytes 3145736 | tf_op jit(solution)/shard_map/ppermute | solution.py:464
  183.4 16.3 %collective-permute-start.27 = (bf16[512,1024]{1,0:T(8,128)(2,1)}, bf16[512,1024]{1,0:T(8,128)(2,1)S(1)}, u32[]{:S(2)}, u32[]{:S(2)}) collective-permute-start(bf16[512,1024]{1,0:T(8,128)(2,1)} %param.29), channel_id=1, source_target_pairs={{0,0},{1,2},{2,1},{3,3},{4,4},{5,6},{6,5},{7,7},{8,8},{9,10},{10,9... | collective-permute-start | bytes 3145736 | tf_op jit(solution)/shard_map/ppermute | solution.py:1147
  194.3 16.7 %all-to-all-start = ((bf16[16,128,128]{2,1,0:T(8,128)(2,1)}), bf16[16,128,128]{2,1,0:T(8,128)(2,1)S(1)}, u32[]{:S(2)}, u32[]{:S(2)}) async-start(bf16[16,128,128]{2,1,0:T(8,128)(2,1)} %broadcast_in_dim.46), calls=%async_computation | async-start | bytes 1048576 | tf_op jit(solution)/shard_map/all_to_all | solution.py:1144
  219.5 12.1 %all-to-all-start.1 = ((f32[16,8,128]{2,1,0:T(8,128)}), f32[16,8,128]{2,1,0:T(8,128)S(1)}, u32[]{:S(2)}, u32[]{:S(2)}) async-start(f32[16,8,128]{2,1,0:T(8,128)} %broadcast_in_dim.47), calls=%async_computation.1 | async-start | bytes 131072 | tf_op jit(solution)/shard_map/all_to_all | solution.py:1165
  225.1 19.8 %collective-permute-start.28 = (bf16[512,1024]{1,0:T(8,128)(2,1)}, bf16[512,1024]{1,0:T(8,128)(2,1)}, u32[]{:S(2)}, u32[]{:S(2)}) collective-permute-start(bf16[512,1024]{1,0:T(8,128)(2,1)} %add_convert_fusion.3), channel_id=1, source_target_pairs={{0,0},{1,2},{2,1},{3,3},{4,4},{5,6},{6,5},{7,7},{8,8},{9,10},{10,9... | collective-permute-start | bytes 3145736 | tf_op jit(solution)/shard_map/ppermute | solution.py:1185
  244.9 21.8 %all-to-all-start.2 = ((bf16[16,128,128]{2,1,0:T(8,128)(2,1)}), bf16[16,128,128]{2,1,0:T(8,128)(2,1)S(1)}, u32[]{:S(2)}, u32[]{:S(2)}) async-start(bf16[16,128,128]{2,1,0:T(8,128)(2,1)} %bitcast.57), calls=%async_computation.2 | async-start | bytes 1048576 | tf_op jit(solution)/shard_map/all_to_all | solution.py:1187
  266.9 5.1 %collective-permute-start.29 = (f32[512,128]{1,0:T(8,128)S(1)}, f32[512,128]{1,0:T(8,128)S(1)}, u32[]{:S(2)}, u32[]{:S(2)}) collective-permute-start(f32[512,128]{1,0:T(8,128)S(1)} %constant_dynamic-slice_fusion.11), channel_id=1, source_target_pairs={{0,2},{2,0},{1,3},{3,1},{4,6},{6,4},{5,7},{7,5},{8,10},{10,8},{9,1... | collective-permute-start | bytes 786440 | tf_op jit(solution)/shard_map/ppermute | solution.py:469
  275.6 4.9 collective-permute-start.30
  287.5 24.7 %collective-permute-start.33 = (bf16[4,2,32,2048]{3,2,0,1:T(8,128)(2,1)S(1)}, bf16[4,2,32,2048]{3,2,0,1:T(8,128)(2,1)S(1)}, u32[]{:S(2)}, u32[]{:S(2)}) collective-permute-start(bf16[4,2,32,2048]{3,2,0,1:T(8,128)(2,1)S(1)} %bitcast.317), channel_id=1, source_target_pairs={{0,4},{4,0},{1,5},{5,1},{2,6},{6,2},{3,7},{7,3},{8,12},{12,8},{9,1... | collective-permute-start | bytes 3145736 | tf_op jit(solution)/shard_map/ppermute | solution.py:464
  288.8 24.4 %collective-permute-start.34 = (bf16[4,2,32,2048]{3,2,0,1:T(8,128)(2,1)S(1)}, bf16[4,2,32,2048]{3,2,0,1:T(8,128)(2,1)S(1)}, u32[]{:S(2)}, u32[]{:S(2)}) collective-permute-start(bf16[4,2,32,2048]{3,2,0,1:T(8,128)(2,1)S(1)} %bitcast.318), channel_id=1, source_target_pairs={{0,1},{1,0},{2,3},{3,2},{4,5},{5,4},{6,7},{7,6},{8,9},{9,8},{10,11... | collective-permute-start | bytes 3145736 | tf_op jit(solution)/shard_map/ppermute | solution.py:464
  303.0 26.5 %collective-permute-start.31 = (bf16[512,1024]{1,0:T(8,128)(2,1)S(1)}, bf16[512,1024]{1,0:T(8,128)(2,1)S(1)}, u32[]{:S(2)}, u32[]{:S(2)}) collective-permute-start(bf16[512,1024]{1,0:T(8,128)(2,1)S(1)} %fusion.14), channel_id=1, source_target_pairs={{0,2},{2,0},{1,3},{3,1},{4,6},{6,4},{5,7},{7,5},{8,10},{10,8},{9,1... | collective-permute-start | bytes 3145736 | tf_op jit(solution)/shard_map/ppermute | solution.py:469
  314.5 20.6 %collective-permute-start.35 = (bf16[4,32,2048]{2,1,0:T(8,128)(2,1)}, bf16[4,32,2048]{2,1,0:T(8,128)(2,1)}, u32[]{:S(2)}, u32[]{:S(2)}) collective-permute-start(bf16[4,32,2048]{2,1,0:T(8,128)(2,1)} %fusion.40), channel_id=1, source_target_pairs={{0,1},{1,0},{2,3},{3,2},{4,5},{5,4},{6,7},{7,6},{8,9},{9,8},{10,11... | collective-permute-start | bytes 1572872 | tf_op jit(solution)/shard_map/ppermute | solution.py:464
  316.7 18.4 %collective-permute-start.36 = (bf16[4,32,2048]{2,1,0:T(8,128)(2,1)}, bf16[4,32,2048]{2,1,0:T(8,128)(2,1)}, u32[]{:S(2)}, u32[]{:S(2)}) collective-permute-start(bf16[4,32,2048]{2,1,0:T(8,128)(2,1)} %fusion.41), channel_id=1, source_target_pairs={{0,4},{4,0},{1,5},{5,1},{2,6},{6,2},{3,7},{7,3},{8,12},{12,8},{9,1... | collective-permute-start | bytes 1572872 | tf_op jit(solution)/shard_map/ppermute | solution.py:464
  325.2 26.2 %collective-permute-start.37 = (bf16[4,2,32,2048]{3,2,0,1:T(8,128)(2,1)}, bf16[4,2,32,2048]{3,2,0,1:T(8,128)(2,1)}, u32[]{:S(2)}, u32[]{:S(2)}) collective-permute-start(bf16[4,2,32,2048]{3,2,0,1:T(8,128)(2,1)} %bitcast.272), channel_id=1, source_target_pairs={{0,4},{4,0},{1,5},{5,1},{2,6},{6,2},{3,7},{7,3},{8,12},{12,8},{9,1... | collective-permute-start | bytes 3145736 | tf_op jit(solution)/shard_map/ppermute | solution.py:464
  328.3 23.0 %collective-permute-start.38 = (bf16[4,2,32,2048]{3,2,0,1:T(8,128)(2,1)}, bf16[4,2,32,2048]{3,2,0,1:T(8,128)(2,1)}, u32[]{:S(2)}, u32[]{:S(2)}) collective-permute-start(bf16[4,2,32,2048]{3,2,0,1:T(8,128)(2,1)} %bitcast.271), channel_id=1, source_target_pairs={{0,1},{1,0},{2,3},{3,2},{4,5},{5,4},{6,7},{7,6},{8,9},{9,8},{10,11... | collective-permute-start | bytes 3145736 | tf_op jit(solution)/shard_map/ppermute | solution.py:464
  332.7 25.9 %collective-permute-start.32 = (bf16[512,1024]{1,0:T(8,128)(2,1)}, bf16[512,1024]{1,0:T(8,128)(2,1)}, u32[]{:S(2)}, u32[]{:S(2)}) collective-permute-start(bf16[512,1024]{1,0:T(8,128)(2,1)} %get-tuple-element.240), channel_id=1, source_target_pairs={{0,2},{2,0},{1,3},{3,1},{4,6},{6,4},{5,7},{7,5},{8,10},{10,8},{9,1... | collective-permute-start | bytes 3145736 | tf_op jit(solution)/shard_map/ppermute | solution.py:469
  366.3 18.2 %collective-permute-start.39 = (bf16[2,64,2048]{2,1,0:T(8,128)(2,1)S(1)}, bf16[2,64,2048]{2,1,0:T(8,128)(2,1)S(1)}, u32[]{:S(2)}, u32[]{:S(2)}) collective-permute-start(bf16[2,64,2048]{2,1,0:T(8,128)(2,1)S(1)} %select_convert_fusion.1), channel_id=1, source_target_pairs={{0,8},{8,0},{16,24},{24,16},{1,9},{9,1},{17,25},{25,17},{2,10},{10... | collective-permute-start | bytes 1572872 | tf_op jit(solution)/shard_map/ppermute | solution.py:464
  367.5 17.1 %collective-permute-start.40 = (bf16[4,32,2048]{2,1,0:T(8,128)(2,1)S(1)}, bf16[4,32,2048]{2,1,0:T(8,128)(2,1)S(1)}, u32[]{:S(2)}, u32[]{:S(2)}) collective-permute-start(bf16[4,32,2048]{2,1,0:T(8,128)(2,1)S(1)} %fusion.42), channel_id=1, source_target_pairs={{0,1},{1,0},{2,3},{3,2},{4,5},{5,4},{6,7},{7,6},{8,9},{9,8},{10,11... | collective-permute-start | bytes 1572872 | tf_op jit(solution)/shard_map/ppermute | solution.py:464
  368.8 15.7 %collective-permute-start.41 = (bf16[4,32,2048]{2,1,0:T(8,128)(2,1)S(1)}, bf16[4,32,2048]{2,1,0:T(8,128)(2,1)S(1)}, u32[]{:S(2)}, u32[]{:S(2)}) collective-permute-start(bf16[4,32,2048]{2,1,0:T(8,128)(2,1)S(1)} %fusion.43), channel_id=1, source_target_pairs={{0,4},{4,0},{1,5},{5,1},{2,6},{6,2},{3,7},{7,3},{8,12},{12,8},{9,1... | collective-permute-start | bytes 1572872 | tf_op jit(solution)/shard_map/ppermute | solution.py:464
  369.4 15.1 %collective-permute-start.42 = (bf16[4,2,32,512]{3,2,0,1:T(8,128)(2,1)S(1)}, bf16[4,2,32,512]{3,2,0,1:T(8,128)(2,1)S(1)}, u32[]{:S(2)}, u32[]{:S(2)}) collective-permute-start(bf16[4,2,32,512]{3,2,0,1:T(8,128)(2,1)S(1)} %dynamic-slice_bitcast_fusion.3), channel_id=1, source_target_pairs={{0,4},{4,0},{1,5},{5,1},{2,6},{6,2},{3,7},{7,3},{8,12},{12,8},{9,1... | collective-permute-start | bytes 786440 | tf_op jit(solution)/shard_map/ppermute | solution.py:464
  370.6 14.0 %collective-permute-start.43 = (bf16[4,2,32,512]{3,2,0,1:T(8,128)(2,1)S(1)}, bf16[4,2,32,512]{3,2,0,1:T(8,128)(2,1)S(1)}, u32[]{:S(2)}, u32[]{:S(2)}) collective-permute-start(bf16[4,2,32,512]{3,2,0,1:T(8,128)(2,1)S(1)} %dynamic-slice_bitcast_fusion.2), channel_id=1, source_target_pairs={{0,1},{1,0},{2,3},{3,2},{4,5},{5,4},{6,7},{7,6},{8,9},{9,8},{10,11... | collective-permute-start | bytes 786440 | tf_op jit(solution)/shard_map/ppermute | solution.py:464
  385.4 5.9 %collective-permute-start.44 = (f32[16,4]{1,0:T(8,128)S(1)}, f32[16,4]{1,0:T(8,128)S(1)}, u32[]{:S(2)}, u32[]{:S(2)}) collective-permute-start(f32[16,4]{1,0:T(8,128)S(1)} %reshape.820), channel_id=1, source_target_pairs={{0,2},{2,0},{1,3},{3,1},{4,6},{6,4},{5,7},{7,5},{8,10},{10,8},{9,1... | collective-permute-start | bytes 776 | tf_op jit(solution)/shard_map/ppermute | solution.py:469
  389.8 15.8 %collective-permute-start.46 = (bf16[64,2048]{1,0:T(8,128)(2,1)S(1)}, bf16[64,2048]{1,0:T(8,128)(2,1)S(1)}, u32[]{:S(2)}, u32[]{:S(2)}) collective-permute-start(bf16[64,2048]{1,0:T(8,128)(2,1)S(1)} %fusion.54), channel_id=1, source_target_pairs={{0,24},{24,0},{8,16},{16,8},{1,25},{25,1},{9,17},{17,9},{2,26},{26... | collective-permute-start | bytes 786440 | tf_op jit(solution)/shard_map/ppermute | solution.py:464
  390.6 18.9 %collective-permute-start.47 = (bf16[2,64,2048]{2,1,0:T(8,128)(2,1)S(1)}, bf16[2,64,2048]{2,1,0:T(8,128)(2,1)S(1)}, u32[]{:S(2)}, u32[]{:S(2)}) collective-permute-start(bf16[2,64,2048]{2,1,0:T(8,128)(2,1)S(1)} %select_convert_fusion), channel_id=1, source_target_pairs={{0,8},{8,0},{16,24},{24,16},{1,9},{9,1},{17,25},{25,17},{2,10},{10... | collective-permute-start | bytes 1572872 | tf_op jit(solution)/shard_map/ppermute | solution.py:464
  391.9 13.8 %collective-permute-start.48 = (bf16[4,32,512]{2,1,0:T(8,128)(2,1)S(1)}, bf16[4,32,512]{2,1,0:T(8,128)(2,1)S(1)}, u32[]{:S(2)}, u32[]{:S(2)}) collective-permute-start(bf16[4,32,512]{2,1,0:T(8,128)(2,1)S(1)} %fusion.62), channel_id=1, source_target_pairs={{0,1},{1,0},{2,3},{3,2},{4,5},{5,4},{6,7},{7,6},{8,9},{9,8},{10,11... | collective-permute-start | bytes 393224 | tf_op jit(solution)/shard_map/ppermute | solution.py:464
  392.2 13.4 %collective-permute-start.49 = (bf16[4,32,512]{2,1,0:T(8,128)(2,1)S(1)}, bf16[4,32,512]{2,1,0:T(8,128)(2,1)S(1)}, u32[]{:S(2)}, u32[]{:S(2)}) collective-permute-start(bf16[4,32,512]{2,1,0:T(8,128)(2,1)S(1)} %fusion.63), channel_id=1, source_target_pairs={{0,4},{4,0},{1,5},{5,1},{2,6},{6,2},{3,7},{7,3},{8,12},{12,8},{9,1... | collective-permute-start | bytes 393224 | tf_op jit(solution)/shard_map/ppermute | solution.py:464
  417.2 18.2 %collective-permute-start.50 = (bf16[4,2,32,1536]{3,2,0,1:T(8,128)(2,1)S(1)}, bf16[4,2,32,1536]{3,2,0,1:T(8,128)(2,1)S(1)}, u32[]{:S(2)}, u32[]{:S(2)}) collective-permute-start(bf16[4,2,32,1536]{3,2,0,1:T(8,128)(2,1)S(1)} %dynamic-slice_bitcast_fusion.1), channel_id=1, source_target_pairs={{0,4},{4,0},{1,5},{5,1},{2,6},{6,2},{3,7},{7,3},{8,12},{12,8},{9,1... | collective-permute-start | bytes 2359304 | tf_op jit(solution)/shard_map/ppermute | solution.py:464
  417.9 17.7 %collective-permute-start.51 = (bf16[4,2,32,1536]{3,2,0,1:T(8,128)(2,1)S(1)}, bf16[4,2,32,1536]{3,2,0,1:T(8,128)(2,1)S(1)}, u32[]{:S(2)}, u32[]{:S(2)}) collective-permute-start(bf16[4,2,32,1536]{3,2,0,1:T(8,128)(2,1)S(1)} %dynamic-slice_bitcast_fusion), channel_id=1, source_target_pairs={{0,1},{1,0},{2,3},{3,2},{4,5},{5,4},{6,7},{7,6},{8,9},{9,8},{10,11... | collective-permute-start | bytes 2359304 | tf_op jit(solution)/shard_map/ppermute | solution.py:464
  419.2 16.2 %collective-permute-start.52 = (bf16[64,2048]{1,0:T(8,128)(2,1)S(1)}, bf16[64,2048]{1,0:T(8,128)(2,1)S(1)}, u32[]{:S(2)}, u32[]{:S(2)}) collective-permute-start(bf16[64,2048]{1,0:T(8,128)(2,1)S(1)} %fusion.55), channel_id=1, source_target_pairs={{0,24},{24,0},{8,16},{16,8},{1,25},{25,1},{9,17},{17,9},{2,26},{26... | collective-permute-start | bytes 786440 | tf_op jit(solution)/shard_map/ppermute | solution.py:464
  421.6 10.6 %collective-permute-start.53 = (bf16[2,64,512]{2,1,0:T(8,128)(2,1)S(1)}, bf16[2,64,512]{2,1,0:T(8,128)(2,1)S(1)}, u32[]{:S(2)}, u32[]{:S(2)}) collective-permute-start(bf16[2,64,512]{2,1,0:T(8,128)(2,1)S(1)} %select_convert_fusion.6), channel_id=1, source_target_pairs={{0,8},{8,0},{16,24},{24,16},{1,9},{9,1},{17,25},{25,17},{2,10},{10... | collective-permute-start | bytes 393224 | tf_op jit(solution)/shard_map/ppermute | solution.py:464
  421.7 13.7 %collective-permute-start.54 = (bf16[584,128]{1,0:T(8,128)(2,1)S(1)}, bf16[584,128]{1,0:T(8,128)(2,1)S(1)}, u32[]{:S(2)}, u32[]{:S(2)}) collective-permute-start(bf16[584,128]{1,0:T(8,128)(2,1)S(1)} %convert_element_type.481), channel_id=1, source_target_pairs={{0,8},{8,0},{16,24},{24,16},{1,9},{9,1},{17,25},{25,17},{2,10},{10... | collective-permute-start | bytes 448520 | tf_op jit(solution)/shard_map/ppermute | solution.py:464
  432.2 10.2 %collective-permute-start.61 = (bf16[512,1024]{1,0:T(8,128)(2,1)S(1)}, bf16[512,1024]{1,0:T(8,128)(2,1)S(1)}, u32[]{:S(2)}, u32[]{:S(2)}) collective-permute-start(bf16[512,1024]{1,0:T(8,128)(2,1)S(1)} %add_convert_fusion.2), channel_id=1, source_target_pairs={{0,2},{2,0},{1,3},{3,1},{4,6},{6,4},{5,7},{7,5},{8,10},{10,8},{9,1... | collective-permute-start | bytes 3145736 | tf_op jit(solution)/shard_map/ppermute | solution.py:469
  435.9 12.9 %collective-permute-start.55 = (bf16[4,32,1536]{2,1,0:T(8,128)(2,1)S(1)}, bf16[4,32,1536]{2,1,0:T(8,128)(2,1)S(1)}, u32[]{:S(2)}, u32[]{:S(2)}) collective-permute-start(bf16[4,32,1536]{2,1,0:T(8,128)(2,1)S(1)} %fusion.49), channel_id=1, source_target_pairs={{0,1},{1,0},{2,3},{3,2},{4,5},{5,4},{6,7},{7,6},{8,9},{9,8},{10,11... | collective-permute-start | bytes 1179656 | tf_op jit(solution)/shard_map/ppermute | solution.py:464
  437.5 11.4 %collective-permute-start.56 = (bf16[4,32,1536]{2,1,0:T(8,128)(2,1)S(1)}, bf16[4,32,1536]{2,1,0:T(8,128)(2,1)S(1)}, u32[]{:S(2)}, u32[]{:S(2)}) collective-permute-start(bf16[4,32,1536]{2,1,0:T(8,128)(2,1)S(1)} %fusion.50), channel_id=1, source_target_pairs={{0,4},{4,0},{1,5},{5,1},{2,6},{6,2},{3,7},{7,3},{8,12},{12,8},{9,1... | collective-permute-start | bytes 1179656 | tf_op jit(solution)/shard_map/ppermute | solution.py:464
  438.9 9.9 %collective-permute-start.57 = (bf16[64,512]{1,0:T(8,128)(2,1)S(1)}, bf16[64,512]{1,0:T(8,128)(2,1)S(1)}, u32[]{:S(2)}, u32[]{:S(2)}) collective-permute-start(bf16[64,512]{1,0:T(8,128)(2,1)S(1)} %fusion.68), channel_id=1, source_target_pairs={{0,24},{24,0},{8,16},{16,8},{1,25},{25,1},{9,17},{17,9},{2,26},{26... | collective-permute-start | bytes 196616 | tf_op jit(solution)/shard_map/ppermute | solution.py:464
  441.3 7.5 %collective-permute-start.58 = (bf16[584,128]{1,0:T(8,128)(2,1)S(1)}, bf16[584,128]{1,0:T(8,128)(2,1)S(1)}, u32[]{:S(2)}, u32[]{:S(2)}) collective-permute-start(bf16[584,128]{1,0:T(8,128)(2,1)S(1)} %fusion.56), channel_id=1, source_target_pairs={{0,24},{24,0},{8,16},{16,8},{1,25},{25,1},{9,17},{17,9},{2,26},{26... | collective-permute-start | bytes 448520 | tf_op jit(solution)/shard_map/ppermute | solution.py:464
  443.6 17.6 %collective-permute-start.62 = (bf16[512,1024]{1,0:T(8,128)(2,1)S(1)}, bf16[512,1024]{1,0:T(8,128)(2,1)S(1)}, u32[]{:S(2)}, u32[]{:S(2)}) collective-permute-start(bf16[512,1024]{1,0:T(8,128)(2,1)S(1)} %add_convert_fusion.1), channel_id=1, source_target_pairs={{0,0},{1,2},{2,1},{3,3},{4,4},{5,6},{6,5},{7,7},{8,8},{9,10},{10,9... | collective-permute-start | bytes 3145736 | tf_op jit(solution)/shard_map/ppermute | solution.py:464
  449.2 8.6 %collective-permute-start.59 = (bf16[2,64,1536]{2,1,0:T(8,128)(2,1)S(1)}, bf16[2,64,1536]{2,1,0:T(8,128)(2,1)S(1)}, u32[]{:S(2)}, u32[]{:S(2)}) collective-permute-start(bf16[2,64,1536]{2,1,0:T(8,128)(2,1)S(1)} %select_convert_fusion.2), channel_id=1, source_target_pairs={{0,8},{8,0},{16,24},{24,16},{1,9},{9,1},{17,25},{25,17},{2,10},{10... | collective-permute-start | bytes 1179656 | tf_op jit(solution)/shard_map/ppermute | solution.py:464
  461.4 13.0 %collective-permute-start.65 = (bf16[64,4096]{1,0:T(8,128)(2,1)S(1)}, bf16[64,4096]{1,0:T(8,128)(2,1)S(1)}, u32[]{:S(2)}, u32[]{:S(2)}) collective-permute-start(bf16[64,4096]{1,0:T(8,128)(2,1)S(1)} %pad_maximum_fusion.17), channel_id=1, source_target_pairs={{0,0},{1,2},{2,1},{3,3},{4,4},{5,6},{6,5},{7,7},{8,8},{9,10},{10,9... | collective-permute-start | bytes 1572872 | tf_op jit(solution)/shard_map/ppermute | solution.py:464
  465.1 9.3 %collective-permute-start.63 = (bf16[64,1536]{1,0:T(8,128)(2,1)S(1)}, bf16[64,1536]{1,0:T(8,128)(2,1)S(1)}, u32[]{:S(2)}, u32[]{:S(2)}) collective-permute-start(bf16[64,1536]{1,0:T(8,128)(2,1)S(1)} %fusion.58), channel_id=1, source_target_pairs={{0,24},{24,0},{8,16},{16,8},{1,25},{25,1},{9,17},{17,9},{2,26},{26... | collective-permute-start | bytes 589832 | tf_op jit(solution)/shard_map/ppermute | solution.py:464
  467.5 6.8 %collective-permute-start.64 = (bf16[584,128]{1,0:T(8,128)(2,1)S(1)}, bf16[584,128]{1,0:T(8,128)(2,1)S(1)}, u32[]{:S(2)}, u32[]{:S(2)}) collective-permute-start(bf16[584,128]{1,0:T(8,128)(2,1)S(1)} %fusion.57), channel_id=1, source_target_pairs={{0,1},{1,0},{2,3},{3,2},{4,5},{5,4},{6,7},{7,6},{8,9},{9,8},{10,11... | collective-permute-start | bytes 448520 | tf_op jit(solution)/shard_map/ppermute | solution.py:464
  474.4 7.7 %collective-permute-start.66 = (bf16[64,2048]{1,0:T(8,128)(2,1)S(1)}, bf16[64,2048]{1,0:T(8,128)(2,1)S(1)}, u32[]{:S(2)}, u32[]{:S(2)}) collective-permute-start(bf16[64,2048]{1,0:T(8,128)(2,1)S(1)} %pad_maximum_fusion.20), channel_id=1, source_target_pairs={{0,0},{1,2},{2,1},{3,3},{4,4},{5,6},{6,5},{7,7},{8,8},{9,10},{10,9... | collective-permute-start | bytes 786440 | tf_op jit(solution)/shard_map/ppermute | solution.py:464
  (60 other events, 616.4 us)

commit v6 on v5

--- a/solution.py
+++ b/solution.py
@@ -1065,14 +1065,13 @@
     mid_line = whole_line(mid_pair, near, z)
     full_qkv = full_rows(qkv_parts, exchange(*last_moves(qkv_parts)), x, y)
     down_rows, mid_line = lax.optimization_barrier((down_rows, mid_line))
-    got = exchange((down_rows, "z", FAR), *first_moves(mid_line))
-    down_pair = far_pair(down_rows, got[0], z)
-    mid_parts = first_parts(mid_line, got[1:], x, y)
+    (far,) = exchange((down_rows, "z", FAR))
+    down_pair = far_pair(down_rows, far, z)
     (near,) = exchange((down_pair, "z", NEAR))
     down_line = whole_line(down_pair, near, z)
-    got = exchange(*last_moves(mid_parts), *first_moves(down_line))
-    full_mid = full_rows(mid_parts, got, x, y)
-    down_parts = first_parts(down_line, got[2:], x, y)
+    mid_parts = first_parts(mid_line, exchange(*first_moves(mid_line)), x, y)
+    full_mid = full_rows(mid_parts, exchange(*last_moves(mid_parts)), x, y)
+    down_parts = first_parts(down_line, exchange(*first_moves(down_line)), x, y)
     full_out = full_mid[:, up_wide : up_wide + half_width]
     pairs = full_mid[:, up_wide + half_width :].reshape(chip_count, 64, 128)
     pairs = pairs[:, 0, :half_queries].astype(jnp.int32).reshape(1, query_total)

time: 497 us -> 489 us (0.984)
  starting transfers between devices: 119 us -> 130 us
  waiting for transfers between devices: 161 us -> 154 us
  local copies, waits for them, and re-layouts: 43.9 us -> 38.2 us
  matrix products: 62.2 us -> 57 us
    ppermute x54, starting transfers between devices: 73.3 us -> 82.3 us  [exchange(): lax.ppermute(value, axis, steps)]
    ppermute x54, waiting for transfers between devices: 133 us -> 126 us  [exchange(): lax.ppermute(value, axis, steps)]
    unnamed x127 -> x109, local copies, waits for them, and re-layouts: 19.5 us -> 14.8 us
  transfers between devices with their start and end apart: 71 -> 71, of which waited for: 32 -> 31; matrix products, arithmetic and copies ran while one was open for 15% -> 15% of each run, Pallas kernels for 13% -> 13%
where the time goes in v6:
time: 489 us; the launch traced here: 484 us
  waiting for transfers between devices  154 us (31%)
  starting transfers between devices  130 us (27%)
  Pallas kernels  69.8 us (14%)
  matrix products  57 us (12%)
  local copies, waits for them, and re-layouts  38.2 us (8%)
  other arithmetic  31.3 us (6%)
    ppermute x54, waiting for transfers between devices, exchange(): lax.ppermute(value, axis, steps)  126 us
    ppermute x54, starting transfers between devices, exchange(): lax.ppermute(value, axis, steps)  82.3 us
    pallas_call x2, Pallas kernels, attend_back(): pl.pallas_call(partial(attend_back_kernel, group * heads), grid=(count //...  23.6 us
    dot_general x7, matrix products, contract_rows(): lax.dot_general(left, right, (((0,), (0,)), ((), ())), precision=precisio...  22.6 us
    ppermute x12, starting transfers between devices, swap(): return lax.ppermute(value, axis, SWAP)  20.3 us
    dot_general x12, matrix products, contract_cols(): lax.dot_general(left, right, (((1,), (1,)), ((), ())), precision=precisio...  17.3 us
    pallas_call x1, Pallas kernels, expand(): pl.pallas_call(expand_kernel, grid=(tiles,), in_specs=[pl.BlockSpec((coun...  16.3 us
    dot_general x4, matrix products, dot(): return jnp.dot(left, right, preferred_element_type=F32)  15.7 us
  transfers between devices with their start and end apart: 71, of which 31 were waited for; matrix products, arithmetic and copies ran while one was open for 15% of the time, Pallas kernels for 13%

profile of v6, /device:TPU:1, one launch (start us, length us, event | category | flops | bytes accessed | tf_op | source)
XLA Modules:
  0.0 483.8 jit_solution(17101369780941842531)
XLA Ops:
  1.7 4.5 collective-permute-start
  11.3 1.8 broadcast_select_fusion
  13.1 3.9 collective-permute-start.9
  17.0 3.4 collective-permute-start.3
  20.5 3.8 collective-permute-done.3
  24.4 3.7 collective-permute-start.4
  28.1 9.5 %collective-permute-done.4 = bf16[2,64,1536]{2,1,0:T(8,128)(2,1)S(1)} collective-permute-done((bf16[2,64,1536]{2,1,0:T(8,128)(2,1)S(1)}, bf16[2,64,1536]{2,1,0:T(8,128)(2,1)S(1)}, u32[]{:S(2)}, u32[]{:S(2)}) %collective-permute-start.4) | collective-permute-done | bytes 393248 | tf_op jit(solution)/shard_map/ppermute | solution.py:464
  43.0 7.0 %collective-permute-done.10 = bf16[64,2688]{1,0:T(8,128)(2,1)S(1)} collective-permute-done((bf16[64,2688]{1,0:T(8,128)(2,1)S(1)}, bf16[64,2688]{1,0:T(8,128)(2,1)S(1)}, u32[]{:S(2)}, u32[]{:S(2)}) %collective-permute-start.10) | collective-permute-done | bytes 344096 | tf_op jit(solution)/shard_map/ppermute | solution.py:464
  50.2 6.9 %collective-permute-start.11 = (bf16[2,64,2688]{2,1,0:T(8,128)(2,1)S(1)}, bf16[2,64,2688]{2,1,0:T(8,128)(2,1)S(1)}, u32[]{:S(2)}, u32[]{:S(2)}) collective-permute-start(bf16[2,64,2688]{2,1,0:T(8,128)(2,1)S(1)} %maximum_select_fusion.19), channel_id=1, source_target_pairs={{0,8},{8,0},{16,24},{24,16},{1,9},{9,1},{17,25},{25,17},{2,10},{10... | collective-permute-start | bytes 2064392 | tf_op jit(solution)/shard_map/ppermute | solution.py:464
  59.1 12.5 %collective-permute-done.11 = bf16[2,64,2688]{2,1,0:T(8,128)(2,1)S(1)} collective-permute-done((bf16[2,64,2688]{2,1,0:T(8,128)(2,1)S(1)}, bf16[2,64,2688]{2,1,0:T(8,128)(2,1)S(1)}, u32[]{:S(2)}, u32[]{:S(2)}) %collective-permute-start.11) | collective-permute-done | bytes 688160 | tf_op jit(solution)/shard_map/ppermute | solution.py:464
  73.7 3.2 collective-permute-start.12
  77.7 3.6 add_convert_fusion.own_ref.qkv_ref
  81.5 8.0 %collective-permute-start.13 = (bf16[2,64,2048]{2,1,0:T(8,128)(2,1)S(1)}, bf16[2,64,2048]{2,1,0:T(8,128)(2,1)S(1)}, u32[]{:S(2)}, u32[]{:S(2)}) collective-permute-start(bf16[2,64,2048]{2,1,0:T(8,128)(2,1)S(1)} %maximum_select_fusion.20), channel_id=1, source_target_pairs={{0,8},{8,0},{16,24},{24,16},{1,9},{9,1},{17,25},{25,17},{2,10},{10... | collective-permute-start | bytes 1572872 | tf_op jit(solution)/shard_map/ppermute | solution.py:464
  93.3 8.0 %collective-permute-done.13 = bf16[2,64,2048]{2,1,0:T(8,128)(2,1)S(1)} collective-permute-done((bf16[2,64,2048]{2,1,0:T(8,128)(2,1)S(1)}, bf16[2,64,2048]{2,1,0:T(8,128)(2,1)S(1)}, u32[]{:S(2)}, u32[]{:S(2)}) %collective-permute-start.13) | collective-permute-done | bytes 524320 | tf_op jit(solution)/shard_map/ppermute | solution.py:464
  101.6 10.4 %shard_map.254 = (bf16[1024,512]{1,0:T(8,128)(2,1)S(1)}, f32[8,1024]{1,0:T(8,128)S(1)}) custom-call(s32[2,4]{1,0:T(2,128)S(1)} %pad_add_fusion.1.bounds, bf16[1024,1536]{1,0:T(8,128)(2,1)S(1)} %add_convert_fusion.own_ref.qkv_ref, bf16[1024,1536]{1,0:T(8,128)(2,1)S(1)} %add_convert_fusion.own_ref.qkv_ref, s32[2,1024]{1,0:T(2,128)S(1)} %pad_add_fusion.spans), custom_call_target="tpu_custom_call" | custom-call | flops 2147483648 | bytes 12582912 | tf_op jit(solution)/shard_map/pallas_call | solution.py:679
  111.9 7.8 %collective-permute-done.16 = bf16[4,2,32,2688]{3,2,0,1:T(8,128)(2,1)S(1)} collective-permute-done((bf16[4,2,32,2688]{3,2,0,1:T(8,128)(2,1)S(1)}, bf16[4,2,32,2688]{3,2,0,1:T(8,128)(2,1)S(1)}, u32[]{:S(2)}, u32[]{:S(2)}) %collective-permute-start.16) | collective-permute-done | bytes 1376288 | tf_op jit(solution)/shard_map/ppermute | solution.py:464
  123.4 3.9 collective-permute-start.18
  132.2 8.9 %collective-permute-done.21 = bf16[4,32,2048]{2,1,0:T(8,128)(2,1)S(1)} collective-permute-done((bf16[4,32,2048]{2,1,0:T(8,128)(2,1)S(1)}, bf16[4,32,2048]{2,1,0:T(8,128)(2,1)S(1)}, u32[]{:S(2)}, u32[]{:S(2)}) %collective-permute-start.21) | collective-permute-done | bytes 524320 | tf_op jit(solution)/shard_map/ppermute | solution.py:464
  146.2 16.3 %shard_map.255 = (bf16[1024,2048]{1,0:T(8,128)(2,1)S(1)}, bf16[1024,2048]{1,0:T(8,128)(2,1)S(1)}) custom-call(bf16[1024,1024]{1,0:T(8,128)(2,1)S(1)} %pad_maximum_fusion.5.x_ref, bf16[1024,2688]{1,0:T(8,128)(2,1)S(1)} %bitcast.277, f32[1,2048]{1,0:T(1,128)S(1)} %slice.503.b_ref), custom_call_target="tpu_custom_call" | custom-call | flops 4294967296 | bytes 14680064 | tf_op jit(solution)/shard_map/pallas_call | solution.py:849
  162.5 2.1 copy-done.7
  164.6 4.0 collective-permute-done.23
  170.3 2.4 fusion.11
  174.2 2.5 collective-permute-start.27
  176.9 2.8 fusion.119
  185.5 4.9 %all-to-all-start = ((bf16[16,128,128]{2,1,0:T(8,128)(2,1)}), bf16[16,128,128]{2,1,0:T(8,128)(2,1)S(1)}, u32[]{:S(2)}, u32[]{:S(2)}) async-start(bf16[16,128,128]{2,1,0:T(8,128)(2,1)} %broadcast_in_dim.46), calls=%async_computation | async-start | bytes 1048576 | tf_op jit(solution)/shard_map/all_to_all | solution.py:1143
  191.6 11.4 %all-to-all-done = bf16[16,128,128]{2,1,0:T(8,128)(2,1)S(1)} async-done(((bf16[16,128,128]{2,1,0:T(8,128)(2,1)}), bf16[16,128,128]{2,1,0:T(8,128)(2,1)S(1)}, u32[]{:S(2)}, u32[]{:S(2)}) %all-to-all-start) | async-done | bytes 524320 | tf_op jit(solution)/shard_map/all_to_all | solution.py:1143
  203.0 7.0 %shard_map.256 = f32[24,2048]{1,0:T(8,128)S(1)} custom-call(bf16[2048,128]{1,0:T(8,128)(2,1)S(1)} %bitcast.284, bf16[1024,128]{1,0:T(8,128)(2,1)S(1)} %maximum_select_fusion.25.d_ref, s32[1,1024]{1,0:T(1,128)S(1)} %compare_select_fusion.seg_ref), custom_call_target="tpu_custom_call" | custom-call | flops 3221225472 | bytes 786432 | tf_op jit(solution)/shard_map/pallas_call | solution.py:904
  211.4 5.7 %all-to-all-start.1 = ((f32[16,8,128]{2,1,0:T(8,128)}), f32[16,8,128]{2,1,0:T(8,128)S(1)}, u32[]{:S(2)}, u32[]{:S(2)}) async-start(f32[16,8,128]{2,1,0:T(8,128)} %broadcast_in_dim.47), calls=%async_computation.1 | async-start | bytes 131072 | tf_op jit(solution)/shard_map/all_to_all | solution.py:1164
  217.1 5.1 %collective-permute-start.28 = (bf16[512,1024]{1,0:T(8,128)(2,1)}, bf16[512,1024]{1,0:T(8,128)(2,1)}, u32[]{:S(2)}, u32[]{:S(2)}) collective-permute-start(bf16[512,1024]{1,0:T(8,128)(2,1)} %add_convert_fusion.3), channel_id=1, source_target_pairs={{0,0},{1,2},{2,1},{3,3},{4,4},{5,6},{6,5},{7,7},{8,8},{9,10},{10,9... | collective-permute-start | bytes 3145736 | tf_op jit(solution)/shard_map/ppermute | solution.py:1184
  224.3 12.5 %shard_map.257 = (bf16[2048,128]{1,0:T(8,128)(2,1)}, f32[768,128]{1,0:T(8,128)S(1)}) custom-call(bf16[2048,128]{1,0:T(8,128)(2,1)S(1)} %bitcast.285, bf16[1024,128]{1,0:T(8,128)(2,1)S(1)} %maximum_select_fusion.25.d_ref, s32[1,1024]{1,0:T(1,128)S(1)} %compare_select_fusion.seg_ref, f32[24,2048]{1,0:T(8,128)S(1)} %convolution_divide_fusion.coef_ref), custom_call_target="tpu_custom_call" | custom-call | flops 4831838208 | bytes 1572864 | tf_op jit(solution)/shard_map/pallas_call | solution.py:980
  236.9 9.6 %all-to-all-start.2 = ((bf16[16,128,128]{2,1,0:T(8,128)(2,1)}), bf16[16,128,128]{2,1,0:T(8,128)(2,1)S(1)}, u32[]{:S(2)}, u32[]{:S(2)}) async-start(bf16[16,128,128]{2,1,0:T(8,128)(2,1)} %bitcast.57), calls=%async_computation.2 | async-start | bytes 1048576 | tf_op jit(solution)/shard_map/all_to_all | solution.py:1186
  246.5 12.1 %all-to-all-done.2 = bf16[16,128,128]{2,1,0:T(8,128)(2,1)S(1)} async-done(((bf16[16,128,128]{2,1,0:T(8,128)(2,1)}), bf16[16,128,128]{2,1,0:T(8,128)(2,1)S(1)}, u32[]{:S(2)}, u32[]{:S(2)}) %all-to-all-start.2) | async-done | bytes 524320 | tf_op jit(solution)/shard_map/all_to_all | solution.py:1186
  258.8 4.0 collective-permute-start.29
  267.9 1.8 fusion.121
  272.4 6.4 %convolution_convert_fusion.1 = bf16[1024,2048]{1,0:T(8,128)(2,1)S(1)} fusion(bf16[1024,2048]{1,0:T(8,128)(2,1)S(1)} %copy-done.6, bf16[512,1024]{1,0:T(8,128)(2,1)} %collective-permute-done.30, bf16[512,1024]{1,0:T(8,128)(2,1)} %get-tuple-element.235), kind=kOutput, calls=%fused_computation.6 | convolution fusion | flops 4301258752 | bytes 10485760 | tf_op jit(solution)/shard_map/dot_general | solution.py:33
  282.9 6.6 %convert_reduce_fusion = (f32[2048]{0:T(1024)S(1)}, bf16[1024,2048]{1,0:T(8,128)(2,1)S(1)}) fusion(bf16[1024,2048]{1,0:T(8,128)(2,1)S(1)} %copy-done.8, bf16[1024,2048]{1,0:T(8,128)(2,1)S(1)} %bitcast.295, bf16[512,1024]{1,0:T(8,128)(2,1)} %collective-permute-done.30, bf16[512,1024]{1,0:T(8,128)(2,1)} %get-tuple-element.235), kind=kOutput, calls=%fused_computation | convolution fusion | flops 4309645312 | bytes 14688256 | tf_op jit(solution)/shard_map/dot_general | solution.py:448
  289.5 2.4 fusion.14
  292.3 2.4 fusion.2
  294.6 9.4 %collective-permute-done.33 = bf16[4,2,32,2048]{3,2,0,1:T(8,128)(2,1)S(1)} collective-permute-done((bf16[4,2,32,2048]{3,2,0,1:T(8,128)(2,1)S(1)}, bf16[4,2,32,2048]{3,2,0,1:T(8,128)(2,1)S(1)}, u32[]{:S(2)}, u32[]{:S(2)}) %collective-permute-start.33) | collective-permute-done | bytes 1048608 | tf_op jit(solution)/shard_map/ppermute | solution.py:464
  309.1 5.3 %convolution_convert_fusion = bf16[1024,2048]{1,0:T(8,128)(2,1)S(1)} fusion(bf16[1024,2048]{1,0:T(8,128)(2,1)S(1)} %get-tuple-element.151, bf16[512,1024]{1,0:T(8,128)(2,1)S(1)} %copy-done.35, bf16[512,1024]{1,0:T(8,128)(2,1)S(1)} %copy-done.25), kind=kOutput, calls=%fused_computation.5 | convolution fusion | flops 4301258752 | bytes 10485760 | tf_op jit(solution)/shard_map/dot_general | solution.py:33
  324.7 2.4 collective-permute-start.32
  327.2 16.1 %collective-permute-done.37 = bf16[4,2,32,2048]{3,2,0,1:T(8,128)(2,1)} collective-permute-done((bf16[4,2,32,2048]{3,2,0,1:T(8,128)(2,1)}, bf16[4,2,32,2048]{3,2,0,1:T(8,128)(2,1)}, u32[]{:S(2)}, u32[]{:S(2)}) %collective-permute-start.37) | collective-permute-done | bytes 1048608 | tf_op jit(solution)/shard_map/ppermute | solution.py:464
  350.5 3.8 convolution_convert_fusion.5.grad_ref
  354.3 3.6 convolution_convert_fusion.4
  362.9 11.7 %shard_map.258 = (bf16[1024,768]{1,0:T(8,128)(2,1)S(1)}, f32[8,256]{1,0:T(8,128)S(1)}) custom-call(s32[2,4]{1,0:T(2,128)S(1)} %pad_add_fusion.1.bounds, bf16[1024,1536]{1,0:T(8,128)(2,1)S(1)} %copy-done.4, bf16[1024,1536]{1,0:T(8,128)(2,1)S(1)} %copy-done.4, bf16[1024,512]{1,0:T(8,128)(2,1)S(1)} %get-tuple-element.126.out_ref, ...), custom_call_target="tpu_custom_call" | custom-call | flops 2684354560 | bytes 12582912 | tf_op jit(solution)/shard_map/pallas_call | solution.py:782
  377.2 4.5 collective-permute-start.44
  386.1 11.9 %shard_map.259 = (bf16[1024,768]{1,0:T(8,128)(2,1)S(1)}, f32[8,256]{1,0:T(8,128)S(1)}) custom-call(s32[2,4]{1,0:T(2,128)S(1)} %pad_add_fusion.1.bounds, bf16[1024,1536]{1,0:T(8,128)(2,1)S(1)} %copy-done.4, bf16[1024,1536]{1,0:T(8,128)(2,1)S(1)} %copy-done.4, bf16[1024,512]{1,0:T(8,128)(2,1)S(1)} %get-tuple-element.126.out_ref, ...), custom_call_target="tpu_custom_call" | custom-call | flops 2684354560 | bytes 12582912 | tf_op jit(solution)/shard_map/pallas_call | solution.py:782
  398.2 3.3 collective-permute-done.47
  403.3 1.9 convolution_convert_fusion.3
  406.3 1.9 convolution_convert_fusion.2
  417.2 7.4 %collective-permute-done.53 = bf16[2,64,512]{2,1,0:T(8,128)(2,1)S(1)} collective-permute-done((bf16[2,64,512]{2,1,0:T(8,128)(2,1)S(1)}, bf16[2,64,512]{2,1,0:T(8,128)(2,1)S(1)}, u32[]{:S(2)}, u32[]{:S(2)}) %collective-permute-start.53) | collective-permute-done | bytes 131104 | tf_op jit(solution)/shard_map/ppermute | solution.py:464
  425.3 2.5 collective-permute-done.54
  428.4 1.8 collective-permute-start.55
  430.9 2.3 collective-permute-start.57
  435.6 5.1 %collective-permute-start.62 = (bf16[512,1024]{1,0:T(8,128)(2,1)S(1)}, bf16[512,1024]{1,0:T(8,128)(2,1)S(1)}, u32[]{:S(2)}, u32[]{:S(2)}) collective-permute-start(bf16[512,1024]{1,0:T(8,128)(2,1)S(1)} %add_convert_fusion.1), channel_id=1, source_target_pairs={{0,0},{1,2},{2,1},{3,3},{4,4},{5,6},{6,5},{7,7},{8,8},{9,10},{10,9... | collective-permute-start | bytes 3145736 | tf_op jit(solution)/shard_map/ppermute | solution.py:464
  442.2 3.2 collective-permute-done.60
  445.3 4.4 collective-permute-done.59
  449.8 3.4 collective-permute-done.62
  453.3 3.6 collective-permute-start.65
  457.0 2.3 collective-permute-start.63
  459.6 6.7 %collective-permute-done.64 = bf16[584,128]{1,0:T(8,128)(2,1)S(1)} collective-permute-done((bf16[584,128]{1,0:T(8,128)(2,1)S(1)}, bf16[584,128]{1,0:T(8,128)(2,1)S(1)}, u32[]{:S(2)}, u32[]{:S(2)}) %collective-permute-start.64) | collective-permute-done | bytes 149536 | tf_op jit(solution)/shard_map/ppermute | solution.py:464
  466.4 2.8 collective-permute-start.66
  471.1 2.9 collective-permute-done.66
  480.3 2.3 copy.165
  (433 shorter events, 121.2 us)
Async XLA Ops:
  1.7 9.5 %collective-permute-start = (bf16[64,1536]{1,0:T(8,128)(2,1)S(1)}, bf16[64,1536]{1,0:T(8,128)(2,1)S(1)}, u32[]{:S(2)}, u32[]{:S(2)}) collective-permute-start(bf16[64,1536]{1,0:T(8,128)(2,1)S(1)} %slice_dynamic-update-slice_fusion), channel_id=1, source_target_pairs={{0,0},{1,2},{2,1},{3,3},{4,4},{5,6},{6,5},{7,7},{8,8},{9,10},{10,9... | collective-permute-start | bytes 589832 | tf_op jit(solution)/shard_map/ppermute | solution.py:464
  6.3 5.0 %collective-permute-start.1 = (bf16[1024,1024]{1,0:T(8,128)(2,1)}, bf16[1024,1024]{1,0:T(8,128)(2,1)}, u32[]{:S(2)}, u32[]{:S(2)}) collective-permute-start(bf16[1024,1024]{1,0:T(8,128)(2,1)} %param.15), channel_id=1, source_target_pairs={{0,2},{2,0},{1,3},{3,1},{4,6},{6,4},{5,7},{7,5},{8,10},{10,8},{9,1... | collective-permute-start | bytes 6291464 | tf_op jit(solution)/shard_map/ppermute | solution.py:464
  13.1 24.7 %collective-permute-start.9 = (bf16[64,4736]{1,0:T(8,128)(2,1)S(1)}, bf16[64,4736]{1,0:T(8,128)(2,1)}, u32[]{:S(2)}, u32[]{:S(2)}) collective-permute-start(bf16[64,4736]{1,0:T(8,128)(2,1)S(1)} %fusion.39), channel_id=1, source_target_pairs={{0,0},{1,2},{2,1},{3,3},{4,4},{5,6},{6,5},{7,7},{8,8},{9,10},{10,9... | collective-permute-start | bytes 1818632 | tf_op jit(solution)/shard_map/ppermute | solution.py:464
  17.0 7.3 %collective-permute-start.3 = (bf16[64,1536]{1,0:T(8,128)(2,1)S(1)}, bf16[64,1536]{1,0:T(8,128)(2,1)S(1)}, u32[]{:S(2)}, u32[]{:S(2)}) collective-permute-start(bf16[64,1536]{1,0:T(8,128)(2,1)S(1)} %collective-permute-done), channel_id=1, source_target_pairs={{0,24},{24,0},{8,16},{16,8},{1,25},{25,1},{9,17},{17,9},{2,26},{26... | collective-permute-start | bytes 589832 | tf_op jit(solution)/shard_map/ppermute | solution.py:464
  24.4 13.2 %collective-permute-start.4 = (bf16[2,64,1536]{2,1,0:T(8,128)(2,1)S(1)}, bf16[2,64,1536]{2,1,0:T(8,128)(2,1)S(1)}, u32[]{:S(2)}, u32[]{:S(2)}) collective-permute-start(bf16[2,64,1536]{2,1,0:T(8,128)(2,1)S(1)} %maximum_select_fusion.22), channel_id=1, source_target_pairs={{0,8},{8,0},{16,24},{24,16},{1,9},{9,1},{17,25},{25,17},{2,10},{10... | collective-permute-start | bytes 1179656 | tf_op jit(solution)/shard_map/ppermute | solution.py:464
  38.9 11.2 %collective-permute-start.10 = (bf16[64,2688]{1,0:T(8,128)(2,1)S(1)}, bf16[64,2688]{1,0:T(8,128)(2,1)S(1)}, u32[]{:S(2)}, u32[]{:S(2)}) collective-permute-start(bf16[64,2688]{1,0:T(8,128)(2,1)S(1)} %get-tuple-element.290), channel_id=1, source_target_pairs={{0,24},{24,0},{8,16},{16,8},{1,25},{25,1},{9,17},{17,9},{2,26},{26... | collective-permute-start | bytes 1032200 | tf_op jit(solution)/shard_map/ppermute | solution.py:464
  40.8 16.4 %collective-permute-start.5 = (bf16[4,32,1536]{2,1,0:T(8,128)(2,1)S(1)}, bf16[4,32,1536]{2,1,0:T(8,128)(2,1)S(1)}, u32[]{:S(2)}, u32[]{:S(2)}) collective-permute-start(bf16[4,32,1536]{2,1,0:T(8,128)(2,1)S(1)} %get-tuple-element.282), channel_id=1, source_target_pairs={{0,4},{4,0},{1,5},{5,1},{2,6},{6,2},{3,7},{7,3},{8,12},{12,8},{9,1... | collective-permute-start | bytes 1179656 | tf_op jit(solution)/shard_map/ppermute | solution.py:464
  42.0 15.1 %collective-permute-start.6 = (bf16[4,32,1536]{2,1,0:T(8,128)(2,1)S(1)}, bf16[4,32,1536]{2,1,0:T(8,128)(2,1)S(1)}, u32[]{:S(2)}, u32[]{:S(2)}) collective-permute-start(bf16[4,32,1536]{2,1,0:T(8,128)(2,1)S(1)} %get-tuple-element.281), channel_id=1, source_target_pairs={{0,1},{1,0},{2,3},{3,2},{4,5},{5,4},{6,7},{7,6},{8,9},{9,8},{10,11... | collective-permute-start | bytes 1179656 | tf_op jit(solution)/shard_map/ppermute | solution.py:464
  50.2 21.5 %collective-permute-start.11 = (bf16[2,64,2688]{2,1,0:T(8,128)(2,1)S(1)}, bf16[2,64,2688]{2,1,0:T(8,128)(2,1)S(1)}, u32[]{:S(2)}, u32[]{:S(2)}) collective-permute-start(bf16[2,64,2688]{2,1,0:T(8,128)(2,1)S(1)} %maximum_select_fusion.19), channel_id=1, source_target_pairs={{0,8},{8,0},{16,24},{24,16},{1,9},{9,1},{17,25},{25,17},{2,10},{10... | collective-permute-start | bytes 2064392 | tf_op jit(solution)/shard_map/ppermute | solution.py:464
  57.3 19.6 %collective-permute-start.7 = (bf16[4,2,32,1536]{3,2,0,1:T(8,128)(2,1)S(1)}, bf16[4,2,32,1536]{3,2,0,1:T(8,128)(2,1)S(1)}, u32[]{:S(2)}, u32[]{:S(2)}) collective-permute-start(bf16[4,2,32,1536]{3,2,0,1:T(8,128)(2,1)S(1)} %maximum_select_fusion.17), channel_id=1, source_target_pairs={{0,1},{1,0},{2,3},{3,2},{4,5},{5,4},{6,7},{7,6},{8,9},{9,8},{10,11... | collective-permute-start | bytes 2359304 | tf_op jit(solution)/shard_map/ppermute | solution.py:464
  57.5 19.4 %collective-permute-start.8 = (bf16[4,2,32,1536]{3,2,1,0:T(8,128)(2,1)S(1)}, bf16[4,2,32,1536]{3,2,1,0:T(8,128)(2,1)S(1)}, u32[]{:S(2)}, u32[]{:S(2)}) collective-permute-start(bf16[4,2,32,1536]{3,2,1,0:T(8,128)(2,1)S(1)} %maximum_select_fusion.18), channel_id=1, source_target_pairs={{0,4},{4,0},{1,5},{5,1},{2,6},{6,2},{3,7},{7,3},{8,12},{12,8},{9,1... | collective-permute-start | bytes 2359304 | tf_op jit(solution)/shard_map/ppermute | solution.py:464
  72.4 17.6 %collective-permute-start.14 = (bf16[4,32,2688]{2,1,0:T(8,128)(2,1)S(1)}, bf16[4,32,2688]{2,1,0:T(8,128)(2,1)S(1)}, u32[]{:S(2)}, u32[]{:S(2)}) collective-permute-start(bf16[4,32,2688]{2,1,0:T(8,128)(2,1)S(1)} %get-tuple-element.272), channel_id=1, source_target_pairs={{0,4},{4,0},{1,5},{5,1},{2,6},{6,2},{3,7},{7,3},{8,12},{12,8},{9,1... | collective-permute-start | bytes 2064392 | tf_op jit(solution)/shard_map/ppermute | solution.py:464
  73.7 16.3 %collective-permute-start.15 = (bf16[4,32,2688]{2,1,0:T(8,128)(2,1)S(1)}, bf16[4,32,2688]{2,1,0:T(8,128)(2,1)S(1)}, u32[]{:S(2)}, u32[]{:S(2)}) collective-permute-start(bf16[4,32,2688]{2,1,0:T(8,128)(2,1)S(1)} %get-tuple-element.271), channel_id=1, source_target_pairs={{0,1},{1,0},{2,3},{3,2},{4,5},{5,4},{6,7},{7,6},{8,9},{9,8},{10,11... | collective-permute-start | bytes 2064392 | tf_op jit(solution)/shard_map/ppermute | solution.py:464
  73.7 7.7 %collective-permute-start.12 = (bf16[64,2048]{1,0:T(8,128)(2,1)S(1)}, bf16[64,2048]{1,0:T(8,128)(2,1)S(1)}, u32[]{:S(2)}, u32[]{:S(2)}) collective-permute-start(bf16[64,2048]{1,0:T(8,128)(2,1)S(1)} %slice.390), channel_id=1, source_target_pairs={{0,24},{24,0},{8,16},{16,8},{1,25},{25,1},{9,17},{17,9},{2,26},{26... | collective-permute-start | bytes 786440 | tf_op jit(solution)/shard_map/ppermute | solution.py:464
  81.5 19.8 %collective-permute-start.13 = (bf16[2,64,2048]{2,1,0:T(8,128)(2,1)S(1)}, bf16[2,64,2048]{2,1,0:T(8,128)(2,1)S(1)}, u32[]{:S(2)}, u32[]{:S(2)}) collective-permute-start(bf16[2,64,2048]{2,1,0:T(8,128)(2,1)S(1)} %maximum_select_fusion.20), channel_id=1, source_target_pairs={{0,8},{8,0},{16,24},{24,16},{1,9},{9,1},{17,25},{25,17},{2,10},{10... | collective-permute-start | bytes 1572872 | tf_op jit(solution)/shard_map/ppermute | solution.py:464
  90.2 29.5 %collective-permute-start.16 = (bf16[4,2,32,2688]{3,2,0,1:T(8,128)(2,1)S(1)}, bf16[4,2,32,2688]{3,2,0,1:T(8,128)(2,1)S(1)}, u32[]{:S(2)}, u32[]{:S(2)}) collective-permute-start(bf16[4,2,32,2688]{3,2,0,1:T(8,128)(2,1)S(1)} %maximum_select_fusion.9), channel_id=1, source_target_pairs={{0,1},{1,0},{2,3},{3,2},{4,5},{5,4},{6,7},{7,6},{8,9},{9,8},{10,11... | collective-permute-start | bytes 4128776 | tf_op jit(solution)/shard_map/ppermute | solution.py:464
  91.6 28.8 %collective-permute-start.17 = (bf16[4,2,32,2688]{3,2,0,1:T(8,128)(2,1)S(1)}, bf16[4,2,32,2688]{3,2,0,1:T(8,128)(2,1)S(1)}, u32[]{:S(2)}, u32[]{:S(2)}) collective-permute-start(bf16[4,2,32,2688]{3,2,0,1:T(8,128)(2,1)S(1)} %maximum_select_fusion.10), channel_id=1, source_target_pairs={{0,4},{4,0},{1,5},{5,1},{2,6},{6,2},{3,7},{7,3},{8,12},{12,8},{9,1... | collective-permute-start | bytes 4128776 | tf_op jit(solution)/shard_map/ppermute | solution.py:464
  123.4 6.8 %collective-permute-start.18 = (bf16[512,1024]{1,0:T(8,128)(2,1)S(1)}, bf16[512,1024]{1,0:T(8,128)(2,1)S(1)}, u32[]{:S(2)}, u32[]{:S(2)}) collective-permute-start(bf16[512,1024]{1,0:T(8,128)(2,1)S(1)} %convolution_convert_fusion.6), channel_id=1, source_target_pairs={{0,2},{2,0},{1,3},{3,1},{4,6},{6,4},{5,7},{7,5},{8,10},{10,8},{9,1... | collective-permute-start | bytes 3145736 | tf_op jit(solution)/shard_map/ppermute | solution.py:469
  127.6 13.6 %collective-permute-start.21 = (bf16[4,32,2048]{2,1,0:T(8,128)(2,1)S(1)}, bf16[4,32,2048]{2,1,0:T(8,128)(2,1)S(1)}, u32[]{:S(2)}, u32[]{:S(2)}) collective-permute-start(bf16[4,32,2048]{2,1,0:T(8,128)(2,1)S(1)} %get-tuple-element.276), channel_id=1, source_target_pairs={{0,4},{4,0},{1,5},{5,1},{2,6},{6,2},{3,7},{7,3},{8,12},{12,8},{9,1... | collective-permute-start | bytes 1572872 | tf_op jit(solution)/shard_map/ppermute | solution.py:464
  128.7 13.2 %collective-permute-start.22 = (bf16[4,32,2048]{2,1,0:T(8,128)(2,1)S(1)}, bf16[4,32,2048]{2,1,0:T(8,128)(2,1)S(1)}, u32[]{:S(2)}, u32[]{:S(2)}) collective-permute-start(bf16[4,32,2048]{2,1,0:T(8,128)(2,1)S(1)} %get-tuple-element.275), channel_id=1, source_target_pairs={{0,1},{1,0},{2,3},{3,2},{4,5},{5,4},{6,7},{7,6},{8,9},{9,8},{10,11... | collective-permute-start | bytes 1572872 | tf_op jit(solution)/shard_map/ppermute | solution.py:464
  131.5 13.4 %collective-permute-start.19 = (bf16[512,1024]{1,0:T(8,128)(2,1)S(1)}, bf16[512,1024]{1,0:T(8,128)(2,1)S(1)}, u32[]{:S(2)}, u32[]{:S(2)}) collective-permute-start(bf16[512,1024]{1,0:T(8,128)(2,1)S(1)} %fusion.10), channel_id=1, source_target_pairs={{0,2},{2,0},{1,3},{3,1},{4,6},{6,4},{5,7},{7,5},{8,10},{10,8},{9,1... | collective-permute-start | bytes 3145736 | tf_op jit(solution)/shard_map/ppermute | solution.py:469
  144.1 24.4 %collective-permute-start.23 = (bf16[4,2,32,2048]{3,2,0,1:T(8,128)(2,1)S(1)}, bf16[4,2,32,2048]{3,2,0,1:T(8,128)(2,1)S(1)}, u32[]{:S(2)}, u32[]{:S(2)}) collective-permute-start(bf16[4,2,32,2048]{3,2,0,1:T(8,128)(2,1)S(1)} %maximum_select_fusion.13), channel_id=1, source_target_pairs={{0,1},{1,0},{2,3},{3,2},{4,5},{5,4},{6,7},{7,6},{8,9},{9,8},{10,11... | collective-permute-start | bytes 3145736 | tf_op jit(solution)/shard_map/ppermute | solution.py:464
  144.9 24.1 %collective-permute-start.24 = (bf16[4,2,32,2048]{3,2,1,0:T(8,128)(2,1)S(1)}, bf16[4,2,32,2048]{3,2,1,0:T(8,128)(2,1)S(1)}, u32[]{:S(2)}, u32[]{:S(2)}) collective-permute-start(bf16[4,2,32,2048]{3,2,1,0:T(8,128)(2,1)S(1)} %maximum_select_fusion.14), channel_id=1, source_target_pairs={{0,4},{4,0},{1,5},{5,1},{2,6},{6,2},{3,7},{7,3},{8,12},{12,8},{9,1... | collective-permute-start | bytes 3145736 | tf_op jit(solution)/shard_map/ppermute | solution.py:464
  174.2 17.4 %collective-permute-start.27 = (bf16[512,1024]{1,0:T(8,128)(2,1)}, bf16[512,1024]{1,0:T(8,128)(2,1)S(1)}, u32[]{:S(2)}, u32[]{:S(2)}) collective-permute-start(bf16[512,1024]{1,0:T(8,128)(2,1)} %param.29), channel_id=1, source_target_pairs={{0,0},{1,2},{2,1},{3,3},{4,4},{5,6},{6,5},{7,7},{8,8},{9,10},{10,9... | collective-permute-start | bytes 3145736 | tf_op jit(solution)/shard_map/ppermute | solution.py:1146
  185.5 17.5 %all-to-all-start = ((bf16[16,128,128]{2,1,0:T(8,128)(2,1)}), bf16[16,128,128]{2,1,0:T(8,128)(2,1)S(1)}, u32[]{:S(2)}, u32[]{:S(2)}) async-start(bf16[16,128,128]{2,1,0:T(8,128)(2,1)} %broadcast_in_dim.46), calls=%async_computation | async-start | bytes 1048576 | tf_op jit(solution)/shard_map/all_to_all | solution.py:1143
  211.4 12.1 %all-to-all-start.1 = ((f32[16,8,128]{2,1,0:T(8,128)}), f32[16,8,128]{2,1,0:T(8,128)S(1)}, u32[]{:S(2)}, u32[]{:S(2)}) async-start(f32[16,8,128]{2,1,0:T(8,128)} %broadcast_in_dim.47), calls=%async_computation.1 | async-start | bytes 131072 | tf_op jit(solution)/shard_map/all_to_all | solution.py:1164
  217.1 19.8 %collective-permute-start.28 = (bf16[512,1024]{1,0:T(8,128)(2,1)}, bf16[512,1024]{1,0:T(8,128)(2,1)}, u32[]{:S(2)}, u32[]{:S(2)}) collective-permute-start(bf16[512,1024]{1,0:T(8,128)(2,1)} %add_convert_fusion.3), channel_id=1, source_target_pairs={{0,0},{1,2},{2,1},{3,3},{4,4},{5,6},{6,5},{7,7},{8,8},{9,10},{10,9... | collective-permute-start | bytes 3145736 | tf_op jit(solution)/shard_map/ppermute | solution.py:1184
  236.9 21.7 %all-to-all-start.2 = ((bf16[16,128,128]{2,1,0:T(8,128)(2,1)}), bf16[16,128,128]{2,1,0:T(8,128)(2,1)S(1)}, u32[]{:S(2)}, u32[]{:S(2)}) async-start(bf16[16,128,128]{2,1,0:T(8,128)(2,1)} %bitcast.57), calls=%async_computation.2 | async-start | bytes 1048576 | tf_op jit(solution)/shard_map/all_to_all | solution.py:1186
  258.8 5.1 %collective-permute-start.29 = (f32[512,128]{1,0:T(8,128)S(1)}, f32[512,128]{1,0:T(8,128)S(1)}, u32[]{:S(2)}, u32[]{:S(2)}) collective-permute-start(f32[512,128]{1,0:T(8,128)S(1)} %constant_dynamic-slice_fusion.11), channel_id=1, source_target_pairs={{0,2},{2,0},{1,3},{3,1},{4,6},{6,4},{5,7},{7,5},{8,10},{10,8},{9,1... | collective-permute-start | bytes 786440 | tf_op jit(solution)/shard_map/ppermute | solution.py:469
  267.4 4.9 %collective-permute-start.30 = (bf16[512,1024]{1,0:T(8,128)(2,1)}, bf16[512,1024]{1,0:T(8,128)(2,1)}, u32[]{:S(2)}, u32[]{:S(2)}) collective-permute-start(bf16[512,1024]{1,0:T(8,128)(2,1)} %get-tuple-element.235), channel_id=1, source_target_pairs={{0,2},{2,0},{1,3},{3,1},{4,6},{6,4},{5,7},{7,5},{8,10},{10,8},{9,1... | collective-permute-start | bytes 3145736 | tf_op jit(solution)/shard_map/ppermute | solution.py:469
  279.3 24.7 %collective-permute-start.33 = (bf16[4,2,32,2048]{3,2,0,1:T(8,128)(2,1)S(1)}, bf16[4,2,32,2048]{3,2,0,1:T(8,128)(2,1)S(1)}, u32[]{:S(2)}, u32[]{:S(2)}) collective-permute-start(bf16[4,2,32,2048]{3,2,0,1:T(8,128)(2,1)S(1)} %bitcast.315), channel_id=1, source_target_pairs={{0,4},{4,0},{1,5},{5,1},{2,6},{6,2},{3,7},{7,3},{8,12},{12,8},{9,1... | collective-permute-start | bytes 3145736 | tf_op jit(solution)/shard_map/ppermute | solution.py:464
  280.7 24.4 %collective-permute-start.34 = (bf16[4,2,32,2048]{3,2,0,1:T(8,128)(2,1)S(1)}, bf16[4,2,32,2048]{3,2,0,1:T(8,128)(2,1)S(1)}, u32[]{:S(2)}, u32[]{:S(2)}) collective-permute-start(bf16[4,2,32,2048]{3,2,0,1:T(8,128)(2,1)S(1)} %bitcast.316), channel_id=1, source_target_pairs={{0,1},{1,0},{2,3},{3,2},{4,5},{5,4},{6,7},{7,6},{8,9},{9,8},{10,11... | collective-permute-start | bytes 3145736 | tf_op jit(solution)/shard_map/ppermute | solution.py:464
  291.9 29.6 %collective-permute-start.31 = (bf16[512,1024]{1,0:T(8,128)(2,1)S(1)}, bf16[512,1024]{1,0:T(8,128)(2,1)S(1)}, u32[]{:S(2)}, u32[]{:S(2)}) collective-permute-start(bf16[512,1024]{1,0:T(8,128)(2,1)S(1)} %fusion.14), channel_id=1, source_target_pairs={{0,2},{2,0},{1,3},{3,1},{4,6},{6,4},{5,7},{7,5},{8,10},{10,8},{9,1... | collective-permute-start | bytes 3145736 | tf_op jit(solution)/shard_map/ppermute | solution.py:469
  306.4 20.8 %collective-permute-start.35 = (bf16[4,32,2048]{2,1,0:T(8,128)(2,1)}, bf16[4,32,2048]{2,1,0:T(8,128)(2,1)}, u32[]{:S(2)}, u32[]{:S(2)}) collective-permute-start(bf16[4,32,2048]{2,1,0:T(8,128)(2,1)} %fusion.40), channel_id=1, source_target_pairs={{0,1},{1,0},{2,3},{3,2},{4,5},{5,4},{6,7},{7,6},{8,9},{9,8},{10,11... | collective-permute-start | bytes 1572872 | tf_op jit(solution)/shard_map/ppermute | solution.py:464
  308.6 18.6 %collective-permute-start.36 = (bf16[4,32,2048]{2,1,0:T(8,128)(2,1)}, bf16[4,32,2048]{2,1,0:T(8,128)(2,1)}, u32[]{:S(2)}, u32[]{:S(2)}) collective-permute-start(bf16[4,32,2048]{2,1,0:T(8,128)(2,1)} %fusion.41), channel_id=1, source_target_pairs={{0,4},{4,0},{1,5},{5,1},{2,6},{6,2},{3,7},{7,3},{8,12},{12,8},{9,1... | collective-permute-start | bytes 1572872 | tf_op jit(solution)/shard_map/ppermute | solution.py:464
  317.1 26.1 %collective-permute-start.37 = (bf16[4,2,32,2048]{3,2,0,1:T(8,128)(2,1)}, bf16[4,2,32,2048]{3,2,0,1:T(8,128)(2,1)}, u32[]{:S(2)}, u32[]{:S(2)}) collective-permute-start(bf16[4,2,32,2048]{3,2,0,1:T(8,128)(2,1)} %bitcast.272), channel_id=1, source_target_pairs={{0,4},{4,0},{1,5},{5,1},{2,6},{6,2},{3,7},{7,3},{8,12},{12,8},{9,1... | collective-permute-start | bytes 3145736 | tf_op jit(solution)/shard_map/ppermute | solution.py:464
  320.3 22.9 %collective-permute-start.38 = (bf16[4,2,32,2048]{3,2,0,1:T(8,128)(2,1)}, bf16[4,2,32,2048]{3,2,0,1:T(8,128)(2,1)}, u32[]{:S(2)}, u32[]{:S(2)}) collective-permute-start(bf16[4,2,32,2048]{3,2,0,1:T(8,128)(2,1)} %bitcast.271), channel_id=1, source_target_pairs={{0,1},{1,0},{2,3},{3,2},{4,5},{5,4},{6,7},{7,6},{8,9},{9,8},{10,11... | collective-permute-start | bytes 3145736 | tf_op jit(solution)/shard_map/ppermute | solution.py:464
  324.7 25.8 %collective-permute-start.32 = (bf16[512,1024]{1,0:T(8,128)(2,1)}, bf16[512,1024]{1,0:T(8,128)(2,1)}, u32[]{:S(2)}, u32[]{:S(2)}) collective-permute-start(bf16[512,1024]{1,0:T(8,128)(2,1)} %get-tuple-element.238), channel_id=1, source_target_pairs={{0,2},{2,0},{1,3},{3,1},{4,6},{6,4},{5,7},{7,5},{8,10},{10,8},{9,1... | collective-permute-start | bytes 3145736 | tf_op jit(solution)/shard_map/ppermute | solution.py:469
  358.3 18.0 %collective-permute-start.39 = (bf16[2,64,2048]{2,1,0:T(8,128)(2,1)S(1)}, bf16[2,64,2048]{2,1,0:T(8,128)(2,1)S(1)}, u32[]{:S(2)}, u32[]{:S(2)}) collective-permute-start(bf16[2,64,2048]{2,1,0:T(8,128)(2,1)S(1)} %select_convert_fusion.1), channel_id=1, source_target_pairs={{0,8},{8,0},{16,24},{24,16},{1,9},{9,1},{17,25},{25,17},{2,10},{10... | collective-permute-start | bytes 1572872 | tf_op jit(solution)/shard_map/ppermute | solution.py:464
  359.4 16.9 %collective-permute-start.40 = (bf16[4,32,2048]{2,1,0:T(8,128)(2,1)S(1)}, bf16[4,32,2048]{2,1,0:T(8,128)(2,1)S(1)}, u32[]{:S(2)}, u32[]{:S(2)}) collective-permute-start(bf16[4,32,2048]{2,1,0:T(8,128)(2,1)S(1)} %fusion.42), channel_id=1, source_target_pairs={{0,1},{1,0},{2,3},{3,2},{4,5},{5,4},{6,7},{7,6},{8,9},{9,8},{10,11... | collective-permute-start | bytes 1572872 | tf_op jit(solution)/shard_map/ppermute | solution.py:464
  360.8 15.6 %collective-permute-start.41 = (bf16[4,32,2048]{2,1,0:T(8,128)(2,1)S(1)}, bf16[4,32,2048]{2,1,0:T(8,128)(2,1)S(1)}, u32[]{:S(2)}, u32[]{:S(2)}) collective-permute-start(bf16[4,32,2048]{2,1,0:T(8,128)(2,1)S(1)} %fusion.43), channel_id=1, source_target_pairs={{0,4},{4,0},{1,5},{5,1},{2,6},{6,2},{3,7},{7,3},{8,12},{12,8},{9,1... | collective-permute-start | bytes 1572872 | tf_op jit(solution)/shard_map/ppermute | solution.py:464
  361.4 15.0 %collective-permute-start.42 = (bf16[4,2,32,512]{3,2,0,1:T(8,128)(2,1)S(1)}, bf16[4,2,32,512]{3,2,0,1:T(8,128)(2,1)S(1)}, u32[]{:S(2)}, u32[]{:S(2)}) collective-permute-start(bf16[4,2,32,512]{3,2,0,1:T(8,128)(2,1)S(1)} %dynamic-slice_bitcast_fusion.3), channel_id=1, source_target_pairs={{0,4},{4,0},{1,5},{5,1},{2,6},{6,2},{3,7},{7,3},{8,12},{12,8},{9,1... | collective-permute-start | bytes 786440 | tf_op jit(solution)/shard_map/ppermute | solution.py:464
  362.5 13.8 %collective-permute-start.43 = (bf16[4,2,32,512]{3,2,0,1:T(8,128)(2,1)S(1)}, bf16[4,2,32,512]{3,2,0,1:T(8,128)(2,1)S(1)}, u32[]{:S(2)}, u32[]{:S(2)}) collective-permute-start(bf16[4,2,32,512]{3,2,0,1:T(8,128)(2,1)S(1)} %dynamic-slice_bitcast_fusion.2), channel_id=1, source_target_pairs={{0,1},{1,0},{2,3},{3,2},{4,5},{5,4},{6,7},{7,6},{8,9},{9,8},{10,11... | collective-permute-start | bytes 786440 | tf_op jit(solution)/shard_map/ppermute | solution.py:464
  377.2 6.0 %collective-permute-start.44 = (f32[16,4]{1,0:T(8,128)S(1)}, f32[16,4]{1,0:T(8,128)S(1)}, u32[]{:S(2)}, u32[]{:S(2)}) collective-permute-start(f32[16,4]{1,0:T(8,128)S(1)} %reshape.820), channel_id=1, source_target_pairs={{0,2},{2,0},{1,3},{3,1},{4,6},{6,4},{5,7},{7,5},{8,10},{10,8},{9,1... | collective-permute-start | bytes 776 | tf_op jit(solution)/shard_map/ppermute | solution.py:469
  381.8 16.4 %collective-permute-start.46 = (bf16[64,2048]{1,0:T(8,128)(2,1)S(1)}, bf16[64,2048]{1,0:T(8,128)(2,1)S(1)}, u32[]{:S(2)}, u32[]{:S(2)}) collective-permute-start(bf16[64,2048]{1,0:T(8,128)(2,1)S(1)} %fusion.54), channel_id=1, source_target_pairs={{0,24},{24,0},{8,16},{16,8},{1,25},{25,1},{9,17},{17,9},{2,26},{26... | collective-permute-start | bytes 786440 | tf_op jit(solution)/shard_map/ppermute | solution.py:464
  382.6 18.9 %collective-permute-start.47 = (bf16[2,64,2048]{2,1,0:T(8,128)(2,1)S(1)}, bf16[2,64,2048]{2,1,0:T(8,128)(2,1)S(1)}, u32[]{:S(2)}, u32[]{:S(2)}) collective-permute-start(bf16[2,64,2048]{2,1,0:T(8,128)(2,1)S(1)} %select_convert_fusion), channel_id=1, source_target_pairs={{0,8},{8,0},{16,24},{24,16},{1,9},{9,1},{17,25},{25,17},{2,10},{10... | collective-permute-start | bytes 1572872 | tf_op jit(solution)/shard_map/ppermute | solution.py:464
  383.8 14.3 %collective-permute-start.48 = (bf16[4,32,512]{2,1,0:T(8,128)(2,1)S(1)}, bf16[4,32,512]{2,1,0:T(8,128)(2,1)S(1)}, u32[]{:S(2)}, u32[]{:S(2)}) collective-permute-start(bf16[4,32,512]{2,1,0:T(8,128)(2,1)S(1)} %fusion.62), channel_id=1, source_target_pairs={{0,1},{1,0},{2,3},{3,2},{4,5},{5,4},{6,7},{7,6},{8,9},{9,8},{10,11... | collective-permute-start | bytes 393224 | tf_op jit(solution)/shard_map/ppermute | solution.py:464
  385.5 12.7 %collective-permute-start.49 = (bf16[4,32,512]{2,1,0:T(8,128)(2,1)S(1)}, bf16[4,32,512]{2,1,0:T(8,128)(2,1)S(1)}, u32[]{:S(2)}, u32[]{:S(2)}) collective-permute-start(bf16[4,32,512]{2,1,0:T(8,128)(2,1)S(1)} %fusion.63), channel_id=1, source_target_pairs={{0,4},{4,0},{1,5},{5,1},{2,6},{6,2},{3,7},{7,3},{8,12},{12,8},{9,1... | collective-permute-start | bytes 393224 | tf_op jit(solution)/shard_map/ppermute | solution.py:464
  409.2 18.6 %collective-permute-start.50 = (bf16[4,2,32,1536]{3,2,0,1:T(8,128)(2,1)S(1)}, bf16[4,2,32,1536]{3,2,0,1:T(8,128)(2,1)S(1)}, u32[]{:S(2)}, u32[]{:S(2)}) collective-permute-start(bf16[4,2,32,1536]{3,2,0,1:T(8,128)(2,1)S(1)} %dynamic-slice_bitcast_fusion.1), channel_id=1, source_target_pairs={{0,4},{4,0},{1,5},{5,1},{2,6},{6,2},{3,7},{7,3},{8,12},{12,8},{9,1... | collective-permute-start | bytes 2359304 | tf_op jit(solution)/shard_map/ppermute | solution.py:464
  409.8 18.3 %collective-permute-start.51 = (bf16[4,2,32,1536]{3,2,0,1:T(8,128)(2,1)S(1)}, bf16[4,2,32,1536]{3,2,0,1:T(8,128)(2,1)S(1)}, u32[]{:S(2)}, u32[]{:S(2)}) collective-permute-start(bf16[4,2,32,1536]{3,2,0,1:T(8,128)(2,1)S(1)} %dynamic-slice_bitcast_fusion), channel_id=1, source_target_pairs={{0,1},{1,0},{2,3},{3,2},{4,5},{5,4},{6,7},{7,6},{8,9},{9,8},{10,11... | collective-permute-start | bytes 2359304 | tf_op jit(solution)/shard_map/ppermute | solution.py:464
  411.7 16.1 %collective-permute-start.52 = (bf16[64,2048]{1,0:T(8,128)(2,1)S(1)}, bf16[64,2048]{1,0:T(8,128)(2,1)S(1)}, u32[]{:S(2)}, u32[]{:S(2)}) collective-permute-start(bf16[64,2048]{1,0:T(8,128)(2,1)S(1)} %fusion.55), channel_id=1, source_target_pairs={{0,24},{24,0},{8,16},{16,8},{1,25},{25,1},{9,17},{17,9},{2,26},{26... | collective-permute-start | bytes 786440 | tf_op jit(solution)/shard_map/ppermute | solution.py:464
  413.5 11.0 %collective-permute-start.53 = (bf16[2,64,512]{2,1,0:T(8,128)(2,1)S(1)}, bf16[2,64,512]{2,1,0:T(8,128)(2,1)S(1)}, u32[]{:S(2)}, u32[]{:S(2)}) collective-permute-start(bf16[2,64,512]{2,1,0:T(8,128)(2,1)S(1)} %select_convert_fusion.6), channel_id=1, source_target_pairs={{0,8},{8,0},{16,24},{24,16},{1,9},{9,1},{17,25},{25,17},{2,10},{10... | collective-permute-start | bytes 393224 | tf_op jit(solution)/shard_map/ppermute | solution.py:464
  413.6 14.1 %collective-permute-start.54 = (bf16[584,128]{1,0:T(8,128)(2,1)S(1)}, bf16[584,128]{1,0:T(8,128)(2,1)S(1)}, u32[]{:S(2)}, u32[]{:S(2)}) collective-permute-start(bf16[584,128]{1,0:T(8,128)(2,1)S(1)} %convert_element_type.481), channel_id=1, source_target_pairs={{0,8},{8,0},{16,24},{24,16},{1,9},{9,1},{17,25},{25,17},{2,10},{10... | collective-permute-start | bytes 448520 | tf_op jit(solution)/shard_map/ppermute | solution.py:464
  424.5 9.9 %collective-permute-start.61 = (bf16[512,1024]{1,0:T(8,128)(2,1)S(1)}, bf16[512,1024]{1,0:T(8,128)(2,1)S(1)}, u32[]{:S(2)}, u32[]{:S(2)}) collective-permute-start(bf16[512,1024]{1,0:T(8,128)(2,1)S(1)} %add_convert_fusion.2), channel_id=1, source_target_pairs={{0,2},{2,0},{1,3},{3,1},{4,6},{6,4},{5,7},{7,5},{8,10},{10,8},{9,1... | collective-permute-start | bytes 3145736 | tf_op jit(solution)/shard_map/ppermute | solution.py:469
  428.4 12.4 %collective-permute-start.55 = (bf16[4,32,1536]{2,1,0:T(8,128)(2,1)S(1)}, bf16[4,32,1536]{2,1,0:T(8,128)(2,1)S(1)}, u32[]{:S(2)}, u32[]{:S(2)}) collective-permute-start(bf16[4,32,1536]{2,1,0:T(8,128)(2,1)S(1)} %fusion.49), channel_id=1, source_target_pairs={{0,1},{1,0},{2,3},{3,2},{4,5},{5,4},{6,7},{7,6},{8,9},{9,8},{10,11... | collective-permute-start | bytes 1179656 | tf_op jit(solution)/shard_map/ppermute | solution.py:464
  430.5 10.2 %collective-permute-start.56 = (bf16[4,32,1536]{2,1,0:T(8,128)(2,1)S(1)}, bf16[4,32,1536]{2,1,0:T(8,128)(2,1)S(1)}, u32[]{:S(2)}, u32[]{:S(2)}) collective-permute-start(bf16[4,32,1536]{2,1,0:T(8,128)(2,1)S(1)} %fusion.50), channel_id=1, source_target_pairs={{0,4},{4,0},{1,5},{5,1},{2,6},{6,2},{3,7},{7,3},{8,12},{12,8},{9,1... | collective-permute-start | bytes 1179656 | tf_op jit(solution)/shard_map/ppermute | solution.py:464
  430.9 9.9 %collective-permute-start.57 = (bf16[64,512]{1,0:T(8,128)(2,1)S(1)}, bf16[64,512]{1,0:T(8,128)(2,1)S(1)}, u32[]{:S(2)}, u32[]{:S(2)}) collective-permute-start(bf16[64,512]{1,0:T(8,128)(2,1)S(1)} %fusion.68), channel_id=1, source_target_pairs={{0,24},{24,0},{8,16},{16,8},{1,25},{25,1},{9,17},{17,9},{2,26},{26... | collective-permute-start | bytes 196616 | tf_op jit(solution)/shard_map/ppermute | solution.py:464
  433.2 7.6 %collective-permute-start.58 = (bf16[584,128]{1,0:T(8,128)(2,1)S(1)}, bf16[584,128]{1,0:T(8,128)(2,1)S(1)}, u32[]{:S(2)}, u32[]{:S(2)}) collective-permute-start(bf16[584,128]{1,0:T(8,128)(2,1)S(1)} %fusion.56), channel_id=1, source_target_pairs={{0,24},{24,0},{8,16},{16,8},{1,25},{25,1},{9,17},{17,9},{2,26},{26... | collective-permute-start | bytes 448520 | tf_op jit(solution)/shard_map/ppermute | solution.py:464
  435.6 17.6 %collective-permute-start.62 = (bf16[512,1024]{1,0:T(8,128)(2,1)S(1)}, bf16[512,1024]{1,0:T(8,128)(2,1)S(1)}, u32[]{:S(2)}, u32[]{:S(2)}) collective-permute-start(bf16[512,1024]{1,0:T(8,128)(2,1)S(1)} %add_convert_fusion.1), channel_id=1, source_target_pairs={{0,0},{1,2},{2,1},{3,3},{4,4},{5,6},{6,5},{7,7},{8,8},{9,10},{10,9... | collective-permute-start | bytes 3145736 | tf_op jit(solution)/shard_map/ppermute | solution.py:464
  441.1 8.6 %collective-permute-start.59 = (bf16[2,64,1536]{2,1,0:T(8,128)(2,1)S(1)}, bf16[2,64,1536]{2,1,0:T(8,128)(2,1)S(1)}, u32[]{:S(2)}, u32[]{:S(2)}) collective-permute-start(bf16[2,64,1536]{2,1,0:T(8,128)(2,1)S(1)} %select_convert_fusion.2), channel_id=1, source_target_pairs={{0,8},{8,0},{16,24},{24,16},{1,9},{9,1},{17,25},{25,17},{2,10},{10... | collective-permute-start | bytes 1179656 | tf_op jit(solution)/shard_map/ppermute | solution.py:464
  453.3 13.0 %collective-permute-start.65 = (bf16[64,4096]{1,0:T(8,128)(2,1)S(1)}, bf16[64,4096]{1,0:T(8,128)(2,1)S(1)}, u32[]{:S(2)}, u32[]{:S(2)}) collective-permute-start(bf16[64,4096]{1,0:T(8,128)(2,1)S(1)} %pad_maximum_fusion.17), channel_id=1, source_target_pairs={{0,0},{1,2},{2,1},{3,3},{4,4},{5,6},{6,5},{7,7},{8,8},{9,10},{10,9... | collective-permute-start | bytes 1572872 | tf_op jit(solution)/shard_map/ppermute | solution.py:464
  457.0 9.3 %collective-permute-start.63 = (bf16[64,1536]{1,0:T(8,128)(2,1)S(1)}, bf16[64,1536]{1,0:T(8,128)(2,1)S(1)}, u32[]{:S(2)}, u32[]{:S(2)}) collective-permute-start(bf16[64,1536]{1,0:T(8,128)(2,1)S(1)} %fusion.58), channel_id=1, source_target_pairs={{0,24},{24,0},{8,16},{16,8},{1,25},{25,1},{9,17},{17,9},{2,26},{26... | collective-permute-start | bytes 589832 | tf_op jit(solution)/shard_map/ppermute | solution.py:464
  459.5 6.8 %collective-permute-start.64 = (bf16[584,128]{1,0:T(8,128)(2,1)S(1)}, bf16[584,128]{1,0:T(8,128)(2,1)S(1)}, u32[]{:S(2)}, u32[]{:S(2)}) collective-permute-start(bf16[584,128]{1,0:T(8,128)(2,1)S(1)} %fusion.57), channel_id=1, source_target_pairs={{0,1},{1,0},{2,3},{3,2},{4,5},{5,4},{6,7},{7,6},{8,9},{9,8},{10,11... | collective-permute-start | bytes 448520 | tf_op jit(solution)/shard_map/ppermute | solution.py:464
  466.4 7.7 %collective-permute-start.66 = (bf16[64,2048]{1,0:T(8,128)(2,1)S(1)}, bf16[64,2048]{1,0:T(8,128)(2,1)S(1)}, u32[]{:S(2)}, u32[]{:S(2)}) collective-permute-start(bf16[64,2048]{1,0:T(8,128)(2,1)S(1)} %pad_maximum_fusion.20), channel_id=1, source_target_pairs={{0,0},{1,2},{2,1},{3,3},{4,4},{5,6},{6,5},{7,7},{8,8},{9,10},{10,9... | collective-permute-start | bytes 786440 | tf_op jit(solution)/shard_map/ppermute | solution.py:464
  (51 other events, 590.6 us)

commit v7 on v6

--- a/solution.py
+++ b/solution.py
@@ -1320,13 +1320,15 @@
     grad_input = moved[2]
     ffn_part = jnp.concatenate([down_part, up_part], axis=1).astype(BF)
     moved = exchange(
-        far_move(qkv_pair, z), (small.astype(BF), "y", SWAP), (tie(ffn_part, qkv_pair), CORES, TURN)
-    )
+        far_move(qkv_pair, z), (tie(ffn_part, qkv_pair), CORES, TURN)
+    )
+    (other_side,) = exchange((small.astype(BF), "y", SWAP))
     attn_part = jnp.concatenate([far_sum(qkv_pair, moved[0], z), out_part], axis=1).astype(BF)
-    small = small + moved[1].astype(F32)
-    ffn_part = moved[2].astype(F32)
+    small = small + other_side.astype(F32)
+    ffn_part = moved[1].astype(F32)
     down_part, up_part = ffn_part[:, :up_wide], ffn_part[:, up_wide:]
-    attn_part, other_small = exchange((attn_part, CORES, TURN), (small.astype(BF), "c", SWAP))
+    (attn_part,) = exchange((attn_part, CORES, TURN))
+    (other_small,) = exchange((small.astype(BF), "c", SWAP))
     attn_part = attn_part.astype(F32)
     other_small = other_small.astype(F32)
     qkv_part, out_part = attn_part[:, : 3 * half_width], attn_part[:, 3 * half_width :]

time: 489 us -> 487 us (level)
  transfers between devices with their start and end apart: 71 -> 71, of which waited for: 31 -> 33; matrix products, arithmetic and copies ran while one was open for 15% -> 16% of each run, Pallas kernels for 13% -> 13%
where the time goes in v7:
time: 487 us; the launch traced here: 482 us
  waiting for transfers between devices  151 us (31%)
  starting transfers between devices  131 us (27%)
  Pallas kernels  69.8 us (14%)
  matrix products  57 us (12%)
  local copies, waits for them, and re-layouts  38.3 us (8%)
  other arithmetic  32 us (7%)
    ppermute x54, waiting for transfers between devices, exchange(): lax.ppermute(value, axis, steps)  123 us
    ppermute x54, starting transfers between devices, exchange(): lax.ppermute(value, axis, steps)  83.2 us
    pallas_call x2, Pallas kernels, attend_back(): pl.pallas_call(partial(attend_back_kernel, group * heads), grid=(count //...  23.6 us
    dot_general x7, matrix products, contract_rows(): lax.dot_general(left, right, (((0,), (0,)), ((), ())), precision=precisio...  22.6 us
    ppermute x12, starting transfers between devices, swap(): return lax.ppermute(value, axis, SWAP)  20.2 us
    dot_general x12, matrix products, contract_cols(): lax.dot_general(left, right, (((1,), (1,)), ((), ())), precision=precisio...  17.3 us
    pallas_call x1, Pallas kernels, expand(): pl.pallas_call(expand_kernel, grid=(tiles,), in_specs=[pl.BlockSpec((coun...  16.3 us
    dot_general x4, matrix products, dot(): return jnp.dot(left, right, preferred_element_type=F32)  15.7 us
  transfers between devices with their start and end apart: 71, of which 33 were waited for; matrix products, arithmetic and copies ran while one was open for 16% of the time, Pallas kernels for 13%

profile of v7, /device:TPU:1, one launch (start us, length us, event | category | flops | bytes accessed | tf_op | source)
XLA Modules:
  0.0 482.2 jit_solution(10836686090157595473)
XLA Ops:
  1.7 4.5 collective-permute-start
  11.3 1.8 broadcast_select_fusion
  13.1 3.9 collective-permute-start.9
  17.0 3.4 collective-permute-start.3
  20.5 3.8 collective-permute-done.3
  24.4 3.7 collective-permute-start.4
  28.1 9.5 %collective-permute-done.4 = bf16[2,64,1536]{2,1,0:T(8,128)(2,1)S(1)} collective-permute-done((bf16[2,64,1536]{2,1,0:T(8,128)(2,1)S(1)}, bf16[2,64,1536]{2,1,0:T(8,128)(2,1)S(1)}, u32[]{:S(2)}, u32[]{:S(2)}) %collective-permute-start.4) | collective-permute-done | bytes 393248 | tf_op jit(solution)/shard_map/ppermute | solution.py:464
  43.0 7.0 %collective-permute-done.10 = bf16[64,2688]{1,0:T(8,128)(2,1)S(1)} collective-permute-done((bf16[64,2688]{1,0:T(8,128)(2,1)S(1)}, bf16[64,2688]{1,0:T(8,128)(2,1)S(1)}, u32[]{:S(2)}, u32[]{:S(2)}) %collective-permute-start.10) | collective-permute-done | bytes 344096 | tf_op jit(solution)/shard_map/ppermute | solution.py:464
  50.2 6.9 %collective-permute-start.11 = (bf16[2,64,2688]{2,1,0:T(8,128)(2,1)S(1)}, bf16[2,64,2688]{2,1,0:T(8,128)(2,1)S(1)}, u32[]{:S(2)}, u32[]{:S(2)}) collective-permute-start(bf16[2,64,2688]{2,1,0:T(8,128)(2,1)S(1)} %maximum_select_fusion.19), channel_id=1, source_target_pairs={{0,8},{8,0},{16,24},{24,16},{1,9},{9,1},{17,25},{25,17},{2,10},{10... | collective-permute-start | bytes 2064392 | tf_op jit(solution)/shard_map/ppermute | solution.py:464
  59.1 12.5 %collective-permute-done.11 = bf16[2,64,2688]{2,1,0:T(8,128)(2,1)S(1)} collective-permute-done((bf16[2,64,2688]{2,1,0:T(8,128)(2,1)S(1)}, bf16[2,64,2688]{2,1,0:T(8,128)(2,1)S(1)}, u32[]{:S(2)}, u32[]{:S(2)}) %collective-permute-start.11) | collective-permute-done | bytes 688160 | tf_op jit(solution)/shard_map/ppermute | solution.py:464
  73.7 3.2 collective-permute-start.12
  77.7 3.6 add_convert_fusion.own_ref.qkv_ref
  81.5 8.1 %collective-permute-start.13 = (bf16[2,64,2048]{2,1,0:T(8,128)(2,1)S(1)}, bf16[2,64,2048]{2,1,0:T(8,128)(2,1)S(1)}, u32[]{:S(2)}, u32[]{:S(2)}) collective-permute-start(bf16[2,64,2048]{2,1,0:T(8,128)(2,1)S(1)} %maximum_select_fusion.20), channel_id=1, source_target_pairs={{0,8},{8,0},{16,24},{24,16},{1,9},{9,1},{17,25},{25,17},{2,10},{10... | collective-permute-start | bytes 1572872 | tf_op jit(solution)/shard_map/ppermute | solution.py:464
  93.3 8.0 %collective-permute-done.13 = bf16[2,64,2048]{2,1,0:T(8,128)(2,1)S(1)} collective-permute-done((bf16[2,64,2048]{2,1,0:T(8,128)(2,1)S(1)}, bf16[2,64,2048]{2,1,0:T(8,128)(2,1)S(1)}, u32[]{:S(2)}, u32[]{:S(2)}) %collective-permute-start.13) | collective-permute-done | bytes 524320 | tf_op jit(solution)/shard_map/ppermute | solution.py:464
  101.6 10.4 %shard_map.254 = (bf16[1024,512]{1,0:T(8,128)(2,1)S(1)}, f32[8,1024]{1,0:T(8,128)S(1)}) custom-call(s32[2,4]{1,0:T(2,128)S(1)} %pad_add_fusion.1.bounds, bf16[1024,1536]{1,0:T(8,128)(2,1)S(1)} %add_convert_fusion.own_ref.qkv_ref, bf16[1024,1536]{1,0:T(8,128)(2,1)S(1)} %add_convert_fusion.own_ref.qkv_ref, s32[2,1024]{1,0:T(2,128)S(1)} %pad_add_fusion.spans), custom_call_target="tpu_custom_call" | custom-call | flops 2147483648 | bytes 12582912 | tf_op jit(solution)/shard_map/pallas_call | solution.py:679
  111.9 7.8 %collective-permute-done.16 = bf16[4,2,32,2688]{3,2,0,1:T(8,128)(2,1)S(1)} collective-permute-done((bf16[4,2,32,2688]{3,2,0,1:T(8,128)(2,1)S(1)}, bf16[4,2,32,2688]{3,2,0,1:T(8,128)(2,1)S(1)}, u32[]{:S(2)}, u32[]{:S(2)}) %collective-permute-start.16) | collective-permute-done | bytes 1376288 | tf_op jit(solution)/shard_map/ppermute | solution.py:464
  123.4 3.9 collective-permute-start.18
  132.2 8.9 %collective-permute-done.21 = bf16[4,32,2048]{2,1,0:T(8,128)(2,1)S(1)} collective-permute-done((bf16[4,32,2048]{2,1,0:T(8,128)(2,1)S(1)}, bf16[4,32,2048]{2,1,0:T(8,128)(2,1)S(1)}, u32[]{:S(2)}, u32[]{:S(2)}) %collective-permute-start.21) | collective-permute-done | bytes 524320 | tf_op jit(solution)/shard_map/ppermute | solution.py:464
  146.2 16.3 %shard_map.255 = (bf16[1024,2048]{1,0:T(8,128)(2,1)S(1)}, bf16[1024,2048]{1,0:T(8,128)(2,1)S(1)}) custom-call(bf16[1024,1024]{1,0:T(8,128)(2,1)S(1)} %pad_maximum_fusion.5.x_ref, bf16[1024,2688]{1,0:T(8,128)(2,1)S(1)} %bitcast.277, f32[1,2048]{1,0:T(1,128)S(1)} %slice.503.b_ref), custom_call_target="tpu_custom_call" | custom-call | flops 4294967296 | bytes 14680064 | tf_op jit(solution)/shard_map/pallas_call | solution.py:849
  162.5 2.1 copy-done.7
  164.6 4.0 collective-permute-done.23
  170.3 2.4 fusion.11
  174.2 2.5 collective-permute-start.27
  176.9 2.8 fusion.119
  185.5 4.9 %all-to-all-start = ((bf16[16,128,128]{2,1,0:T(8,128)(2,1)}), bf16[16,128,128]{2,1,0:T(8,128)(2,1)S(1)}, u32[]{:S(2)}, u32[]{:S(2)}) async-start(bf16[16,128,128]{2,1,0:T(8,128)(2,1)} %broadcast_in_dim.46), calls=%async_computation | async-start | bytes 1048576 | tf_op jit(solution)/shard_map/all_to_all | solution.py:1143
  191.6 11.4 %all-to-all-done = bf16[16,128,128]{2,1,0:T(8,128)(2,1)S(1)} async-done(((bf16[16,128,128]{2,1,0:T(8,128)(2,1)}), bf16[16,128,128]{2,1,0:T(8,128)(2,1)S(1)}, u32[]{:S(2)}, u32[]{:S(2)}) %all-to-all-start) | async-done | bytes 524320 | tf_op jit(solution)/shard_map/all_to_all | solution.py:1143
  203.0 7.0 %shard_map.256 = f32[24,2048]{1,0:T(8,128)S(1)} custom-call(bf16[2048,128]{1,0:T(8,128)(2,1)S(1)} %bitcast.284, bf16[1024,128]{1,0:T(8,128)(2,1)S(1)} %maximum_select_fusion.25.d_ref, s32[1,1024]{1,0:T(1,128)S(1)} %compare_select_fusion.seg_ref), custom_call_target="tpu_custom_call" | custom-call | flops 3221225472 | bytes 786432 | tf_op jit(solution)/shard_map/pallas_call | solution.py:904
  211.4 5.7 %all-to-all-start.1 = ((f32[16,8,128]{2,1,0:T(8,128)}), f32[16,8,128]{2,1,0:T(8,128)S(1)}, u32[]{:S(2)}, u32[]{:S(2)}) async-start(f32[16,8,128]{2,1,0:T(8,128)} %broadcast_in_dim.47), calls=%async_computation.1 | async-start | bytes 131072 | tf_op jit(solution)/shard_map/all_to_all | solution.py:1164
  217.1 5.1 %collective-permute-start.28 = (bf16[512,1024]{1,0:T(8,128)(2,1)}, bf16[512,1024]{1,0:T(8,128)(2,1)}, u32[]{:S(2)}, u32[]{:S(2)}) collective-permute-start(bf16[512,1024]{1,0:T(8,128)(2,1)} %add_convert_fusion.3), channel_id=1, source_target_pairs={{0,0},{1,2},{2,1},{3,3},{4,4},{5,6},{6,5},{7,7},{8,8},{9,10},{10,9... | collective-permute-start | bytes 3145736 | tf_op jit(solution)/shard_map/ppermute | solution.py:1184
  224.3 12.5 %shard_map.257 = (bf16[2048,128]{1,0:T(8,128)(2,1)}, f32[768,128]{1,0:T(8,128)S(1)}) custom-call(bf16[2048,128]{1,0:T(8,128)(2,1)S(1)} %bitcast.285, bf16[1024,128]{1,0:T(8,128)(2,1)S(1)} %maximum_select_fusion.25.d_ref, s32[1,1024]{1,0:T(1,128)S(1)} %compare_select_fusion.seg_ref, f32[24,2048]{1,0:T(8,128)S(1)} %convolution_divide_fusion.coef_ref), custom_call_target="tpu_custom_call" | custom-call | flops 4831838208 | bytes 1572864 | tf_op jit(solution)/shard_map/pallas_call | solution.py:980
  236.9 9.6 %all-to-all-start.2 = ((bf16[16,128,128]{2,1,0:T(8,128)(2,1)}), bf16[16,128,128]{2,1,0:T(8,128)(2,1)S(1)}, u32[]{:S(2)}, u32[]{:S(2)}) async-start(bf16[16,128,128]{2,1,0:T(8,128)(2,1)} %bitcast.57), calls=%async_computation.2 | async-start | bytes 1048576 | tf_op jit(solution)/shard_map/all_to_all | solution.py:1186
  246.5 12.1 %all-to-all-done.2 = bf16[16,128,128]{2,1,0:T(8,128)(2,1)S(1)} async-done(((bf16[16,128,128]{2,1,0:T(8,128)(2,1)}), bf16[16,128,128]{2,1,0:T(8,128)(2,1)S(1)}, u32[]{:S(2)}, u32[]{:S(2)}) %all-to-all-start.2) | async-done | bytes 524320 | tf_op jit(solution)/shard_map/all_to_all | solution.py:1186
  258.8 4.0 collective-permute-start.29
  267.9 1.8 fusion.121
  269.8 1.7 convolution_add_fusion
  272.4 6.4 %convolution_convert_fusion.1 = bf16[1024,2048]{1,0:T(8,128)(2,1)S(1)} fusion(bf16[1024,2048]{1,0:T(8,128)(2,1)S(1)} %copy-done.6, bf16[512,1024]{1,0:T(8,128)(2,1)} %collective-permute-done.30, bf16[512,1024]{1,0:T(8,128)(2,1)} %get-tuple-element.229), kind=kOutput, calls=%fused_computation.6 | convolution fusion | flops 4301258752 | bytes 10485760 | tf_op jit(solution)/shard_map/dot_general | solution.py:33
  282.9 6.6 %convert_reduce_fusion = (f32[2048]{0:T(1024)S(1)}, bf16[1024,2048]{1,0:T(8,128)(2,1)S(1)}) fusion(bf16[1024,2048]{1,0:T(8,128)(2,1)S(1)} %copy-done.8, bf16[1024,2048]{1,0:T(8,128)(2,1)S(1)} %bitcast.295, bf16[512,1024]{1,0:T(8,128)(2,1)} %collective-permute-done.30, bf16[512,1024]{1,0:T(8,128)(2,1)} %get-tuple-element.229), kind=kOutput, calls=%fused_computation | convolution fusion | flops 4309645312 | bytes 14688256 | tf_op jit(solution)/shard_map/dot_general | solution.py:448
  289.6 2.4 fusion.14
  292.3 2.4 fusion.2
  294.6 9.4 %collective-permute-done.33 = bf16[4,2,32,2048]{3,2,0,1:T(8,128)(2,1)S(1)} collective-permute-done((bf16[4,2,32,2048]{3,2,0,1:T(8,128)(2,1)S(1)}, bf16[4,2,32,2048]{3,2,0,1:T(8,128)(2,1)S(1)}, u32[]{:S(2)}, u32[]{:S(2)}) %collective-permute-start.33) | collective-permute-done | bytes 1048608 | tf_op jit(solution)/shard_map/ppermute | solution.py:464
  309.1 5.3 %convolution_convert_fusion = bf16[1024,2048]{1,0:T(8,128)(2,1)S(1)} fusion(bf16[1024,2048]{1,0:T(8,128)(2,1)S(1)} %get-tuple-element.148, bf16[512,1024]{1,0:T(8,128)(2,1)S(1)} %copy-done.35, bf16[512,1024]{1,0:T(8,128)(2,1)S(1)} %copy-done.25), kind=kOutput, calls=%fused_computation.5 | convolution fusion | flops 4301258752 | bytes 10485760 | tf_op jit(solution)/shard_map/dot_general | solution.py:33
  324.7 2.4 collective-permute-start.32
  327.2 16.1 %collective-permute-done.37 = bf16[4,2,32,2048]{3,2,0,1:T(8,128)(2,1)} collective-permute-done((bf16[4,2,32,2048]{3,2,0,1:T(8,128)(2,1)}, bf16[4,2,32,2048]{3,2,0,1:T(8,128)(2,1)}, u32[]{:S(2)}, u32[]{:S(2)}) %collective-permute-start.37) | collective-permute-done | bytes 1048608 | tf_op jit(solution)/shard_map/ppermute | solution.py:464
  350.5 3.8 convolution_convert_fusion.5.grad_ref
  354.3 3.6 convolution_convert_fusion.4
  362.9 11.7 %shard_map.258 = (bf16[1024,768]{1,0:T(8,128)(2,1)S(1)}, f32[8,256]{1,0:T(8,128)S(1)}) custom-call(s32[2,4]{1,0:T(2,128)S(1)} %pad_add_fusion.1.bounds, bf16[1024,1536]{1,0:T(8,128)(2,1)S(1)} %copy-done.4, bf16[1024,1536]{1,0:T(8,128)(2,1)S(1)} %copy-done.4, bf16[1024,512]{1,0:T(8,128)(2,1)S(1)} %get-tuple-element.123.out_ref, ...), custom_call_target="tpu_custom_call" | custom-call | flops 2684354560 | bytes 12582912 | tf_op jit(solution)/shard_map/pallas_call | solution.py:782
  374.6 1.7 collective-permute-done.42
  377.2 4.5 collective-permute-start.44
  386.1 11.9 %shard_map.259 = (bf16[1024,768]{1,0:T(8,128)(2,1)S(1)}, f32[8,256]{1,0:T(8,128)S(1)}) custom-call(s32[2,4]{1,0:T(2,128)S(1)} %pad_add_fusion.1.bounds, bf16[1024,1536]{1,0:T(8,128)(2,1)S(1)} %copy-done.4, bf16[1024,1536]{1,0:T(8,128)(2,1)S(1)} %copy-done.4, bf16[1024,512]{1,0:T(8,128)(2,1)S(1)} %get-tuple-element.123.out_ref, ...), custom_call_target="tpu_custom_call" | custom-call | flops 2684354560 | bytes 12582912 | tf_op jit(solution)/shard_map/pallas_call | solution.py:782
  398.2 3.3 collective-permute-done.47
  403.3 1.9 convolution_convert_fusion.3
  406.3 1.9 convolution_convert_fusion.2
  409.2 2.3 collective-permute-start.50
  411.6 1.8 collective-permute-start.52
  417.2 7.4 %collective-permute-done.53 = bf16[2,64,512]{2,1,0:T(8,128)(2,1)S(1)} collective-permute-done((bf16[2,64,512]{2,1,0:T(8,128)(2,1)S(1)}, bf16[2,64,512]{2,1,0:T(8,128)(2,1)S(1)}, u32[]{:S(2)}, u32[]{:S(2)}) %collective-permute-start.53) | collective-permute-done | bytes 131104 | tf_op jit(solution)/shard_map/ppermute | solution.py:464
  425.2 2.6 collective-permute-done.54
  430.9 2.2 collective-permute-start.57
  436.5 6.0 %collective-permute-start.62 = (bf16[512,1024]{1,0:T(8,128)(2,1)S(1)}, bf16[512,1024]{1,0:T(8,128)(2,1)S(1)}, u32[]{:S(2)}, u32[]{:S(2)}) collective-permute-start(bf16[512,1024]{1,0:T(8,128)(2,1)S(1)} %add_convert_fusion.1), channel_id=1, source_target_pairs={{0,0},{1,2},{2,1},{3,3},{4,4},{5,6},{6,5},{7,7},{8,8},{9,10},{10,9... | collective-permute-start | bytes 3145736 | tf_op jit(solution)/shard_map/ppermute | solution.py:464
  444.6 2.8 collective-permute-done.60
  447.4 6.0 %collective-permute-done.59 = bf16[2,64,1536]{2,1,0:T(8,128)(2,1)S(1)} collective-permute-done((bf16[2,64,1536]{2,1,0:T(8,128)(2,1)S(1)}, bf16[2,64,1536]{2,1,0:T(8,128)(2,1)S(1)}, u32[]{:S(2)}, u32[]{:S(2)}) %collective-permute-start.59) | collective-permute-done | bytes 393248 | tf_op jit(solution)/shard_map/ppermute | solution.py:464
  456.7 3.9 collective-permute-start.64
  468.7 3.6 collective-permute-start.65
  473.2 3.2 collective-permute-done.65
  478.7 2.3 copy.165
  (433 shorter events, 122.6 us)
Async XLA Ops:
  1.7 9.5 %collective-permute-start = (bf16[64,1536]{1,0:T(8,128)(2,1)S(1)}, bf16[64,1536]{1,0:T(8,128)(2,1)S(1)}, u32[]{:S(2)}, u32[]{:S(2)}) collective-permute-start(bf16[64,1536]{1,0:T(8,128)(2,1)S(1)} %slice_dynamic-update-slice_fusion), channel_id=1, source_target_pairs={{0,0},{1,2},{2,1},{3,3},{4,4},{5,6},{6,5},{7,7},{8,8},{9,10},{10,9... | collective-permute-start | bytes 589832 | tf_op jit(solution)/shard_map/ppermute | solution.py:464
  6.3 5.0 %collective-permute-start.1 = (bf16[1024,1024]{1,0:T(8,128)(2,1)}, bf16[1024,1024]{1,0:T(8,128)(2,1)}, u32[]{:S(2)}, u32[]{:S(2)}) collective-permute-start(bf16[1024,1024]{1,0:T(8,128)(2,1)} %param.15), channel_id=1, source_target_pairs={{0,2},{2,0},{1,3},{3,1},{4,6},{6,4},{5,7},{7,5},{8,10},{10,8},{9,1... | collective-permute-start | bytes 6291464 | tf_op jit(solution)/shard_map/ppermute | solution.py:464
  13.1 24.7 %collective-permute-start.9 = (bf16[64,4736]{1,0:T(8,128)(2,1)S(1)}, bf16[64,4736]{1,0:T(8,128)(2,1)}, u32[]{:S(2)}, u32[]{:S(2)}) collective-permute-start(bf16[64,4736]{1,0:T(8,128)(2,1)S(1)} %fusion.39), channel_id=1, source_target_pairs={{0,0},{1,2},{2,1},{3,3},{4,4},{5,6},{6,5},{7,7},{8,8},{9,10},{10,9... | collective-permute-start | bytes 1818632 | tf_op jit(solution)/shard_map/ppermute | solution.py:464
  17.0 7.3 %collective-permute-start.3 = (bf16[64,1536]{1,0:T(8,128)(2,1)S(1)}, bf16[64,1536]{1,0:T(8,128)(2,1)S(1)}, u32[]{:S(2)}, u32[]{:S(2)}) collective-permute-start(bf16[64,1536]{1,0:T(8,128)(2,1)S(1)} %collective-permute-done), channel_id=1, source_target_pairs={{0,24},{24,0},{8,16},{16,8},{1,25},{25,1},{9,17},{17,9},{2,26},{26... | collective-permute-start | bytes 589832 | tf_op jit(solution)/shard_map/ppermute | solution.py:464
  24.4 13.2 %collective-permute-start.4 = (bf16[2,64,1536]{2,1,0:T(8,128)(2,1)S(1)}, bf16[2,64,1536]{2,1,0:T(8,128)(2,1)S(1)}, u32[]{:S(2)}, u32[]{:S(2)}) collective-permute-start(bf16[2,64,1536]{2,1,0:T(8,128)(2,1)S(1)} %maximum_select_fusion.22), channel_id=1, source_target_pairs={{0,8},{8,0},{16,24},{24,16},{1,9},{9,1},{17,25},{25,17},{2,10},{10... | collective-permute-start | bytes 1179656 | tf_op jit(solution)/shard_map/ppermute | solution.py:464
  38.9 11.2 %collective-permute-start.10 = (bf16[64,2688]{1,0:T(8,128)(2,1)S(1)}, bf16[64,2688]{1,0:T(8,128)(2,1)S(1)}, u32[]{:S(2)}, u32[]{:S(2)}) collective-permute-start(bf16[64,2688]{1,0:T(8,128)(2,1)S(1)} %get-tuple-element.284), channel_id=1, source_target_pairs={{0,24},{24,0},{8,16},{16,8},{1,25},{25,1},{9,17},{17,9},{2,26},{26... | collective-permute-start | bytes 1032200 | tf_op jit(solution)/shard_map/ppermute | solution.py:464
  40.8 16.4 %collective-permute-start.5 = (bf16[4,32,1536]{2,1,0:T(8,128)(2,1)S(1)}, bf16[4,32,1536]{2,1,0:T(8,128)(2,1)S(1)}, u32[]{:S(2)}, u32[]{:S(2)}) collective-permute-start(bf16[4,32,1536]{2,1,0:T(8,128)(2,1)S(1)} %get-tuple-element.276), channel_id=1, source_target_pairs={{0,4},{4,0},{1,5},{5,1},{2,6},{6,2},{3,7},{7,3},{8,12},{12,8},{9,1... | collective-permute-start | bytes 1179656 | tf_op jit(solution)/shard_map/ppermute | solution.py:464
  42.0 15.1 %collective-permute-start.6 = (bf16[4,32,1536]{2,1,0:T(8,128)(2,1)S(1)}, bf16[4,32,1536]{2,1,0:T(8,128)(2,1)S(1)}, u32[]{:S(2)}, u32[]{:S(2)}) collective-permute-start(bf16[4,32,1536]{2,1,0:T(8,128)(2,1)S(1)} %get-tuple-element.275), channel_id=1, source_target_pairs={{0,1},{1,0},{2,3},{3,2},{4,5},{5,4},{6,7},{7,6},{8,9},{9,8},{10,11... | collective-permute-start | bytes 1179656 | tf_op jit(solution)/shard_map/ppermute | solution.py:464
  50.2 21.5 %collective-permute-start.11 = (bf16[2,64,2688]{2,1,0:T(8,128)(2,1)S(1)}, bf16[2,64,2688]{2,1,0:T(8,128)(2,1)S(1)}, u32[]{:S(2)}, u32[]{:S(2)}) collective-permute-start(bf16[2,64,2688]{2,1,0:T(8,128)(2,1)S(1)} %maximum_select_fusion.19), channel_id=1, source_target_pairs={{0,8},{8,0},{16,24},{24,16},{1,9},{9,1},{17,25},{25,17},{2,10},{10... | collective-permute-start | bytes 2064392 | tf_op jit(solution)/shard_map/ppermute | solution.py:464
  57.3 19.6 %collective-permute-start.7 = (bf16[4,2,32,1536]{3,2,0,1:T(8,128)(2,1)S(1)}, bf16[4,2,32,1536]{3,2,0,1:T(8,128)(2,1)S(1)}, u32[]{:S(2)}, u32[]{:S(2)}) collective-permute-start(bf16[4,2,32,1536]{3,2,0,1:T(8,128)(2,1)S(1)} %maximum_select_fusion.17), channel_id=1, source_target_pairs={{0,1},{1,0},{2,3},{3,2},{4,5},{5,4},{6,7},{7,6},{8,9},{9,8},{10,11... | collective-permute-start | bytes 2359304 | tf_op jit(solution)/shard_map/ppermute | solution.py:464
  57.5 19.4 %collective-permute-start.8 = (bf16[4,2,32,1536]{3,2,1,0:T(8,128)(2,1)S(1)}, bf16[4,2,32,1536]{3,2,1,0:T(8,128)(2,1)S(1)}, u32[]{:S(2)}, u32[]{:S(2)}) collective-permute-start(bf16[4,2,32,1536]{3,2,1,0:T(8,128)(2,1)S(1)} %maximum_select_fusion.18), channel_id=1, source_target_pairs={{0,4},{4,0},{1,5},{5,1},{2,6},{6,2},{3,7},{7,3},{8,12},{12,8},{9,1... | collective-permute-start | bytes 2359304 | tf_op jit(solution)/shard_map/ppermute | solution.py:464
  72.4 17.6 %collective-permute-start.14 = (bf16[4,32,2688]{2,1,0:T(8,128)(2,1)S(1)}, bf16[4,32,2688]{2,1,0:T(8,128)(2,1)S(1)}, u32[]{:S(2)}, u32[]{:S(2)}) collective-permute-start(bf16[4,32,2688]{2,1,0:T(8,128)(2,1)S(1)} %get-tuple-element.266), channel_id=1, source_target_pairs={{0,4},{4,0},{1,5},{5,1},{2,6},{6,2},{3,7},{7,3},{8,12},{12,8},{9,1... | collective-permute-start | bytes 2064392 | tf_op jit(solution)/shard_map/ppermute | solution.py:464
  73.7 16.3 %collective-permute-start.15 = (bf16[4,32,2688]{2,1,0:T(8,128)(2,1)S(1)}, bf16[4,32,2688]{2,1,0:T(8,128)(2,1)S(1)}, u32[]{:S(2)}, u32[]{:S(2)}) collective-permute-start(bf16[4,32,2688]{2,1,0:T(8,128)(2,1)S(1)} %get-tuple-element.265), channel_id=1, source_target_pairs={{0,1},{1,0},{2,3},{3,2},{4,5},{5,4},{6,7},{7,6},{8,9},{9,8},{10,11... | collective-permute-start | bytes 2064392 | tf_op jit(solution)/shard_map/ppermute | solution.py:464
  73.7 7.7 %collective-permute-start.12 = (bf16[64,2048]{1,0:T(8,128)(2,1)S(1)}, bf16[64,2048]{1,0:T(8,128)(2,1)S(1)}, u32[]{:S(2)}, u32[]{:S(2)}) collective-permute-start(bf16[64,2048]{1,0:T(8,128)(2,1)S(1)} %slice.390), channel_id=1, source_target_pairs={{0,24},{24,0},{8,16},{16,8},{1,25},{25,1},{9,17},{17,9},{2,26},{26... | collective-permute-start | bytes 786440 | tf_op jit(solution)/shard_map/ppermute | solution.py:464
  81.5 19.8 %collective-permute-start.13 = (bf16[2,64,2048]{2,1,0:T(8,128)(2,1)S(1)}, bf16[2,64,2048]{2,1,0:T(8,128)(2,1)S(1)}, u32[]{:S(2)}, u32[]{:S(2)}) collective-permute-start(bf16[2,64,2048]{2,1,0:T(8,128)(2,1)S(1)} %maximum_select_fusion.20), channel_id=1, source_target_pairs={{0,8},{8,0},{16,24},{24,16},{1,9},{9,1},{17,25},{25,17},{2,10},{10... | collective-permute-start | bytes 1572872 | tf_op jit(solution)/shard_map/ppermute | solution.py:464
  90.2 29.5 %collective-permute-start.16 = (bf16[4,2,32,2688]{3,2,0,1:T(8,128)(2,1)S(1)}, bf16[4,2,32,2688]{3,2,0,1:T(8,128)(2,1)S(1)}, u32[]{:S(2)}, u32[]{:S(2)}) collective-permute-start(bf16[4,2,32,2688]{3,2,0,1:T(8,128)(2,1)S(1)} %maximum_select_fusion.9), channel_id=1, source_target_pairs={{0,1},{1,0},{2,3},{3,2},{4,5},{5,4},{6,7},{7,6},{8,9},{9,8},{10,11... | collective-permute-start | bytes 4128776 | tf_op jit(solution)/shard_map/ppermute | solution.py:464
  91.6 28.8 %collective-permute-start.17 = (bf16[4,2,32,2688]{3,2,0,1:T(8,128)(2,1)S(1)}, bf16[4,2,32,2688]{3,2,0,1:T(8,128)(2,1)S(1)}, u32[]{:S(2)}, u32[]{:S(2)}) collective-permute-start(bf16[4,2,32,2688]{3,2,0,1:T(8,128)(2,1)S(1)} %maximum_select_fusion.10), channel_id=1, source_target_pairs={{0,4},{4,0},{1,5},{5,1},{2,6},{6,2},{3,7},{7,3},{8,12},{12,8},{9,1... | collective-permute-start | bytes 4128776 | tf_op jit(solution)/shard_map/ppermute | solution.py:464
  123.4 6.8 %collective-permute-start.18 = (bf16[512,1024]{1,0:T(8,128)(2,1)S(1)}, bf16[512,1024]{1,0:T(8,128)(2,1)S(1)}, u32[]{:S(2)}, u32[]{:S(2)}) collective-permute-start(bf16[512,1024]{1,0:T(8,128)(2,1)S(1)} %convolution_convert_fusion.6), channel_id=1, source_target_pairs={{0,2},{2,0},{1,3},{3,1},{4,6},{6,4},{5,7},{7,5},{8,10},{10,8},{9,1... | collective-permute-start | bytes 3145736 | tf_op jit(solution)/shard_map/ppermute | solution.py:469
  127.6 13.6 %collective-permute-start.21 = (bf16[4,32,2048]{2,1,0:T(8,128)(2,1)S(1)}, bf16[4,32,2048]{2,1,0:T(8,128)(2,1)S(1)}, u32[]{:S(2)}, u32[]{:S(2)}) collective-permute-start(bf16[4,32,2048]{2,1,0:T(8,128)(2,1)S(1)} %get-tuple-element.270), channel_id=1, source_target_pairs={{0,4},{4,0},{1,5},{5,1},{2,6},{6,2},{3,7},{7,3},{8,12},{12,8},{9,1... | collective-permute-start | bytes 1572872 | tf_op jit(solution)/shard_map/ppermute | solution.py:464
  128.7 13.2 %collective-permute-start.22 = (bf16[4,32,2048]{2,1,0:T(8,128)(2,1)S(1)}, bf16[4,32,2048]{2,1,0:T(8,128)(2,1)S(1)}, u32[]{:S(2)}, u32[]{:S(2)}) collective-permute-start(bf16[4,32,2048]{2,1,0:T(8,128)(2,1)S(1)} %get-tuple-element.269), channel_id=1, source_target_pairs={{0,1},{1,0},{2,3},{3,2},{4,5},{5,4},{6,7},{7,6},{8,9},{9,8},{10,11... | collective-permute-start | bytes 1572872 | tf_op jit(solution)/shard_map/ppermute | solution.py:464
  131.5 13.4 %collective-permute-start.19 = (bf16[512,1024]{1,0:T(8,128)(2,1)S(1)}, bf16[512,1024]{1,0:T(8,128)(2,1)S(1)}, u32[]{:S(2)}, u32[]{:S(2)}) collective-permute-start(bf16[512,1024]{1,0:T(8,128)(2,1)S(1)} %fusion.10), channel_id=1, source_target_pairs={{0,2},{2,0},{1,3},{3,1},{4,6},{6,4},{5,7},{7,5},{8,10},{10,8},{9,1... | collective-permute-start | bytes 3145736 | tf_op jit(solution)/shard_map/ppermute | solution.py:469
  144.1 24.4 %collective-permute-start.23 = (bf16[4,2,32,2048]{3,2,0,1:T(8,128)(2,1)S(1)}, bf16[4,2,32,2048]{3,2,0,1:T(8,128)(2,1)S(1)}, u32[]{:S(2)}, u32[]{:S(2)}) collective-permute-start(bf16[4,2,32,2048]{3,2,0,1:T(8,128)(2,1)S(1)} %maximum_select_fusion.13), channel_id=1, source_target_pairs={{0,1},{1,0},{2,3},{3,2},{4,5},{5,4},{6,7},{7,6},{8,9},{9,8},{10,11... | collective-permute-start | bytes 3145736 | tf_op jit(solution)/shard_map/ppermute | solution.py:464
  144.9 24.1 %collective-permute-start.24 = (bf16[4,2,32,2048]{3,2,1,0:T(8,128)(2,1)S(1)}, bf16[4,2,32,2048]{3,2,1,0:T(8,128)(2,1)S(1)}, u32[]{:S(2)}, u32[]{:S(2)}) collective-permute-start(bf16[4,2,32,2048]{3,2,1,0:T(8,128)(2,1)S(1)} %maximum_select_fusion.14), channel_id=1, source_target_pairs={{0,4},{4,0},{1,5},{5,1},{2,6},{6,2},{3,7},{7,3},{8,12},{12,8},{9,1... | collective-permute-start | bytes 3145736 | tf_op jit(solution)/shard_map/ppermute | solution.py:464
  174.2 17.4 %collective-permute-start.27 = (bf16[512,1024]{1,0:T(8,128)(2,1)}, bf16[512,1024]{1,0:T(8,128)(2,1)S(1)}, u32[]{:S(2)}, u32[]{:S(2)}) collective-permute-start(bf16[512,1024]{1,0:T(8,128)(2,1)} %param.29), channel_id=1, source_target_pairs={{0,0},{1,2},{2,1},{3,3},{4,4},{5,6},{6,5},{7,7},{8,8},{9,10},{10,9... | collective-permute-start | bytes 3145736 | tf_op jit(solution)/shard_map/ppermute | solution.py:1146
  185.5 17.5 %all-to-all-start = ((bf16[16,128,128]{2,1,0:T(8,128)(2,1)}), bf16[16,128,128]{2,1,0:T(8,128)(2,1)S(1)}, u32[]{:S(2)}, u32[]{:S(2)}) async-start(bf16[16,128,128]{2,1,0:T(8,128)(2,1)} %broadcast_in_dim.46), calls=%async_computation | async-start | bytes 1048576 | tf_op jit(solution)/shard_map/all_to_all | solution.py:1143
  211.4 12.1 %all-to-all-start.1 = ((f32[16,8,128]{2,1,0:T(8,128)}), f32[16,8,128]{2,1,0:T(8,128)S(1)}, u32[]{:S(2)}, u32[]{:S(2)}) async-start(f32[16,8,128]{2,1,0:T(8,128)} %broadcast_in_dim.47), calls=%async_computation.1 | async-start | bytes 131072 | tf_op jit(solution)/shard_map/all_to_all | solution.py:1164
  217.1 19.8 %collective-permute-start.28 = (bf16[512,1024]{1,0:T(8,128)(2,1)}, bf16[512,1024]{1,0:T(8,128)(2,1)}, u32[]{:S(2)}, u32[]{:S(2)}) collective-permute-start(bf16[512,1024]{1,0:T(8,128)(2,1)} %add_convert_fusion.3), channel_id=1, source_target_pairs={{0,0},{1,2},{2,1},{3,3},{4,4},{5,6},{6,5},{7,7},{8,8},{9,10},{10,9... | collective-permute-start | bytes 3145736 | tf_op jit(solution)/shard_map/ppermute | solution.py:1184
  236.9 21.7 %all-to-all-start.2 = ((bf16[16,128,128]{2,1,0:T(8,128)(2,1)}), bf16[16,128,128]{2,1,0:T(8,128)(2,1)S(1)}, u32[]{:S(2)}, u32[]{:S(2)}) async-start(bf16[16,128,128]{2,1,0:T(8,128)(2,1)} %bitcast.57), calls=%async_computation.2 | async-start | bytes 1048576 | tf_op jit(solution)/shard_map/all_to_all | solution.py:1186
  258.8 5.1 %collective-permute-start.29 = (f32[512,128]{1,0:T(8,128)S(1)}, f32[512,128]{1,0:T(8,128)S(1)}, u32[]{:S(2)}, u32[]{:S(2)}) collective-permute-start(f32[512,128]{1,0:T(8,128)S(1)} %constant_dynamic-slice_fusion.11), channel_id=1, source_target_pairs={{0,2},{2,0},{1,3},{3,1},{4,6},{6,4},{5,7},{7,5},{8,10},{10,8},{9,1... | collective-permute-start | bytes 786440 | tf_op jit(solution)/shard_map/ppermute | solution.py:469
  267.4 4.9 %collective-permute-start.30 = (bf16[512,1024]{1,0:T(8,128)(2,1)}, bf16[512,1024]{1,0:T(8,128)(2,1)}, u32[]{:S(2)}, u32[]{:S(2)}) collective-permute-start(bf16[512,1024]{1,0:T(8,128)(2,1)} %get-tuple-element.229), channel_id=1, source_target_pairs={{0,2},{2,0},{1,3},{3,1},{4,6},{6,4},{5,7},{7,5},{8,10},{10,8},{9,1... | collective-permute-start | bytes 3145736 | tf_op jit(solution)/shard_map/ppermute | solution.py:469
  279.4 24.7 %collective-permute-start.33 = (bf16[4,2,32,2048]{3,2,0,1:T(8,128)(2,1)S(1)}, bf16[4,2,32,2048]{3,2,0,1:T(8,128)(2,1)S(1)}, u32[]{:S(2)}, u32[]{:S(2)}) collective-permute-start(bf16[4,2,32,2048]{3,2,0,1:T(8,128)(2,1)S(1)} %bitcast.315), channel_id=1, source_target_pairs={{0,4},{4,0},{1,5},{5,1},{2,6},{6,2},{3,7},{7,3},{8,12},{12,8},{9,1... | collective-permute-start | bytes 3145736 | tf_op jit(solution)/shard_map/ppermute | solution.py:464
  280.7 24.4 %collective-permute-start.34 = (bf16[4,2,32,2048]{3,2,0,1:T(8,128)(2,1)S(1)}, bf16[4,2,32,2048]{3,2,0,1:T(8,128)(2,1)S(1)}, u32[]{:S(2)}, u32[]{:S(2)}) collective-permute-start(bf16[4,2,32,2048]{3,2,0,1:T(8,128)(2,1)S(1)} %bitcast.316), channel_id=1, source_target_pairs={{0,1},{1,0},{2,3},{3,2},{4,5},{5,4},{6,7},{7,6},{8,9},{9,8},{10,11... | collective-permute-start | bytes 3145736 | tf_op jit(solution)/shard_map/ppermute | solution.py:464
  291.9 29.6 %collective-permute-start.31 = (bf16[512,1024]{1,0:T(8,128)(2,1)S(1)}, bf16[512,1024]{1,0:T(8,128)(2,1)S(1)}, u32[]{:S(2)}, u32[]{:S(2)}) collective-permute-start(bf16[512,1024]{1,0:T(8,128)(2,1)S(1)} %fusion.14), channel_id=1, source_target_pairs={{0,2},{2,0},{1,3},{3,1},{4,6},{6,4},{5,7},{7,5},{8,10},{10,8},{9,1... | collective-permute-start | bytes 3145736 | tf_op jit(solution)/shard_map/ppermute | solution.py:469
  306.4 20.8 %collective-permute-start.35 = (bf16[4,32,2048]{2,1,0:T(8,128)(2,1)}, bf16[4,32,2048]{2,1,0:T(8,128)(2,1)}, u32[]{:S(2)}, u32[]{:S(2)}) collective-permute-start(bf16[4,32,2048]{2,1,0:T(8,128)(2,1)} %fusion.40), channel_id=1, source_target_pairs={{0,1},{1,0},{2,3},{3,2},{4,5},{5,4},{6,7},{7,6},{8,9},{9,8},{10,11... | collective-permute-start | bytes 1572872 | tf_op jit(solution)/shard_map/ppermute | solution.py:464
  308.6 18.6 %collective-permute-start.36 = (bf16[4,32,2048]{2,1,0:T(8,128)(2,1)}, bf16[4,32,2048]{2,1,0:T(8,128)(2,1)}, u32[]{:S(2)}, u32[]{:S(2)}) collective-permute-start(bf16[4,32,2048]{2,1,0:T(8,128)(2,1)} %fusion.41), channel_id=1, source_target_pairs={{0,4},{4,0},{1,5},{5,1},{2,6},{6,2},{3,7},{7,3},{8,12},{12,8},{9,1... | collective-permute-start | bytes 1572872 | tf_op jit(solution)/shard_map/ppermute | solution.py:464
  317.1 26.1 %collective-permute-start.37 = (bf16[4,2,32,2048]{3,2,0,1:T(8,128)(2,1)}, bf16[4,2,32,2048]{3,2,0,1:T(8,128)(2,1)}, u32[]{:S(2)}, u32[]{:S(2)}) collective-permute-start(bf16[4,2,32,2048]{3,2,0,1:T(8,128)(2,1)} %bitcast.272), channel_id=1, source_target_pairs={{0,4},{4,0},{1,5},{5,1},{2,6},{6,2},{3,7},{7,3},{8,12},{12,8},{9,1... | collective-permute-start | bytes 3145736 | tf_op jit(solution)/shard_map/ppermute | solution.py:464
  320.3 22.9 %collective-permute-start.38 = (bf16[4,2,32,2048]{3,2,0,1:T(8,128)(2,1)}, bf16[4,2,32,2048]{3,2,0,1:T(8,128)(2,1)}, u32[]{:S(2)}, u32[]{:S(2)}) collective-permute-start(bf16[4,2,32,2048]{3,2,0,1:T(8,128)(2,1)} %bitcast.271), channel_id=1, source_target_pairs={{0,1},{1,0},{2,3},{3,2},{4,5},{5,4},{6,7},{7,6},{8,9},{9,8},{10,11... | collective-permute-start | bytes 3145736 | tf_op jit(solution)/shard_map/ppermute | solution.py:464
  324.7 25.8 %collective-permute-start.32 = (bf16[512,1024]{1,0:T(8,128)(2,1)}, bf16[512,1024]{1,0:T(8,128)(2,1)}, u32[]{:S(2)}, u32[]{:S(2)}) collective-permute-start(bf16[512,1024]{1,0:T(8,128)(2,1)} %get-tuple-element.232), channel_id=1, source_target_pairs={{0,2},{2,0},{1,3},{3,1},{4,6},{6,4},{5,7},{7,5},{8,10},{10,8},{9,1... | collective-permute-start | bytes 3145736 | tf_op jit(solution)/shard_map/ppermute | solution.py:469
  358.3 18.0 %collective-permute-start.39 = (bf16[2,64,2048]{2,1,0:T(8,128)(2,1)S(1)}, bf16[2,64,2048]{2,1,0:T(8,128)(2,1)S(1)}, u32[]{:S(2)}, u32[]{:S(2)}) collective-permute-start(bf16[2,64,2048]{2,1,0:T(8,128)(2,1)S(1)} %select_convert_fusion.1), channel_id=1, source_target_pairs={{0,8},{8,0},{16,24},{24,16},{1,9},{9,1},{17,25},{25,17},{2,10},{10... | collective-permute-start | bytes 1572872 | tf_op jit(solution)/shard_map/ppermute | solution.py:464
  359.4 16.9 %collective-permute-start.40 = (bf16[4,32,2048]{2,1,0:T(8,128)(2,1)S(1)}, bf16[4,32,2048]{2,1,0:T(8,128)(2,1)S(1)}, u32[]{:S(2)}, u32[]{:S(2)}) collective-permute-start(bf16[4,32,2048]{2,1,0:T(8,128)(2,1)S(1)} %fusion.42), channel_id=1, source_target_pairs={{0,1},{1,0},{2,3},{3,2},{4,5},{5,4},{6,7},{7,6},{8,9},{9,8},{10,11... | collective-permute-start | bytes 1572872 | tf_op jit(solution)/shard_map/ppermute | solution.py:464
  360.8 15.6 %collective-permute-start.41 = (bf16[4,32,2048]{2,1,0:T(8,128)(2,1)S(1)}, bf16[4,32,2048]{2,1,0:T(8,128)(2,1)S(1)}, u32[]{:S(2)}, u32[]{:S(2)}) collective-permute-start(bf16[4,32,2048]{2,1,0:T(8,128)(2,1)S(1)} %fusion.43), channel_id=1, source_target_pairs={{0,4},{4,0},{1,5},{5,1},{2,6},{6,2},{3,7},{7,3},{8,12},{12,8},{9,1... | collective-permute-start | bytes 1572872 | tf_op jit(solution)/shard_map/ppermute | solution.py:464
  361.4 15.0 %collective-permute-start.42 = (bf16[4,2,32,512]{3,2,0,1:T(8,128)(2,1)S(1)}, bf16[4,2,32,512]{3,2,0,1:T(8,128)(2,1)S(1)}, u32[]{:S(2)}, u32[]{:S(2)}) collective-permute-start(bf16[4,2,32,512]{3,2,0,1:T(8,128)(2,1)S(1)} %dynamic-slice_bitcast_fusion.3), channel_id=1, source_target_pairs={{0,4},{4,0},{1,5},{5,1},{2,6},{6,2},{3,7},{7,3},{8,12},{12,8},{9,1... | collective-permute-start | bytes 786440 | tf_op jit(solution)/shard_map/ppermute | solution.py:464
  362.5 13.8 %collective-permute-start.43 = (bf16[4,2,32,512]{3,2,0,1:T(8,128)(2,1)S(1)}, bf16[4,2,32,512]{3,2,0,1:T(8,128)(2,1)S(1)}, u32[]{:S(2)}, u32[]{:S(2)}) collective-permute-start(bf16[4,2,32,512]{3,2,0,1:T(8,128)(2,1)S(1)} %dynamic-slice_bitcast_fusion.2), channel_id=1, source_target_pairs={{0,1},{1,0},{2,3},{3,2},{4,5},{5,4},{6,7},{7,6},{8,9},{9,8},{10,11... | collective-permute-start | bytes 786440 | tf_op jit(solution)/shard_map/ppermute | solution.py:464
  377.2 6.4 %collective-permute-start.44 = (f32[16,4]{1,0:T(8,128)S(1)}, f32[16,4]{1,0:T(8,128)S(1)}, u32[]{:S(2)}, u32[]{:S(2)}) collective-permute-start(f32[16,4]{1,0:T(8,128)S(1)} %reshape.820), channel_id=1, source_target_pairs={{0,2},{2,0},{1,3},{3,1},{4,6},{6,4},{5,7},{7,5},{8,10},{10,8},{9,1... | collective-permute-start | bytes 776 | tf_op jit(solution)/shard_map/ppermute | solution.py:469
  381.8 16.4 %collective-permute-start.46 = (bf16[64,2048]{1,0:T(8,128)(2,1)S(1)}, bf16[64,2048]{1,0:T(8,128)(2,1)S(1)}, u32[]{:S(2)}, u32[]{:S(2)}) collective-permute-start(bf16[64,2048]{1,0:T(8,128)(2,1)S(1)} %fusion.54), channel_id=1, source_target_pairs={{0,24},{24,0},{8,16},{16,8},{1,25},{25,1},{9,17},{17,9},{2,26},{26... | collective-permute-start | bytes 786440 | tf_op jit(solution)/shard_map/ppermute | solution.py:464
  382.6 18.9 %collective-permute-start.47 = (bf16[2,64,2048]{2,1,0:T(8,128)(2,1)S(1)}, bf16[2,64,2048]{2,1,0:T(8,128)(2,1)S(1)}, u32[]{:S(2)}, u32[]{:S(2)}) collective-permute-start(bf16[2,64,2048]{2,1,0:T(8,128)(2,1)S(1)} %select_convert_fusion), channel_id=1, source_target_pairs={{0,8},{8,0},{16,24},{24,16},{1,9},{9,1},{17,25},{25,17},{2,10},{10... | collective-permute-start | bytes 1572872 | tf_op jit(solution)/shard_map/ppermute | solution.py:464
  384.2 13.9 %collective-permute-start.48 = (bf16[4,32,512]{2,1,0:T(8,128)(2,1)S(1)}, bf16[4,32,512]{2,1,0:T(8,128)(2,1)S(1)}, u32[]{:S(2)}, u32[]{:S(2)}) collective-permute-start(bf16[4,32,512]{2,1,0:T(8,128)(2,1)S(1)} %fusion.62), channel_id=1, source_target_pairs={{0,1},{1,0},{2,3},{3,2},{4,5},{5,4},{6,7},{7,6},{8,9},{9,8},{10,11... | collective-permute-start | bytes 393224 | tf_op jit(solution)/shard_map/ppermute | solution.py:464
  385.5 12.7 %collective-permute-start.49 = (bf16[4,32,512]{2,1,0:T(8,128)(2,1)S(1)}, bf16[4,32,512]{2,1,0:T(8,128)(2,1)S(1)}, u32[]{:S(2)}, u32[]{:S(2)}) collective-permute-start(bf16[4,32,512]{2,1,0:T(8,128)(2,1)S(1)} %fusion.63), channel_id=1, source_target_pairs={{0,4},{4,0},{1,5},{5,1},{2,6},{6,2},{3,7},{7,3},{8,12},{12,8},{9,1... | collective-permute-start | bytes 393224 | tf_op jit(solution)/shard_map/ppermute | solution.py:464
  409.2 19.6 %collective-permute-start.50 = (bf16[4,2,32,1536]{3,2,0,1:T(8,128)(2,1)S(1)}, bf16[4,2,32,1536]{3,2,0,1:T(8,128)(2,1)S(1)}, u32[]{:S(2)}, u32[]{:S(2)}) collective-permute-start(bf16[4,2,32,1536]{3,2,0,1:T(8,128)(2,1)S(1)} %dynamic-slice_bitcast_fusion.1), channel_id=1, source_target_pairs={{0,4},{4,0},{1,5},{5,1},{2,6},{6,2},{3,7},{7,3},{8,12},{12,8},{9,1... | collective-permute-start | bytes 2359304 | tf_op jit(solution)/shard_map/ppermute | solution.py:464
  411.5 18.4 %collective-permute-start.51 = (bf16[4,2,32,1536]{3,2,0,1:T(8,128)(2,1)S(1)}, bf16[4,2,32,1536]{3,2,0,1:T(8,128)(2,1)S(1)}, u32[]{:S(2)}, u32[]{:S(2)}) collective-permute-start(bf16[4,2,32,1536]{3,2,0,1:T(8,128)(2,1)S(1)} %dynamic-slice_bitcast_fusion), channel_id=1, source_target_pairs={{0,1},{1,0},{2,3},{3,2},{4,5},{5,4},{6,7},{7,6},{8,9},{9,8},{10,11... | collective-permute-start | bytes 2359304 | tf_op jit(solution)/shard_map/ppermute | solution.py:464
  411.6 16.2 %collective-permute-start.52 = (bf16[64,2048]{1,0:T(8,128)(2,1)S(1)}, bf16[64,2048]{1,0:T(8,128)(2,1)S(1)}, u32[]{:S(2)}, u32[]{:S(2)}) collective-permute-start(bf16[64,2048]{1,0:T(8,128)(2,1)S(1)} %fusion.55), channel_id=1, source_target_pairs={{0,24},{24,0},{8,16},{16,8},{1,25},{25,1},{9,17},{17,9},{2,26},{26... | collective-permute-start | bytes 786440 | tf_op jit(solution)/shard_map/ppermute | solution.py:464
  413.5 11.1 %collective-permute-start.53 = (bf16[2,64,512]{2,1,0:T(8,128)(2,1)S(1)}, bf16[2,64,512]{2,1,0:T(8,128)(2,1)S(1)}, u32[]{:S(2)}, u32[]{:S(2)}) collective-permute-start(bf16[2,64,512]{2,1,0:T(8,128)(2,1)S(1)} %select_convert_fusion.6), channel_id=1, source_target_pairs={{0,8},{8,0},{16,24},{24,16},{1,9},{9,1},{17,25},{25,17},{2,10},{10... | collective-permute-start | bytes 393224 | tf_op jit(solution)/shard_map/ppermute | solution.py:464
  413.6 14.2 %collective-permute-start.54 = (bf16[584,128]{1,0:T(8,128)(2,1)S(1)}, bf16[584,128]{1,0:T(8,128)(2,1)S(1)}, u32[]{:S(2)}, u32[]{:S(2)}) collective-permute-start(bf16[584,128]{1,0:T(8,128)(2,1)S(1)} %convert_element_type.481), channel_id=1, source_target_pairs={{0,8},{8,0},{16,24},{24,16},{1,9},{9,1},{17,25},{25,17},{2,10},{10... | collective-permute-start | bytes 448520 | tf_op jit(solution)/shard_map/ppermute | solution.py:464
  424.6 10.7 %collective-permute-start.61 = (bf16[512,1024]{1,0:T(8,128)(2,1)S(1)}, bf16[512,1024]{1,0:T(8,128)(2,1)S(1)}, u32[]{:S(2)}, u32[]{:S(2)}) collective-permute-start(bf16[512,1024]{1,0:T(8,128)(2,1)S(1)} %add_convert_fusion.2), channel_id=1, source_target_pairs={{0,2},{2,0},{1,3},{3,1},{4,6},{6,4},{5,7},{7,5},{8,10},{10,8},{9,1... | collective-permute-start | bytes 3145736 | tf_op jit(solution)/shard_map/ppermute | solution.py:469
  430.2 12.4 %collective-permute-start.55 = (bf16[4,32,1536]{2,1,0:T(8,128)(2,1)S(1)}, bf16[4,32,1536]{2,1,0:T(8,128)(2,1)S(1)}, u32[]{:S(2)}, u32[]{:S(2)}) collective-permute-start(bf16[4,32,1536]{2,1,0:T(8,128)(2,1)S(1)} %fusion.49), channel_id=1, source_target_pairs={{0,1},{1,0},{2,3},{3,2},{4,5},{5,4},{6,7},{7,6},{8,9},{9,8},{10,11... | collective-permute-start | bytes 1179656 | tf_op jit(solution)/shard_map/ppermute | solution.py:464
  430.6 12.0 %collective-permute-start.56 = (bf16[4,32,1536]{2,1,0:T(8,128)(2,1)S(1)}, bf16[4,32,1536]{2,1,0:T(8,128)(2,1)S(1)}, u32[]{:S(2)}, u32[]{:S(2)}) collective-permute-start(bf16[4,32,1536]{2,1,0:T(8,128)(2,1)S(1)} %fusion.50), channel_id=1, source_target_pairs={{0,4},{4,0},{1,5},{5,1},{2,6},{6,2},{3,7},{7,3},{8,12},{12,8},{9,1... | collective-permute-start | bytes 1179656 | tf_op jit(solution)/shard_map/ppermute | solution.py:464
  430.9 11.6 %collective-permute-start.57 = (bf16[64,512]{1,0:T(8,128)(2,1)S(1)}, bf16[64,512]{1,0:T(8,128)(2,1)S(1)}, u32[]{:S(2)}, u32[]{:S(2)}) collective-permute-start(bf16[64,512]{1,0:T(8,128)(2,1)S(1)} %fusion.68), channel_id=1, source_target_pairs={{0,24},{24,0},{8,16},{16,8},{1,25},{25,1},{9,17},{17,9},{2,26},{26... | collective-permute-start | bytes 196616 | tf_op jit(solution)/shard_map/ppermute | solution.py:464
  433.2 9.4 %collective-permute-start.58 = (bf16[584,128]{1,0:T(8,128)(2,1)S(1)}, bf16[584,128]{1,0:T(8,128)(2,1)S(1)}, u32[]{:S(2)}, u32[]{:S(2)}) collective-permute-start(bf16[584,128]{1,0:T(8,128)(2,1)S(1)} %fusion.56), channel_id=1, source_target_pairs={{0,24},{24,0},{8,16},{16,8},{1,25},{25,1},{9,17},{17,9},{2,26},{26... | collective-permute-start | bytes 448520 | tf_op jit(solution)/shard_map/ppermute | solution.py:464
  436.5 18.3 %collective-permute-start.62 = (bf16[512,1024]{1,0:T(8,128)(2,1)S(1)}, bf16[512,1024]{1,0:T(8,128)(2,1)S(1)}, u32[]{:S(2)}, u32[]{:S(2)}) collective-permute-start(bf16[512,1024]{1,0:T(8,128)(2,1)S(1)} %add_convert_fusion.1), channel_id=1, source_target_pairs={{0,0},{1,2},{2,1},{3,3},{4,4},{5,6},{6,5},{7,7},{8,8},{9,10},{10,9... | collective-permute-start | bytes 3145736 | tf_op jit(solution)/shard_map/ppermute | solution.py:464
  442.9 10.5 %collective-permute-start.59 = (bf16[2,64,1536]{2,1,0:T(8,128)(2,1)S(1)}, bf16[2,64,1536]{2,1,0:T(8,128)(2,1)S(1)}, u32[]{:S(2)}, u32[]{:S(2)}) collective-permute-start(bf16[2,64,1536]{2,1,0:T(8,128)(2,1)S(1)} %select_convert_fusion.2), channel_id=1, source_target_pairs={{0,8},{8,0},{16,24},{24,16},{1,9},{9,1},{17,25},{25,17},{2,10},{10... | collective-permute-start | bytes 1179656 | tf_op jit(solution)/shard_map/ppermute | solution.py:464
  455.0 5.6 %collective-permute-start.66 = (bf16[584,128]{1,0:T(8,128)(2,1)S(1)}, bf16[584,128]{1,0:T(8,128)(2,1)S(1)}, u32[]{:S(2)}, u32[]{:S(2)}) collective-permute-start(bf16[584,128]{1,0:T(8,128)(2,1)S(1)} %fusion.57), channel_id=1, source_target_pairs={{0,1},{1,0},{2,3},{3,2},{4,5},{5,4},{6,7},{7,6},{8,9},{9,8},{10,11... | collective-permute-start | bytes 448520 | tf_op jit(solution)/shard_map/ppermute | solution.py:464
  455.1 11.4 %collective-permute-start.63 = (bf16[64,1536]{1,0:T(8,128)(2,1)S(1)}, bf16[64,1536]{1,0:T(8,128)(2,1)S(1)}, u32[]{:S(2)}, u32[]{:S(2)}) collective-permute-start(bf16[64,1536]{1,0:T(8,128)(2,1)S(1)} %fusion.58), channel_id=1, source_target_pairs={{0,24},{24,0},{8,16},{16,8},{1,25},{25,1},{9,17},{17,9},{2,26},{26... | collective-permute-start | bytes 589832 | tf_op jit(solution)/shard_map/ppermute | solution.py:464
  456.7 11.0 %collective-permute-start.64 = (bf16[64,4096]{1,0:T(8,128)(2,1)}, bf16[64,4096]{1,0:T(8,128)(2,1)S(1)}, u32[]{:S(2)}, u32[]{:S(2)}) collective-permute-start(bf16[64,4096]{1,0:T(8,128)(2,1)} %pad_maximum_fusion.17), channel_id=1, source_target_pairs={{0,0},{1,2},{2,1},{3,3},{4,4},{5,6},{6,5},{7,7},{8,8},{9,10},{10,9... | collective-permute-start | bytes 1572872 | tf_op jit(solution)/shard_map/ppermute | solution.py:464
  468.7 7.7 %collective-permute-start.65 = (bf16[64,2048]{1,0:T(8,128)(2,1)S(1)}, bf16[64,2048]{1,0:T(8,128)(2,1)S(1)}, u32[]{:S(2)}, u32[]{:S(2)}) collective-permute-start(bf16[64,2048]{1,0:T(8,128)(2,1)S(1)} %pad_maximum_fusion.20), channel_id=1, source_target_pairs={{0,0},{1,2},{2,1},{3,3},{4,4},{5,6},{6,5},{7,7},{8,8},{9,10},{10,9... | collective-permute-start | bytes 786440 | tf_op jit(solution)/shard_map/ppermute | solution.py:464
  (51 other events, 590.9 us)
